TPU v7x, 32 devices: a whole 2x2x4 slice. The times are simulated.
32 devices in a mesh: rad: 4 (over x, core), col: 8 (over z, y).
Axes of the slice: x: 2, y: 2, z: 4, core: 2. Of those that a mesh axis runs over, the one named last changes fastest.
Arguments:
- cotangent: float32 [512, 3, 128, 256], P('rad', None, 'col'), may hold values from -6 to 6
- state_axial: float32 [512, 128, 256], P('rad', 'col'), may hold values from -6 to 6
- helm_inverse: float32 [3, 512, 512], P(None, None, 'rad'), as said below
- rotation_rate: float32 [512], P('rad'), may hold values from 0.5 to 2
Outputs:
- gradient: float32 [512, 3, 128, 256], P('rad', None, 'col')
Inputs may be any that keep to these rules, and one draw needn't show every extreme that they name: `helm_inverse`: entries of every matrix lie between -1 and 2.
All inputs are finite; a program needn't handle non-finite values.
Results may differ from a plain program's by a relative error of at most 0.00018.
Values sent between devices are 32-bit elements; how exact they have to be, the bound alone decides.
No kernel may reach another device: no remote copies, remote signals or barrier semaphores. Data moves between devices by JAX's collectives and lax.ppermute only.
A program may use at most 128 MiB of HBM per device.

v0:
```python
import jax
import jax.numpy as jnp
from jax import lax
from jax.sharding import PartitionSpec as P

SECTIONS = 2


diffusion_coeff = 0.2
advection_coeff = 0.15
rotation_coeff = 0.25


def padded_2(array, sides, width):
    for axis, dim in sides:
        peers, length = (lax.axis_size(axis), array.shape[dim])
        up = [(i, (i + 1) % peers) for i in range(peers)]
        down = [(j, i) for i, j in up]
        last = lax.slice_in_dim(array, length - width, length, axis=dim)
        leading = lax.slice_in_dim(array, 0, width, axis=dim)
        before = lax.ppermute(last, axis, up)
        after = lax.ppermute(leading, axis, down)
        array = jnp.concatenate([before, array, after], axis=dim)
    return array


def axial_adjoint(current, state_axial, rotation_rate):
    padded = padded_2(current, (("col", 2),), 1)
    upper = padded[:, :, 2:]
    lower = padded[:, :, :-2]
    laplace = upper - 2.0 * current + lower
    transport = state_axial[:, None] * (lower - upper)
    rate = rotation_rate[:, None, None]
    turning = jnp.stack(
        (rate * current[:, 1], -rate * current[:, 0], jnp.zeros_like(current[:, 2])), axis=1
    )
    return (
        current + diffusion_coeff * laplace + advection_coeff * transport + rotation_coeff * turning
    )


def on_device(cotangent, state_axial, helm_inverse, rotation_rate):
    current = cotangent
    for section_index in range(SECTIONS):
        stenciled = axial_adjoint(current, state_axial, rotation_rate)
        current = jnp.einsum(
            "cji,jczp->iczp",
            helm_inverse,
            lax.all_gather(stenciled, "rad", axis=0, tiled=True),
            precision=lax.Precision.HIGHEST,
        )
    return current


def solution(mesh):
    in_specs = (P("rad", None, "col", None), P("rad", "col", None), P(None, None, "rad"), P("rad"))
    out_specs = P("rad", None, "col", None)
    return jax.shard_map(
        on_device, mesh=mesh, in_specs=in_specs, out_specs=out_specs, check_vma=False
    )
```

profile of v0, /device:TPU:0, one launch (start us, length us, event | category | flops | bytes accessed | tf_op | source)
XLA Modules:
  0.0 447.5 jit_solution(570968864435880623)
XLA Ops:
  6.5 0.0 copy-start
  6.5 0.0 copy-start.3
  6.5 0.0 all-gather.3.cloned.1.call-start
  6.5 6.6 %copy.10 = f32[128,3,16,256]{0,3,2,1:T(8,128)} copy(f32[128,3,16,256]{3,2,1,0:T(8,128)} %param.4) | data formatting | bytes 12582912 | tf_op args[0]
  13.2 1.9 fusion.5
  15.1 6.0 %collective-permute-start = (f32[128,3,1,256]{0,3,2,1:T(8,128)}, f32[128,3,1,256]{0,3,2,1:T(8,128)}, u32[]{:S(2)}, u32[]{:S(2)}) collective-permute-start(f32[128,3,1,256]{0,3,2,1:T(8,128)} %get-tuple-element.9), channel_id=1, source_target_pairs={{1,0},{2,1},{3,2},{4,3},{5,4},{6,5},{7,6},{0,7},{9,8},{10,9},{11,1... | collective-permute-start | bytes 1179656 | tf_op jit(solution)/shard_map/ppermute | solution.py:22
  21.1 0.0 collective-permute-start.1
  21.1 0.0 copy-done.3
  21.1 0.0 slice-start
  21.1 3.1 copy.11
  24.3 0.0 copy-start.1
  24.3 0.1 pad.9.clone
  24.3 0.0 slice-start.1
  24.3 2.8 slice_multiply_fusion.3
  27.2 8.7 %collective-permute-done = f32[128,3,1,256]{0,3,2,1:T(8,128)} collective-permute-done((f32[128,3,1,256]{0,3,2,1:T(8,128)}, f32[128,3,1,256]{0,3,2,1:T(8,128)}, u32[]{:S(2)}, u32[]{:S(2)}) %collective-permute-start) | collective-permute-done | bytes 393248 | tf_op jit(solution)/shard_map/ppermute | solution.py:22
  35.9 0.1 collective-permute-done.1
  36.0 0.0 slice-done
  36.0 0.0 copy-done.1
  36.0 0.0 slice-done.1
  36.0 5.7 %fusion = f32[128,3,16,256]{0,3,2,1:T(8,128)} fusion(f32[128,1,16,256]{0,3,2,1:T(8,128)S(1)} %get-tuple-element.12, f32[128,1,16,256]{0,3,2,1:T(8,128)S(1)} %get-tuple-element.11, f32[128,3,16,256]{0,3,2,1:T(8,128)S(1)} %bitcast.15, f32[128,3,1,256]{0,3,2,1:T(8,128)} %collective-permute-done.1, f32[128,3,1,256]{0,3,2,1:T(8,128)} %collective-permute-done, ...), kind=kLoop, calls=%fused_computation.5 | loop fusion | flops 23592960 | bytes 19660812 | tf_op jit(solution)/shard_map/add | solution.py:38
  41.6 0.0 all-gather.3.cloned.1.call-update
  41.7 0.0 all-gather.5.cloned.1.call-start
  41.7 159.7 %all-gather.3.cloned.1.call-done = f32[512,3,16,256]{0,3,2,1:T(8,128)} async-done(((f32[128,3,16,256]{0,3,2,1:T(8,128)}), f32[512,3,16,256]{0,3,2,1:T(8,128)}) %all-gather.3.cloned.1.call-update) | async-done | bytes 25165840 | tf_op jit(solution)/shard_map/all_gather | solution.py:49
  201.4 0.0 copy-done
  201.4 24.3 %convolution_bitcast_fusion.1 = f32[128,3,16,256]{0,3,2,1:T(8,128)S(1)} fusion(f32[512,3,16,256]{0,3,2,1:T(8,128)} %all-gather.3.cloned.1.call-done, f32[3,512,128]{2,1,0:T(8,128)S(1)} %copy-done), kind=kOutput, calls=%fused_computation.9 | convolution fusion | flops 9663676416 | bytes 32243712 | tf_op jit(solution)/shard_map/cji,jczp->iczp/dot_general | solution.py:46
  225.8 0.0 copy-start.2
  225.8 0.1 fusion.4
  225.9 4.3 collective-permute-start.2
  230.2 0.0 collective-permute-start.3
  230.2 0.6 slice_multiply_fusion.1
  230.7 14.9 %collective-permute-done.2 = f32[128,3,1,256]{0,3,2,1:T(8,128)S(1)} collective-permute-done((f32[128,3,1,256]{0,3,2,1:T(8,128)S(1)}, f32[128,3,1,256]{0,3,2,1:T(8,128)S(1)}, u32[]{:S(2)}, u32[]{:S(2)}) %collective-permute-start.2) | collective-permute-done | bytes 393248 | tf_op jit(solution)/shard_map/ppermute | solution.py:22
  245.6 0.0 collective-permute-done.3
  245.6 0.0 copy-done.2
  245.6 4.9 %fusion.1 = f32[128,3,16,256]{0,3,2,1:T(8,128)} fusion(f32[128,1,16,256]{0,3,2,1:T(8,128)S(1)} %get-tuple-element.8, f32[128,1,16,256]{0,3,2,1:T(8,128)S(1)} %get-tuple-element.7, f32[128,3,16,256]{0,3,2,1:T(8,128)S(1)} %convolution_bitcast_fusion.1, f32[128,3,1,256]{0,3,2,1:T(8,128)S(1)} %collective-permute-done.3, ...), kind=kLoop, calls=%fused_computation.7 | loop fusion | flops 23592960 | bytes 19660812 | tf_op jit(solution)/shard_map/add | solution.py:38
  250.6 0.0 all-gather.5.cloned.1.call-update
  250.6 158.6 %all-gather.5.cloned.1.call-done = f32[512,3,16,256]{0,3,2,1:T(8,128)} async-done(((f32[128,3,16,256]{0,3,2,1:T(8,128)}), f32[512,3,16,256]{0,3,2,1:T(8,128)}) %all-gather.5.cloned.1.call-update) | async-done | bytes 25165840 | tf_op jit(solution)/shard_map/all_gather | solution.py:49
  409.2 24.9 %convolution_bitcast_fusion = f32[128,3,16,256]{0,3,2,1:T(8,128)} fusion(f32[512,3,16,256]{0,3,2,1:T(8,128)} %all-gather.5.cloned.1.call-done, f32[3,512,128]{2,1,0:T(8,128)S(1)} %copy-done), kind=kOutput, calls=%fused_computation.8 | convolution fusion | flops 9663676416 | bytes 32243712 | tf_op jit(solution)/shard_map/cji,jczp->iczp/dot_general | solution.py:46
  434.1 6.6 %copy.14 = f32[128,3,16,256]{3,2,1,0:T(8,128)} copy(f32[128,3,16,256]{0,3,2,1:T(8,128)} %convolution_bitcast_fusion) | data formatting | bytes 12582912 | tf_op jit(solution)/shard_map/cji,jczp->iczp/transpose | solution.py:46
  (2 shorter events, 0.0 us)
Async XLA Ops:
  6.5 194.9 %copy-start = (f32[3,512,128]{2,1,0:T(8,128)S(1)}, f32[3,512,128]{2,1,0:T(8,128)}, u32[]{:S(2)}) copy-start(f32[3,512,128]{2,1,0:T(8,128)} %param.6) | copy-start | bytes 2359300
  6.5 14.6 %copy-start.3 = (f32[128]{0:T(128)S(1)}, f32[128]{0:T(128)}, u32[]{:S(2)}) copy-start(f32[128]{0:T(128)} %param.7) | copy-start | bytes 1540
  6.5 194.9 %all-gather.3.cloned.1.call-start = ((), (), s32[]{:S(2)}) async-start(), calls=%async_computation | async-start | bytes 31457280 | tf_op jit(solution)/shard_map/all_gather | solution.py:49
  15.1 20.8 %collective-permute-start = (f32[128,3,1,256]{0,3,2,1:T(8,128)}, f32[128,3,1,256]{0,3,2,1:T(8,128)}, u32[]{:S(2)}, u32[]{:S(2)}) collective-permute-start(f32[128,3,1,256]{0,3,2,1:T(8,128)} %get-tuple-element.9), channel_id=1, source_target_pairs={{1,0},{2,1},{3,2},{4,3},{5,4},{6,5},{7,6},{0,7},{9,8},{10,9},{11,1... | collective-permute-start | bytes 1179656 | tf_op jit(solution)/shard_map/ppermute | solution.py:22
  21.1 14.9 %collective-permute-start.1 = (f32[128,3,1,256]{0,3,2,1:T(8,128)S(1)}, f32[128,3,1,256]{0,3,2,1:T(8,128)}, u32[]{:S(2)}, u32[]{:S(2)}) collective-permute-start(f32[128,3,1,256]{0,3,2,1:T(8,128)S(1)} %get-tuple-element.10), channel_id=1, source_target_pairs={{0,1},{1,2},{2,3},{3,4},{4,5},{5,6},{6,7},{7,0},{8,9},{9,10},{10,1... | collective-permute-start | bytes 1179656 | tf_op jit(solution)/shard_map/ppermute | solution.py:21
  21.1 14.9 %slice-start = ((s8[6291456]{0:T(1024)(128)(4,1)}), s8[2097152]{0:T(1024)(128)(4,1)S(1)}, s32[]{:S(2)}) async-start(s8[6291456]{0:T(1024)(128)(4,1)} %bitcast.14), calls=%async_computation.2 | async-start | bytes 4194304
  24.3 11.7 %copy-start.1 = (f32[128,16,256]{0,2,1:T(8,128)S(1)}, f32[128,16,256]{0,2,1:T(8,128)}, u32[]{:S(2)}) copy-start(f32[128,16,256]{0,2,1:T(8,128)} %copy.11) | copy-start | bytes 6291460
  24.3 11.6 %slice-start.1 = ((s8[6291456]{0:T(1024)(128)(4,1)}), s8[4194304]{0:T(1024)(128)(4,1)S(1)}, s32[]{:S(2)}) async-start(s8[6291456]{0:T(1024)(128)(4,1)} %bitcast.14), calls=%async_computation.3 | async-start | bytes 8388608
  41.7 367.5 %all-gather.5.cloned.1.call-start = ((), (), s32[]{:S(2)}) async-start(), calls=%async_computation.1 | async-start | bytes 31457280 | tf_op jit(solution)/shard_map/all_gather | solution.py:49
  225.8 19.8 %copy-start.2 = (f32[128,16,256]{0,2,1:T(8,128)S(1)}, f32[128,16,256]{0,2,1:T(8,128)}, u32[]{:S(2)}) copy-start(f32[128,16,256]{0,2,1:T(8,128)} %copy.11) | copy-start | bytes 6291460
  225.9 19.8 %collective-permute-start.2 = (f32[128,3,1,256]{0,3,2,1:T(8,128)S(1)}, f32[128,3,1,256]{0,3,2,1:T(8,128)S(1)}, u32[]{:S(2)}, u32[]{:S(2)}) collective-permute-start(f32[128,3,1,256]{0,3,2,1:T(8,128)S(1)} %get-tuple-element.5), channel_id=1, source_target_pairs={{1,0},{2,1},{3,2},{4,3},{5,4},{6,5},{7,6},{0,7},{9,8},{10,9},{11,1... | collective-permute-start | bytes 1179656 | tf_op jit(solution)/shard_map/ppermute | solution.py:22
  230.2 15.5 %collective-permute-start.3 = (f32[128,3,1,256]{0,3,2,1:T(8,128)S(1)}, f32[128,3,1,256]{0,3,2,1:T(8,128)S(1)}, u32[]{:S(2)}, u32[]{:S(2)}) collective-permute-start(f32[128,3,1,256]{0,3,2,1:T(8,128)S(1)} %get-tuple-element.6), channel_id=1, source_target_pairs={{0,1},{1,2},{2,3},{3,4},{4,5},{5,6},{6,7},{7,0},{8,9},{9,10},{10,1... | collective-permute-start | bytes 1179656 | tf_op jit(solution)/shard_map/ppermute | solution.py:21
Sparse Core Ops, SparseCore 0:
  41.8 159.6 all-gather.2
  250.7 158.4 all-gather.4
where the time goes:
time: 448 us
  waiting for transfers between devices  342 us (76%)
  matrix products  49.3 us (11%)
  local copies, waits for them, and re-layouts  18.4 us (4%)
  other arithmetic  14 us (3%)
  between operations  13.5 us (3%)
  starting transfers between devices  10.3 us (2%)
    all_gather x2, waiting for transfers between devices, on_device(): lax.all_gather(stenciled, 'rad', axis=0, tiled=True)  318 us
    dot_general x2, matrix products, on_device(): jnp.einsum('cji,jczp->iczp', helm_inverse, lax.all_gather(stenciled, 'rad...  49.3 us
    ppermute x2, waiting for transfers between devices, padded_2(): after = lax.ppermute(leading, axis, down)  23.6 us
    add x2, other arithmetic, axial_adjoint(): current + diffusion_coeff * laplace + advection_coeff * transport  10.6 us
    ppermute x2, starting transfers between devices, padded_2(): after = lax.ppermute(leading, axis, down)  10.3 us
    unnamed x14, local copies, waits for them, and re-layouts  9.81 us
  transfers between devices with their start and end apart: 6, of which 5 were waited for; matrix products, arithmetic and copies ran while one was open for 1% of the time, Pallas kernels for 0%

commit v1 on v0

v1 whole, which is shorter than its diff:
```python
import jax
import jax.numpy as jnp
from jax import lax
from jax.experimental import pallas as pl
from jax.experimental.pallas import tpu as pltpu
from jax.sharding import PartitionSpec as P

SECTIONS = 2
CHUNKS = 4

diffusion_coeff = 0.2
advection_coeff = 0.15
rotation_coeff = 0.25

F32 = jnp.float32
BF16 = jnp.bfloat16
MB = 1 << 20


def shape(dims, dtype=F32):
    return jax.ShapeDtypeStruct(dims, dtype)


def cost(flops, moved):
    return pl.CostEstimate(flops=int(flops), bytes_accessed=int(moved), transcendentals=0)


def params(limit=40):
    return pltpu.CompilerParams(vmem_limit_bytes=limit * MB)


def stencil(cur, upper, lower, other, state):
    up = diffusion_coeff - advection_coeff * state
    down = diffusion_coeff + advection_coeff * state
    out = (1.0 - 2.0 * diffusion_coeff) * cur + up * upper + down * lower
    return out if other is None else out + other


def split(values):
    high = values.astype(BF16)
    return high, (values - high.astype(F32)).astype(BF16)


def product(x_parts, h_high, h_low):
    pairs = [split(x) for x in x_parts]
    high = jnp.concatenate([p[0] for p in pairs], axis=1)
    low = jnp.concatenate([p[1] for p in pairs], axis=1)

    def dot(a, b):
        return jnp.dot(a, b, preferred_element_type=F32)

    return dot(high, h_high) + (dot(high, h_low) + dot(low, h_high))


def state_kernel(where, state, rate, out, *, modes, nz):
    width = state.shape[1]
    for z in range(nz):
        out[z * width : (z + 1) * width, :] = state[pl.ds(z, modes, stride=nz), :].T
    if out.shape[0] > nz * width:
        out[nz * width :, :] = jnp.broadcast_to(rate[...], (out.shape[0] - nz * width, modes))


def turn_state(where, state, rate, foreign, extra):
    modes, nz, nphi = state.shape
    half = nphi // 2
    side = (lambda i, w: (0, 1 - (w[0] >> 1))) if foreign else (lambda i, w: (0, w[0] >> 1))
    rows = nz * half + extra
    return pl.pallas_call(
        lambda *refs: state_kernel(*refs, modes=modes, nz=nz),
        out_shape=shape((rows, modes)),
        grid_spec=pltpu.PrefetchScalarGridSpec(
            num_scalar_prefetch=1,
            grid=(1,),
            in_specs=[pl.BlockSpec((modes * nz, half), side), pl.BlockSpec((1, modes), lambda i, w: (0, 0))],
            out_specs=pl.BlockSpec((rows, modes), lambda i, w: (0, 0)),
        ),
        compiler_params=params(16),
        cost_estimate=cost(rows * modes, 8 * rows * modes),
        name="turn_state",
    )(where, state.reshape(modes * nz, nphi), rate)


def first_kernel(where, cot, state, after, before, rate, *rest, modes, nz, chunks):
    outs, turned = rest[:-1], rest[-1]
    half = cot.shape[1]
    width = half // chunks
    for c in range(3):
        turned[c, 0] = before[c * modes : (c + 1) * modes, :].T
        for z in range(nz):
            turned[c, z + 1] = cot[pl.ds(c * nz + z, modes, stride=3 * nz), :].T
        turned[c, nz + 1] = after[c * modes : (c + 1) * modes, :].T
    turn = rotation_coeff * rate[...]
    for z in range(nz):
        for k in range(chunks):
            at = slice(k * width, (k + 1) * width)
            st = state[z * half + k * width : z * half + (k + 1) * width, :]
            cur = [turned[c, z + 1, at, :] for c in range(3)]
            others = (turn * cur[1], -turn * cur[0], None)
            for c in range(3):
                outs[k][c, z] = stencil(cur[c], turned[c, z + 2, at, :], turned[c, z, at, :], others[c], st)


def first_stencil(where, cot, state_turned, after, before, rate, foreign, chunks):
    modes, comps, nz, nphi = cot.shape
    half = nphi // 2
    side = (lambda i, w: (0, 1 - (w[0] >> 1))) if foreign else (lambda i, w: (0, w[0] >> 1))
    whole = lambda i, w: (0, 0)
    out = (comps, nz, half // chunks, modes)
    return pl.pallas_call(
        lambda *refs: first_kernel(*refs, modes=modes, nz=nz, chunks=chunks),
        out_shape=[shape(out)] * chunks,
        grid_spec=pltpu.PrefetchScalarGridSpec(
            num_scalar_prefetch=1,
            grid=(1,),
            in_specs=[
                pl.BlockSpec((modes * comps * nz, half), side),
                pl.BlockSpec((nz * half, modes), whole),
                pl.BlockSpec((comps * modes, half), side),
                pl.BlockSpec((comps * modes, half), side),
                pl.BlockSpec((1, modes), whole),
            ],
            out_specs=[pl.BlockSpec(out, lambda i, w: (0, 0, 0, 0))] * chunks,
            scratch_shapes=[pltpu.VMEM((comps, nz + 2, half, modes), F32)],
        ),
        compiler_params=params(32),
        cost_estimate=cost(12 * modes * comps * nz * half, 8 * modes * comps * nz * half),
        name="first_stencil",
    )(where, cot.reshape(modes * comps * nz, nphi), state_turned, after, before, rate)


def helm_kernel(where, own, far, high, low):
    for g, part in enumerate((own, far)):
        h, l = split(part[...])
        cols = slice(g * part.shape[2], (g + 1) * part.shape[2])
        high[:, :, cols] = h
        low[:, :, cols] = l


def split_helm(where, own, far):
    comps, rows, modes = own.shape
    block = lambda k, w: (0, w[0] ^ (((k & 1) << 1) | (k >> 1)), 0)
    out = (comps, rows, 2 * modes)
    return pl.pallas_call(
        helm_kernel,
        out_shape=[shape(out, BF16)] * 2,
        grid_spec=pltpu.PrefetchScalarGridSpec(
            num_scalar_prefetch=1,
            grid=(rows // modes,),
            in_specs=[pl.BlockSpec((comps, modes, modes), block)] * 2,
            out_specs=[pl.BlockSpec((comps, modes, 2 * modes), lambda k, w: (0, k, 0))] * 2,
        ),
        compiler_params=params(16),
        cost_estimate=cost(4 * comps * rows * modes, 16 * comps * rows * modes),
        name="split_helm",
    )(where, own, far)


def map1_kernel(own, far, own_peer, far_peer, high, low, out, first, last):
    _, nz, width, modes = own.shape
    rows = nz * width
    parts = [ref[0].reshape(rows, modes) for ref in (own, far, own_peer, far_peer)]
    res = product(parts, high[0], low[0]).reshape(nz, width, high.shape[2])
    out[0] = res
    first[0] = res[0]
    last[0] = res[nz - 1]


def map1(own, far, own_peer, far_peer, high, low, k):
    comps, nz, width, modes = far.shape
    rows, cols = high.shape[1:]
    here = pl.BlockSpec((1, nz, width, modes), lambda c: (c, 0, k, 0))
    chunk = pl.BlockSpec((1, nz, width, modes), lambda c: (c, 0, 0, 0))
    helm = pl.BlockSpec((1, rows, cols), lambda c: (c, 0, 0))
    layer = pl.BlockSpec((1, width, cols), lambda c: (c, 0, 0))
    return pl.pallas_call(
        map1_kernel,
        out_shape=[shape((comps, nz, width, cols)), shape((comps, width, cols)), shape((comps, width, cols))],
        grid=(comps,),
        in_specs=[here, chunk, here, chunk, helm, helm],
        out_specs=[pl.BlockSpec((1, nz, width, cols), lambda c: (c, 0, 0, 0)), layer, layer],
        compiler_params=params(24),
        cost_estimate=cost(6 * comps * nz * width * rows * cols, 4 * comps * (nz * width * (rows + cols) + rows * cols)),
        name=f"map1_{k}",
    )(own, far, own_peer, far_peer, high, low)


def second_kernel(cur, after, before, state_own, state_far, rate, out, *, k, half):
    comps, nz, width, cols = cur.shape
    modes = cols // 2
    rates = (rate[...], state_far[nz * half : nz * half + 1, :])
    for g in range(2):
        lanes = slice(g * modes, (g + 1) * modes)
        turn = rotation_coeff * rates[g]
        state = (state_own, state_far)[g]
        for z in range(nz):
            st = state[z * half + k * width : z * half + (k + 1) * width, :]
            here = [cur[c, z, :, lanes] for c in range(comps)]
            others = (turn * here[1], -turn * here[0], None)
            for c in range(comps):
                upper = cur[c, z + 1, :, lanes] if z + 1 < nz else after[c, :, lanes]
                lower = cur[c, z - 1, :, lanes] if z else before[c, :, lanes]
                out[c, z, :, lanes] = stencil(here[c], upper, lower, others[c], st)


def second_stencil(cur, after, before, state_own, state_far, rate, k, half):
    return pl.pallas_call(
        lambda *refs: second_kernel(*refs, k=k, half=half),
        out_shape=shape(cur.shape),
        compiler_params=params(16),
        cost_estimate=cost(12 * cur.size, 8 * cur.size),
        name=f"second_stencil_{k}",
    )(cur, after, before, state_own, state_far, rate)


def map2_kernel(own, peer, high, low, out_own, out_far):
    _, nz, width, cols = own.shape
    parts = [ref[0].reshape(nz * width, cols) for ref in (own, peer)]
    res = product(parts, high[0], low[0]).reshape(nz, width, cols)
    out_own[0] = res[:, :, : cols // 2]
    out_far[0] = res[:, :, cols // 2 :]


def map2(own, peer, high, low, k):
    comps, nz, width, cols = own.shape
    rows = high.shape[1]
    chunk = pl.BlockSpec((1, nz, width, cols), lambda c: (c, 0, 0, 0))
    helm = pl.BlockSpec((1, rows, cols), lambda c: (c, 0, 0))
    out = (comps, nz, width, cols // 2)
    return pl.pallas_call(
        map2_kernel,
        out_shape=[shape(out)] * 2,
        grid=(comps,),
        in_specs=[chunk, chunk, helm, helm],
        out_specs=[pl.BlockSpec((1, nz, width, cols // 2), lambda c: (c, 0, 0, 0))] * 2,
        compiler_params=params(24),
        cost_estimate=cost(6 * comps * nz * width * rows * cols, 4 * comps * (nz * width * (rows + cols) + rows * cols)),
        name=f"map2_{k}",
    )(own, peer, high, low)


def last_kernel(where, *refs, nz, chunks, extra):
    ins, out = refs[:chunks], refs[-1]
    width, modes = ins[0].shape[2:]
    for c in range(ins[0].shape[0]):
        for z in range(nz):
            whole = jnp.concatenate([ref[c, z] for ref in ins], axis=0)
            out[pl.ds(c * nz + z, modes, stride=3 * nz), :] = whole.T


def write_half(where, pieces, nphi, foreign, base=None):
    comps, nz, width, modes = pieces[0].shape
    chunks = len(pieces)
    side = (lambda i, w: (0, 1 - (w[0] >> 1))) if foreign else (lambda i, w: (0, w[0] >> 1))
    rows = modes * comps * nz
    extra = () if base is None else (base,)
    return pl.pallas_call(
        lambda *refs: last_kernel(*refs, nz=nz, chunks=chunks, extra=len(extra)),
        out_shape=shape((rows, nphi)),
        grid_spec=pltpu.PrefetchScalarGridSpec(
            num_scalar_prefetch=1,
            grid=(1,),
            in_specs=[pl.BlockSpec(p.shape, lambda i, w: (0, 0, 0, 0)) for p in pieces]
            + [pl.BlockSpec(memory_space=pl.ANY)] * len(extra),
            out_specs=pl.BlockSpec((rows, nphi // 2), side),
        ),
        input_output_aliases={1 + chunks: 0} if extra else {},
        compiler_params=params(24),
        cost_estimate=cost(rows * nphi, 4 * rows * nphi),
        name="write_foreign" if foreign else "write_own",
    )(where, *pieces, *extra)


def on_device(cotangent, state_axial, helm_inverse, rotation_rate):
    modes, comps, nz, nphi = cotangent.shape
    half = nphi // 2
    peers, cols = lax.axis_size("rad"), lax.axis_size("col")
    up = [(i, (i + 1) % cols) for i in range(cols)]
    down = [(j, i) for i, j in up]

    def across(array):
        return lax.ppermute(array, "rad", [(i, i ^ 2) for i in range(peers)])

    def beside(array):
        return lax.ppermute(array, "rad", [(i, i ^ 1) for i in range(peers)])

    where = lax.axis_index("rad").astype(jnp.int32).reshape(1)
    rate = rotation_rate.reshape(1, modes)

    helm_far = across(helm_inverse)
    state_foreign = turn_state(where, state_axial, rate, True, 8)
    state_far = across(state_foreign)
    leading = jnp.transpose(cotangent[:, :, 0], (1, 0, 2)).reshape(comps * modes, nphi)
    last = jnp.transpose(cotangent[:, :, nz - 1], (1, 0, 2)).reshape(comps * modes, nphi)
    before = lax.ppermute(last, "col", up)
    after = lax.ppermute(leading, "col", down)
    state_own = turn_state(where, state_axial, rate, False, 0)

    sent = first_stencil(where, cotangent, state_foreign, after, before, rate, True, CHUNKS)
    far = [across(s) for s in sent]
    (own,) = first_stencil(where, cotangent, state_own, after, before, rate, False, 1)
    own_peer = beside(own)
    high, low = split_helm(where, helm_inverse, helm_far)

    kept, back = [], []
    for k in range(CHUNKS):
        cur, leading, last = map1(own, far[k], own_peer, beside(far[k]), high, low, k)
        before = lax.ppermute(last, "col", up)
        after = lax.ppermute(leading, "col", down)
        nxt = second_stencil(cur, after, before, state_own, state_far, rate, k, half)
        mine, theirs = map2(nxt, beside(nxt), high, low, k)
        kept.append(mine)
        back.append(across(theirs))
    out = write_half(where, kept, nphi, False)
    out = write_half(where, back, nphi, True, out)
    return out.reshape(modes, comps, nz, nphi)


def solution(mesh):
    in_specs = (P("rad", None, "col", None), P("rad", "col", None), P(None, None, "rad"), P("rad"))
    out_specs = P("rad", None, "col", None)
    return jax.shard_map(
        on_device, mesh=mesh, in_specs=in_specs, out_specs=out_specs, check_vma=False
    )
```

time: 448 us -> 246 us (0.55)
  waiting for transfers between devices: 342 us -> 174 us
  matrix products: 49.3 us -> 0 us
  Pallas kernels: 0 us -> 28.3 us
  starting transfers between devices: 10.3 us -> 36.8 us
  other arithmetic: 14 us -> 0 us
  between operations: 13.5 us -> 0.21 us
  local copies, waits for them, and re-layouts: 18.4 us -> 7.13 us
    all_gather x2 -> x0, waiting for transfers between devices: 318 us -> none  [on_device(): lax.all_gather(stenciled, 'rad', axis=0, tiled=True)]
    ppermute x4 -> x29, waiting for transfers between devices: 23.7 us -> 174 us  [the longest x10 147 us: across(): return lax.ppermute(array, 'rad', [(i, i ^ 2) for i in range(peers)])]
    dot_general x2 -> x0, matrix products: 49.3 us -> none  [on_device(): jnp.einsum('cji,jczp->iczp', helm_inverse, lax.all_gather(stenciled, 'rad...]
    pallas_call x0 -> x19, Pallas kernels: none -> 28.3 us  [the longest x4 7.66 us: map1(): pl.pallas_call(map1_kernel, out_shape=[shape((comps, nz, width, cols)), s...]
    ppermute x4 -> x29, starting transfers between devices: 10.3 us -> 36.8 us  [the longest x5 22.7 us: on_device(): after = lax.ppermute(leading, 'col', down)]
    add x2 -> x0, other arithmetic: 10.6 us -> none  [axial_adjoint(): current + diffusion_coeff * laplace + advection_coeff * transport]
    transpose x1 -> x0, local copies, waits for them, and re-layouts: 6.57 us -> none  [on_device(): jnp.einsum('cji,jczp->iczp', helm_inverse, lax.all_gather(stenciled, 'rad...]
    unnamed x14 -> x10, local copies, waits for them, and re-layouts: 9.81 us -> 3.6 us
  transfers between devices with their start and end apart: 6 -> 29, of which waited for: 5 -> 17; matrix products, arithmetic and copies ran while one was open for 1% -> 0% of each run, Pallas kernels for 0% -> 9%
where the time goes in v1:
time: 246 us
  waiting for transfers between devices  174 us (71%)
  starting transfers between devices  36.8 us (15%)
  Pallas kernels  28.3 us (12%)
  local copies, waits for them, and re-layouts  7.13 us (3%)
    ppermute x10, waiting for transfers between devices, across(): return lax.ppermute(array, 'rad', [(i, i ^ 2) for i in range(peers)])  147 us
    ppermute x5, starting transfers between devices, on_device(): after = lax.ppermute(leading, 'col', down)  22.7 us
    ppermute x5, waiting for transfers between devices, on_device(): after = lax.ppermute(leading, 'col', down)  18.4 us
    ppermute x10, starting transfers between devices, across(): return lax.ppermute(array, 'rad', [(i, i ^ 2) for i in range(peers)])  11.5 us
    ppermute x5, waiting for transfers between devices, on_device(): before = lax.ppermute(last, 'col', up)  8.34 us
    pallas_call x4, Pallas kernels, map1(): pl.pallas_call(map1_kernel, out_shape=[shape((comps, nz, width, cols)), s...  7.66 us
    pallas_call x4, Pallas kernels, map2(): pl.pallas_call(map2_kernel, out_shape=[shape(out)] * 2, grid=(comps,), in...  7.18 us
    pallas_call x2, Pallas kernels, write_half(): pl.pallas_call(lambda *refs: last_kernel(*refs, nz=nz, chunks=chunks, ext...  5.53 us
  transfers between devices with their start and end apart: 29, of which 17 were waited for; matrix products, arithmetic and copies ran while one was open for 0% of the time, Pallas kernels for 9%

profile of v1, /device:TPU:0, one launch (start us, length us, event | category | flops | bytes accessed | tf_op | source)
XLA Modules:
  0.0 246.2 jit_solution(17793454222514880298)
XLA Ops:
  0.0 3.5 %fusion = (f32[128,3,1,256]{3,2,1,0:T(1,128)S(1)}, f32[128,3,1,256]{3,2,1,0:T(1,128)S(1)}) fusion(f32[128,3,16,256]{3,2,1,0:T(8,128)} %param.4), kind=kLoop, calls=%fused_computation | loop fusion | bytes 1572864 | tf_op jit(solution)/shard_map/slice | solution.py:293
  3.6 6.1 %collective-permute-start = (f32[384,256]{1,0:T(8,128)S(1)}, f32[384,256]{1,0:T(8,128)S(1)}, u32[]{:S(2)}, u32[]{:S(2)}) collective-permute-start(f32[384,256]{1,0:T(8,128)S(1)} %bitcast.27), channel_id=1, source_target_pairs={{1,0},{2,1},{3,2},{4,3},{5,4},{6,5},{7,6},{0,7},{9,8},{10,9},{11,1... | collective-permute-start | bytes 1179656 | tf_op jit(solution)/shard_map/ppermute | solution.py:295
  9.6 0.8 copy.11
  10.4 0.5 turn_state.2.refs_2_.refs_3_
  10.9 13.2 %collective-permute-done.refs_3_ = f32[384,256]{1,0:T(8,128)S(1)} collective-permute-done((f32[384,256]{1,0:T(8,128)S(1)}, f32[384,256]{1,0:T(8,128)S(1)}, u32[]{:S(2)}, u32[]{:S(2)}) %collective-permute-start) | collective-permute-done | bytes 393248 | tf_op jit(solution)/shard_map/ppermute | solution.py:295
  24.4 2.8 %copy-done = f32[128,3,16,256]{3,2,1,0:T(8,128)S(1)} copy-done((f32[128,3,16,256]{3,2,1,0:T(8,128)S(1)}, f32[128,3,16,256]{3,2,1,0:T(8,128)}, u32[]{:S(2)}) %copy-start) | copy-done | bytes 6291480
  27.2 2.3 first_stencil.2.own
  29.6 1.6 collective-permute-start.5
  31.2 0.5 turn_state.3.refs_2_
  31.8 2.4 first_stencil.3
  34.2 0.4 collective-permute-start.2
  34.6 1.7 collective-permute-start.11
  36.6 13.4 %collective-permute-done.5.far = f32[3,512,128]{2,1,0:T(8,128)S(1)} collective-permute-done((f32[3,512,128]{2,1,0:T(8,128)S(1)}, f32[3,512,128]{2,1,0:T(8,128)S(1)}, u32[]{:S(2)}, u32[]{:S(2)}) %collective-permute-start.5) | collective-permute-done | bytes 786464 | tf_op jit(solution)/shard_map/ppermute | solution.py:281
  50.0 1.6 collective-permute-start.23
  51.6 15.3 %collective-permute-done.2.far = f32[3,16,32,128]{3,2,1,0:T(8,128)S(1)} collective-permute-done((f32[3,16,32,128]{3,2,1,0:T(8,128)S(1)}, f32[3,16,32,128]{3,2,1,0:T(8,128)S(1)}, u32[]{:S(2)}, u32[]{:S(2)}) %collective-permute-start.2) | collective-permute-done | bytes 786464 | tf_op jit(solution)/shard_map/ppermute | solution.py:281
  66.9 16.8 %collective-permute-done.11.far = f32[3,16,32,128]{3,2,1,0:T(8,128)S(1)} collective-permute-done((f32[3,16,32,128]{3,2,1,0:T(8,128)S(1)}, f32[3,16,32,128]{3,2,1,0:T(8,128)S(1)}, u32[]{:S(2)}, u32[]{:S(2)}) %collective-permute-start.11) | collective-permute-done | bytes 786464 | tf_op jit(solution)/shard_map/ppermute | solution.py:281
  83.7 1.6 collective-permute-start.8
  85.3 15.3 %collective-permute-done.17.far = f32[3,16,32,128]{3,2,1,0:T(8,128)S(1)} collective-permute-done((f32[3,16,32,128]{3,2,1,0:T(8,128)S(1)}, f32[3,16,32,128]{3,2,1,0:T(8,128)S(1)}, u32[]{:S(2)}, u32[]{:S(2)}) %collective-permute-start.17) | collective-permute-done | bytes 786464 | tf_op jit(solution)/shard_map/ppermute | solution.py:281
  100.6 16.8 %collective-permute-done.23.far = f32[3,16,32,128]{3,2,1,0:T(8,128)S(1)} collective-permute-done((f32[3,16,32,128]{3,2,1,0:T(8,128)S(1)}, f32[3,16,32,128]{3,2,1,0:T(8,128)S(1)}, u32[]{:S(2)}, u32[]{:S(2)}) %collective-permute-start.23) | collective-permute-done | bytes 786464 | tf_op jit(solution)/shard_map/ppermute | solution.py:281
  117.4 0.5 collective-permute-start.24
  117.9 0.6 split_helm.1
  118.6 1.9 map1_0.1
  120.5 5.8 %collective-permute-start.6 = (f32[3,32,256]{2,1,0:T(8,128)S(1)}, f32[3,32,256]{2,1,0:T(8,128)S(1)}, u32[]{:S(2)}, u32[]{:S(2)}) collective-permute-start(f32[3,32,256]{2,1,0:T(8,128)S(1)} %get-tuple-element.35), channel_id=1, source_target_pairs={{1,0},{2,1},{3,2},{4,3},{5,4},{6,5},{7,6},{0,7},{9,8},{10,9},{11,1... | collective-permute-start | bytes 294920 | tf_op jit(solution)/shard_map/ppermute | solution.py:308
  126.3 1.9 map1_1.1
  128.2 11.3 %collective-permute-done.8.refs_4_ = f32[2056,128]{1,0:T(8,128)S(1)} collective-permute-done((f32[2056,128]{1,0:T(8,128)S(1)}, f32[2056,128]{1,0:T(8,128)S(1)}, u32[]{:S(2)}, u32[]{:S(2)}) %collective-permute-start.8) | collective-permute-done | bytes 1052704 | tf_op jit(solution)/shard_map/ppermute | solution.py:281
  139.5 5.7 %collective-permute-start.13 = (f32[3,32,256]{2,1,0:T(8,128)S(1)}, f32[3,32,256]{2,1,0:T(8,128)S(1)}, u32[]{:S(2)}, u32[]{:S(2)}) collective-permute-start(f32[3,32,256]{2,1,0:T(8,128)S(1)} %get-tuple-element.40), channel_id=1, source_target_pairs={{1,0},{2,1},{3,2},{4,3},{5,4},{6,5},{7,6},{0,7},{9,8},{10,9},{11,1... | collective-permute-start | bytes 294920 | tf_op jit(solution)/shard_map/ppermute | solution.py:308
  145.8 1.9 map1_2.1
  147.7 4.8 %collective-permute-start.19 = (f32[3,32,256]{2,1,0:T(8,128)S(1)}, f32[3,32,256]{2,1,0:T(8,128)S(1)}, u32[]{:S(2)}, u32[]{:S(2)}) collective-permute-start(f32[3,32,256]{2,1,0:T(8,128)S(1)} %get-tuple-element.45), channel_id=1, source_target_pairs={{1,0},{2,1},{3,2},{4,3},{5,4},{6,5},{7,6},{0,7},{9,8},{10,9},{11,1... | collective-permute-start | bytes 294920 | tf_op jit(solution)/shard_map/ppermute | solution.py:308
  153.1 2.0 collective-permute-done.19.refs_1_
  155.1 4.9 %collective-permute-done.20.refs_2_ = f32[3,32,256]{2,1,0:T(8,128)S(1)} collective-permute-done((f32[3,32,256]{2,1,0:T(8,128)S(1)}, f32[3,32,256]{2,1,0:T(8,128)S(1)}, u32[]{:S(2)}, u32[]{:S(2)}) %collective-permute-start.20) | collective-permute-done | bytes 98336 | tf_op jit(solution)/shard_map/ppermute | solution.py:307
  160.5 1.9 map1_3.1
  162.8 1.7 collective-permute-start.26
  164.5 3.2 %collective-permute-done.25.refs_1_ = f32[3,32,256]{2,1,0:T(8,128)S(1)} collective-permute-done((f32[3,32,256]{2,1,0:T(8,128)S(1)}, f32[3,32,256]{2,1,0:T(8,128)S(1)}, u32[]{:S(2)}, u32[]{:S(2)}) %collective-permute-start.25) | collective-permute-done | bytes 98336 | tf_op jit(solution)/shard_map/ppermute | solution.py:308
  167.7 2.9 %collective-permute-done.26.refs_2_ = f32[3,32,256]{2,1,0:T(8,128)S(1)} collective-permute-done((f32[3,32,256]{2,1,0:T(8,128)S(1)}, f32[3,32,256]{2,1,0:T(8,128)S(1)}, u32[]{:S(2)}, u32[]{:S(2)}) %collective-permute-start.26) | collective-permute-done | bytes 98336 | tf_op jit(solution)/shard_map/ppermute | solution.py:307
  171.1 1.8 map2_0.1
  172.9 1.6 collective-permute-start.10
  174.5 1.8 map2_1.1
  176.3 0.5 collective-permute-start.16
  176.8 1.8 map2_2.1
  178.7 1.6 collective-permute-start.22
  180.3 1.8 map2_3.1
  182.1 0.6 collective-permute-start.28
  182.6 2.8 %write_own.1.refs_5_ = f32[6144,256]{1,0:T(8,128)} custom-call(s32[1]{0:T(128)} %bitcast.refs_0_.where, f32[3,16,32,128]{3,2,1,0:T(8,128)S(1)} %get-tuple-element.53.refs_1_, f32[3,16,32,128]{3,2,1,0:T(8,128)S(1)} %get-tuple-element.54.refs_2_, f32[3,16,32,128]{3,2,1,0:T(8,128)S(1)} %get-tuple-element.55.refs_3_, ...), custom_call_target="tpu_custom_call" | custom-call | flops 1572864 | bytes 6291456 | tf_op jit(solution)/shard_map/write_own/pallas_call | solution.py:256
  185.4 7.9 %collective-permute-done.10.refs_1_ = f32[3,16,32,128]{3,2,1,0:T(8,128)S(1)} collective-permute-done((f32[3,16,32,128]{3,2,1,0:T(8,128)S(1)}, f32[3,16,32,128]{3,2,1,0:T(8,128)S(1)}, u32[]{:S(2)}, u32[]{:S(2)}) %collective-permute-start.10) | collective-permute-done | bytes 786464 | tf_op jit(solution)/shard_map/ppermute | solution.py:281
  193.3 16.9 %collective-permute-done.16.refs_2_ = f32[3,16,32,128]{3,2,1,0:T(8,128)S(1)} collective-permute-done((f32[3,16,32,128]{3,2,1,0:T(8,128)S(1)}, f32[3,16,32,128]{3,2,1,0:T(8,128)S(1)}, u32[]{:S(2)}, u32[]{:S(2)}) %collective-permute-start.16) | collective-permute-done | bytes 786464 | tf_op jit(solution)/shard_map/ppermute | solution.py:281
  210.2 16.9 %collective-permute-done.22.refs_3_ = f32[3,16,32,128]{3,2,1,0:T(8,128)S(1)} collective-permute-done((f32[3,16,32,128]{3,2,1,0:T(8,128)S(1)}, f32[3,16,32,128]{3,2,1,0:T(8,128)S(1)}, u32[]{:S(2)}, u32[]{:S(2)}) %collective-permute-start.22) | collective-permute-done | bytes 786464 | tf_op jit(solution)/shard_map/ppermute | solution.py:281
  227.0 16.4 %collective-permute-done.28.refs_4_ = f32[3,16,32,128]{3,2,1,0:T(8,128)S(1)} collective-permute-done((f32[3,16,32,128]{3,2,1,0:T(8,128)S(1)}, f32[3,16,32,128]{3,2,1,0:T(8,128)S(1)}, u32[]{:S(2)}, u32[]{:S(2)}) %collective-permute-start.28) | collective-permute-done | bytes 786464 | tf_op jit(solution)/shard_map/ppermute | solution.py:281
  243.4 2.8 %write_foreign.1 = f32[6144,256]{1,0:T(8,128)} custom-call(s32[1]{0:T(128)} %bitcast.refs_0_.where, f32[3,16,32,128]{3,2,1,0:T(8,128)S(1)} %collective-permute-done.10.refs_1_, f32[3,16,32,128]{3,2,1,0:T(8,128)S(1)} %collective-permute-done.16.refs_2_, f32[3,16,32,128]{3,2,1,0:T(8,128)S(1)} %collective-permute-done.22.refs_3_, ...), custom_call_target="tpu_custom_call", output_to_operand_aliasing={{}: (5, {})} | custom-call | flops 1572864 | bytes 6291456 | tf_op jit(solution)/shard_map/write_foreign/pallas_call | solution.py:256
  (40 shorter events, 3.2 us)
Async XLA Ops:
  0.0 10.4 %copy-start.3 = (f32[128]{0:T(128)S(1)}, f32[128]{0:T(128)}, u32[]{:S(2)}) copy-start(f32[128]{0:T(128)} %param.7) | copy-start | bytes 1540
  0.0 10.4 %copy-start.1 = (f32[128,16,256]{2,1,0:T(8,128)S(1)}, f32[128,16,256]{2,1,0:T(8,128)}, u32[]{:S(2)}) copy-start(f32[128,16,256]{2,1,0:T(8,128)} %param.5) | copy-start | bytes 6291460
  3.6 20.6 %collective-permute-start = (f32[384,256]{1,0:T(8,128)S(1)}, f32[384,256]{1,0:T(8,128)S(1)}, u32[]{:S(2)}, u32[]{:S(2)}) collective-permute-start(f32[384,256]{1,0:T(8,128)S(1)} %bitcast.27), channel_id=1, source_target_pairs={{1,0},{2,1},{3,2},{4,3},{5,4},{6,5},{7,6},{0,7},{9,8},{10,9},{11,1... | collective-permute-start | bytes 1179656 | tf_op jit(solution)/shard_map/ppermute | solution.py:295
  10.4 14.0 %collective-permute-start.1 = (f32[384,256]{1,0:T(8,128)}, f32[384,256]{1,0:T(8,128)S(1)}, u32[]{:S(2)}, u32[]{:S(2)}) collective-permute-start(f32[384,256]{1,0:T(8,128)} %bitcast.9), channel_id=1, source_target_pairs={{0,1},{1,2},{2,3},{3,4},{4,5},{5,6},{6,7},{7,0},{8,9},{9,10},{10,1... | collective-permute-start | bytes 1179656 | tf_op jit(solution)/shard_map/ppermute | solution.py:294
  24.4 2.8 %copy-start = (f32[128,3,16,256]{3,2,1,0:T(8,128)S(1)}, f32[128,3,16,256]{3,2,1,0:T(8,128)}, u32[]{:S(2)}) copy-start(f32[128,3,16,256]{3,2,1,0:T(8,128)} %param.4) | copy-start | bytes 18874372
  27.2 2.4 copy-start.2
  29.5 89.1 %collective-permute-start.3 = (f32[3,16,128,128]{3,2,1,0:T(8,128)S(1)}, f32[3,16,128,128]{3,2,1,0:T(8,128)S(1)}, u32[]{:S(2)}, u32[]{:S(2)}) collective-permute-start(f32[3,16,128,128]{3,2,1,0:T(8,128)S(1)} %first_stencil.2.own), channel_id=1, source_target_pairs={{0,8},{8,0},{16,24},{24,16},{1,9},{9,1},{17,25},{25,17},{2,10},{10... | collective-permute-start | bytes 9437192 | tf_op jit(solution)/shard_map/ppermute | solution.py:284
  29.6 20.4 %collective-permute-start.5 = (f32[3,512,128]{2,1,0:T(8,128)S(1)}, f32[3,512,128]{2,1,0:T(8,128)S(1)}, u32[]{:S(2)}, u32[]{:S(2)}) collective-permute-start(f32[3,512,128]{2,1,0:T(8,128)S(1)} %copy-done.2), channel_id=1, source_target_pairs={{0,16},{8,24},{16,0},{24,8},{1,17},{9,25},{17,1},{25,9},{2,18},{10... | collective-permute-start | bytes 2359304 | tf_op jit(solution)/shard_map/ppermute | solution.py:281
  34.2 32.7 %collective-permute-start.2 = (f32[3,16,32,128]{3,2,1,0:T(8,128)S(1)}, f32[3,16,32,128]{3,2,1,0:T(8,128)S(1)}, u32[]{:S(2)}, u32[]{:S(2)}) collective-permute-start(f32[3,16,32,128]{3,2,1,0:T(8,128)S(1)} %get-tuple-element.31), channel_id=1, source_target_pairs={{0,16},{8,24},{16,0},{24,8},{1,17},{9,25},{17,1},{25,9},{2,18},{10... | collective-permute-start | bytes 2359304 | tf_op jit(solution)/shard_map/ppermute | solution.py:281
  34.6 49.1 %collective-permute-start.11 = (f32[3,16,32,128]{3,2,1,0:T(8,128)S(1)}, f32[3,16,32,128]{3,2,1,0:T(8,128)S(1)}, u32[]{:S(2)}, u32[]{:S(2)}) collective-permute-start(f32[3,16,32,128]{3,2,1,0:T(8,128)S(1)} %get-tuple-element.38), channel_id=1, source_target_pairs={{0,16},{8,24},{16,0},{24,8},{1,17},{9,25},{17,1},{25,9},{2,18},{10... | collective-permute-start | bytes 2359304 | tf_op jit(solution)/shard_map/ppermute | solution.py:281
  36.2 64.3 %collective-permute-start.17 = (f32[3,16,32,128]{3,2,1,0:T(8,128)S(1)}, f32[3,16,32,128]{3,2,1,0:T(8,128)S(1)}, u32[]{:S(2)}, u32[]{:S(2)}) collective-permute-start(f32[3,16,32,128]{3,2,1,0:T(8,128)S(1)} %get-tuple-element.43), channel_id=1, source_target_pairs={{0,16},{8,24},{16,0},{24,8},{1,17},{9,25},{17,1},{25,9},{2,18},{10... | collective-permute-start | bytes 2359304 | tf_op jit(solution)/shard_map/ppermute | solution.py:281
  50.0 67.4 %collective-permute-start.23 = (f32[3,16,32,128]{3,2,1,0:T(8,128)S(1)}, f32[3,16,32,128]{3,2,1,0:T(8,128)S(1)}, u32[]{:S(2)}, u32[]{:S(2)}) collective-permute-start(f32[3,16,32,128]{3,2,1,0:T(8,128)S(1)} %get-tuple-element.48), channel_id=1, source_target_pairs={{0,16},{8,24},{16,0},{24,8},{1,17},{9,25},{17,1},{25,9},{2,18},{10... | collective-permute-start | bytes 2359304 | tf_op jit(solution)/shard_map/ppermute | solution.py:281
  66.9 50.6 %collective-permute-start.4 = (f32[3,16,32,128]{3,2,1,0:T(8,128)S(1)}, f32[3,16,32,128]{3,2,1,0:T(8,128)S(1)}, u32[]{:S(2)}, u32[]{:S(2)}) collective-permute-start(f32[3,16,32,128]{3,2,1,0:T(8,128)S(1)} %collective-permute-done.2.far), channel_id=1, source_target_pairs={{0,8},{8,0},{16,24},{24,16},{1,9},{9,1},{17,25},{25,17},{2,10},{10... | collective-permute-start | bytes 2359304 | tf_op jit(solution)/shard_map/ppermute | solution.py:284
  83.7 55.8 %collective-permute-start.8 = (f32[2056,128]{1,0:T(8,128)S(1)}, f32[2056,128]{1,0:T(8,128)S(1)}, u32[]{:S(2)}, u32[]{:S(2)}) collective-permute-start(f32[2056,128]{1,0:T(8,128)S(1)} %turn_state.3.refs_2_), channel_id=1, source_target_pairs={{0,16},{8,24},{16,0},{24,8},{1,17},{9,25},{17,1},{25,9},{2,18},{10... | collective-permute-start | bytes 3158024 | tf_op jit(solution)/shard_map/ppermute | solution.py:281
  100.6 25.7 %collective-permute-start.12 = (f32[3,16,32,128]{3,2,1,0:T(8,128)S(1)}, f32[3,16,32,128]{3,2,1,0:T(8,128)S(1)}, u32[]{:S(2)}, u32[]{:S(2)}) collective-permute-start(f32[3,16,32,128]{3,2,1,0:T(8,128)S(1)} %collective-permute-done.11.far), channel_id=1, source_target_pairs={{0,8},{8,0},{16,24},{24,16},{1,9},{9,1},{17,25},{25,17},{2,10},{10... | collective-permute-start | bytes 2359304 | tf_op jit(solution)/shard_map/ppermute | solution.py:284
  117.4 28.3 %collective-permute-start.18 = (f32[3,16,32,128]{3,2,1,0:T(8,128)S(1)}, f32[3,16,32,128]{3,2,1,0:T(8,128)S(1)}, u32[]{:S(2)}, u32[]{:S(2)}) collective-permute-start(f32[3,16,32,128]{3,2,1,0:T(8,128)S(1)} %collective-permute-done.17.far), channel_id=1, source_target_pairs={{0,8},{8,0},{16,24},{24,16},{1,9},{9,1},{17,25},{25,17},{2,10},{10... | collective-permute-start | bytes 2359304 | tf_op jit(solution)/shard_map/ppermute | solution.py:284
  117.4 43.1 %collective-permute-start.24 = (f32[3,16,32,128]{3,2,1,0:T(8,128)S(1)}, f32[3,16,32,128]{3,2,1,0:T(8,128)S(1)}, u32[]{:S(2)}, u32[]{:S(2)}) collective-permute-start(f32[3,16,32,128]{3,2,1,0:T(8,128)S(1)} %collective-permute-done.23.far), channel_id=1, source_target_pairs={{0,8},{8,0},{16,24},{24,16},{1,9},{9,1},{17,25},{25,17},{2,10},{10... | collective-permute-start | bytes 2359304 | tf_op jit(solution)/shard_map/ppermute | solution.py:284
  120.5 24.7 %collective-permute-start.6 = (f32[3,32,256]{2,1,0:T(8,128)S(1)}, f32[3,32,256]{2,1,0:T(8,128)S(1)}, u32[]{:S(2)}, u32[]{:S(2)}) collective-permute-start(f32[3,32,256]{2,1,0:T(8,128)S(1)} %get-tuple-element.35), channel_id=1, source_target_pairs={{1,0},{2,1},{3,2},{4,3},{5,4},{6,5},{7,6},{0,7},{9,8},{10,9},{11,1... | collective-permute-start | bytes 294920 | tf_op jit(solution)/shard_map/ppermute | solution.py:308
  126.3 18.9 %collective-permute-start.7 = (f32[3,32,256]{2,1,0:T(8,128)S(1)}, f32[3,32,256]{2,1,0:T(8,128)S(1)}, u32[]{:S(2)}, u32[]{:S(2)}) collective-permute-start(f32[3,32,256]{2,1,0:T(8,128)S(1)} %get-tuple-element.36), channel_id=1, source_target_pairs={{0,1},{1,2},{2,3},{3,4},{4,5},{5,6},{6,7},{7,0},{8,9},{9,10},{10,1... | collective-permute-start | bytes 294920 | tf_op jit(solution)/shard_map/ppermute | solution.py:307
  139.5 12.9 %collective-permute-start.13 = (f32[3,32,256]{2,1,0:T(8,128)S(1)}, f32[3,32,256]{2,1,0:T(8,128)S(1)}, u32[]{:S(2)}, u32[]{:S(2)}) collective-permute-start(f32[3,32,256]{2,1,0:T(8,128)S(1)} %get-tuple-element.40), channel_id=1, source_target_pairs={{1,0},{2,1},{3,2},{4,3},{5,4},{6,5},{7,6},{0,7},{9,8},{10,9},{11,1... | collective-permute-start | bytes 294920 | tf_op jit(solution)/shard_map/ppermute | solution.py:308
  145.3 7.4 %collective-permute-start.14 = (f32[3,32,256]{2,1,0:T(8,128)S(1)}, f32[3,32,256]{2,1,0:T(8,128)S(1)}, u32[]{:S(2)}, u32[]{:S(2)}) collective-permute-start(f32[3,32,256]{2,1,0:T(8,128)S(1)} %get-tuple-element.41), channel_id=1, source_target_pairs={{0,1},{1,2},{2,3},{3,4},{4,5},{5,6},{6,7},{7,0},{8,9},{9,10},{10,1... | collective-permute-start | bytes 294920 | tf_op jit(solution)/shard_map/ppermute | solution.py:307
  145.7 25.4 %collective-permute-start.9 = (f32[3,16,32,256]{3,2,1,0:T(8,128)S(1)}, f32[3,16,32,256]{3,2,1,0:T(8,128)S(1)}, u32[]{:S(2)}, u32[]{:S(2)}) collective-permute-start(f32[3,16,32,256]{3,2,1,0:T(8,128)S(1)} %second_stencil_0.1.own), channel_id=1, source_target_pairs={{0,8},{8,0},{16,24},{24,16},{1,9},{9,1},{17,25},{25,17},{2,10},{10... | collective-permute-start | bytes 4718600 | tf_op jit(solution)/shard_map/ppermute | solution.py:284
  147.7 7.5 %collective-permute-start.19 = (f32[3,32,256]{2,1,0:T(8,128)S(1)}, f32[3,32,256]{2,1,0:T(8,128)S(1)}, u32[]{:S(2)}, u32[]{:S(2)}) collective-permute-start(f32[3,32,256]{2,1,0:T(8,128)S(1)} %get-tuple-element.45), channel_id=1, source_target_pairs={{1,0},{2,1},{3,2},{4,3},{5,4},{6,5},{7,6},{0,7},{9,8},{10,9},{11,1... | collective-permute-start | bytes 294920 | tf_op jit(solution)/shard_map/ppermute | solution.py:308
  152.4 7.6 %collective-permute-start.20 = (f32[3,32,256]{2,1,0:T(8,128)S(1)}, f32[3,32,256]{2,1,0:T(8,128)S(1)}, u32[]{:S(2)}, u32[]{:S(2)}) collective-permute-start(f32[3,32,256]{2,1,0:T(8,128)S(1)} %get-tuple-element.46), channel_id=1, source_target_pairs={{0,1},{1,2},{2,3},{3,4},{4,5},{5,6},{6,7},{7,0},{8,9},{9,10},{10,1... | collective-permute-start | bytes 294920 | tf_op jit(solution)/shard_map/ppermute | solution.py:307
  153.1 21.4 %collective-permute-start.15 = (f32[3,16,32,256]{3,2,1,0:T(8,128)S(1)}, f32[3,16,32,256]{3,2,1,0:T(8,128)S(1)}, u32[]{:S(2)}, u32[]{:S(2)}) collective-permute-start(f32[3,16,32,256]{3,2,1,0:T(8,128)S(1)} %second_stencil_1.1.own), channel_id=1, source_target_pairs={{0,8},{8,0},{16,24},{24,16},{1,9},{9,1},{17,25},{25,17},{2,10},{10... | collective-permute-start | bytes 4718600 | tf_op jit(solution)/shard_map/ppermute | solution.py:284
  160.4 16.4 %collective-permute-start.21 = (f32[3,16,32,256]{3,2,1,0:T(8,128)S(1)}, f32[3,16,32,256]{3,2,1,0:T(8,128)S(1)}, u32[]{:S(2)}, u32[]{:S(2)}) collective-permute-start(f32[3,16,32,256]{3,2,1,0:T(8,128)S(1)} %second_stencil_2.1.own), channel_id=1, source_target_pairs={{0,8},{8,0},{16,24},{24,16},{1,9},{9,1},{17,25},{25,17},{2,10},{10... | collective-permute-start | bytes 4718600 | tf_op jit(solution)/shard_map/ppermute | solution.py:284
  162.4 5.2 %collective-permute-start.25 = (f32[3,32,256]{2,1,0:T(8,128)S(1)}, f32[3,32,256]{2,1,0:T(8,128)S(1)}, u32[]{:S(2)}, u32[]{:S(2)}) collective-permute-start(f32[3,32,256]{2,1,0:T(8,128)S(1)} %get-tuple-element.50), channel_id=1, source_target_pairs={{1,0},{2,1},{3,2},{4,3},{5,4},{6,5},{7,6},{0,7},{9,8},{10,9},{11,1... | collective-permute-start | bytes 294920 | tf_op jit(solution)/shard_map/ppermute | solution.py:308
  162.8 7.8 %collective-permute-start.26 = (f32[3,32,256]{2,1,0:T(8,128)S(1)}, f32[3,32,256]{2,1,0:T(8,128)S(1)}, u32[]{:S(2)}, u32[]{:S(2)}) collective-permute-start(f32[3,32,256]{2,1,0:T(8,128)S(1)} %get-tuple-element.51), channel_id=1, source_target_pairs={{0,1},{1,2},{2,3},{3,4},{4,5},{5,6},{6,7},{7,0},{8,9},{9,10},{10,1... | collective-permute-start | bytes 294920 | tf_op jit(solution)/shard_map/ppermute | solution.py:307
  171.0 9.3 %collective-permute-start.27 = (f32[3,16,32,256]{3,2,1,0:T(8,128)S(1)}, f32[3,16,32,256]{3,2,1,0:T(8,128)S(1)}, u32[]{:S(2)}, u32[]{:S(2)}) collective-permute-start(f32[3,16,32,256]{3,2,1,0:T(8,128)S(1)} %second_stencil_3.1.own), channel_id=1, source_target_pairs={{0,8},{8,0},{16,24},{24,16},{1,9},{9,1},{17,25},{25,17},{2,10},{10... | collective-permute-start | bytes 4718600 | tf_op jit(solution)/shard_map/ppermute | solution.py:284
  172.9 20.4 %collective-permute-start.10 = (f32[3,16,32,128]{3,2,1,0:T(8,128)S(1)}, f32[3,16,32,128]{3,2,1,0:T(8,128)S(1)}, u32[]{:S(2)}, u32[]{:S(2)}) collective-permute-start(f32[3,16,32,128]{3,2,1,0:T(8,128)S(1)} %get-tuple-element.37), channel_id=1, source_target_pairs={{0,16},{8,24},{16,0},{24,8},{1,17},{9,25},{17,1},{25,9},{2,18},{10... | collective-permute-start | bytes 2359304 | tf_op jit(solution)/shard_map/ppermute | solution.py:281
  176.3 33.9 %collective-permute-start.16 = (f32[3,16,32,128]{3,2,1,0:T(8,128)S(1)}, f32[3,16,32,128]{3,2,1,0:T(8,128)S(1)}, u32[]{:S(2)}, u32[]{:S(2)}) collective-permute-start(f32[3,16,32,128]{3,2,1,0:T(8,128)S(1)} %get-tuple-element.42), channel_id=1, source_target_pairs={{0,16},{8,24},{16,0},{24,8},{1,17},{9,25},{17,1},{25,9},{2,18},{10... | collective-permute-start | bytes 2359304 | tf_op jit(solution)/shard_map/ppermute | solution.py:281
  178.7 48.3 %collective-permute-start.22 = (f32[3,16,32,128]{3,2,1,0:T(8,128)S(1)}, f32[3,16,32,128]{3,2,1,0:T(8,128)S(1)}, u32[]{:S(2)}, u32[]{:S(2)}) collective-permute-start(f32[3,16,32,128]{3,2,1,0:T(8,128)S(1)} %get-tuple-element.47), channel_id=1, source_target_pairs={{0,16},{8,24},{16,0},{24,8},{1,17},{9,25},{17,1},{25,9},{2,18},{10... | collective-permute-start | bytes 2359304 | tf_op jit(solution)/shard_map/ppermute | solution.py:281
  182.1 61.4 %collective-permute-start.28 = (f32[3,16,32,128]{3,2,1,0:T(8,128)S(1)}, f32[3,16,32,128]{3,2,1,0:T(8,128)S(1)}, u32[]{:S(2)}, u32[]{:S(2)}) collective-permute-start(f32[3,16,32,128]{3,2,1,0:T(8,128)S(1)} %get-tuple-element.52), channel_id=1, source_target_pairs={{0,16},{8,24},{16,0},{24,8},{1,17},{9,25},{17,1},{25,9},{2,18},{10... | collective-permute-start | bytes 2359304 | tf_op jit(solution)/shard_map/ppermute | solution.py:281

commit v2 on v1

--- a/solution.py
+++ b/solution.py
@@ -7,6 +7,7 @@
 
 SECTIONS = 2
 CHUNKS = 4
+PIECES = 4
 
 diffusion_coeff = 0.2
 advection_coeff = 0.15
@@ -78,6 +79,27 @@
         cost_estimate=cost(rows * modes, 8 * rows * modes),
         name="turn_state",
     )(where, state.reshape(modes * nz, nphi), rate)
+
+
+def edge_kernel(cot, leading, last, *, modes, nz):
+    for c in range(3):
+        at = slice(c * modes, (c + 1) * modes)
+        leading[at, :] = cot[pl.ds(c * nz, modes, stride=3 * nz), :]
+        last[at, :] = cot[pl.ds(c * nz + nz - 1, modes, stride=3 * nz), :]
+
+
+def edge_layers(cot):
+    modes, comps, nz, nphi = cot.shape
+    return pl.pallas_call(
+        lambda *refs: edge_kernel(*refs, modes=modes, nz=nz),
+        out_shape=[shape((comps * modes, nphi))] * 2,
+        grid=(2,),
+        in_specs=[pl.BlockSpec((modes * comps * nz, nphi // 2), lambda h: (0, h))],
+        out_specs=[pl.BlockSpec((comps * modes, nphi // 2), lambda h: (0, h))] * 2,
+        compiler_params=params(16),
+        cost_estimate=cost(modes * comps * nphi, 16 * modes * comps * nphi),
+        name="edge_layers",
+    )(cot.reshape(modes * comps * nz, nphi))
 
 
 def first_kernel(where, cot, state, after, before, rate, *rest, modes, nz, chunks):
@@ -129,8 +151,8 @@
 
 
 def helm_kernel(where, own, far, high, low):
-    for g, part in enumerate((own, far)):
-        h, l = split(part[...])
+    for g, part in enumerate((own[...], far[0])):
+        h, l = split(part)
         cols = slice(g * part.shape[2], (g + 1) * part.shape[2])
         high[:, :, cols] = h
         low[:, :, cols] = l
@@ -138,7 +160,7 @@
 
 def split_helm(where, own, far):
     comps, rows, modes = own.shape
-    block = lambda k, w: (0, w[0] ^ (((k & 1) << 1) | (k >> 1)), 0)
+    block = lambda k, w: w[0] ^ (((k & 1) << 1) | (k >> 1))
     out = (comps, rows, 2 * modes)
     return pl.pallas_call(
         helm_kernel,
@@ -146,7 +168,10 @@
         grid_spec=pltpu.PrefetchScalarGridSpec(
             num_scalar_prefetch=1,
             grid=(rows // modes,),
-            in_specs=[pl.BlockSpec((comps, modes, modes), block)] * 2,
+            in_specs=[
+                pl.BlockSpec((comps, modes, modes), lambda k, w: (0, block(k, w), 0)),
+                pl.BlockSpec((1, comps, modes, modes), lambda k, w: (block(k, w) ^ w[1], 0, 0, 0)),
+            ],
             out_specs=[pl.BlockSpec((comps, modes, 2 * modes), lambda k, w: (0, k, 0))] * 2,
         ),
         compiler_params=params(16),
@@ -238,36 +263,37 @@
     )(own, peer, high, low)
 
 
-def last_kernel(where, *refs, nz, chunks, extra):
+def last_kernel(where, *refs, nz, chunks):
     ins, out = refs[:chunks], refs[-1]
-    width, modes = ins[0].shape[2:]
-    for c in range(ins[0].shape[0]):
-        for z in range(nz):
-            whole = jnp.concatenate([ref[c, z] for ref in ins], axis=0)
-            out[pl.ds(c * nz + z, modes, stride=3 * nz), :] = whole.T
+    for z in range(nz):
+        whole = jnp.concatenate([ref[0, z] for ref in ins], axis=0)
+        out[:, z, :] = whole.T
 
 
 def write_half(where, pieces, nphi, foreign, base=None):
     comps, nz, width, modes = pieces[0].shape
     chunks = len(pieces)
-    side = (lambda i, w: (0, 1 - (w[0] >> 1))) if foreign else (lambda i, w: (0, w[0] >> 1))
-    rows = modes * comps * nz
+    side = (lambda c, w: (0, c, 1 - (w[0] >> 1))) if foreign else (lambda c, w: (0, c, w[0] >> 1))
     extra = () if base is None else (base,)
     return pl.pallas_call(
-        lambda *refs: last_kernel(*refs, nz=nz, chunks=chunks, extra=len(extra)),
-        out_shape=shape((rows, nphi)),
+        lambda *refs: last_kernel(*refs, nz=nz, chunks=chunks),
+        out_shape=shape((modes, comps * nz, nphi)),
         grid_spec=pltpu.PrefetchScalarGridSpec(
             num_scalar_prefetch=1,
-            grid=(1,),
-            in_specs=[pl.BlockSpec(p.shape, lambda i, w: (0, 0, 0, 0)) for p in pieces]
+            grid=(comps,),
+            in_specs=[pl.BlockSpec((1,) + p.shape[1:], lambda c, w: (c, 0, 0, 0)) for p in pieces]
             + [pl.BlockSpec(memory_space=pl.ANY)] * len(extra),
-            out_specs=pl.BlockSpec((rows, nphi // 2), side),
+            out_specs=pl.BlockSpec((modes, nz, nphi // 2), side),
         ),
         input_output_aliases={1 + chunks: 0} if extra else {},
         compiler_params=params(24),
-        cost_estimate=cost(rows * nphi, 4 * rows * nphi),
+        cost_estimate=cost(comps * nz * modes * nphi, 4 * comps * nz * modes * nphi),
         name="write_foreign" if foreign else "write_own",
     )(where, *pieces, *extra)
+
+
+def tied(value, *others):
+    return lax.optimization_barrier((value, *others))[0]
 
 
 def on_device(cotangent, state_axial, helm_inverse, rotation_rate):
@@ -283,31 +309,48 @@
     def beside(array):
         return lax.ppermute(array, "rad", [(i, i ^ 1) for i in range(peers)])
 
-    where = lax.axis_index("rad").astype(jnp.int32).reshape(1)
+    def hop(array, mask):
+        return lax.ppermute(array, "col", [(i, i ^ mask) for i in range(cols)])
+
+    lot = lax.axis_index("col").astype(jnp.int32) & (PIECES - 1)
+    where = jnp.stack([lax.axis_index("rad").astype(jnp.int32), lot])
     rate = rotation_rate.reshape(1, modes)
 
-    helm_far = across(helm_inverse)
+    piece = lax.dynamic_slice_in_dim(helm_inverse, lot * modes, modes, axis=1)
+    helm_far = across(piece)[None]
     state_foreign = turn_state(where, state_axial, rate, True, 8)
     state_far = across(state_foreign)
-    leading = jnp.transpose(cotangent[:, :, 0], (1, 0, 2)).reshape(comps * modes, nphi)
-    last = jnp.transpose(cotangent[:, :, nz - 1], (1, 0, 2)).reshape(comps * modes, nphi)
+    leading, last = edge_layers(cotangent)
     before = lax.ppermute(last, "col", up)
     after = lax.ppermute(leading, "col", down)
+    after = tied(after, helm_far)
+    sent = first_stencil(where, cotangent, state_foreign, after, before, rate, True, CHUNKS)
+    far = [across(tied(s, state_far) if k else s) for k, s in enumerate(sent)]
+    mask = 1
+    while mask < PIECES:
+        helm_far = jnp.concatenate([helm_far, hop(helm_far, mask)])
+        mask *= 2
+
     state_own = turn_state(where, state_axial, rate, False, 0)
-
-    sent = first_stencil(where, cotangent, state_foreign, after, before, rate, True, CHUNKS)
-    far = [across(s) for s in sent]
     (own,) = first_stencil(where, cotangent, state_own, after, before, rate, False, 1)
     own_peer = beside(own)
     high, low = split_helm(where, helm_inverse, helm_far)
 
+    once = 1 + (where[0] >> 8)
     kept, back = [], []
     for k in range(CHUNKS):
-        cur, leading, last = map1(own, far[k], own_peer, beside(far[k]), high, low, k)
-        before = lax.ppermute(last, "col", up)
-        after = lax.ppermute(leading, "col", down)
-        nxt = second_stencil(cur, after, before, state_own, state_far, rate, k, half)
-        mine, theirs = map2(nxt, beside(nxt), high, low, k)
+
+        def chain(_, pair, k=k):
+            here = pair[0]
+            cur, leading, last = map1(own, here, own_peer, beside(here), high, low, k)
+            before = lax.ppermute(last, "col", up)
+            after = lax.ppermute(leading, "col", down)
+            nxt = second_stencil(cur, after, before, state_own, state_far, rate, k, half)
+            mine, theirs = map2(nxt, beside(nxt), high, low, k)
+            return theirs, mine
+
+        here = tied(far[k], kept[-1]) if k else far[k]
+        theirs, mine = lax.fori_loop(0, once, chain, (here, sent[k]))
         kept.append(mine)
         back.append(across(theirs))
     out = write_half(where, kept, nphi, False)

time: 246 us -> 204 us (0.83)
  waiting for transfers between devices: 174 us -> 97.6 us
  Pallas kernels: 28.3 us -> 64.9 us
  starting transfers between devices: 36.8 us -> 32 us
    ppermute x10, waiting for transfers between devices: 147 us -> 33.1 us  [across(): return lax.ppermute(array, 'rad', [(i, i ^ 2) for i in range(peers)])]
    ppermute x0 -> x10, waiting for transfers between devices: none -> 34.3 us  [the longest x4 13.2 us: chain(): before = lax.ppermute(last, 'col', up)]
    ppermute x9, waiting for transfers between devices: 0.02 us -> 23.6 us  [beside(): return lax.ppermute(array, 'rad', [(i, i ^ 1) for i in range(peers)])]
    ppermute x5 -> x1, starting transfers between devices: 22.7 us -> 6 us  [on_device(): after = lax.ppermute(leading, 'col', down)]
    ppermute x0 -> x10, starting transfers between devices: none -> 14.3 us  [the longest x4 5.51 us: chain(): after = lax.ppermute(leading, 'col', down)]
    ppermute x5 -> x1, waiting for transfers between devices: 18.4 us -> 6.51 us  [on_device(): after = lax.ppermute(leading, 'col', down)]
    pallas_call x4, Pallas kernels: 7.18 us -> 17 us  [map2(): pl.pallas_call(map2_kernel, out_shape=[shape(out)] * 2, grid=(comps,), in...]
    ppermute x5 -> x1, waiting for transfers between devices: 8.34 us -> 0.16 us  [on_device(): before = lax.ppermute(last, 'col', up)]
  transfers between devices with their start and end apart: 29 -> 31, of which waited for: 17 -> 24; matrix products, arithmetic and copies ran while one was open for 0% -> 1% of each run, Pallas kernels for 9% -> 26%
where the time goes in v2:
time: 204 us; the launch traced here: 203 us
  waiting for transfers between devices  97.6 us (48%)
  Pallas kernels  64.9 us (32%)
  starting transfers between devices  32 us (16%)
  local copies, waits for them, and re-layouts  7.24 us (4%)
    ppermute x10, waiting for transfers between devices, across(): return lax.ppermute(array, 'rad', [(i, i ^ 2) for i in range(peers)])  33.1 us
    ppermute x9, waiting for transfers between devices, beside(): return lax.ppermute(array, 'rad', [(i, i ^ 1) for i in range(peers)])  23.6 us
    pallas_call x4, Pallas kernels, map2(): pl.pallas_call(map2_kernel, out_shape=[shape(out)] * 2, grid=(comps,), in...  17 us
    pallas_call x4, Pallas kernels, map1(): pl.pallas_call(map1_kernel, out_shape=[shape((comps, nz, width, cols)), s...  15.3 us
    ppermute x4, waiting for transfers between devices, chain(): before = lax.ppermute(last, 'col', up)  13.2 us
    ppermute x10, starting transfers between devices, across(): return lax.ppermute(array, 'rad', [(i, i ^ 2) for i in range(peers)])  11.3 us
    pallas_call x2, Pallas kernels, write_half(): pl.pallas_call(lambda *refs: last_kernel(*refs, nz=nz, chunks=chunks), ou...  11 us
    ppermute x4, waiting for transfers between devices, chain(): after = lax.ppermute(leading, 'col', down)  10.8 us
  transfers between devices with their start and end apart: 31, of which 24 were waited for; matrix products, arithmetic and copies ran while one was open for 1% of the time, Pallas kernels for 26%

profile of v2, /device:TPU:0, one launch (start us, length us, event | category | flops | bytes accessed | tf_op | source)
XLA Modules:
  0.0 203.1 jit_solution(11106704176800522621)
XLA Ops:
  0.0 2.8 %copy-done = f32[128,3,16,256]{3,2,1,0:T(8,128)S(1)} copy-done((f32[128,3,16,256]{3,2,1,0:T(8,128)S(1)}, f32[128,3,16,256]{3,2,1,0:T(8,128)}, u32[]{:S(2)}) %copy-start) | copy-done | bytes 6291480
  4.3 6.0 %collective-permute-start.16 = (f32[384,256]{1,0:T(8,128)}, f32[384,256]{1,0:T(8,128)S(1)}, u32[]{:S(2)}, u32[]{:S(2)}) collective-permute-start(f32[384,256]{1,0:T(8,128)} %get-tuple-element.272), channel_id=1, source_target_pairs={{1,0},{2,1},{3,2},{4,3},{5,4},{6,5},{7,6},{0,7},{9,8},{10,9},{11,1... | collective-permute-start | bytes 1179656 | tf_op jit(solution)/shard_map/ppermute | solution.py:325
  10.3 1.6 constant_dynamic-slice_fusion
  14.6 3.9 %collective-permute-done.17 = f32[3,128,128]{2,1,0:T(8,128)S(1)} collective-permute-done((f32[3,128,128]{2,1,0:T(8,128)}, f32[3,128,128]{2,1,0:T(8,128)S(1)}, u32[]{:S(2)}, u32[]{:S(2)}) %collective-permute-start.17) | collective-permute-done | bytes 196640 | tf_op jit(solution)/shard_map/ppermute | solution.py:307
  18.5 6.5 %collective-permute-done.16.refs_3_ = f32[384,256]{1,0:T(8,128)S(1)} collective-permute-done((f32[384,256]{1,0:T(8,128)}, f32[384,256]{1,0:T(8,128)S(1)}, u32[]{:S(2)}, u32[]{:S(2)}) %collective-permute-start.16) | collective-permute-done | bytes 393248 | tf_op jit(solution)/shard_map/ppermute | solution.py:325
  25.2 2.8 %copy-done.1 = f32[128,3,16,256]{3,2,1,0:T(8,128)S(1)} copy-done((f32[128,3,16,256]{3,2,1,0:T(8,128)S(1)}, f32[128,3,16,256]{3,2,1,0:T(8,128)}, u32[]{:S(2)}) %copy-start.1) | copy-done | bytes 6291480
  28.0 4.6 %first_stencil.3 = f32[3,16,128,128]{3,2,1,0:T(8,128)} custom-call(s32[2]{0:T(128)S(1)} %pad_add_fusion.refs_0_.where, f32[6144,256]{1,0:T(8,128)S(1)} %bitcast.8, f32[2048,128]{1,0:T(8,128)S(1)} %turn_state.3.refs_2_, f32[384,256]{1,0:T(8,128)S(1)} %collective-permute-done.16.refs_3_, f32[384,256]{1,0:T(8,128)S(1)} %collective-permute-done.18.refs_4_, ...), custom_call_target="tpu_custom_call" | custom-call | flops 9437184 | bytes 6291456 | tf_op jit(solution)/shard_map/first_stencil/pallas_call | solution.py:131
  35.3 2.4 %collective-permute-start.21 = (f32[1,3,128,128]{3,2,1,0:T(8,128)S(1)}, f32[1,3,128,128]{3,2,1,0:T(8,128)S(1)}, u32[]{:S(2)}, u32[]{:S(2)}) collective-permute-start(f32[1,3,128,128]{3,2,1,0:T(8,128)S(1)} %bitcast.12), channel_id=1, source_target_pairs={{0,1},{1,0},{2,3},{3,2},{4,5},{5,4},{6,7},{7,6},{8,9},{9,8},{10,11... | collective-permute-start | bytes 589832 | tf_op jit(solution)/shard_map/ppermute | solution.py:313
  37.7 4.3 %first_stencil.2 = (f32[3,16,32,128]{3,2,1,0:T(8,128)S(1)}, f32[3,16,32,128]{3,2,1,0:T(8,128)}, f32[3,16,32,128]{3,2,1,0:T(8,128)}, f32[3,16,32,128]{3,2,1,0:T(8,128)}) custom-call(s32[2]{0:T(128)S(1)} %pad_add_fusion.refs_0_.where, f32[6144,256]{1,0:T(8,128)S(1)} %bitcast.9, f32[2056,128]{1,0:T(8,128)S(1)} %turn_state.2.refs_2_, ...), custom_call_target="tpu_custom_call" | custom-call | flops 9437184 | bytes 6291456 | tf_op jit(solution)/shard_map/first_stencil/pallas_call | solution.py:131
  44.0 10.0 %collective-permute-done.22 = f32[2,3,128,128]{3,2,1,0:T(8,128)} collective-permute-done((f32[2,3,128,128]{3,2,1,0:T(8,128)S(1)}, f32[2,3,128,128]{3,2,1,0:T(8,128)}, u32[]{:S(2)}, u32[]{:S(2)}) %collective-permute-start.22) | collective-permute-done | bytes 393248 | tf_op jit(solution)/shard_map/ppermute | solution.py:313
  55.1 2.6 %split_helm.1 = (bf16[3,512,256]{2,1,0:T(8,128)(2,1)}, bf16[3,512,256]{2,1,0:T(8,128)(2,1)}) custom-call(s32[2]{0:T(128)S(1)} %pad_add_fusion.refs_0_.where, f32[3,512,128]{2,1,0:T(8,128)S(1)} %copy-done.6, f32[4,3,128,128]{3,2,1,0:T(8,128)S(1)} %pad_maximum_fusion.far), custom_call_target="tpu_custom_call" | custom-call | flops 786432 | bytes 3145728 | tf_op jit(solution)/shard_map/split_helm/pallas_call | solution.py:165
  57.7 2.3 %collective-permute-done.23 = f32[2056,128]{1,0:T(8,128)} collective-permute-done((f32[2056,128]{1,0:T(8,128)S(1)}, f32[2056,128]{1,0:T(8,128)}, u32[]{:S(2)}, u32[]{:S(2)}) %collective-permute-start.23) | collective-permute-done | bytes 1052704 | tf_op jit(solution)/shard_map/ppermute | solution.py:307
  63.5 13.3 %collective-permute-done.19 = f32[3,16,32,128]{3,2,1,0:T(8,128)} collective-permute-done((f32[3,16,32,128]{3,2,1,0:T(8,128)S(1)}, f32[3,16,32,128]{3,2,1,0:T(8,128)}, u32[]{:S(2)}, u32[]{:S(2)}) %collective-permute-start.19) | collective-permute-done | bytes 786464 | tf_op jit(solution)/shard_map/ppermute | solution.py:307
  76.8 27.7 %while.48 = (s32[]{:T(128)}, f32[3,16,32,128]{3,2,1,0:T(8,128)}, f32[3,16,32,128]{3,2,1,0:T(8,128)}, s32[]{:T(128)}, f32[3,16,128,128]{3,2,1,0:T(8,128)}, /*inde...) while((s32[]{:T(128)}, f32[3,16,32,128]{3,2,1,0:T(8,128)}, ...), condition=%wide.region_1.0_spmd, body=%wide.region_0.0_spmd.sunk | while | flops 2420637696 | bytes 30146864 | solution.py:353
  76.8 2.5 %collective-permute-done.far_peer = f32[3,16,32,128]{3,2,1,0:T(8,128)S(1)} collective-permute-done((f32[3,16,32,128]{3,2,1,0:T(8,128)}, f32[3,16,32,128]{3,2,1,0:T(8,128)S(1)}, u32[]{:S(2)}, u32[]{:S(2)}) %collective-permute-start) | collective-permute-done | bytes 786464 | tf_op jit(solution)/shard_map/while/body/ppermute | solution.py:310
  79.3 3.8 %map1_0.1 = (f32[3,16,32,256]{3,2,1,0:T(8,128)S(1)}, f32[3,32,256]{2,1,0:T(8,128)S(1)}, f32[3,32,256]{2,1,0:T(8,128)S(1)}) custom-call(f32[3,16,128,128]{3,2,1,0:T(8,128)} %get-tuple-element.715.own, f32[3,16,32,128]{3,2,1,0:T(8,128)} %get-tuple-element.700.far, f32[3,16,128,128]{3,2,1,0:T(8,128)} %get-tuple-element.716.own_peer, ...), custom_call_target="tpu_custom_call" | custom-call | flops 1207959552 | bytes 6291456 | tf_op jit(solution)/shard_map/while/body/map1_0/pallas_call | solution.py:200
  83.2 4.7 %collective-permute-start.1 = (f32[3,32,256]{2,1,0:T(8,128)S(1)}, f32[3,32,256]{2,1,0:T(8,128)S(1)}, u32[]{:S(2)}, u32[]{:S(2)}) collective-permute-start(f32[3,32,256]{2,1,0:T(8,128)S(1)} %get-tuple-element.638), channel_id=1, source_target_pairs={{1,0},{2,1},{3,2},{4,3},{5,4},{6,5},{7,6},{0,7},{9,8},{10,9},{11,1... | collective-permute-start | bytes 294920 | tf_op jit(solution)/shard_map/while/body/ppermute | solution.py:347
  87.8 2.4 %collective-permute-done.1.refs_1_ = f32[3,32,256]{2,1,0:T(8,128)S(1)} collective-permute-done((f32[3,32,256]{2,1,0:T(8,128)S(1)}, f32[3,32,256]{2,1,0:T(8,128)S(1)}, u32[]{:S(2)}, u32[]{:S(2)}) %collective-permute-start.1) | collective-permute-done | bytes 98336 | tf_op jit(solution)/shard_map/while/body/ppermute | solution.py:347
  90.2 5.0 %collective-permute-done.2.refs_2_ = f32[3,32,256]{2,1,0:T(8,128)S(1)} collective-permute-done((f32[3,32,256]{2,1,0:T(8,128)S(1)}, f32[3,32,256]{2,1,0:T(8,128)S(1)}, u32[]{:S(2)}, u32[]{:S(2)}) %collective-permute-start.2) | collective-permute-done | bytes 98336 | tf_op jit(solution)/shard_map/while/body/ppermute | solution.py:346
  96.9 3.4 %collective-permute-done.3.peer = f32[3,16,32,256]{3,2,1,0:T(8,128)S(1)} collective-permute-done((f32[3,16,32,256]{3,2,1,0:T(8,128)S(1)}, f32[3,16,32,256]{3,2,1,0:T(8,128)S(1)}, u32[]{:S(2)}, u32[]{:S(2)}) %collective-permute-start.3) | collective-permute-done | bytes 1572896 | tf_op jit(solution)/shard_map/while/body/ppermute | solution.py:310
  100.3 4.2 %map2_0.1 = (f32[3,16,32,128]{3,2,1,0:T(8,128)}, f32[3,16,32,128]{3,2,1,0:T(8,128)}) custom-call(f32[3,16,32,256]{3,2,1,0:T(8,128)S(1)} %second_stencil_0.1.own, f32[3,16,32,256]{3,2,1,0:T(8,128)S(1)} %collective-permute-done.3.peer, bf16[3,512,256]{2,1,0:T(8,128)(2,1)} %get-tuple-element.717.high, bf16[3,512,256]{2,1,0:T(8,128)(2,1)} %get-tuple-element.718.low), custom_call_target="tpu_custom_call" | custom-call | flops 1207959552 | bytes 6291456 | tf_op jit(solution)/shard_map/while/body/map2_0/pallas_call | solution.py:254
  105.9 23.3 %while.49 = (s32[]{:T(128)}, f32[3,16,32,128]{3,2,1,0:T(8,128)}, f32[3,16,32,128]{3,2,1,0:T(8,128)}, s32[]{:T(128)}, f32[3,16,128,128]{3,2,1,0:T(8,128)}, /*inde...) while((s32[]{:T(128)}, f32[3,16,32,128]{3,2,1,0:T(8,128)}, ...), condition=%wide.region_3.0_spmd, body=%wide.region_2.0_spmd.sunk | while | flops 2420637696 | bytes 30146864 | solution.py:353
  105.9 2.5 %collective-permute-done.4.far_peer = f32[3,16,32,128]{3,2,1,0:T(8,128)S(1)} collective-permute-done((f32[3,16,32,128]{3,2,1,0:T(8,128)}, f32[3,16,32,128]{3,2,1,0:T(8,128)S(1)}, u32[]{:S(2)}, u32[]{:S(2)}) %collective-permute-start.4) | collective-permute-done | bytes 786464 | tf_op jit(solution)/shard_map/while/body/ppermute | solution.py:310
  108.4 3.8 %map1_1.1 = (f32[3,16,32,256]{3,2,1,0:T(8,128)S(1)}, f32[3,32,256]{2,1,0:T(8,128)S(1)}, f32[3,32,256]{2,1,0:T(8,128)S(1)}) custom-call(f32[3,16,128,128]{3,2,1,0:T(8,128)} %get-tuple-element.751.own, f32[3,16,32,128]{3,2,1,0:T(8,128)} %get-tuple-element.736.far, f32[3,16,128,128]{3,2,1,0:T(8,128)} %get-tuple-element.752.own_peer, ...), custom_call_target="tpu_custom_call" | custom-call | flops 1207959552 | bytes 6291456 | tf_op jit(solution)/shard_map/while/body/map1_1/pallas_call | solution.py:200
  112.5 1.8 collective-permute-start.6
  114.3 2.8 %collective-permute-done.5.refs_1_ = f32[3,32,256]{2,1,0:T(8,128)S(1)} collective-permute-done((f32[3,32,256]{2,1,0:T(8,128)S(1)}, f32[3,32,256]{2,1,0:T(8,128)S(1)}, u32[]{:S(2)}, u32[]{:S(2)}) %collective-permute-start.5) | collective-permute-done | bytes 98336 | tf_op jit(solution)/shard_map/while/body/ppermute | solution.py:347
  117.1 2.8 %collective-permute-done.6.refs_2_ = f32[3,32,256]{2,1,0:T(8,128)S(1)} collective-permute-done((f32[3,32,256]{2,1,0:T(8,128)S(1)}, f32[3,32,256]{2,1,0:T(8,128)S(1)}, u32[]{:S(2)}, u32[]{:S(2)}) %collective-permute-start.6) | collective-permute-done | bytes 98336 | tf_op jit(solution)/shard_map/while/body/ppermute | solution.py:346
  121.6 3.4 %collective-permute-done.7.peer = f32[3,16,32,256]{3,2,1,0:T(8,128)S(1)} collective-permute-done((f32[3,16,32,256]{3,2,1,0:T(8,128)S(1)}, f32[3,16,32,256]{3,2,1,0:T(8,128)S(1)}, u32[]{:S(2)}, u32[]{:S(2)}) %collective-permute-start.7) | collective-permute-done | bytes 1572896 | tf_op jit(solution)/shard_map/while/body/ppermute | solution.py:310
  125.0 4.2 %map2_1.1 = (f32[3,16,32,128]{3,2,1,0:T(8,128)}, f32[3,16,32,128]{3,2,1,0:T(8,128)}) custom-call(f32[3,16,32,256]{3,2,1,0:T(8,128)S(1)} %second_stencil_1.1.own, f32[3,16,32,256]{3,2,1,0:T(8,128)S(1)} %collective-permute-done.7.peer, bf16[3,512,256]{2,1,0:T(8,128)(2,1)} %get-tuple-element.753.high, bf16[3,512,256]{2,1,0:T(8,128)(2,1)} %get-tuple-element.754.low), custom_call_target="tpu_custom_call" | custom-call | flops 1207959552 | bytes 6291456 | tf_op jit(solution)/shard_map/while/body/map2_1/pallas_call | solution.py:254
  129.8 23.4 %while.50 = (s32[]{:T(128)}, f32[3,16,32,128]{3,2,1,0:T(8,128)}, f32[3,16,32,128]{3,2,1,0:T(8,128)}, s32[]{:T(128)}, f32[3,16,128,128]{3,2,1,0:T(8,128)}, /*inde...) while((s32[]{:T(128)}, f32[3,16,32,128]{3,2,1,0:T(8,128)}, ...), condition=%wide.region_5.0_spmd, body=%wide.region_4.0_spmd.sunk | while | flops 2420637696 | bytes 30146864 | solution.py:353
  129.8 2.5 %collective-permute-done.8.far_peer = f32[3,16,32,128]{3,2,1,0:T(8,128)S(1)} collective-permute-done((f32[3,16,32,128]{3,2,1,0:T(8,128)}, f32[3,16,32,128]{3,2,1,0:T(8,128)S(1)}, u32[]{:S(2)}, u32[]{:S(2)}) %collective-permute-start.8) | collective-permute-done | bytes 786464 | tf_op jit(solution)/shard_map/while/body/ppermute | solution.py:310
  132.3 3.8 %map1_2.1 = (f32[3,16,32,256]{3,2,1,0:T(8,128)S(1)}, f32[3,32,256]{2,1,0:T(8,128)S(1)}, f32[3,32,256]{2,1,0:T(8,128)S(1)}) custom-call(f32[3,16,128,128]{3,2,1,0:T(8,128)} %get-tuple-element.787.own, f32[3,16,32,128]{3,2,1,0:T(8,128)} %get-tuple-element.772.far, f32[3,16,128,128]{3,2,1,0:T(8,128)} %get-tuple-element.788.own_peer, ...), custom_call_target="tpu_custom_call" | custom-call | flops 1207959552 | bytes 6291456 | tf_op jit(solution)/shard_map/while/body/map1_2/pallas_call | solution.py:200
  136.4 1.8 collective-permute-start.10
  138.2 2.8 %collective-permute-done.9.refs_1_ = f32[3,32,256]{2,1,0:T(8,128)S(1)} collective-permute-done((f32[3,32,256]{2,1,0:T(8,128)S(1)}, f32[3,32,256]{2,1,0:T(8,128)S(1)}, u32[]{:S(2)}, u32[]{:S(2)}) %collective-permute-start.9) | collective-permute-done | bytes 98336 | tf_op jit(solution)/shard_map/while/body/ppermute | solution.py:347
  141.1 2.8 %collective-permute-done.10.refs_2_ = f32[3,32,256]{2,1,0:T(8,128)S(1)} collective-permute-done((f32[3,32,256]{2,1,0:T(8,128)S(1)}, f32[3,32,256]{2,1,0:T(8,128)S(1)}, u32[]{:S(2)}, u32[]{:S(2)}) %collective-permute-start.10) | collective-permute-done | bytes 98336 | tf_op jit(solution)/shard_map/while/body/ppermute | solution.py:346
  145.5 3.4 %collective-permute-done.11.peer = f32[3,16,32,256]{3,2,1,0:T(8,128)S(1)} collective-permute-done((f32[3,16,32,256]{3,2,1,0:T(8,128)S(1)}, f32[3,16,32,256]{3,2,1,0:T(8,128)S(1)}, u32[]{:S(2)}, u32[]{:S(2)}) %collective-permute-start.11) | collective-permute-done | bytes 1572896 | tf_op jit(solution)/shard_map/while/body/ppermute | solution.py:310
  148.9 4.3 %map2_2.1 = (f32[3,16,32,128]{3,2,1,0:T(8,128)}, f32[3,16,32,128]{3,2,1,0:T(8,128)}) custom-call(f32[3,16,32,256]{3,2,1,0:T(8,128)S(1)} %second_stencil_2.1.own, f32[3,16,32,256]{3,2,1,0:T(8,128)S(1)} %collective-permute-done.11.peer, bf16[3,512,256]{2,1,0:T(8,128)(2,1)} %get-tuple-element.789.high, bf16[3,512,256]{2,1,0:T(8,128)(2,1)} %get-tuple-element.790.low), custom_call_target="tpu_custom_call" | custom-call | flops 1207959552 | bytes 6291456 | tf_op jit(solution)/shard_map/while/body/map2_2/pallas_call | solution.py:254
  154.6 23.3 %while.51 = (s32[]{:T(128)}, f32[3,16,32,128]{3,2,1,0:T(8,128)}, f32[3,16,32,128]{3,2,1,0:T(8,128)}, s32[]{:T(128)}, f32[3,16,128,128]{3,2,1,0:T(8,128)}, /*inde...) while((s32[]{:T(128)}, f32[3,16,32,128]{3,2,1,0:T(8,128)}, ...), condition=%wide.region_7.0_spmd, body=%wide.region_6.0_spmd.sunk | while | flops 2420637696 | bytes 30146864 | solution.py:353
  154.6 2.5 %collective-permute-done.12.far_peer = f32[3,16,32,128]{3,2,1,0:T(8,128)S(1)} collective-permute-done((f32[3,16,32,128]{3,2,1,0:T(8,128)}, f32[3,16,32,128]{3,2,1,0:T(8,128)S(1)}, u32[]{:S(2)}, u32[]{:S(2)}) %collective-permute-start.12) | collective-permute-done | bytes 786464 | tf_op jit(solution)/shard_map/while/body/ppermute | solution.py:310
  157.1 3.8 %map1_3.1 = (f32[3,16,32,256]{3,2,1,0:T(8,128)S(1)}, f32[3,32,256]{2,1,0:T(8,128)S(1)}, f32[3,32,256]{2,1,0:T(8,128)S(1)}) custom-call(f32[3,16,128,128]{3,2,1,0:T(8,128)} %get-tuple-element.823.own, f32[3,16,32,128]{3,2,1,0:T(8,128)} %get-tuple-element.808.far, f32[3,16,128,128]{3,2,1,0:T(8,128)} %get-tuple-element.824.own_peer, ...), custom_call_target="tpu_custom_call" | custom-call | flops 1207959552 | bytes 6291456 | tf_op jit(solution)/shard_map/while/body/map1_3/pallas_call | solution.py:200
  161.2 1.8 collective-permute-start.14
  163.0 2.8 %collective-permute-done.13.refs_1_ = f32[3,32,256]{2,1,0:T(8,128)S(1)} collective-permute-done((f32[3,32,256]{2,1,0:T(8,128)S(1)}, f32[3,32,256]{2,1,0:T(8,128)S(1)}, u32[]{:S(2)}, u32[]{:S(2)}) %collective-permute-start.13) | collective-permute-done | bytes 98336 | tf_op jit(solution)/shard_map/while/body/ppermute | solution.py:347
  165.8 2.8 %collective-permute-done.14.refs_2_ = f32[3,32,256]{2,1,0:T(8,128)S(1)} collective-permute-done((f32[3,32,256]{2,1,0:T(8,128)S(1)}, f32[3,32,256]{2,1,0:T(8,128)S(1)}, u32[]{:S(2)}, u32[]{:S(2)}) %collective-permute-start.14) | collective-permute-done | bytes 98336 | tf_op jit(solution)/shard_map/while/body/ppermute | solution.py:346
  170.3 3.4 %collective-permute-done.15.peer = f32[3,16,32,256]{3,2,1,0:T(8,128)S(1)} collective-permute-done((f32[3,16,32,256]{3,2,1,0:T(8,128)S(1)}, f32[3,16,32,256]{3,2,1,0:T(8,128)S(1)}, u32[]{:S(2)}, u32[]{:S(2)}) %collective-permute-start.15) | collective-permute-done | bytes 1572896 | tf_op jit(solution)/shard_map/while/body/ppermute | solution.py:310
  173.7 4.2 %map2_3.1 = (f32[3,16,32,128]{3,2,1,0:T(8,128)}, f32[3,16,32,128]{3,2,1,0:T(8,128)}) custom-call(f32[3,16,32,256]{3,2,1,0:T(8,128)S(1)} %second_stencil_3.1.own, f32[3,16,32,256]{3,2,1,0:T(8,128)S(1)} %collective-permute-done.15.peer, bf16[3,512,256]{2,1,0:T(8,128)(2,1)} %get-tuple-element.825.high, bf16[3,512,256]{2,1,0:T(8,128)(2,1)} %get-tuple-element.826.low), custom_call_target="tpu_custom_call" | custom-call | flops 1207959552 | bytes 6291456 | tf_op jit(solution)/shard_map/while/body/map2_3/pallas_call | solution.py:254
  178.5 5.6 %write_own.1.refs_5_ = f32[128,48,256]{2,1,0:T(8,128)} custom-call(s32[2]{0:T(128)S(1)} %pad_add_fusion.refs_0_.where, f32[3,16,32,128]{3,2,1,0:T(8,128)} %get-tuple-element.281.refs_1_, f32[3,16,32,128]{3,2,1,0:T(8,128)} %get-tuple-element.286.refs_2_, f32[3,16,32,128]{3,2,1,0:T(8,128)} %get-tuple-element.291.refs_3_, ...), custom_call_target="tpu_custom_call" | custom-call | flops 1572864 | bytes 6291456 | tf_op jit(solution)/shard_map/write_own/pallas_call | solution.py:278
  184.2 13.5 %collective-permute-done.30.refs_4_ = f32[3,16,32,128]{3,2,1,0:T(8,128)S(1)} collective-permute-done((f32[3,16,32,128]{3,2,1,0:T(8,128)}, f32[3,16,32,128]{3,2,1,0:T(8,128)S(1)}, u32[]{:S(2)}, u32[]{:S(2)}) %collective-permute-start.30) | collective-permute-done | bytes 786464 | tf_op jit(solution)/shard_map/ppermute | solution.py:307
  197.7 5.4 %write_foreign.1 = f32[128,48,256]{2,1,0:T(8,128)} custom-call(s32[2]{0:T(128)S(1)} %pad_add_fusion.refs_0_.where, f32[3,16,32,128]{3,2,1,0:T(8,128)} %collective-permute-done.24.refs_1_, f32[3,16,32,128]{3,2,1,0:T(8,128)} %collective-permute-done.26.refs_2_, f32[3,16,32,128]{3,2,1,0:T(8,128)} %collective-permute-done.28.refs_3_, ...), custom_call_target="tpu_custom_call", output_to_operand_aliasing={{}: (5, {})} | custom-call | flops 1572864 | bytes 6291456 | tf_op jit(solution)/shard_map/write_foreign/pallas_call | solution.py:278
  (76 shorter events, 25.3 us)
Async XLA Ops:
  0.0 2.8 %copy-start = (f32[128,3,16,256]{3,2,1,0:T(8,128)S(1)}, f32[128,3,16,256]{3,2,1,0:T(8,128)}, u32[]{:S(2)}) copy-start(f32[128,3,16,256]{3,2,1,0:T(8,128)} %param.12) | copy-start | bytes 18874372
  2.8 10.7 %copy-start.3 = (f32[128,16,256]{2,1,0:T(8,128)S(1)}, f32[128,16,256]{2,1,0:T(8,128)}, u32[]{:S(2)}) copy-start(f32[128,16,256]{2,1,0:T(8,128)} %param.13) | copy-start | bytes 6291460
  2.8 10.7 %copy-start.16 = (f32[128]{0:T(128)S(1)}, f32[128]{0:T(128)}, u32[]{:S(2)}) copy-start(f32[128]{0:T(128)} %param.15) | copy-start | bytes 1540
  4.3 20.7 %collective-permute-start.16 = (f32[384,256]{1,0:T(8,128)}, f32[384,256]{1,0:T(8,128)S(1)}, u32[]{:S(2)}, u32[]{:S(2)}) collective-permute-start(f32[384,256]{1,0:T(8,128)} %get-tuple-element.272), channel_id=1, source_target_pairs={{1,0},{2,1},{3,2},{4,3},{5,4},{6,5},{7,6},{0,7},{9,8},{10,9},{11,1... | collective-permute-start | bytes 1179656 | tf_op jit(solution)/shard_map/ppermute | solution.py:325
  10.3 14.9 %collective-permute-start.18 = (f32[384,256]{1,0:T(8,128)S(1)}, f32[384,256]{1,0:T(8,128)S(1)}, u32[]{:S(2)}, u32[]{:S(2)}) collective-permute-start(f32[384,256]{1,0:T(8,128)S(1)} %get-tuple-element.274), channel_id=1, source_target_pairs={{0,1},{1,2},{2,3},{3,4},{4,5},{5,6},{6,7},{7,0},{8,9},{9,10},{10,1... | collective-permute-start | bytes 1179656 | tf_op jit(solution)/shard_map/ppermute | solution.py:324
  11.9 6.6 %collective-permute-start.17 = (f32[3,128,128]{2,1,0:T(8,128)}, f32[3,128,128]{2,1,0:T(8,128)S(1)}, u32[]{:S(2)}, u32[]{:S(2)}) collective-permute-start(f32[3,128,128]{2,1,0:T(8,128)} %constant_dynamic-slice_fusion), channel_id=1, source_target_pairs={{0,16},{8,24},{16,0},{24,8},{1,17},{9,25},{17,1},{25,9},{2,18},{10... | collective-permute-start | bytes 589832 | tf_op jit(solution)/shard_map/ppermute | solution.py:307
  14.6 18.0 %copy-start.7 = (f32[2048,128]{1,0:T(8,128)}, f32[2048,128]{1,0:T(8,128)S(1)}, u32[]{:S(2)}) copy-start(f32[2048,128]{1,0:T(8,128)S(1)} %turn_state.3.refs_2_) | copy-start | bytes 3145732
  18.5 14.1 %copy-start.13 = (f32[3,128,128]{2,1,0:T(8,128)}, f32[3,128,128]{2,1,0:T(8,128)S(1)}, u32[]{:S(2)}) copy-start(f32[3,128,128]{2,1,0:T(8,128)S(1)} %collective-permute-done.17) | copy-start | bytes 589828
  25.2 2.8 %copy-start.1 = (f32[128,3,16,256]{3,2,1,0:T(8,128)S(1)}, f32[128,3,16,256]{3,2,1,0:T(8,128)}, u32[]{:S(2)}) copy-start(f32[128,3,16,256]{3,2,1,0:T(8,128)} %param.12) | copy-start | bytes 18874372
  28.0 4.6 %copy-start.4 = (f32[384,256]{1,0:T(8,128)}, f32[384,256]{1,0:T(8,128)S(1)}, u32[]{:S(2)}) copy-start(f32[384,256]{1,0:T(8,128)S(1)} %collective-permute-done.18.refs_4_) | copy-start | bytes 1179652
  28.0 9.7 %copy-start.2 = (f32[128,3,16,256]{3,2,1,0:T(8,128)S(1)}, f32[128,3,16,256]{3,2,1,0:T(8,128)}, u32[]{:S(2)}) copy-start(f32[128,3,16,256]{3,2,1,0:T(8,128)} %param.12) | copy-start | bytes 18874372
  32.6 44.2 %collective-permute-start.20 = (f32[3,16,128,128]{3,2,1,0:T(8,128)}, f32[3,16,128,128]{3,2,1,0:T(8,128)}, u32[]{:S(2)}, u32[]{:S(2)}) collective-permute-start(f32[3,16,128,128]{3,2,1,0:T(8,128)} %first_stencil.3), channel_id=1, source_target_pairs={{0,8},{8,0},{16,24},{24,16},{1,9},{9,1},{17,25},{25,17},{2,10},{10... | collective-permute-start | bytes 9437192 | tf_op jit(solution)/shard_map/ppermute | solution.py:310
  32.7 2.6 %copy-start.14 = (f32[3,128,128]{2,1,0:T(8,128)S(1)}, f32[3,128,128]{2,1,0:T(8,128)}, u32[]{:S(2)}) copy-start(f32[3,128,128]{2,1,0:T(8,128)} %copy-done.13) | copy-start | bytes 589828
  32.7 5.0 %copy-start.5 = (f32[384,256]{1,0:T(8,128)S(1)}, f32[384,256]{1,0:T(8,128)}, u32[]{:S(2)}) copy-start(f32[384,256]{1,0:T(8,128)} %copy-done.4) | copy-start | bytes 1179652
  33.7 20.3 %copy-start.15 = (f32[3,128,128]{2,1,0:T(8,128)S(1)}, f32[3,128,128]{2,1,0:T(8,128)}, u32[]{:S(2)}) copy-start(f32[3,128,128]{2,1,0:T(8,128)} %copy-done.13) | copy-start | bytes 589828
  33.8 26.2 %collective-permute-start.23 = (f32[2056,128]{1,0:T(8,128)S(1)}, f32[2056,128]{1,0:T(8,128)}, u32[]{:S(2)}, u32[]{:S(2)}) collective-permute-start(f32[2056,128]{1,0:T(8,128)S(1)} %turn_state.2.refs_2_), channel_id=1, source_target_pairs={{0,16},{8,24},{16,0},{24,8},{1,17},{9,25},{17,1},{25,9},{2,18},{10... | collective-permute-start | bytes 3158024 | tf_op jit(solution)/shard_map/ppermute | solution.py:307
  35.3 7.7 %collective-permute-start.21 = (f32[1,3,128,128]{3,2,1,0:T(8,128)S(1)}, f32[1,3,128,128]{3,2,1,0:T(8,128)S(1)}, u32[]{:S(2)}, u32[]{:S(2)}) collective-permute-start(f32[1,3,128,128]{3,2,1,0:T(8,128)S(1)} %bitcast.12), channel_id=1, source_target_pairs={{0,1},{1,0},{2,3},{3,2},{4,5},{5,4},{6,7},{7,6},{8,9},{9,8},{10,11... | collective-permute-start | bytes 589832 | tf_op jit(solution)/shard_map/ppermute | solution.py:313
  42.0 15.7 %copy-start.12 = (f32[3,16,32,128]{3,2,1,0:T(8,128)}, f32[3,16,32,128]{3,2,1,0:T(8,128)S(1)}, u32[]{:S(2)}) copy-start(f32[3,16,32,128]{3,2,1,0:T(8,128)S(1)} %get-tuple-element.689) | copy-start | bytes 2359300
  42.0 13.1 %copy-start.6 = (f32[3,512,128]{2,1,0:T(8,128)S(1)}, f32[3,512,128]{2,1,0:T(8,128)}, u32[]{:S(2)}) copy-start(f32[3,512,128]{2,1,0:T(8,128)} %own.1) | copy-start | bytes 2359300
  42.0 34.8 %collective-permute-start.19 = (f32[3,16,32,128]{3,2,1,0:T(8,128)S(1)}, f32[3,16,32,128]{3,2,1,0:T(8,128)}, u32[]{:S(2)}, u32[]{:S(2)}) collective-permute-start(f32[3,16,32,128]{3,2,1,0:T(8,128)S(1)} %get-tuple-element.689), channel_id=1, source_target_pairs={{0,16},{8,24},{16,0},{24,8},{1,17},{9,25},{17,1},{25,9},{2,18},{10... | collective-permute-start | bytes 2359304 | tf_op jit(solution)/shard_map/ppermute | solution.py:307
  43.0 11.0 %collective-permute-start.22 = (f32[2,3,128,128]{3,2,1,0:T(8,128)S(1)}, f32[2,3,128,128]{3,2,1,0:T(8,128)}, u32[]{:S(2)}, u32[]{:S(2)}) collective-permute-start(f32[2,3,128,128]{3,2,1,0:T(8,128)S(1)} %pad_maximum_fusion.1), channel_id=1, source_target_pairs={{0,2},{1,3},{2,0},{3,1},{4,6},{5,7},{6,4},{7,5},{8,10},{9,11},{10,... | collective-permute-start | bytes 1179656 | tf_op jit(solution)/shard_map/ppermute | solution.py:313
  60.0 45.9 %collective-permute-start.25 = (f32[3,16,32,128]{3,2,1,0:T(8,128)}, f32[3,16,32,128]{3,2,1,0:T(8,128)}, u32[]{:S(2)}, u32[]{:S(2)}) collective-permute-start(f32[3,16,32,128]{3,2,1,0:T(8,128)} %get-tuple-element.280), channel_id=1, source_target_pairs={{0,16},{8,24},{16,0},{24,8},{1,17},{9,25},{17,1},{25,9},{2,18},{10... | collective-permute-start | bytes 2359304 | tf_op jit(solution)/shard_map/ppermute | solution.py:307
  61.5 68.4 %collective-permute-start.27 = (f32[3,16,32,128]{3,2,1,0:T(8,128)}, f32[3,16,32,128]{3,2,1,0:T(8,128)}, u32[]{:S(2)}, u32[]{:S(2)}) collective-permute-start(f32[3,16,32,128]{3,2,1,0:T(8,128)} %get-tuple-element.285), channel_id=1, source_target_pairs={{0,16},{8,24},{16,0},{24,8},{1,17},{9,25},{17,1},{25,9},{2,18},{10... | collective-permute-start | bytes 2359304 | tf_op jit(solution)/shard_map/ppermute | solution.py:307
  62.0 92.6 %collective-permute-start.29 = (f32[3,16,32,128]{3,2,1,0:T(8,128)}, f32[3,16,32,128]{3,2,1,0:T(8,128)}, u32[]{:S(2)}, u32[]{:S(2)}) collective-permute-start(f32[3,16,32,128]{3,2,1,0:T(8,128)} %get-tuple-element.290), channel_id=1, source_target_pairs={{0,16},{8,24},{16,0},{24,8},{1,17},{9,25},{17,1},{25,9},{2,18},{10... | collective-permute-start | bytes 2359304 | tf_op jit(solution)/shard_map/ppermute | solution.py:307
  76.8 2.5 %collective-permute-start = (f32[3,16,32,128]{3,2,1,0:T(8,128)}, f32[3,16,32,128]{3,2,1,0:T(8,128)S(1)}, u32[]{:S(2)}, u32[]{:S(2)}) collective-permute-start(f32[3,16,32,128]{3,2,1,0:T(8,128)} %get-tuple-element.700.far), channel_id=1, source_target_pairs={{0,8},{8,0},{16,24},{24,16},{1,9},{9,1},{17,25},{25,17},{2,10},{10... | collective-permute-start | bytes 2359304 | tf_op jit(solution)/shard_map/while/body/ppermute | solution.py:310
  79.3 15.8 %copy-start.8 = (f32[2048,128]{1,0:T(8,128)S(1)}, f32[2048,128]{1,0:T(8,128)}, u32[]{:S(2)}) copy-start(f32[2048,128]{1,0:T(8,128)} %get-tuple-element.719.refs_3_) | copy-start | bytes 3145732 | tf_op jit(solution)/shard_map/while
  83.2 7.0 %collective-permute-start.1 = (f32[3,32,256]{2,1,0:T(8,128)S(1)}, f32[3,32,256]{2,1,0:T(8,128)S(1)}, u32[]{:S(2)}, u32[]{:S(2)}) collective-permute-start(f32[3,32,256]{2,1,0:T(8,128)S(1)} %get-tuple-element.638), channel_id=1, source_target_pairs={{1,0},{2,1},{3,2},{4,3},{5,4},{6,5},{7,6},{0,7},{9,8},{10,9},{11,1... | collective-permute-start | bytes 294920 | tf_op jit(solution)/shard_map/while/body/ppermute | solution.py:347
  87.8 7.3 %collective-permute-start.2 = (f32[3,32,256]{2,1,0:T(8,128)S(1)}, f32[3,32,256]{2,1,0:T(8,128)S(1)}, u32[]{:S(2)}, u32[]{:S(2)}) collective-permute-start(f32[3,32,256]{2,1,0:T(8,128)S(1)} %get-tuple-element.639), channel_id=1, source_target_pairs={{0,1},{1,2},{2,3},{3,4},{4,5},{5,6},{6,7},{7,0},{8,9},{9,10},{10,1... | collective-permute-start | bytes 294920 | tf_op jit(solution)/shard_map/while/body/ppermute | solution.py:346
  96.8 3.5 %collective-permute-start.3 = (f32[3,16,32,256]{3,2,1,0:T(8,128)S(1)}, f32[3,16,32,256]{3,2,1,0:T(8,128)S(1)}, u32[]{:S(2)}, u32[]{:S(2)}) collective-permute-start(f32[3,16,32,256]{3,2,1,0:T(8,128)S(1)} %second_stencil_0.1.own), channel_id=1, source_target_pairs={{0,8},{8,0},{16,24},{24,16},{1,9},{9,1},{17,25},{25,17},{2,10},{10... | collective-permute-start | bytes 4718600 | tf_op jit(solution)/shard_map/while/body/ppermute | solution.py:310
  104.5 79.7 %collective-permute-start.24 = (f32[3,16,32,128]{3,2,1,0:T(8,128)}, f32[3,16,32,128]{3,2,1,0:T(8,128)}, u32[]{:S(2)}, u32[]{:S(2)}) collective-permute-start(f32[3,16,32,128]{3,2,1,0:T(8,128)} %get-tuple-element.278), channel_id=1, source_target_pairs={{0,16},{8,24},{16,0},{24,8},{1,17},{9,25},{17,1},{25,9},{2,18},{10... | collective-permute-start | bytes 2359304 | tf_op jit(solution)/shard_map/ppermute | solution.py:307
  105.9 2.5 %collective-permute-start.4 = (f32[3,16,32,128]{3,2,1,0:T(8,128)}, f32[3,16,32,128]{3,2,1,0:T(8,128)S(1)}, u32[]{:S(2)}, u32[]{:S(2)}) collective-permute-start(f32[3,16,32,128]{3,2,1,0:T(8,128)} %get-tuple-element.736.far), channel_id=1, source_target_pairs={{0,8},{8,0},{16,24},{24,16},{1,9},{9,1},{17,25},{25,17},{2,10},{10... | collective-permute-start | bytes 2359304 | tf_op jit(solution)/shard_map/while/body/ppermute | solution.py:310
  108.4 11.5 %copy-start.9 = (f32[2048,128]{1,0:T(8,128)S(1)}, f32[2048,128]{1,0:T(8,128)}, u32[]{:S(2)}) copy-start(f32[2048,128]{1,0:T(8,128)} %get-tuple-element.755.refs_3_) | copy-start | bytes 3145732 | tf_op jit(solution)/shard_map/while
  112.2 4.9 %collective-permute-start.5 = (f32[3,32,256]{2,1,0:T(8,128)S(1)}, f32[3,32,256]{2,1,0:T(8,128)S(1)}, u32[]{:S(2)}, u32[]{:S(2)}) collective-permute-start(f32[3,32,256]{2,1,0:T(8,128)S(1)} %get-tuple-element.653), channel_id=1, source_target_pairs={{1,0},{2,1},{3,2},{4,3},{5,4},{6,5},{7,6},{0,7},{9,8},{10,9},{11,1... | collective-permute-start | bytes 294920 | tf_op jit(solution)/shard_map/while/body/ppermute | solution.py:347
  112.5 7.4 %collective-permute-start.6 = (f32[3,32,256]{2,1,0:T(8,128)S(1)}, f32[3,32,256]{2,1,0:T(8,128)S(1)}, u32[]{:S(2)}, u32[]{:S(2)}) collective-permute-start(f32[3,32,256]{2,1,0:T(8,128)S(1)} %get-tuple-element.654), channel_id=1, source_target_pairs={{0,1},{1,2},{2,3},{3,4},{4,5},{5,6},{6,7},{7,0},{8,9},{9,10},{10,1... | collective-permute-start | bytes 294920 | tf_op jit(solution)/shard_map/while/body/ppermute | solution.py:346
  121.5 3.5 %collective-permute-start.7 = (f32[3,16,32,256]{3,2,1,0:T(8,128)S(1)}, f32[3,16,32,256]{3,2,1,0:T(8,128)S(1)}, u32[]{:S(2)}, u32[]{:S(2)}) collective-permute-start(f32[3,16,32,256]{3,2,1,0:T(8,128)S(1)} %second_stencil_1.1.own), channel_id=1, source_target_pairs={{0,8},{8,0},{16,24},{24,16},{1,9},{9,1},{17,25},{25,17},{2,10},{10... | collective-permute-start | bytes 4718600 | tf_op jit(solution)/shard_map/while/body/ppermute | solution.py:310
  129.2 55.0 %collective-permute-start.26 = (f32[3,16,32,128]{3,2,1,0:T(8,128)}, f32[3,16,32,128]{3,2,1,0:T(8,128)}, u32[]{:S(2)}, u32[]{:S(2)}) collective-permute-start(f32[3,16,32,128]{3,2,1,0:T(8,128)} %get-tuple-element.283), channel_id=1, source_target_pairs={{0,16},{8,24},{16,0},{24,8},{1,17},{9,25},{17,1},{25,9},{2,18},{10... | collective-permute-start | bytes 2359304 | tf_op jit(solution)/shard_map/ppermute | solution.py:307
  129.8 2.5 %collective-permute-start.8 = (f32[3,16,32,128]{3,2,1,0:T(8,128)}, f32[3,16,32,128]{3,2,1,0:T(8,128)S(1)}, u32[]{:S(2)}, u32[]{:S(2)}) collective-permute-start(f32[3,16,32,128]{3,2,1,0:T(8,128)} %get-tuple-element.772.far), channel_id=1, source_target_pairs={{0,8},{8,0},{16,24},{24,16},{1,9},{9,1},{17,25},{25,17},{2,10},{10... | collective-permute-start | bytes 2359304 | tf_op jit(solution)/shard_map/while/body/ppermute | solution.py:310
  132.3 11.5 %copy-start.10 = (f32[2048,128]{1,0:T(8,128)S(1)}, f32[2048,128]{1,0:T(8,128)}, u32[]{:S(2)}) copy-start(f32[2048,128]{1,0:T(8,128)} %get-tuple-element.791.refs_3_) | copy-start | bytes 3145732 | tf_op jit(solution)/shard_map/while
  136.2 4.9 %collective-permute-start.9 = (f32[3,32,256]{2,1,0:T(8,128)S(1)}, f32[3,32,256]{2,1,0:T(8,128)S(1)}, u32[]{:S(2)}, u32[]{:S(2)}) collective-permute-start(f32[3,32,256]{2,1,0:T(8,128)S(1)} %get-tuple-element.668), channel_id=1, source_target_pairs={{1,0},{2,1},{3,2},{4,3},{5,4},{6,5},{7,6},{0,7},{9,8},{10,9},{11,1... | collective-permute-start | bytes 294920 | tf_op jit(solution)/shard_map/while/body/ppermute | solution.py:347
  136.4 7.4 %collective-permute-start.10 = (f32[3,32,256]{2,1,0:T(8,128)S(1)}, f32[3,32,256]{2,1,0:T(8,128)S(1)}, u32[]{:S(2)}, u32[]{:S(2)}) collective-permute-start(f32[3,32,256]{2,1,0:T(8,128)S(1)} %get-tuple-element.669), channel_id=1, source_target_pairs={{0,1},{1,2},{2,3},{3,4},{4,5},{5,6},{6,7},{7,0},{8,9},{9,10},{10,1... | collective-permute-start | bytes 294920 | tf_op jit(solution)/shard_map/while/body/ppermute | solution.py:346
  145.4 3.5 %collective-permute-start.11 = (f32[3,16,32,256]{3,2,1,0:T(8,128)S(1)}, f32[3,16,32,256]{3,2,1,0:T(8,128)S(1)}, u32[]{:S(2)}, u32[]{:S(2)}) collective-permute-start(f32[3,16,32,256]{3,2,1,0:T(8,128)S(1)} %second_stencil_2.1.own), channel_id=1, source_target_pairs={{0,8},{8,0},{16,24},{24,16},{1,9},{9,1},{17,25},{25,17},{2,10},{10... | collective-permute-start | bytes 4718600 | tf_op jit(solution)/shard_map/while/body/ppermute | solution.py:310
  153.2 31.0 %collective-permute-start.28 = (f32[3,16,32,128]{3,2,1,0:T(8,128)}, f32[3,16,32,128]{3,2,1,0:T(8,128)}, u32[]{:S(2)}, u32[]{:S(2)}) collective-permute-start(f32[3,16,32,128]{3,2,1,0:T(8,128)} %get-tuple-element.288), channel_id=1, source_target_pairs={{0,16},{8,24},{16,0},{24,8},{1,17},{9,25},{17,1},{25,9},{2,18},{10... | collective-permute-start | bytes 2359304 | tf_op jit(solution)/shard_map/ppermute | solution.py:307
  154.6 2.5 %collective-permute-start.12 = (f32[3,16,32,128]{3,2,1,0:T(8,128)}, f32[3,16,32,128]{3,2,1,0:T(8,128)S(1)}, u32[]{:S(2)}, u32[]{:S(2)}) collective-permute-start(f32[3,16,32,128]{3,2,1,0:T(8,128)} %get-tuple-element.808.far), channel_id=1, source_target_pairs={{0,8},{8,0},{16,24},{24,16},{1,9},{9,1},{17,25},{25,17},{2,10},{10... | collective-permute-start | bytes 2359304 | tf_op jit(solution)/shard_map/while/body/ppermute | solution.py:310
  157.1 11.5 %copy-start.11 = (f32[2048,128]{1,0:T(8,128)S(1)}, f32[2048,128]{1,0:T(8,128)}, u32[]{:S(2)}) copy-start(f32[2048,128]{1,0:T(8,128)} %get-tuple-element.827.refs_3_) | copy-start | bytes 3145732 | tf_op jit(solution)/shard_map/while
  160.9 4.9 %collective-permute-start.13 = (f32[3,32,256]{2,1,0:T(8,128)S(1)}, f32[3,32,256]{2,1,0:T(8,128)S(1)}, u32[]{:S(2)}, u32[]{:S(2)}) collective-permute-start(f32[3,32,256]{2,1,0:T(8,128)S(1)} %get-tuple-element.683), channel_id=1, source_target_pairs={{1,0},{2,1},{3,2},{4,3},{5,4},{6,5},{7,6},{0,7},{9,8},{10,9},{11,1... | collective-permute-start | bytes 294920 | tf_op jit(solution)/shard_map/while/body/ppermute | solution.py:347
  161.2 7.4 %collective-permute-start.14 = (f32[3,32,256]{2,1,0:T(8,128)S(1)}, f32[3,32,256]{2,1,0:T(8,128)S(1)}, u32[]{:S(2)}, u32[]{:S(2)}) collective-permute-start(f32[3,32,256]{2,1,0:T(8,128)S(1)} %get-tuple-element.684), channel_id=1, source_target_pairs={{0,1},{1,2},{2,3},{3,4},{4,5},{5,6},{6,7},{7,0},{8,9},{9,10},{10,1... | collective-permute-start | bytes 294920 | tf_op jit(solution)/shard_map/while/body/ppermute | solution.py:346
  170.2 3.5 %collective-permute-start.15 = (f32[3,16,32,256]{3,2,1,0:T(8,128)S(1)}, f32[3,16,32,256]{3,2,1,0:T(8,128)S(1)}, u32[]{:S(2)}, u32[]{:S(2)}) collective-permute-start(f32[3,16,32,256]{3,2,1,0:T(8,128)S(1)} %second_stencil_3.1.own), channel_id=1, source_target_pairs={{0,8},{8,0},{16,24},{24,16},{1,9},{9,1},{17,25},{25,17},{2,10},{10... | collective-permute-start | bytes 4718600 | tf_op jit(solution)/shard_map/while/body/ppermute | solution.py:310
  177.9 19.8 %collective-permute-start.30 = (f32[3,16,32,128]{3,2,1,0:T(8,128)}, f32[3,16,32,128]{3,2,1,0:T(8,128)S(1)}, u32[]{:S(2)}, u32[]{:S(2)}) collective-permute-start(f32[3,16,32,128]{3,2,1,0:T(8,128)} %get-tuple-element.293), channel_id=1, source_target_pairs={{0,16},{8,24},{16,0},{24,8},{1,17},{9,25},{17,1},{25,9},{2,18},{10... | collective-permute-start | bytes 2359304 | tf_op jit(solution)/shard_map/ppermute | solution.py:307

commit v3 on v2

--- a/solution.py
+++ b/solution.py
@@ -81,25 +81,39 @@
     )(where, state.reshape(modes * nz, nphi), rate)
 
 
-def edge_kernel(cot, leading, last, *, modes, nz):
+def edge_kernel(where, cot, leading, last, *, modes, nz):
     for c in range(3):
         at = slice(c * modes, (c + 1) * modes)
         leading[at, :] = cot[pl.ds(c * nz, modes, stride=3 * nz), :]
         last[at, :] = cot[pl.ds(c * nz + nz - 1, modes, stride=3 * nz), :]
 
 
-def edge_layers(cot):
+def edge_layers(where, cot, foreign):
     modes, comps, nz, nphi = cot.shape
+    half = nphi // 2
+    side = (lambda i, w: (0, 1 - (w[0] >> 1))) if foreign else (lambda i, w: (0, w[0] >> 1))
     return pl.pallas_call(
         lambda *refs: edge_kernel(*refs, modes=modes, nz=nz),
-        out_shape=[shape((comps * modes, nphi))] * 2,
-        grid=(2,),
-        in_specs=[pl.BlockSpec((modes * comps * nz, nphi // 2), lambda h: (0, h))],
-        out_specs=[pl.BlockSpec((comps * modes, nphi // 2), lambda h: (0, h))] * 2,
+        out_shape=[shape((comps * modes, half))] * 2,
+        grid_spec=pltpu.PrefetchScalarGridSpec(
+            num_scalar_prefetch=1,
+            grid=(1,),
+            in_specs=[pl.BlockSpec((modes * comps * nz, half), side)],
+            out_specs=[pl.BlockSpec((comps * modes, half), lambda i, w: (0, 0))] * 2,
+        ),
         compiler_params=params(16),
-        cost_estimate=cost(modes * comps * nphi, 16 * modes * comps * nphi),
+        cost_estimate=cost(modes * comps * nphi, 4 * modes * comps * nz * half),
         name="edge_layers",
-    )(cot.reshape(modes * comps * nz, nphi))
+    )(where, cot.reshape(modes * comps * nz, nphi))
+
+
+def blanks(*like):
+    return pl.pallas_call(
+        lambda *outs: None,
+        out_shape=[shape(dims, dtype) for dims, dtype in like],
+        out_specs=[pl.BlockSpec(memory_space=pl.ANY)] * len(like),
+        name="blanks",
+    )()
 
 
 def first_kernel(where, cot, state, after, before, rate, *rest, modes, nz, chunks):
@@ -137,8 +151,8 @@
             in_specs=[
                 pl.BlockSpec((modes * comps * nz, half), side),
                 pl.BlockSpec((nz * half, modes), whole),
-                pl.BlockSpec((comps * modes, half), side),
-                pl.BlockSpec((comps * modes, half), side),
+                pl.BlockSpec((comps * modes, half), whole),
+                pl.BlockSpec((comps * modes, half), whole),
                 pl.BlockSpec((1, modes), whole),
             ],
             out_specs=[pl.BlockSpec(out, lambda i, w: (0, 0, 0, 0))] * chunks,
@@ -316,41 +330,55 @@
     where = jnp.stack([lax.axis_index("rad").astype(jnp.int32), lot])
     rate = rotation_rate.reshape(1, modes)
 
-    piece = lax.dynamic_slice_in_dim(helm_inverse, lot * modes, modes, axis=1)
-    helm_far = across(piece)[None]
+    once = 1 + (where[0] >> 8)
+
+    piece = across(lax.dynamic_slice_in_dim(helm_inverse, lot * modes, modes, axis=1))
     state_foreign = turn_state(where, state_axial, rate, True, 8)
     state_far = across(state_foreign)
-    leading, last = edge_layers(cotangent)
-    before = lax.ppermute(last, "col", up)
-    after = lax.ppermute(leading, "col", down)
-    after = tied(after, helm_far)
-    sent = first_stencil(where, cotangent, state_foreign, after, before, rate, True, CHUNKS)
-    far = [across(tied(s, state_far) if k else s) for k, s in enumerate(sent)]
-    mask = 1
-    while mask < PIECES:
-        helm_far = jnp.concatenate([helm_far, hop(helm_far, mask)])
-        mask *= 2
-
-    state_own = turn_state(where, state_axial, rate, False, 0)
-    (own,) = first_stencil(where, cotangent, state_own, after, before, rate, False, 1)
-    own_peer = beside(own)
-    high, low = split_helm(where, helm_inverse, helm_far)
-
-    once = 1 + (where[0] >> 8)
+
+    def halos(leading, last):
+        return lax.ppermute(leading, "col", down), lax.ppermute(last, "col", up)
+
+    def foreign_half(step, sent):
+        here = where + (step >> 8)
+        edges = halos(*edge_layers(here, cotangent, True))
+        return tuple(first_stencil(here, cotangent, state_foreign, *edges, rate, True, CHUNKS))
+
+    chunk = (comps, nz, half // CHUNKS, modes)
+    sent = lax.fori_loop(0, once, foreign_half, tuple(blanks(*[(chunk, F32)] * CHUNKS)))
+    far = [across(s) for k, s in enumerate(sent)]
+
+    def own_half(step, carry):
+        here = where + (step >> 8)
+        edges = halos(*edge_layers(here, entry, False))
+        helm_far, mask = tied(piece, here)[None], 1
+        while mask < PIECES:
+            helm_far = jnp.concatenate([helm_far, hop(helm_far, mask)])
+            mask *= 2
+        state_own = turn_state(here, state_axial, rate, False, 0)
+        (own,) = first_stencil(here, entry, state_own, *edges, rate, False, 1)
+        own_peer = beside(own)
+        return (state_own, own, own_peer, *split_helm(here, helm_inverse, helm_far))
+
+    entry = tied(cotangent, sent[0])
+    columns = (comps, nz, half, modes)
+    helm = (comps, peers * modes, 2 * modes)
+    state_own, own, own_peer, high, low = lax.fori_loop(
+        0, once, own_half, tuple(blanks(((nz * half, modes), F32), (columns, F32), (columns, F32), (helm, BF16), (helm, BF16)))
+    )
+
     kept, back = [], []
     for k in range(CHUNKS):
 
         def chain(_, pair, k=k):
             here = pair[0]
             cur, leading, last = map1(own, here, own_peer, beside(here), high, low, k)
-            before = lax.ppermute(last, "col", up)
-            after = lax.ppermute(leading, "col", down)
-            nxt = second_stencil(cur, after, before, state_own, state_far, rate, k, half)
+            nxt = second_stencil(cur, *halos(leading, last), state_own, state_far, rate, k, half)
             mine, theirs = map2(nxt, beside(nxt), high, low, k)
             return theirs, mine
 
-        here = tied(far[k], kept[-1]) if k else far[k]
-        theirs, mine = lax.fori_loop(0, once, chain, (here, sent[k]))
+        spare = tied(sent[k], kept[-1], back[0]) if k > 2 else tied(sent[k], kept[-1]) if k else sent[k]
+        theirs, mine = lax.fori_loop(0, once, chain, (far[k], spare))
         kept.append(mine)
         back.append(across(theirs))
     out = write_half(where, kept, nphi, False)

time: 204 us -> 205 us (level)
  Pallas kernels: 64.9 us -> 71.8 us
  local copies, waits for them, and re-layouts: 7.24 us -> 0.99 us
  starting transfers between devices: 32 us -> 27.4 us
  waiting for transfers between devices: 97.6 us -> 102 us
    ppermute x10, waiting for transfers between devices: 33.1 us -> 22.1 us  [across(): return lax.ppermute(array, 'rad', [(i, i ^ 2) for i in range(peers)])]
    ppermute x2, waiting for transfers between devices: 10.3 us -> 18.3 us  [hop(): return lax.ppermute(array, 'col', [(i, i ^ mask) for i in range(cols)])]
    ppermute x10 -> x12, waiting for transfers between devices: 30.7 us -> 38.1 us  [halos(): return (lax.ppermute(leading, 'col', down), lax.ppermute(last, 'col', up))]
    unnamed x26 -> x2, local copies, waits for them, and re-layouts: 5.61 us -> 0.01 us
    pallas_call x1 -> x2, Pallas kernels: 1.52 us -> 5.38 us  [edge_layers(): pl.pallas_call(lambda *refs: edge_kernel(*refs, modes=modes, nz=nz), out_...]
    ppermute x2, starting transfers between devices: 3.38 us -> 0.07 us  [hop(): return lax.ppermute(array, 'col', [(i, i ^ mask) for i in range(cols)])]
    pallas_call x2, Pallas kernels: 2.13 us -> 5.27 us  [turn_state(): pl.pallas_call(lambda *refs: state_kernel(*refs, modes=modes, nz=nz), out...]
    ppermute x10 -> x12, starting transfers between devices: 16.9 us -> 15.5 us  [halos(): return (lax.ppermute(leading, 'col', down), lax.ppermute(last, 'col', up))]
  transfers between devices with their start and end apart: 31 -> 33, of which waited for: 24 -> 24; matrix products, arithmetic and copies ran while one was open for 1% -> 1% of each run, Pallas kernels for 26% -> 32%
where the time goes in v3:
time: 205 us; the launch traced here: 204 us
  waiting for transfers between devices  102 us (50%)
  Pallas kernels  71.8 us (35%)
  starting transfers between devices  27.4 us (13%)
    ppermute x12, waiting for transfers between devices, halos(): return (lax.ppermute(leading, 'col', down), lax.ppermute(last, 'col', up))  38.1 us
    ppermute x9, waiting for transfers between devices, beside(): return lax.ppermute(array, 'rad', [(i, i ^ 1) for i in range(peers)])  23.4 us
    ppermute x10, waiting for transfers between devices, across(): return lax.ppermute(array, 'rad', [(i, i ^ 2) for i in range(peers)])  22.1 us
    ppermute x2, waiting for transfers between devices, hop(): return lax.ppermute(array, 'col', [(i, i ^ mask) for i in range(cols)])  18.3 us
    pallas_call x4, Pallas kernels, map2(): pl.pallas_call(map2_kernel, out_shape=[shape(out)] * 2, grid=(comps,), in...  17 us
    ppermute x12, starting transfers between devices, halos(): return (lax.ppermute(leading, 'col', down), lax.ppermute(last, 'col', up))  15.5 us
    pallas_call x4, Pallas kernels, map1(): pl.pallas_call(map1_kernel, out_shape=[shape((comps, nz, width, cols)), s...  15.3 us
    ppermute x10, starting transfers between devices, across(): return lax.ppermute(array, 'rad', [(i, i ^ 2) for i in range(peers)])  11.2 us
  transfers between devices with their start and end apart: 33, of which 24 were waited for; matrix products, arithmetic and copies ran while one was open for 1% of the time, Pallas kernels for 32%

profile of v3, /device:TPU:0, one launch (start us, length us, event | category | flops | bytes accessed | tf_op | source)
XLA Modules:
  0.0 204.2 jit_solution(9030913431498884962)
XLA Ops:
  1.0 3.0 %collective-permute-start.24 = (f32[3,128,128]{2,1,0:T(8,128)S(1)}, f32[3,128,128]{2,1,0:T(8,128)S(1)}, u32[]{:S(2)}, u32[]{:S(2)}) collective-permute-start(f32[3,128,128]{2,1,0:T(8,128)S(1)} %constant_dynamic-slice_fusion), channel_id=1, source_target_pairs={{0,16},{8,24},{16,0},{24,8},{1,17},{9,25},{17,1},{25,9},{2,18},{10... | collective-permute-start | bytes 589832 | tf_op jit(solution)/shard_map/ppermute | solution.py:321
  4.0 3.1 %turn_state.2 = f32[2056,128]{1,0:T(8,128)} custom-call(s32[2]{0:T(128)S(1)} %pad_add_fusion.refs_0_, f32[2048,256]{1,0:T(8,128)} %bitcast.6.refs_1_, f32[1,128]{1,0:T(1,128)} %bitcast.24), custom_call_target="tpu_custom_call" | custom-call | flops 263168 | bytes 2105344 | tf_op jit(solution)/shard_map/turn_state/pallas_call | solution.py:69
  7.2 22.5 %while.82 = (s32[]{:T(128)}, f32[3,16,32,128]{3,2,1,0:T(8,128)}, f32[3,16,32,128]{3,2,1,0:T(8,128)}, f32[3,16,32,128]{3,2,1,0:T(8,128)}, f32[3,16,32,128]{3,2,1,...) while((s32[]{:T(128)}, f32[3,16,32,128]{3,2,1,0:T(8,128)}, ...), condition=%wide.region_1.0_spmd, body=%wide.region_0.0_spmd.sunk | while | flops 9535493 | bytes 11010277 | solution.py:348
  7.2 2.6 %edge_layers.2 = (f32[384,128]{1,0:T(8,128)S(1)}, f32[384,128]{1,0:T(8,128)S(1)}) custom-call(s32[2]{0:T(128)S(1)} %broadcast_add_fusion.4.refs_0_, f32[6144,256]{1,0:T(8,128)} %bitcast.17), custom_call_target="tpu_custom_call" | custom-call | flops 98304 | bytes 3145728 | tf_op jit(solution)/shard_map/while/body/edge_layers/pallas_call | solution.py:95
  9.8 5.1 %collective-permute-start = (f32[384,128]{1,0:T(8,128)S(1)}, f32[384,128]{1,0:T(8,128)S(1)}, u32[]{:S(2)}, u32[]{:S(2)}) collective-permute-start(f32[384,128]{1,0:T(8,128)S(1)} %get-tuple-element.935), channel_id=1, source_target_pairs={{1,0},{2,1},{3,2},{4,3},{5,4},{6,5},{7,6},{0,7},{9,8},{10,9},{11,1... | collective-permute-start | bytes 589832 | tf_op jit(solution)/shard_map/while/body/ppermute | solution.py:340
  14.9 3.6 %collective-permute-done.refs_3_ = f32[384,128]{1,0:T(8,128)S(1)} collective-permute-done((f32[384,128]{1,0:T(8,128)S(1)}, f32[384,128]{1,0:T(8,128)S(1)}, u32[]{:S(2)}, u32[]{:S(2)}) %collective-permute-start) | collective-permute-done | bytes 196640 | tf_op jit(solution)/shard_map/while/body/ppermute | solution.py:340
  18.5 4.9 %collective-permute-done.1.refs_4_ = f32[384,128]{1,0:T(8,128)S(1)} collective-permute-done((f32[384,128]{1,0:T(8,128)S(1)}, f32[384,128]{1,0:T(8,128)S(1)}, u32[]{:S(2)}, u32[]{:S(2)}) %collective-permute-start.1) | collective-permute-done | bytes 196640 | tf_op jit(solution)/shard_map/while/body/ppermute | solution.py:340
  23.4 6.3 %first_stencil.2 = (f32[3,16,32,128]{3,2,1,0:T(8,128)}, f32[3,16,32,128]{3,2,1,0:T(8,128)}, f32[3,16,32,128]{3,2,1,0:T(8,128)}, f32[3,16,32,128]{3,2,1,0:T(8,128)}) custom-call(s32[2]{0:T(128)S(1)} %broadcast_add_fusion.4.refs_0_, f32[6144,256]{1,0:T(8,128)} %bitcast.18, f32[2056,128]{1,0:T(8,128)} %get-tuple-element.1046.refs_2_, ...), custom_call_target="tpu_custom_call" | custom-call | flops 9437184 | bytes 6291456 | tf_op jit(solution)/shard_map/while/body/first_stencil/pallas_call | solution.py:145
  31.7 38.8 %while.83 = (s32[]{:T(128)}, f32[2048,128]{1,0:T(8,128)}, f32[3,16,128,128]{3,2,1,0:T(8,128)}, f32[3,16,128,128]{3,2,1,0:T(8,128)}, bf16[3,512,256]{2,1,0:T(8,12...) while((s32[]{:T(128)}, f32[2048,128]{1,0:T(8,128)}, ...), condition=%wide.region_3.0_spmd, body=%wide.region_2.0_spmd.sunk | while | flops 11075589 | bytes 78643688 | solution.py:366
  31.7 2.8 %edge_layers.3 = (f32[384,128]{1,0:T(8,128)S(1)}, f32[384,128]{1,0:T(8,128)S(1)}) custom-call(s32[2]{0:T(128)S(1)} %broadcast_add_fusion.5.refs_0_.where, f32[6144,256]{1,0:T(8,128)} %bitcast.19), custom_call_target="tpu_custom_call" | custom-call | flops 98304 | bytes 3145728 | tf_op jit(solution)/shard_map/while/body/edge_layers/pallas_call | solution.py:95
  38.7 3.1 %collective-permute-done.2.refs_3_ = f32[384,128]{1,0:T(8,128)S(1)} collective-permute-done((f32[384,128]{1,0:T(8,128)S(1)}, f32[384,128]{1,0:T(8,128)S(1)}, u32[]{:S(2)}, u32[]{:S(2)}) %collective-permute-start.2) | collective-permute-done | bytes 196640 | tf_op jit(solution)/shard_map/while/body/ppermute | solution.py:340
  41.9 3.1 %collective-permute-done.3.refs_4_ = f32[384,128]{1,0:T(8,128)S(1)} collective-permute-done((f32[384,128]{1,0:T(8,128)S(1)}, f32[384,128]{1,0:T(8,128)S(1)}, u32[]{:S(2)}, u32[]{:S(2)}) %collective-permute-start.3) | collective-permute-done | bytes 196640 | tf_op jit(solution)/shard_map/while/body/ppermute | solution.py:340
  45.0 2.7 %first_stencil.3 = f32[3,16,128,128]{3,2,1,0:T(8,128)S(1)} custom-call(s32[2]{0:T(128)S(1)} %broadcast_add_fusion.5.refs_0_.where, f32[6144,256]{1,0:T(8,128)S(1)} %bitcast.20, f32[2048,128]{1,0:T(8,128)S(1)} %turn_state.3.refs_2_, f32[384,128]{1,0:T(8,128)S(1)} %collective-permute-done.2.refs_3_, f32[384,128]{1,0:T(8,128)S(1)} %collective-permute-done.3.refs_4_, ...), custom_call_target="tpu_custom_call" | custom-call | flops 9437184 | bytes 6291456 | tf_op jit(solution)/shard_map/while/body/first_stencil/pallas_call | solution.py:145
  47.8 7.2 %collective-permute-done.5 = f32[1,3,128,128]{3,2,1,0:T(8,128)S(1)} collective-permute-done((f32[1,3,128,128]{3,2,1,0:T(8,128)S(1)}, f32[1,3,128,128]{3,2,1,0:T(8,128)S(1)}, u32[]{:S(2)}, u32[]{:S(2)}) %collective-permute-start.5) | collective-permute-done | bytes 196640 | tf_op jit(solution)/shard_map/while/body/ppermute | solution.py:327
  55.9 11.1 %collective-permute-done.6 = f32[2,3,128,128]{3,2,1,0:T(8,128)} collective-permute-done((f32[2,3,128,128]{3,2,1,0:T(8,128)}, f32[2,3,128,128]{3,2,1,0:T(8,128)}, u32[]{:S(2)}, u32[]{:S(2)}) %collective-permute-start.6) | collective-permute-done | bytes 393248 | tf_op jit(solution)/shard_map/while/body/ppermute | solution.py:327
  68.0 2.4 %split_helm.1 = (bf16[3,512,256]{2,1,0:T(8,128)(2,1)}, bf16[3,512,256]{2,1,0:T(8,128)(2,1)}) custom-call(s32[2]{0:T(128)S(1)} %broadcast_add_fusion.5.refs_0_.where, f32[3,512,128]{2,1,0:T(8,128)S(1)} %copy-done.7, f32[4,3,128,128]{3,2,1,0:T(8,128)S(1)} %pad_maximum_fusion.5.far), custom_call_target="tpu_custom_call" | custom-call | flops 786432 | bytes 3145728 | tf_op jit(solution)/shard_map/while/body/split_helm/pallas_call | solution.py:179
  72.6 24.4 %while.84 = (s32[]{:T(128)}, f32[3,16,32,128]{3,2,1,0:T(8,128)}, f32[3,16,32,128]{3,2,1,0:T(8,128)}, s32[]{:T(128)}, f32[3,16,128,128]{3,2,1,0:T(8,128)}, /*inde...) while((s32[]{:T(128)}, f32[3,16,32,128]{3,2,1,0:T(8,128)}, ...), condition=%wide.region_5.0_spmd, body=%wide.region_4.0_spmd.sunk | while | flops 2420637696 | bytes 30146864 | solution.py:381
  72.6 2.5 %collective-permute-done.7.far_peer = f32[3,16,32,128]{3,2,1,0:T(8,128)S(1)} collective-permute-done((f32[3,16,32,128]{3,2,1,0:T(8,128)}, f32[3,16,32,128]{3,2,1,0:T(8,128)S(1)}, u32[]{:S(2)}, u32[]{:S(2)}) %collective-permute-start.7) | collective-permute-done | bytes 786464 | tf_op jit(solution)/shard_map/while/body/ppermute | solution.py:324
  75.1 3.8 %map1_0.1 = (f32[3,16,32,256]{3,2,1,0:T(8,128)S(1)}, f32[3,32,256]{2,1,0:T(8,128)S(1)}, f32[3,32,256]{2,1,0:T(8,128)S(1)}) custom-call(f32[3,16,128,128]{3,2,1,0:T(8,128)} %get-tuple-element.1123.own, f32[3,16,32,128]{3,2,1,0:T(8,128)} %get-tuple-element.1108.far, f32[3,16,128,128]{3,2,1,0:T(8,128)} %get-tuple-element.1124.own_peer, ...), custom_call_target="tpu_custom_call" | custom-call | flops 1207959552 | bytes 6291456 | tf_op jit(solution)/shard_map/while/body/map1_0/pallas_call | solution.py:214
  81.0 2.8 %collective-permute-done.8.refs_1_ = f32[3,32,256]{2,1,0:T(8,128)S(1)} collective-permute-done((f32[3,32,256]{2,1,0:T(8,128)S(1)}, f32[3,32,256]{2,1,0:T(8,128)S(1)}, u32[]{:S(2)}, u32[]{:S(2)}) %collective-permute-start.8) | collective-permute-done | bytes 98336 | tf_op jit(solution)/shard_map/while/body/ppermute | solution.py:340
  83.8 3.8 %collective-permute-done.9.refs_2_ = f32[3,32,256]{2,1,0:T(8,128)S(1)} collective-permute-done((f32[3,32,256]{2,1,0:T(8,128)S(1)}, f32[3,32,256]{2,1,0:T(8,128)S(1)}, u32[]{:S(2)}, u32[]{:S(2)}) %collective-permute-start.9) | collective-permute-done | bytes 98336 | tf_op jit(solution)/shard_map/while/body/ppermute | solution.py:340
  89.3 3.4 %collective-permute-done.10.peer = f32[3,16,32,256]{3,2,1,0:T(8,128)S(1)} collective-permute-done((f32[3,16,32,256]{3,2,1,0:T(8,128)S(1)}, f32[3,16,32,256]{3,2,1,0:T(8,128)S(1)}, u32[]{:S(2)}, u32[]{:S(2)}) %collective-permute-start.10) | collective-permute-done | bytes 1572896 | tf_op jit(solution)/shard_map/while/body/ppermute | solution.py:324
  92.7 4.2 %map2_0.1 = (f32[3,16,32,128]{3,2,1,0:T(8,128)}, f32[3,16,32,128]{3,2,1,0:T(8,128)}) custom-call(f32[3,16,32,256]{3,2,1,0:T(8,128)S(1)} %second_stencil_0.1.own, f32[3,16,32,256]{3,2,1,0:T(8,128)S(1)} %collective-permute-done.10.peer, bf16[3,512,256]{2,1,0:T(8,128)(2,1)} %get-tuple-element.1125.high, bf16[3,512,256]{2,1,0:T(8,128)(2,1)} %get-tuple-element.1126.low), custom_call_target="tpu_custom_call" | custom-call | flops 1207959552 | bytes 6291456 | tf_op jit(solution)/shard_map/while/body/map2_0/pallas_call | solution.py:268
  97.0 23.4 %while.85 = (s32[]{:T(128)}, f32[3,16,32,128]{3,2,1,0:T(8,128)}, f32[3,16,32,128]{3,2,1,0:T(8,128)}, s32[]{:T(128)}, f32[3,16,128,128]{3,2,1,0:T(8,128)}, /*inde...) while((s32[]{:T(128)}, f32[3,16,32,128]{3,2,1,0:T(8,128)}, ...), condition=%wide.region_7.0_spmd, body=%wide.region_6.0_spmd.sunk | while | flops 2420637696 | bytes 30146864 | solution.py:381
  97.2 2.4 %collective-permute-done.11.far_peer = f32[3,16,32,128]{3,2,1,0:T(8,128)S(1)} collective-permute-done((f32[3,16,32,128]{3,2,1,0:T(8,128)}, f32[3,16,32,128]{3,2,1,0:T(8,128)S(1)}, u32[]{:S(2)}, u32[]{:S(2)}) %collective-permute-start.11) | collective-permute-done | bytes 786464 | tf_op jit(solution)/shard_map/while/body/ppermute | solution.py:324
  99.5 3.8 %map1_1.1 = (f32[3,16,32,256]{3,2,1,0:T(8,128)S(1)}, f32[3,32,256]{2,1,0:T(8,128)S(1)}, f32[3,32,256]{2,1,0:T(8,128)S(1)}) custom-call(f32[3,16,128,128]{3,2,1,0:T(8,128)} %get-tuple-element.1159.own, f32[3,16,32,128]{3,2,1,0:T(8,128)} %get-tuple-element.1144.far, f32[3,16,128,128]{3,2,1,0:T(8,128)} %get-tuple-element.1160.own_peer, ...), custom_call_target="tpu_custom_call" | custom-call | flops 1207959552 | bytes 6291456 | tf_op jit(solution)/shard_map/while/body/map1_1/pallas_call | solution.py:214
  105.4 2.8 %collective-permute-done.12.refs_1_ = f32[3,32,256]{2,1,0:T(8,128)S(1)} collective-permute-done((f32[3,32,256]{2,1,0:T(8,128)S(1)}, f32[3,32,256]{2,1,0:T(8,128)S(1)}, u32[]{:S(2)}, u32[]{:S(2)}) %collective-permute-start.12) | collective-permute-done | bytes 98336 | tf_op jit(solution)/shard_map/while/body/ppermute | solution.py:340
  108.2 2.8 %collective-permute-done.13.refs_2_ = f32[3,32,256]{2,1,0:T(8,128)S(1)} collective-permute-done((f32[3,32,256]{2,1,0:T(8,128)S(1)}, f32[3,32,256]{2,1,0:T(8,128)S(1)}, u32[]{:S(2)}, u32[]{:S(2)}) %collective-permute-start.13) | collective-permute-done | bytes 98336 | tf_op jit(solution)/shard_map/while/body/ppermute | solution.py:340
  112.7 3.4 %collective-permute-done.14.peer = f32[3,16,32,256]{3,2,1,0:T(8,128)S(1)} collective-permute-done((f32[3,16,32,256]{3,2,1,0:T(8,128)S(1)}, f32[3,16,32,256]{3,2,1,0:T(8,128)S(1)}, u32[]{:S(2)}, u32[]{:S(2)}) %collective-permute-start.14) | collective-permute-done | bytes 1572896 | tf_op jit(solution)/shard_map/while/body/ppermute | solution.py:324
  116.1 4.2 %map2_1.1 = (f32[3,16,32,128]{3,2,1,0:T(8,128)}, f32[3,16,32,128]{3,2,1,0:T(8,128)}) custom-call(f32[3,16,32,256]{3,2,1,0:T(8,128)S(1)} %second_stencil_1.1.own, f32[3,16,32,256]{3,2,1,0:T(8,128)S(1)} %collective-permute-done.14.peer, bf16[3,512,256]{2,1,0:T(8,128)(2,1)} %get-tuple-element.1161.high, bf16[3,512,256]{2,1,0:T(8,128)(2,1)} %get-tuple-element.1162.low), custom_call_target="tpu_custom_call" | custom-call | flops 1207959552 | bytes 6291456 | tf_op jit(solution)/shard_map/while/body/map2_1/pallas_call | solution.py:268
  122.0 23.3 %while.86 = (s32[]{:T(128)}, f32[3,16,32,128]{3,2,1,0:T(8,128)}, f32[3,16,32,128]{3,2,1,0:T(8,128)}, s32[]{:T(128)}, f32[3,16,128,128]{3,2,1,0:T(8,128)}, /*inde...) while((s32[]{:T(128)}, f32[3,16,32,128]{3,2,1,0:T(8,128)}, ...), condition=%wide.region_9.0_spmd, body=%wide.region_8.0_spmd.sunk | while | flops 2420637696 | bytes 30146864 | solution.py:381
  122.0 2.5 %collective-permute-done.15.far_peer = f32[3,16,32,128]{3,2,1,0:T(8,128)S(1)} collective-permute-done((f32[3,16,32,128]{3,2,1,0:T(8,128)}, f32[3,16,32,128]{3,2,1,0:T(8,128)S(1)}, u32[]{:S(2)}, u32[]{:S(2)}) %collective-permute-start.15) | collective-permute-done | bytes 786464 | tf_op jit(solution)/shard_map/while/body/ppermute | solution.py:324
  124.5 3.8 %map1_2.1 = (f32[3,16,32,256]{3,2,1,0:T(8,128)S(1)}, f32[3,32,256]{2,1,0:T(8,128)S(1)}, f32[3,32,256]{2,1,0:T(8,128)S(1)}) custom-call(f32[3,16,128,128]{3,2,1,0:T(8,128)} %get-tuple-element.1195.own, f32[3,16,32,128]{3,2,1,0:T(8,128)} %get-tuple-element.1180.far, f32[3,16,128,128]{3,2,1,0:T(8,128)} %get-tuple-element.1196.own_peer, ...), custom_call_target="tpu_custom_call" | custom-call | flops 1207959552 | bytes 6291456 | tf_op jit(solution)/shard_map/while/body/map1_2/pallas_call | solution.py:214
  130.4 2.8 %collective-permute-done.16.refs_1_ = f32[3,32,256]{2,1,0:T(8,128)S(1)} collective-permute-done((f32[3,32,256]{2,1,0:T(8,128)S(1)}, f32[3,32,256]{2,1,0:T(8,128)S(1)}, u32[]{:S(2)}, u32[]{:S(2)}) %collective-permute-start.16) | collective-permute-done | bytes 98336 | tf_op jit(solution)/shard_map/while/body/ppermute | solution.py:340
  133.2 2.8 %collective-permute-done.17.refs_2_ = f32[3,32,256]{2,1,0:T(8,128)S(1)} collective-permute-done((f32[3,32,256]{2,1,0:T(8,128)S(1)}, f32[3,32,256]{2,1,0:T(8,128)S(1)}, u32[]{:S(2)}, u32[]{:S(2)}) %collective-permute-start.17) | collective-permute-done | bytes 98336 | tf_op jit(solution)/shard_map/while/body/ppermute | solution.py:340
  137.6 3.4 %collective-permute-done.18.peer = f32[3,16,32,256]{3,2,1,0:T(8,128)S(1)} collective-permute-done((f32[3,16,32,256]{3,2,1,0:T(8,128)S(1)}, f32[3,16,32,256]{3,2,1,0:T(8,128)S(1)}, u32[]{:S(2)}, u32[]{:S(2)}) %collective-permute-start.18) | collective-permute-done | bytes 1572896 | tf_op jit(solution)/shard_map/while/body/ppermute | solution.py:324
  141.0 4.2 %map2_2.1 = (f32[3,16,32,128]{3,2,1,0:T(8,128)}, f32[3,16,32,128]{3,2,1,0:T(8,128)}) custom-call(f32[3,16,32,256]{3,2,1,0:T(8,128)S(1)} %second_stencil_2.1.own, f32[3,16,32,256]{3,2,1,0:T(8,128)S(1)} %collective-permute-done.18.peer, bf16[3,512,256]{2,1,0:T(8,128)(2,1)} %get-tuple-element.1197.high, bf16[3,512,256]{2,1,0:T(8,128)(2,1)} %get-tuple-element.1198.low), custom_call_target="tpu_custom_call" | custom-call | flops 1207959552 | bytes 6291456 | tf_op jit(solution)/shard_map/while/body/map2_2/pallas_call | solution.py:268
  147.3 23.3 %while.87 = (s32[]{:T(128)}, f32[3,16,32,128]{3,2,1,0:T(8,128)}, f32[3,16,32,128]{3,2,1,0:T(8,128)}, s32[]{:T(128)}, f32[3,16,128,128]{3,2,1,0:T(8,128)}, /*inde...) while((s32[]{:T(128)}, f32[3,16,32,128]{3,2,1,0:T(8,128)}, ...), condition=%wide.region_11.0_spmd, body=%wide.region_10.0_spmd.sunk | while | flops 2420637696 | bytes 30146864 | solution.py:381
  147.3 2.5 %collective-permute-done.19.far_peer = f32[3,16,32,128]{3,2,1,0:T(8,128)S(1)} collective-permute-done((f32[3,16,32,128]{3,2,1,0:T(8,128)}, f32[3,16,32,128]{3,2,1,0:T(8,128)S(1)}, u32[]{:S(2)}, u32[]{:S(2)}) %collective-permute-start.19) | collective-permute-done | bytes 786464 | tf_op jit(solution)/shard_map/while/body/ppermute | solution.py:324
  149.8 3.8 %map1_3.1 = (f32[3,16,32,256]{3,2,1,0:T(8,128)S(1)}, f32[3,32,256]{2,1,0:T(8,128)S(1)}, f32[3,32,256]{2,1,0:T(8,128)S(1)}) custom-call(f32[3,16,128,128]{3,2,1,0:T(8,128)} %get-tuple-element.1231.own, f32[3,16,32,128]{3,2,1,0:T(8,128)} %get-tuple-element.1216.far, f32[3,16,128,128]{3,2,1,0:T(8,128)} %get-tuple-element.1232.own_peer, ...), custom_call_target="tpu_custom_call" | custom-call | flops 1207959552 | bytes 6291456 | tf_op jit(solution)/shard_map/while/body/map1_3/pallas_call | solution.py:214
  155.7 2.8 %collective-permute-done.20.refs_1_ = f32[3,32,256]{2,1,0:T(8,128)S(1)} collective-permute-done((f32[3,32,256]{2,1,0:T(8,128)S(1)}, f32[3,32,256]{2,1,0:T(8,128)S(1)}, u32[]{:S(2)}, u32[]{:S(2)}) %collective-permute-start.20) | collective-permute-done | bytes 98336 | tf_op jit(solution)/shard_map/while/body/ppermute | solution.py:340
  158.5 2.8 %collective-permute-done.21.refs_2_ = f32[3,32,256]{2,1,0:T(8,128)S(1)} collective-permute-done((f32[3,32,256]{2,1,0:T(8,128)S(1)}, f32[3,32,256]{2,1,0:T(8,128)S(1)}, u32[]{:S(2)}, u32[]{:S(2)}) %collective-permute-start.21) | collective-permute-done | bytes 98336 | tf_op jit(solution)/shard_map/while/body/ppermute | solution.py:340
  163.0 3.4 %collective-permute-done.22.peer = f32[3,16,32,256]{3,2,1,0:T(8,128)S(1)} collective-permute-done((f32[3,16,32,256]{3,2,1,0:T(8,128)S(1)}, f32[3,16,32,256]{3,2,1,0:T(8,128)S(1)}, u32[]{:S(2)}, u32[]{:S(2)}) %collective-permute-start.22) | collective-permute-done | bytes 1572896 | tf_op jit(solution)/shard_map/while/body/ppermute | solution.py:324
  166.4 4.2 %map2_3.1 = (f32[3,16,32,128]{3,2,1,0:T(8,128)}, f32[3,16,32,128]{3,2,1,0:T(8,128)}) custom-call(f32[3,16,32,256]{3,2,1,0:T(8,128)S(1)} %second_stencil_3.1.own, f32[3,16,32,256]{3,2,1,0:T(8,128)S(1)} %collective-permute-done.22.peer, bf16[3,512,256]{2,1,0:T(8,128)(2,1)} %get-tuple-element.1233.high, bf16[3,512,256]{2,1,0:T(8,128)(2,1)} %get-tuple-element.1234.low), custom_call_target="tpu_custom_call" | custom-call | flops 1207959552 | bytes 6291456 | tf_op jit(solution)/shard_map/while/body/map2_3/pallas_call | solution.py:268
  171.0 5.6 %write_own.1.refs_5_ = f32[128,48,256]{2,1,0:T(8,128)} custom-call(s32[2]{0:T(128)S(1)} %get-tuple-element.1304, f32[3,16,32,128]{3,2,1,0:T(8,128)} %get-tuple-element.418.refs_1_, f32[3,16,32,128]{3,2,1,0:T(8,128)} %get-tuple-element.422.refs_2_, f32[3,16,32,128]{3,2,1,0:T(8,128)} %get-tuple-element.426.refs_3_, f32[3,16,32,128]{3,2,1,0:T(8,128)} %get-tuple-element.429.refs_4_), custom_call_target="tpu_custom_call" | custom-call | flops 1572864 | bytes 6291456 | tf_op jit(solution)/shard_map/write_own/pallas_call | solution.py:292
  176.7 6.2 %collective-permute-done.28.refs_2_ = f32[3,16,32,128]{3,2,1,0:T(8,128)} collective-permute-done((f32[3,16,32,128]{3,2,1,0:T(8,128)}, f32[3,16,32,128]{3,2,1,0:T(8,128)}, u32[]{:S(2)}, u32[]{:S(2)}) %collective-permute-start.28) | collective-permute-done | bytes 786464 | tf_op jit(solution)/shard_map/ppermute | solution.py:321
  182.8 15.9 %collective-permute-done.32.refs_4_ = f32[3,16,32,128]{3,2,1,0:T(8,128)S(1)} collective-permute-done((f32[3,16,32,128]{3,2,1,0:T(8,128)}, f32[3,16,32,128]{3,2,1,0:T(8,128)S(1)}, u32[]{:S(2)}, u32[]{:S(2)}) %collective-permute-start.32) | collective-permute-done | bytes 786464 | tf_op jit(solution)/shard_map/ppermute | solution.py:321
  198.8 5.4 %write_foreign.1 = f32[128,48,256]{2,1,0:T(8,128)} custom-call(s32[2]{0:T(128)S(1)} %get-tuple-element.1304, f32[3,16,32,128]{3,2,1,0:T(8,128)} %collective-permute-done.26.refs_1_, f32[3,16,32,128]{3,2,1,0:T(8,128)} %collective-permute-done.28.refs_2_, f32[3,16,32,128]{3,2,1,0:T(8,128)} %collective-permute-done.30.refs_3_, ...), custom_call_target="tpu_custom_call", output_to_operand_aliasing={{}: (5, {})} | custom-call | flops 1572864 | bytes 6291456 | tf_op jit(solution)/shard_map/write_foreign/pallas_call | solution.py:292
  (71 shorter events, 30.7 us)
Async XLA Ops:
  0.0 7.2 %copy-start.8 = (f32[128]{0:T(128)S(1)}, f32[128]{0:T(128)}, u32[]{:S(2)}) copy-start(f32[128]{0:T(128)} %param.19) | copy-start | bytes 1540
  1.0 30.7 %collective-permute-start.24 = (f32[3,128,128]{2,1,0:T(8,128)S(1)}, f32[3,128,128]{2,1,0:T(8,128)S(1)}, u32[]{:S(2)}, u32[]{:S(2)}) collective-permute-start(f32[3,128,128]{2,1,0:T(8,128)S(1)} %constant_dynamic-slice_fusion), channel_id=1, source_target_pairs={{0,16},{8,24},{16,0},{24,8},{1,17},{9,25},{17,1},{25,9},{2,18},{10... | collective-permute-start | bytes 589832 | tf_op jit(solution)/shard_map/ppermute | solution.py:321
  7.2 65.4 %collective-permute-start.25 = (f32[2056,128]{1,0:T(8,128)}, f32[2056,128]{1,0:T(8,128)}, u32[]{:S(2)}, u32[]{:S(2)}) collective-permute-start(f32[2056,128]{1,0:T(8,128)} %turn_state.2), channel_id=1, source_target_pairs={{0,16},{8,24},{16,0},{24,8},{1,17},{9,25},{17,1},{25,9},{2,18},{10... | collective-permute-start | bytes 3158024 | tf_op jit(solution)/shard_map/ppermute | solution.py:321
  9.8 8.7 %collective-permute-start = (f32[384,128]{1,0:T(8,128)S(1)}, f32[384,128]{1,0:T(8,128)S(1)}, u32[]{:S(2)}, u32[]{:S(2)}) collective-permute-start(f32[384,128]{1,0:T(8,128)S(1)} %get-tuple-element.935), channel_id=1, source_target_pairs={{1,0},{2,1},{3,2},{4,3},{5,4},{6,5},{7,6},{0,7},{9,8},{10,9},{11,1... | collective-permute-start | bytes 589832 | tf_op jit(solution)/shard_map/while/body/ppermute | solution.py:340
  14.9 8.5 %collective-permute-start.1 = (f32[384,128]{1,0:T(8,128)S(1)}, f32[384,128]{1,0:T(8,128)S(1)}, u32[]{:S(2)}, u32[]{:S(2)}) collective-permute-start(f32[384,128]{1,0:T(8,128)S(1)} %get-tuple-element.936), channel_id=1, source_target_pairs={{0,1},{1,2},{2,3},{3,4},{4,5},{5,6},{6,7},{7,0},{8,9},{9,10},{10,1... | collective-permute-start | bytes 589832 | tf_op jit(solution)/shard_map/while/body/ppermute | solution.py:340
  29.7 42.9 %collective-permute-start.23 = (f32[3,16,32,128]{3,2,1,0:T(8,128)}, f32[3,16,32,128]{3,2,1,0:T(8,128)}, u32[]{:S(2)}, u32[]{:S(2)}) collective-permute-start(f32[3,16,32,128]{3,2,1,0:T(8,128)} %get-tuple-element.1097), channel_id=1, source_target_pairs={{0,16},{8,24},{16,0},{24,8},{1,17},{9,25},{17,1},{25,9},{2,18},{10... | collective-permute-start | bytes 2359304 | tf_op jit(solution)/shard_map/ppermute | solution.py:321
  31.1 65.8 %collective-permute-start.27 = (f32[3,16,32,128]{3,2,1,0:T(8,128)}, f32[3,16,32,128]{3,2,1,0:T(8,128)}, u32[]{:S(2)}, u32[]{:S(2)}) collective-permute-start(f32[3,16,32,128]{3,2,1,0:T(8,128)} %get-tuple-element.1133), channel_id=1, source_target_pairs={{0,16},{8,24},{16,0},{24,8},{1,17},{9,25},{17,1},{25,9},{2,18},{10... | collective-permute-start | bytes 2359304 | tf_op jit(solution)/shard_map/ppermute | solution.py:321
  31.7 13.3 %copy-start = (f32[128,3,16,256]{3,2,1,0:T(8,128)S(1)}, f32[128,3,16,256]{3,2,1,0:T(8,128)}, u32[]{:S(2)}) copy-start(f32[128,3,16,256]{3,2,1,0:T(8,128)} %get-tuple-element.1090) | copy-start | bytes 18874372 | tf_op jit(solution)/shard_map/while
  34.5 7.3 %collective-permute-start.2 = (f32[384,128]{1,0:T(8,128)S(1)}, f32[384,128]{1,0:T(8,128)S(1)}, u32[]{:S(2)}, u32[]{:S(2)}) collective-permute-start(f32[384,128]{1,0:T(8,128)S(1)} %get-tuple-element.949), channel_id=1, source_target_pairs={{1,0},{2,1},{3,2},{4,3},{5,4},{6,5},{7,6},{0,7},{9,8},{10,9},{11,1... | collective-permute-start | bytes 589832 | tf_op jit(solution)/shard_map/while/body/ppermute | solution.py:340
  36.6 8.4 %collective-permute-start.3 = (f32[384,128]{1,0:T(8,128)S(1)}, f32[384,128]{1,0:T(8,128)S(1)}, u32[]{:S(2)}, u32[]{:S(2)}) collective-permute-start(f32[384,128]{1,0:T(8,128)S(1)} %get-tuple-element.950), channel_id=1, source_target_pairs={{0,1},{1,2},{2,3},{3,4},{4,5},{5,6},{6,7},{7,0},{8,9},{9,10},{10,1... | collective-permute-start | bytes 589832 | tf_op jit(solution)/shard_map/while/body/ppermute | solution.py:340
  38.7 8.9 %copy-start.2 = (f32[2048,128]{1,0:T(8,128)}, f32[2048,128]{1,0:T(8,128)S(1)}, u32[]{:S(2)}) copy-start(f32[2048,128]{1,0:T(8,128)S(1)} %turn_state.3.refs_2_) | copy-start | bytes 3145732 | tf_op jit(solution)/shard_map/while
  47.7 22.8 %copy-start.1 = (f32[3,16,128,128]{3,2,1,0:T(8,128)}, f32[3,16,128,128]{3,2,1,0:T(8,128)S(1)}, u32[]{:S(2)}) copy-start(f32[3,16,128,128]{3,2,1,0:T(8,128)S(1)} %first_stencil.3) | copy-start | bytes 9437188 | tf_op jit(solution)/shard_map/while
  47.7 22.8 %collective-permute-start.4 = (f32[3,16,128,128]{3,2,1,0:T(8,128)S(1)}, f32[3,16,128,128]{3,2,1,0:T(8,128)}, u32[]{:S(2)}, u32[]{:S(2)}) collective-permute-start(f32[3,16,128,128]{3,2,1,0:T(8,128)S(1)} %first_stencil.3), channel_id=1, source_target_pairs={{0,8},{8,0},{16,24},{24,16},{1,9},{9,1},{17,25},{25,17},{2,10},{10... | collective-permute-start | bytes 9437192 | tf_op jit(solution)/shard_map/while/body/ppermute | solution.py:324
  47.8 7.3 %collective-permute-start.5 = (f32[1,3,128,128]{3,2,1,0:T(8,128)S(1)}, f32[1,3,128,128]{3,2,1,0:T(8,128)S(1)}, u32[]{:S(2)}, u32[]{:S(2)}) collective-permute-start(f32[1,3,128,128]{3,2,1,0:T(8,128)S(1)} %bitcast.21), channel_id=1, source_target_pairs={{0,1},{1,0},{2,3},{3,2},{4,5},{5,4},{6,7},{7,6},{8,9},{9,8},{10,11... | collective-permute-start | bytes 589832 | tf_op jit(solution)/shard_map/while/body/ppermute | solution.py:327
  55.9 11.1 %collective-permute-start.6 = (f32[2,3,128,128]{3,2,1,0:T(8,128)}, f32[2,3,128,128]{3,2,1,0:T(8,128)}, u32[]{:S(2)}, u32[]{:S(2)}) collective-permute-start(f32[2,3,128,128]{3,2,1,0:T(8,128)} %pad_maximum_fusion.4), channel_id=1, source_target_pairs={{0,2},{1,3},{2,0},{3,1},{4,6},{5,7},{6,4},{7,5},{8,10},{9,11},{10,... | collective-permute-start | bytes 1179656 | tf_op jit(solution)/shard_map/while/body/ppermute | solution.py:327
  55.9 12.2 %copy-start.7 = (f32[3,512,128]{2,1,0:T(8,128)S(1)}, f32[3,512,128]{2,1,0:T(8,128)}, u32[]{:S(2)}) copy-start(f32[3,512,128]{2,1,0:T(8,128)} %get-tuple-element.1092.own) | copy-start | bytes 2359300 | tf_op jit(solution)/shard_map/while
  70.5 51.5 %collective-permute-start.29 = (f32[3,16,32,128]{3,2,1,0:T(8,128)}, f32[3,16,32,128]{3,2,1,0:T(8,128)}, u32[]{:S(2)}, u32[]{:S(2)}) collective-permute-start(f32[3,16,32,128]{3,2,1,0:T(8,128)} %get-tuple-element.1169), channel_id=1, source_target_pairs={{0,16},{8,24},{16,0},{24,8},{1,17},{9,25},{17,1},{25,9},{2,18},{10... | collective-permute-start | bytes 2359304 | tf_op jit(solution)/shard_map/ppermute | solution.py:321
  72.2 75.1 %collective-permute-start.31 = (f32[3,16,32,128]{3,2,1,0:T(8,128)}, f32[3,16,32,128]{3,2,1,0:T(8,128)}, u32[]{:S(2)}, u32[]{:S(2)}) collective-permute-start(f32[3,16,32,128]{3,2,1,0:T(8,128)} %get-tuple-element.1205), channel_id=1, source_target_pairs={{0,16},{8,24},{16,0},{24,8},{1,17},{9,25},{17,1},{25,9},{2,18},{10... | collective-permute-start | bytes 2359304 | tf_op jit(solution)/shard_map/ppermute | solution.py:321
  72.6 2.5 %collective-permute-start.7 = (f32[3,16,32,128]{3,2,1,0:T(8,128)}, f32[3,16,32,128]{3,2,1,0:T(8,128)S(1)}, u32[]{:S(2)}, u32[]{:S(2)}) collective-permute-start(f32[3,16,32,128]{3,2,1,0:T(8,128)} %get-tuple-element.1108.far), channel_id=1, source_target_pairs={{0,8},{8,0},{16,24},{24,16},{1,9},{9,1},{17,25},{25,17},{2,10},{10... | collective-permute-start | bytes 2359304 | tf_op jit(solution)/shard_map/while/body/ppermute | solution.py:324
  75.1 12.6 %copy-start.3 = (f32[2048,128]{1,0:T(8,128)S(1)}, f32[2048,128]{1,0:T(8,128)}, u32[]{:S(2)}) copy-start(f32[2048,128]{1,0:T(8,128)} %get-tuple-element.1127.refs_3_) | copy-start | bytes 3145732 | tf_op jit(solution)/shard_map/while
  78.9 4.9 %collective-permute-start.8 = (f32[3,32,256]{2,1,0:T(8,128)S(1)}, f32[3,32,256]{2,1,0:T(8,128)S(1)}, u32[]{:S(2)}, u32[]{:S(2)}) collective-permute-start(f32[3,32,256]{2,1,0:T(8,128)S(1)} %get-tuple-element.965), channel_id=1, source_target_pairs={{1,0},{2,1},{3,2},{4,3},{5,4},{6,5},{7,6},{0,7},{9,8},{10,9},{11,1... | collective-permute-start | bytes 294920 | tf_op jit(solution)/shard_map/while/body/ppermute | solution.py:340
  80.3 7.3 %collective-permute-start.9 = (f32[3,32,256]{2,1,0:T(8,128)S(1)}, f32[3,32,256]{2,1,0:T(8,128)S(1)}, u32[]{:S(2)}, u32[]{:S(2)}) collective-permute-start(f32[3,32,256]{2,1,0:T(8,128)S(1)} %get-tuple-element.966), channel_id=1, source_target_pairs={{0,1},{1,2},{2,3},{3,4},{4,5},{5,6},{6,7},{7,0},{8,9},{9,10},{10,1... | collective-permute-start | bytes 294920 | tf_op jit(solution)/shard_map/while/body/ppermute | solution.py:340
  89.2 3.5 %collective-permute-start.10 = (f32[3,16,32,256]{3,2,1,0:T(8,128)S(1)}, f32[3,16,32,256]{3,2,1,0:T(8,128)S(1)}, u32[]{:S(2)}, u32[]{:S(2)}) collective-permute-start(f32[3,16,32,256]{3,2,1,0:T(8,128)S(1)} %second_stencil_0.1.own), channel_id=1, source_target_pairs={{0,8},{8,0},{16,24},{24,16},{1,9},{9,1},{17,25},{25,17},{2,10},{10... | collective-permute-start | bytes 4718600 | tf_op jit(solution)/shard_map/while/body/ppermute | solution.py:324
  97.0 2.6 %collective-permute-start.11 = (f32[3,16,32,128]{3,2,1,0:T(8,128)}, f32[3,16,32,128]{3,2,1,0:T(8,128)S(1)}, u32[]{:S(2)}, u32[]{:S(2)}) collective-permute-start(f32[3,16,32,128]{3,2,1,0:T(8,128)} %get-tuple-element.1144.far), channel_id=1, source_target_pairs={{0,8},{8,0},{16,24},{24,16},{1,9},{9,1},{17,25},{25,17},{2,10},{10... | collective-permute-start | bytes 2359304 | tf_op jit(solution)/shard_map/while/body/ppermute | solution.py:324
  99.5 11.5 %copy-start.4 = (f32[2048,128]{1,0:T(8,128)S(1)}, f32[2048,128]{1,0:T(8,128)}, u32[]{:S(2)}) copy-start(f32[2048,128]{1,0:T(8,128)} %get-tuple-element.1163.refs_3_) | copy-start | bytes 3145732 | tf_op jit(solution)/shard_map/while
  103.3 4.9 %collective-permute-start.12 = (f32[3,32,256]{2,1,0:T(8,128)S(1)}, f32[3,32,256]{2,1,0:T(8,128)S(1)}, u32[]{:S(2)}, u32[]{:S(2)}) collective-permute-start(f32[3,32,256]{2,1,0:T(8,128)S(1)} %get-tuple-element.980), channel_id=1, source_target_pairs={{1,0},{2,1},{3,2},{4,3},{5,4},{6,5},{7,6},{0,7},{9,8},{10,9},{11,1... | collective-permute-start | bytes 294920 | tf_op jit(solution)/shard_map/while/body/ppermute | solution.py:340
  103.6 7.4 %collective-permute-start.13 = (f32[3,32,256]{2,1,0:T(8,128)S(1)}, f32[3,32,256]{2,1,0:T(8,128)S(1)}, u32[]{:S(2)}, u32[]{:S(2)}) collective-permute-start(f32[3,32,256]{2,1,0:T(8,128)S(1)} %get-tuple-element.981), channel_id=1, source_target_pairs={{0,1},{1,2},{2,3},{3,4},{4,5},{5,6},{6,7},{7,0},{8,9},{9,10},{10,1... | collective-permute-start | bytes 294920 | tf_op jit(solution)/shard_map/while/body/ppermute | solution.py:340
  112.6 3.5 %collective-permute-start.14 = (f32[3,16,32,256]{3,2,1,0:T(8,128)S(1)}, f32[3,16,32,256]{3,2,1,0:T(8,128)S(1)}, u32[]{:S(2)}, u32[]{:S(2)}) collective-permute-start(f32[3,16,32,256]{3,2,1,0:T(8,128)S(1)} %second_stencil_1.1.own), channel_id=1, source_target_pairs={{0,8},{8,0},{16,24},{24,16},{1,9},{9,1},{17,25},{25,17},{2,10},{10... | collective-permute-start | bytes 4718600 | tf_op jit(solution)/shard_map/while/body/ppermute | solution.py:324
  120.3 27.0 %collective-permute-start.26 = (f32[3,16,32,128]{3,2,1,0:T(8,128)}, f32[3,16,32,128]{3,2,1,0:T(8,128)}, u32[]{:S(2)}, u32[]{:S(2)}) collective-permute-start(f32[3,16,32,128]{3,2,1,0:T(8,128)} %get-tuple-element.416), channel_id=1, source_target_pairs={{0,16},{8,24},{16,0},{24,8},{1,17},{9,25},{17,1},{25,9},{2,18},{10... | collective-permute-start | bytes 2359304 | tf_op jit(solution)/shard_map/ppermute | solution.py:321
  122.0 2.5 %collective-permute-start.15 = (f32[3,16,32,128]{3,2,1,0:T(8,128)}, f32[3,16,32,128]{3,2,1,0:T(8,128)S(1)}, u32[]{:S(2)}, u32[]{:S(2)}) collective-permute-start(f32[3,16,32,128]{3,2,1,0:T(8,128)} %get-tuple-element.1180.far), channel_id=1, source_target_pairs={{0,8},{8,0},{16,24},{24,16},{1,9},{9,1},{17,25},{25,17},{2,10},{10... | collective-permute-start | bytes 2359304 | tf_op jit(solution)/shard_map/while/body/ppermute | solution.py:324
  124.5 11.5 %copy-start.5 = (f32[2048,128]{1,0:T(8,128)S(1)}, f32[2048,128]{1,0:T(8,128)}, u32[]{:S(2)}) copy-start(f32[2048,128]{1,0:T(8,128)} %get-tuple-element.1199.refs_3_) | copy-start | bytes 3145732 | tf_op jit(solution)/shard_map/while
  128.3 4.9 %collective-permute-start.16 = (f32[3,32,256]{2,1,0:T(8,128)S(1)}, f32[3,32,256]{2,1,0:T(8,128)S(1)}, u32[]{:S(2)}, u32[]{:S(2)}) collective-permute-start(f32[3,32,256]{2,1,0:T(8,128)S(1)} %get-tuple-element.995), channel_id=1, source_target_pairs={{1,0},{2,1},{3,2},{4,3},{5,4},{6,5},{7,6},{0,7},{9,8},{10,9},{11,1... | collective-permute-start | bytes 294920 | tf_op jit(solution)/shard_map/while/body/ppermute | solution.py:340
  128.6 7.4 %collective-permute-start.17 = (f32[3,32,256]{2,1,0:T(8,128)S(1)}, f32[3,32,256]{2,1,0:T(8,128)S(1)}, u32[]{:S(2)}, u32[]{:S(2)}) collective-permute-start(f32[3,32,256]{2,1,0:T(8,128)S(1)} %get-tuple-element.996), channel_id=1, source_target_pairs={{0,1},{1,2},{2,3},{3,4},{4,5},{5,6},{6,7},{7,0},{8,9},{9,10},{10,1... | collective-permute-start | bytes 294920 | tf_op jit(solution)/shard_map/while/body/ppermute | solution.py:340
  137.6 3.5 %collective-permute-start.18 = (f32[3,16,32,256]{3,2,1,0:T(8,128)S(1)}, f32[3,16,32,256]{3,2,1,0:T(8,128)S(1)}, u32[]{:S(2)}, u32[]{:S(2)}) collective-permute-start(f32[3,16,32,256]{3,2,1,0:T(8,128)S(1)} %second_stencil_2.1.own), channel_id=1, source_target_pairs={{0,8},{8,0},{16,24},{24,16},{1,9},{9,1},{17,25},{25,17},{2,10},{10... | collective-permute-start | bytes 4718600 | tf_op jit(solution)/shard_map/while/body/ppermute | solution.py:324
  145.3 31.4 %collective-permute-start.30 = (f32[3,16,32,128]{3,2,1,0:T(8,128)}, f32[3,16,32,128]{3,2,1,0:T(8,128)}, u32[]{:S(2)}, u32[]{:S(2)}) collective-permute-start(f32[3,16,32,128]{3,2,1,0:T(8,128)} %get-tuple-element.424), channel_id=1, source_target_pairs={{0,16},{8,24},{16,0},{24,8},{1,17},{9,25},{17,1},{25,9},{2,18},{10... | collective-permute-start | bytes 2359304 | tf_op jit(solution)/shard_map/ppermute | solution.py:321
  145.7 37.2 %collective-permute-start.28 = (f32[3,16,32,128]{3,2,1,0:T(8,128)}, f32[3,16,32,128]{3,2,1,0:T(8,128)}, u32[]{:S(2)}, u32[]{:S(2)}) collective-permute-start(f32[3,16,32,128]{3,2,1,0:T(8,128)} %get-tuple-element.420), channel_id=1, source_target_pairs={{0,16},{8,24},{16,0},{24,8},{1,17},{9,25},{17,1},{25,9},{2,18},{10... | collective-permute-start | bytes 2359304 | tf_op jit(solution)/shard_map/ppermute | solution.py:321
  147.3 2.5 %collective-permute-start.19 = (f32[3,16,32,128]{3,2,1,0:T(8,128)}, f32[3,16,32,128]{3,2,1,0:T(8,128)S(1)}, u32[]{:S(2)}, u32[]{:S(2)}) collective-permute-start(f32[3,16,32,128]{3,2,1,0:T(8,128)} %get-tuple-element.1216.far), channel_id=1, source_target_pairs={{0,8},{8,0},{16,24},{24,16},{1,9},{9,1},{17,25},{25,17},{2,10},{10... | collective-permute-start | bytes 2359304 | tf_op jit(solution)/shard_map/while/body/ppermute | solution.py:324
  149.8 11.5 %copy-start.6 = (f32[2048,128]{1,0:T(8,128)S(1)}, f32[2048,128]{1,0:T(8,128)}, u32[]{:S(2)}) copy-start(f32[2048,128]{1,0:T(8,128)} %get-tuple-element.1235.refs_3_) | copy-start | bytes 3145732 | tf_op jit(solution)/shard_map/while
  153.7 4.9 %collective-permute-start.20 = (f32[3,32,256]{2,1,0:T(8,128)S(1)}, f32[3,32,256]{2,1,0:T(8,128)S(1)}, u32[]{:S(2)}, u32[]{:S(2)}) collective-permute-start(f32[3,32,256]{2,1,0:T(8,128)S(1)} %get-tuple-element.1010), channel_id=1, source_target_pairs={{1,0},{2,1},{3,2},{4,3},{5,4},{6,5},{7,6},{0,7},{9,8},{10,9},{11,1... | collective-permute-start | bytes 294920 | tf_op jit(solution)/shard_map/while/body/ppermute | solution.py:340
  153.9 7.4 %collective-permute-start.21 = (f32[3,32,256]{2,1,0:T(8,128)S(1)}, f32[3,32,256]{2,1,0:T(8,128)S(1)}, u32[]{:S(2)}, u32[]{:S(2)}) collective-permute-start(f32[3,32,256]{2,1,0:T(8,128)S(1)} %get-tuple-element.1011), channel_id=1, source_target_pairs={{0,1},{1,2},{2,3},{3,4},{4,5},{5,6},{6,7},{7,0},{8,9},{9,10},{10,1... | collective-permute-start | bytes 294920 | tf_op jit(solution)/shard_map/while/body/ppermute | solution.py:340
  162.9 3.5 %collective-permute-start.22 = (f32[3,16,32,256]{3,2,1,0:T(8,128)S(1)}, f32[3,16,32,256]{3,2,1,0:T(8,128)S(1)}, u32[]{:S(2)}, u32[]{:S(2)}) collective-permute-start(f32[3,16,32,256]{3,2,1,0:T(8,128)S(1)} %second_stencil_3.1.own), channel_id=1, source_target_pairs={{0,8},{8,0},{16,24},{24,16},{1,9},{9,1},{17,25},{25,17},{2,10},{10... | collective-permute-start | bytes 4718600 | tf_op jit(solution)/shard_map/while/body/ppermute | solution.py:324
  170.6 28.2 %collective-permute-start.32 = (f32[3,16,32,128]{3,2,1,0:T(8,128)}, f32[3,16,32,128]{3,2,1,0:T(8,128)S(1)}, u32[]{:S(2)}, u32[]{:S(2)}) collective-permute-start(f32[3,16,32,128]{3,2,1,0:T(8,128)} %get-tuple-element.428), channel_id=1, source_target_pairs={{0,16},{8,24},{16,0},{24,8},{1,17},{9,25},{17,1},{25,9},{2,18},{10... | collective-permute-start | bytes 2359304 | tf_op jit(solution)/shard_map/ppermute | solution.py:321

commit v4 on v3

--- a/solution.py
+++ b/solution.py
@@ -7,6 +7,7 @@
 
 SECTIONS = 2
 CHUNKS = 4
+TOGETHER = 2
 PIECES = 4
 
 diffusion_coeff = 0.2
@@ -346,7 +347,7 @@
 
     chunk = (comps, nz, half // CHUNKS, modes)
     sent = lax.fori_loop(0, once, foreign_half, tuple(blanks(*[(chunk, F32)] * CHUNKS)))
-    far = [across(s) for k, s in enumerate(sent)]
+    far = [across(tied(s, state_far) if k >= TOGETHER else s) for k, s in enumerate(sent)]
 
     def own_half(step, carry):
         here = where + (step >> 8)
@@ -354,6 +355,8 @@
         helm_far, mask = tied(piece, here)[None], 1
         while mask < PIECES:
             helm_far = jnp.concatenate([helm_far, hop(helm_far, mask)])
+            if mask == 1:
+                edges = tuple(tied(e, helm_far) for e in edges)
             mask *= 2
         state_own = turn_state(here, state_axial, rate, False, 0)
         (own,) = first_stencil(here, entry, state_own, *edges, rate, False, 1)
@@ -368,19 +371,25 @@
     )
 
     kept, back = [], []
-    for k in range(CHUNKS):
-
-        def chain(_, pair, k=k):
-            here = pair[0]
-            cur, leading, last = map1(own, here, own_peer, beside(here), high, low, k)
-            nxt = second_stencil(cur, *halos(leading, last), state_own, state_far, rate, k, half)
-            mine, theirs = map2(nxt, beside(nxt), high, low, k)
-            return theirs, mine
-
-        spare = tied(sent[k], kept[-1], back[0]) if k > 2 else tied(sent[k], kept[-1]) if k else sent[k]
-        theirs, mine = lax.fori_loop(0, once, chain, (far[k], spare))
-        kept.append(mine)
-        back.append(across(theirs))
+    for first in range(0, CHUNKS, TOGETHER):
+        group = range(first, first + TOGETHER)
+
+        def chains(_, carry, group=group):
+            here = carry[:TOGETHER]
+            there = [beside(h) for h in here]
+            moved = []
+            for k, h, t in zip(group, here, there):
+                cur, leading, last = map1(own, h, own_peer, t, high, low, k)
+                moved.append((cur, *halos(leading, last)))
+            nxt = [second_stencil(*m, state_own, state_far, rate, k, half) for k, m in zip(group, moved)]
+            there = [beside(n) for n in nxt]
+            results = [map2(n, t, high, low, k) for k, n, t in zip(group, nxt, there)]
+            return tuple(r[1] for r in results) + tuple(r[0] for r in results)
+
+        spare = [tied(sent[k], kept[-1]) if kept else sent[k] for k in group]
+        results = lax.fori_loop(0, once, chains, (*[far[k] for k in group], *spare))
+        kept += results[TOGETHER:]
+        back += [across(t) for t in results[:TOGETHER]]
     out = write_half(where, kept, nphi, False)
     out = write_half(where, back, nphi, True, out)
     return out.reshape(modes, comps, nz, nphi)

time: 205 us -> 192 us (0.937)
  waiting for transfers between devices: 102 us -> 85.7 us
  Pallas kernels: 71.8 us -> 66.7 us
  starting transfers between devices: 27.4 us -> 32.1 us
  local copies, waits for them, and re-layouts: 0.99 us -> 4.77 us
    ppermute x9, waiting for transfers between devices: 23.4 us -> 3.99 us  [beside(): return lax.ppermute(array, 'rad', [(i, i ^ 1) for i in range(peers)])]
    ppermute x10, waiting for transfers between devices: 22.1 us -> 32.3 us  [across(): return lax.ppermute(array, 'rad', [(i, i ^ 2) for i in range(peers)])]
    ppermute x2, waiting for transfers between devices: 18.3 us -> 11.8 us  [hop(): return lax.ppermute(array, 'col', [(i, i ^ mask) for i in range(cols)])]
    pallas_call x4, Pallas kernels: 6.42 us -> 1.51 us  [second_stencil(): pl.pallas_call(lambda *refs: second_kernel(*refs, k=k, half=half), out_sh...]
    while x16 -> x36, local copies, waits for them, and re-layouts: 0.03 us -> 3.82 us
    ppermute x2, starting transfers between devices: 0.07 us -> 2.16 us  [hop(): return lax.ppermute(array, 'col', [(i, i ^ mask) for i in range(cols)])]
  transfers between devices with their start and end apart: 33 -> 33, of which waited for: 24 -> 18; matrix products, arithmetic and copies ran while one was open for 1% -> 2% of each run, Pallas kernels for 32% -> 30%
where the time goes in v4:
time: 192 us
  waiting for transfers between devices  85.7 us (45%)
  Pallas kernels  66.7 us (35%)
  starting transfers between devices  32.1 us (17%)
  local copies, waits for them, and re-layouts  4.77 us (2%)
  other arithmetic  2.04 us (1%)
    ppermute x12, waiting for transfers between devices, halos(): return (lax.ppermute(leading, 'col', down), lax.ppermute(last, 'col', up))  37.7 us
    ppermute x10, waiting for transfers between devices, across(): return lax.ppermute(array, 'rad', [(i, i ^ 2) for i in range(peers)])  32.3 us
    pallas_call x4, Pallas kernels, map2(): pl.pallas_call(map2_kernel, out_shape=[shape(out)] * 2, grid=(comps,), in...  17.9 us
    ppermute x12, starting transfers between devices, halos(): return (lax.ppermute(leading, 'col', down), lax.ppermute(last, 'col', up))  17.3 us
    pallas_call x4, Pallas kernels, map1(): pl.pallas_call(map1_kernel, out_shape=[shape((comps, nz, width, cols)), s...  14.4 us
    ppermute x2, waiting for transfers between devices, hop(): return lax.ppermute(array, 'col', [(i, i ^ mask) for i in range(cols)])  11.8 us
    ppermute x10, starting transfers between devices, across(): return lax.ppermute(array, 'rad', [(i, i ^ 2) for i in range(peers)])  11.2 us
    pallas_call x2, Pallas kernels, write_half(): pl.pallas_call(lambda *refs: last_kernel(*refs, nz=nz, chunks=chunks), ou...  10.9 us
  transfers between devices with their start and end apart: 33, of which 18 were waited for; matrix products, arithmetic and copies ran while one was open for 2% of the time, Pallas kernels for 30%

profile of v4, /device:TPU:0, one launch (start us, length us, event | category | flops | bytes accessed | tf_op | source)
XLA Modules:
  0.0 191.7 jit_solution(13843392568824451774)
XLA Ops:
  0.1 3.1 %turn_state.2 = f32[2056,128]{1,0:T(8,128)} custom-call(s32[2]{0:T(128)S(1)} %pad_add_fusion.refs_0_, f32[2048,256]{1,0:T(8,128)} %bitcast.21, f32[1,128]{1,0:T(1,128)} %bitcast.26), custom_call_target="tpu_custom_call" | custom-call | flops 263168 | bytes 2105344 | tf_op jit(solution)/shard_map/turn_state/pallas_call | solution.py:70
  3.2 2.9 %collective-permute-start.26 = (f32[2056,128]{1,0:T(8,128)}, f32[2056,128]{1,0:T(8,128)S(1)}, u32[]{:S(2)}, u32[]{:S(2)}) collective-permute-start(f32[2056,128]{1,0:T(8,128)} %turn_state.2), channel_id=1, source_target_pairs={{0,16},{8,24},{16,0},{24,8},{1,17},{9,25},{17,1},{25,9},{2,18},{10... | collective-permute-start | bytes 3158024 | tf_op jit(solution)/shard_map/ppermute | solution.py:322
  7.2 22.5 %while.66 = (s32[]{:T(128)}, f32[3,16,32,128]{3,2,1,0:T(8,128)}, f32[3,16,32,128]{3,2,1,0:T(8,128)}, f32[3,16,32,128]{3,2,1,0:T(8,128)}, f32[3,16,32,128]{3,2,1,...) while((s32[]{:T(128)}, f32[3,16,32,128]{3,2,1,0:T(8,128)}, ...), condition=%wide.region_1.0_spmd, body=%wide.region_0.0_spmd.sunk | while | flops 9535493 | bytes 11010277 | solution.py:349
  7.2 2.6 %edge_layers.2 = (f32[384,128]{1,0:T(8,128)S(1)}, f32[384,128]{1,0:T(8,128)S(1)}) custom-call(s32[2]{0:T(128)S(1)} %broadcast_add_fusion.4.refs_0_, f32[6144,256]{1,0:T(8,128)} %bitcast.17), custom_call_target="tpu_custom_call" | custom-call | flops 98304 | bytes 3145728 | tf_op jit(solution)/shard_map/while/body/edge_layers/pallas_call | solution.py:96
  9.8 5.1 %collective-permute-start = (f32[384,128]{1,0:T(8,128)S(1)}, f32[384,128]{1,0:T(8,128)S(1)}, u32[]{:S(2)}, u32[]{:S(2)}) collective-permute-start(f32[384,128]{1,0:T(8,128)S(1)} %get-tuple-element.717), channel_id=1, source_target_pairs={{1,0},{2,1},{3,2},{4,3},{5,4},{6,5},{7,6},{0,7},{9,8},{10,9},{11,1... | collective-permute-start | bytes 589832 | tf_op jit(solution)/shard_map/while/body/ppermute | solution.py:341
  14.9 3.6 %collective-permute-done.refs_3_ = f32[384,128]{1,0:T(8,128)S(1)} collective-permute-done((f32[384,128]{1,0:T(8,128)S(1)}, f32[384,128]{1,0:T(8,128)S(1)}, u32[]{:S(2)}, u32[]{:S(2)}) %collective-permute-start) | collective-permute-done | bytes 196640 | tf_op jit(solution)/shard_map/while/body/ppermute | solution.py:341
  18.5 4.9 %collective-permute-done.1.refs_4_ = f32[384,128]{1,0:T(8,128)S(1)} collective-permute-done((f32[384,128]{1,0:T(8,128)S(1)}, f32[384,128]{1,0:T(8,128)S(1)}, u32[]{:S(2)}, u32[]{:S(2)}) %collective-permute-start.1) | collective-permute-done | bytes 196640 | tf_op jit(solution)/shard_map/while/body/ppermute | solution.py:341
  23.4 6.3 %first_stencil.2 = (f32[3,16,32,128]{3,2,1,0:T(8,128)}, f32[3,16,32,128]{3,2,1,0:T(8,128)}, f32[3,16,32,128]{3,2,1,0:T(8,128)}, f32[3,16,32,128]{3,2,1,0:T(8,128)}) custom-call(s32[2]{0:T(128)S(1)} %broadcast_add_fusion.4.refs_0_, f32[6144,256]{1,0:T(8,128)} %bitcast.18, f32[2056,128]{1,0:T(8,128)} %get-tuple-element.812.refs_2_, ...), custom_call_target="tpu_custom_call" | custom-call | flops 9437184 | bytes 6291456 | tf_op jit(solution)/shard_map/while/body/first_stencil/pallas_call | solution.py:146
  31.7 2.9 %collective-permute-done.25 = f32[3,128,128]{2,1,0:T(8,128)S(1)} collective-permute-done((f32[3,128,128]{2,1,0:T(8,128)S(1)}, f32[3,128,128]{2,1,0:T(8,128)S(1)}, u32[]{:S(2)}, u32[]{:S(2)}) %collective-permute-start.25) | collective-permute-done | bytes 196640 | tf_op jit(solution)/shard_map/ppermute | solution.py:322
  34.6 35.0 %while.67 = (s32[]{:T(128)}, f32[2048,128]{1,0:T(8,128)}, f32[3,16,128,128]{3,2,1,0:T(8,128)}, f32[3,16,128,128]{3,2,1,0:T(8,128)}, bf16[3,512,256]{2,1,0:T(8,12...) while((s32[]{:T(128)}, f32[2048,128]{1,0:T(8,128)}, ...), condition=%wide.region_3.0_spmd, body=%wide.region_2.0_spmd.sunk | while | flops 11075589 | bytes 78643688 | solution.py:369
  34.6 2.1 %collective-permute-start.3 = (f32[1,3,128,128]{3,2,1,0:T(8,128)S(1)}, f32[1,3,128,128]{3,2,1,0:T(8,128)S(1)}, u32[]{:S(2)}, u32[]{:S(2)}) collective-permute-start(f32[1,3,128,128]{3,2,1,0:T(8,128)S(1)} %bitcast.23), channel_id=1, source_target_pairs={{0,1},{1,0},{2,3},{3,2},{4,5},{5,4},{6,7},{7,6},{8,9},{9,8},{10,11... | collective-permute-start | bytes 589832 | tf_op jit(solution)/shard_map/while/body/ppermute | solution.py:328
  36.7 2.8 %edge_layers.3 = (f32[384,128]{1,0:T(8,128)S(1)}, f32[384,128]{1,0:T(8,128)S(1)}) custom-call(s32[2]{0:T(128)S(1)} %broadcast_add_fusion.5.refs_0_.where, f32[6144,256]{1,0:T(8,128)} %bitcast.19), custom_call_target="tpu_custom_call" | custom-call | flops 98304 | bytes 3145728 | tf_op jit(solution)/shard_map/while/body/edge_layers/pallas_call | solution.py:96
  39.5 3.6 %collective-permute-start.2 = (f32[384,128]{1,0:T(8,128)S(1)}, f32[384,128]{1,0:T(8,128)S(1)}, u32[]{:S(2)}, u32[]{:S(2)}) collective-permute-start(f32[384,128]{1,0:T(8,128)S(1)} %get-tuple-element.731), channel_id=1, source_target_pairs={{1,0},{2,1},{3,2},{4,3},{5,4},{6,5},{7,6},{0,7},{9,8},{10,9},{11,1... | collective-permute-start | bytes 589832 | tf_op jit(solution)/shard_map/while/body/ppermute | solution.py:341
  43.1 2.1 %turn_state.3.refs_2_ = f32[2048,128]{1,0:T(8,128)S(1)} custom-call(s32[2]{0:T(128)S(1)} %broadcast_add_fusion.5.refs_0_.where, f32[2048,256]{1,0:T(8,128)} %bitcast.22, f32[1,128]{1,0:T(1,128)S(1)} %get-tuple-element.855.refs_2_.refs_5_), custom_call_target="tpu_custom_call" | custom-call | flops 262144 | bytes 2097152 | tf_op jit(solution)/shard_map/while/body/turn_state/pallas_call | solution.py:70
  46.3 5.2 %collective-permute-done.4.refs_4_ = f32[384,128]{1,0:T(8,128)S(1)} collective-permute-done((f32[384,128]{1,0:T(8,128)S(1)}, f32[384,128]{1,0:T(8,128)S(1)}, u32[]{:S(2)}, u32[]{:S(2)}) %collective-permute-start.4) | collective-permute-done | bytes 196640 | tf_op jit(solution)/shard_map/while/body/ppermute | solution.py:341
  51.5 2.7 %first_stencil.3 = f32[3,16,128,128]{3,2,1,0:T(8,128)S(1)} custom-call(s32[2]{0:T(128)S(1)} %broadcast_add_fusion.5.refs_0_.where, f32[6144,256]{1,0:T(8,128)S(1)} %bitcast.20, f32[2048,128]{1,0:T(8,128)S(1)} %turn_state.3.refs_2_, f32[384,128]{1,0:T(8,128)S(1)} %collective-permute-done.2.refs_3_, f32[384,128]{1,0:T(8,128)S(1)} %collective-permute-done.4.refs_4_, ...), custom_call_target="tpu_custom_call" | custom-call | flops 9437184 | bytes 6291456 | tf_op jit(solution)/shard_map/while/body/first_stencil/pallas_call | solution.py:146
  54.4 11.8 %collective-permute-done.6 = f32[2,3,128,128]{3,2,1,0:T(8,128)} collective-permute-done((f32[2,3,128,128]{3,2,1,0:T(8,128)}, f32[2,3,128,128]{3,2,1,0:T(8,128)}, u32[]{:S(2)}, u32[]{:S(2)}) %collective-permute-start.6) | collective-permute-done | bytes 393248 | tf_op jit(solution)/shard_map/while/body/ppermute | solution.py:328
  67.2 2.4 %split_helm.1 = (bf16[3,512,256]{2,1,0:T(8,128)(2,1)}, bf16[3,512,256]{2,1,0:T(8,128)(2,1)}) custom-call(s32[2]{0:T(128)S(1)} %broadcast_add_fusion.5.refs_0_.where, f32[3,512,128]{2,1,0:T(8,128)S(1)} %copy-done.18, f32[4,3,128,128]{3,2,1,0:T(8,128)S(1)} %pad_maximum_fusion.5.far), custom_call_target="tpu_custom_call" | custom-call | flops 786432 | bytes 3145728 | tf_op jit(solution)/shard_map/while/body/split_helm/pallas_call | solution.py:180
  69.6 1.7 collective-permute-start.29
  71.7 38.8 %while.68 = (s32[]{:T(128)}, f32[3,16,32,128]{3,2,1,0:T(8,128)}, f32[3,16,32,128]{3,2,1,0:T(8,128)}, f32[3,16,32,128]{3,2,1,0:T(8,128)}, f32[3,16,32,128]{3,2,1,...) while((s32[]{:T(128)}, f32[3,16,32,128]{3,2,1,0:T(8,128)}, ...), condition=%wide.region_5.0_spmd, body=%wide.region_4.0_spmd.sunk | while | flops 4841275392 | bytes 85475976 | solution.py:390
  72.2 2.0 %collective-permute-done.11.far_peer = f32[3,16,32,128]{3,2,1,0:T(8,128)S(1)} collective-permute-done((f32[3,16,32,128]{3,2,1,0:T(8,128)}, f32[3,16,32,128]{3,2,1,0:T(8,128)S(1)}, u32[]{:S(2)}, u32[]{:S(2)}) %collective-permute-start.11) | collective-permute-done | bytes 786464 | tf_op jit(solution)/shard_map/while/body/ppermute | solution.py:325
  74.2 3.9 %map1_1.1 = (f32[3,16,32,256]{3,2,1,0:T(8,128)S(1)}, f32[3,32,256]{2,1,0:T(8,128)S(1)}, f32[3,32,256]{2,1,0:T(8,128)S(1)}) custom-call(f32[3,16,128,128]{3,2,1,0:T(8,128)} %get-tuple-element.895.own, f32[3,16,32,128]{3,2,1,0:T(8,128)} %get-tuple-element.877.far, f32[3,16,128,128]{3,2,1,0:T(8,128)} %get-tuple-element.896.own_peer, ...), custom_call_target="tpu_custom_call" | custom-call | flops 1207959552 | bytes 6291456 | tf_op jit(solution)/shard_map/while/body/map1_1/pallas_call | solution.py:215
  78.1 2.4 %collective-permute-start.12 = (f32[3,32,256]{2,1,0:T(8,128)S(1)}, f32[3,32,256]{2,1,0:T(8,128)S(1)}, u32[]{:S(2)}, u32[]{:S(2)}) collective-permute-start(f32[3,32,256]{2,1,0:T(8,128)S(1)} %get-tuple-element.754), channel_id=1, source_target_pairs={{1,0},{2,1},{3,2},{4,3},{5,4},{6,5},{7,6},{0,7},{9,8},{10,9},{11,1... | collective-permute-start | bytes 294920 | tf_op jit(solution)/shard_map/while/body/ppermute | solution.py:341
  80.5 2.5 %collective-permute-done.12.refs_1_ = f32[3,32,256]{2,1,0:T(8,128)S(1)} collective-permute-done((f32[3,32,256]{2,1,0:T(8,128)S(1)}, f32[3,32,256]{2,1,0:T(8,128)S(1)}, u32[]{:S(2)}, u32[]{:S(2)}) %collective-permute-start.12) | collective-permute-done | bytes 98336 | tf_op jit(solution)/shard_map/while/body/ppermute | solution.py:341
  83.0 4.8 %collective-permute-done.13.refs_2_ = f32[3,32,256]{2,1,0:T(8,128)S(1)} collective-permute-done((f32[3,32,256]{2,1,0:T(8,128)S(1)}, f32[3,32,256]{2,1,0:T(8,128)S(1)}, u32[]{:S(2)}, u32[]{:S(2)}) %collective-permute-start.13) | collective-permute-done | bytes 98336 | tf_op jit(solution)/shard_map/while/body/ppermute | solution.py:341
  90.2 3.3 %map1_0.1 = (f32[3,16,32,256]{3,2,1,0:T(8,128)S(1)}, f32[3,32,256]{2,1,0:T(8,128)S(1)}, f32[3,32,256]{2,1,0:T(8,128)S(1)}) custom-call(f32[3,16,128,128]{3,2,1,0:T(8,128)S(1)} %copy-done.10, f32[3,16,32,128]{3,2,1,0:T(8,128)} %get-tuple-element.876.far, f32[3,16,128,128]{3,2,1,0:T(8,128)} %get-tuple-element.896.own_peer, ...), custom_call_target="tpu_custom_call" | custom-call | flops 1207959552 | bytes 6291456 | tf_op jit(solution)/shard_map/while/body/map1_0/pallas_call | solution.py:215
  93.8 1.8 collective-permute-start.9
  95.6 2.6 %collective-permute-done.8.refs_1_ = f32[3,32,256]{2,1,0:T(8,128)S(1)} collective-permute-done((f32[3,32,256]{2,1,0:T(8,128)S(1)}, f32[3,32,256]{2,1,0:T(8,128)S(1)}, u32[]{:S(2)}, u32[]{:S(2)}) %collective-permute-start.8) | collective-permute-done | bytes 98336 | tf_op jit(solution)/shard_map/while/body/ppermute | solution.py:341
  98.2 2.9 %collective-permute-done.9.refs_2_ = f32[3,32,256]{2,1,0:T(8,128)S(1)} collective-permute-done((f32[3,32,256]{2,1,0:T(8,128)S(1)}, f32[3,32,256]{2,1,0:T(8,128)S(1)}, u32[]{:S(2)}, u32[]{:S(2)}) %collective-permute-start.9) | collective-permute-done | bytes 98336 | tf_op jit(solution)/shard_map/while/body/ppermute | solution.py:341
  101.6 4.7 %map2_1.1 = (f32[3,16,32,128]{3,2,1,0:T(8,128)}, f32[3,16,32,128]{3,2,1,0:T(8,128)}) custom-call(f32[3,16,32,256]{3,2,1,0:T(8,128)S(1)} %second_stencil_1.1.own, f32[3,16,32,256]{3,2,1,0:T(8,128)} %collective-permute-done.14.peer, bf16[3,512,256]{2,1,0:T(8,128)(2,1)} %get-tuple-element.897.high, bf16[3,512,256]{2,1,0:T(8,128)(2,1)} %get-tuple-element.898.low), custom_call_target="tpu_custom_call" | custom-call | flops 1207959552 | bytes 6291456 | tf_op jit(solution)/shard_map/while/body/map2_1/pallas_call | solution.py:269
  106.3 4.2 %map2_0.1 = (f32[3,16,32,128]{3,2,1,0:T(8,128)}, f32[3,16,32,128]{3,2,1,0:T(8,128)}) custom-call(f32[3,16,32,256]{3,2,1,0:T(8,128)S(1)} %second_stencil_0.1.own, f32[3,16,32,256]{3,2,1,0:T(8,128)} %collective-permute-done.10.peer, bf16[3,512,256]{2,1,0:T(8,128)(2,1)S(1)} %copy-done.2, bf16[3,512,256]{2,1,0:T(8,128)(2,1)S(1)} %copy-done.6), custom_call_target="tpu_custom_call" | custom-call | flops 1207959552 | bytes 6291456 | tf_op jit(solution)/shard_map/while/body/map2_0/pallas_call | solution.py:269
  110.5 1.6 collective-permute-start.27
  112.6 36.8 %while.69 = (s32[]{:T(128)}, f32[3,16,32,128]{3,2,1,0:T(8,128)}, f32[3,16,32,128]{3,2,1,0:T(8,128)}, f32[3,16,32,128]{3,2,1,0:T(8,128)}, f32[3,16,32,128]{3,2,1,...) while((s32[]{:T(128)}, f32[3,16,32,128]{3,2,1,0:T(8,128)}, ...), condition=%wide.region_7.0_spmd, body=%wide.region_6.0_spmd.sunk | while | flops 4841275392 | bytes 85475976 | solution.py:390
  113.1 2.0 %collective-permute-done.19.far_peer = f32[3,16,32,128]{3,2,1,0:T(8,128)S(1)} collective-permute-done((f32[3,16,32,128]{3,2,1,0:T(8,128)}, f32[3,16,32,128]{3,2,1,0:T(8,128)S(1)}, u32[]{:S(2)}, u32[]{:S(2)}) %collective-permute-start.19) | collective-permute-done | bytes 786464 | tf_op jit(solution)/shard_map/while/body/ppermute | solution.py:325
  115.1 3.9 %map1_3.1 = (f32[3,16,32,256]{3,2,1,0:T(8,128)S(1)}, f32[3,32,256]{2,1,0:T(8,128)S(1)}, f32[3,32,256]{2,1,0:T(8,128)S(1)}) custom-call(f32[3,16,128,128]{3,2,1,0:T(8,128)} %get-tuple-element.937.own, f32[3,16,32,128]{3,2,1,0:T(8,128)} %get-tuple-element.919.far, f32[3,16,128,128]{3,2,1,0:T(8,128)} %get-tuple-element.938.own_peer, ...), custom_call_target="tpu_custom_call" | custom-call | flops 1207959552 | bytes 6291456 | tf_op jit(solution)/shard_map/while/body/map1_3/pallas_call | solution.py:215
  119.1 2.0 %collective-permute-start.21 = (f32[3,32,256]{2,1,0:T(8,128)S(1)}, f32[3,32,256]{2,1,0:T(8,128)S(1)}, u32[]{:S(2)}, u32[]{:S(2)}) collective-permute-start(f32[3,32,256]{2,1,0:T(8,128)S(1)} %get-tuple-element.776), channel_id=1, source_target_pairs={{0,1},{1,2},{2,3},{3,4},{4,5},{5,6},{6,7},{7,0},{8,9},{9,10},{10,1... | collective-permute-start | bytes 294920 | tf_op jit(solution)/shard_map/while/body/ppermute | solution.py:341
  121.1 2.8 %collective-permute-done.20.refs_1_ = f32[3,32,256]{2,1,0:T(8,128)S(1)} collective-permute-done((f32[3,32,256]{2,1,0:T(8,128)S(1)}, f32[3,32,256]{2,1,0:T(8,128)S(1)}, u32[]{:S(2)}, u32[]{:S(2)}) %collective-permute-start.20) | collective-permute-done | bytes 98336 | tf_op jit(solution)/shard_map/while/body/ppermute | solution.py:341
  123.9 2.8 %collective-permute-done.21.refs_2_ = f32[3,32,256]{2,1,0:T(8,128)S(1)} collective-permute-done((f32[3,32,256]{2,1,0:T(8,128)S(1)}, f32[3,32,256]{2,1,0:T(8,128)S(1)}, u32[]{:S(2)}, u32[]{:S(2)}) %collective-permute-start.21) | collective-permute-done | bytes 98336 | tf_op jit(solution)/shard_map/while/body/ppermute | solution.py:341
  129.0 3.3 %map1_2.1 = (f32[3,16,32,256]{3,2,1,0:T(8,128)S(1)}, f32[3,32,256]{2,1,0:T(8,128)S(1)}, f32[3,32,256]{2,1,0:T(8,128)S(1)}) custom-call(f32[3,16,128,128]{3,2,1,0:T(8,128)S(1)} %copy-done.11, f32[3,16,32,128]{3,2,1,0:T(8,128)} %get-tuple-element.918.far, f32[3,16,128,128]{3,2,1,0:T(8,128)} %get-tuple-element.938.own_peer, ...), custom_call_target="tpu_custom_call" | custom-call | flops 1207959552 | bytes 6291456 | tf_op jit(solution)/shard_map/while/body/map1_2/pallas_call | solution.py:215
  132.6 1.8 collective-permute-start.17
  134.4 2.6 %collective-permute-done.16.refs_1_ = f32[3,32,256]{2,1,0:T(8,128)S(1)} collective-permute-done((f32[3,32,256]{2,1,0:T(8,128)S(1)}, f32[3,32,256]{2,1,0:T(8,128)S(1)}, u32[]{:S(2)}, u32[]{:S(2)}) %collective-permute-start.16) | collective-permute-done | bytes 98336 | tf_op jit(solution)/shard_map/while/body/ppermute | solution.py:341
  137.0 2.9 %collective-permute-done.17.refs_2_ = f32[3,32,256]{2,1,0:T(8,128)S(1)} collective-permute-done((f32[3,32,256]{2,1,0:T(8,128)S(1)}, f32[3,32,256]{2,1,0:T(8,128)S(1)}, u32[]{:S(2)}, u32[]{:S(2)}) %collective-permute-start.17) | collective-permute-done | bytes 98336 | tf_op jit(solution)/shard_map/while/body/ppermute | solution.py:341
  140.4 4.7 %map2_3.1 = (f32[3,16,32,128]{3,2,1,0:T(8,128)}, f32[3,16,32,128]{3,2,1,0:T(8,128)}) custom-call(f32[3,16,32,256]{3,2,1,0:T(8,128)S(1)} %second_stencil_3.1.own, f32[3,16,32,256]{3,2,1,0:T(8,128)} %collective-permute-done.22.peer, bf16[3,512,256]{2,1,0:T(8,128)(2,1)} %get-tuple-element.939.high, bf16[3,512,256]{2,1,0:T(8,128)(2,1)} %get-tuple-element.940.low), custom_call_target="tpu_custom_call" | custom-call | flops 1207959552 | bytes 6291456 | tf_op jit(solution)/shard_map/while/body/map2_3/pallas_call | solution.py:269
  145.1 4.3 %map2_2.1 = (f32[3,16,32,128]{3,2,1,0:T(8,128)}, f32[3,16,32,128]{3,2,1,0:T(8,128)}) custom-call(f32[3,16,32,256]{3,2,1,0:T(8,128)S(1)} %second_stencil_2.1.own, f32[3,16,32,256]{3,2,1,0:T(8,128)} %collective-permute-done.18.peer, bf16[3,512,256]{2,1,0:T(8,128)(2,1)S(1)} %copy-done.4, bf16[3,512,256]{2,1,0:T(8,128)(2,1)S(1)} %copy-done.8), custom_call_target="tpu_custom_call" | custom-call | flops 1207959552 | bytes 6291456 | tf_op jit(solution)/shard_map/while/body/map2_2/pallas_call | solution.py:269
  151.4 5.6 %write_own.1.refs_5_ = f32[128,48,256]{2,1,0:T(8,128)} custom-call(s32[2]{0:T(128)S(1)} %get-tuple-element.999, f32[3,16,32,128]{3,2,1,0:T(8,128)} %get-tuple-element.337.refs_1_, f32[3,16,32,128]{3,2,1,0:T(8,128)} %get-tuple-element.332.refs_2_, f32[3,16,32,128]{3,2,1,0:T(8,128)} %get-tuple-element.338.refs_3_, f32[3,16,32,128]{3,2,1,0:T(8,128)} %get-tuple-element.339.refs_4_), custom_call_target="tpu_custom_call" | custom-call | flops 1572864 | bytes 6291456 | tf_op jit(solution)/shard_map/write_own/pallas_call | solution.py:293
  157.1 12.9 %collective-permute-done.31.refs_3_ = f32[3,16,32,128]{3,2,1,0:T(8,128)S(1)} collective-permute-done((f32[3,16,32,128]{3,2,1,0:T(8,128)}, f32[3,16,32,128]{3,2,1,0:T(8,128)S(1)}, u32[]{:S(2)}, u32[]{:S(2)}) %collective-permute-start.31) | collective-permute-done | bytes 786464 | tf_op jit(solution)/shard_map/ppermute | solution.py:322
  170.0 16.4 %collective-permute-done.32.refs_4_ = f32[3,16,32,128]{3,2,1,0:T(8,128)S(1)} collective-permute-done((f32[3,16,32,128]{3,2,1,0:T(8,128)}, f32[3,16,32,128]{3,2,1,0:T(8,128)S(1)}, u32[]{:S(2)}, u32[]{:S(2)}) %collective-permute-start.32) | collective-permute-done | bytes 786464 | tf_op jit(solution)/shard_map/ppermute | solution.py:322
  186.4 5.3 %write_foreign.1 = f32[128,48,256]{2,1,0:T(8,128)} custom-call(s32[2]{0:T(128)S(1)} %get-tuple-element.999, f32[3,16,32,128]{3,2,1,0:T(8,128)} %collective-permute-done.27.refs_1_, f32[3,16,32,128]{3,2,1,0:T(8,128)} %collective-permute-done.28.refs_2_, f32[3,16,32,128]{3,2,1,0:T(8,128)S(1)} %collective-permute-done.31.refs_3_, ...), custom_call_target="tpu_custom_call", output_to_operand_aliasing={{}: (5, {})} | custom-call | flops 1572864 | bytes 6291456 | tf_op jit(solution)/shard_map/write_foreign/pallas_call | solution.py:293
  (91 shorter events, 15.5 us)
Async XLA Ops:
  0.0 7.2 %copy-start.19 = (f32[128]{0:T(128)S(1)}, f32[128]{0:T(128)}, u32[]{:S(2)}) copy-start(f32[128]{0:T(128)} %param.15) | copy-start | bytes 1540
  3.2 28.5 %collective-permute-start.26 = (f32[2056,128]{1,0:T(8,128)}, f32[2056,128]{1,0:T(8,128)S(1)}, u32[]{:S(2)}, u32[]{:S(2)}) collective-permute-start(f32[2056,128]{1,0:T(8,128)} %turn_state.2), channel_id=1, source_target_pairs={{0,16},{8,24},{16,0},{24,8},{1,17},{9,25},{17,1},{25,9},{2,18},{10... | collective-permute-start | bytes 3158024 | tf_op jit(solution)/shard_map/ppermute | solution.py:322
  7.1 27.6 %collective-permute-start.25 = (f32[3,128,128]{2,1,0:T(8,128)S(1)}, f32[3,128,128]{2,1,0:T(8,128)S(1)}, u32[]{:S(2)}, u32[]{:S(2)}) collective-permute-start(f32[3,128,128]{2,1,0:T(8,128)S(1)} %constant_dynamic-slice_fusion), channel_id=1, source_target_pairs={{0,16},{8,24},{16,0},{24,8},{1,17},{9,25},{17,1},{25,9},{2,18},{10... | collective-permute-start | bytes 589832 | tf_op jit(solution)/shard_map/ppermute | solution.py:322
  9.8 8.7 %collective-permute-start = (f32[384,128]{1,0:T(8,128)S(1)}, f32[384,128]{1,0:T(8,128)S(1)}, u32[]{:S(2)}, u32[]{:S(2)}) collective-permute-start(f32[384,128]{1,0:T(8,128)S(1)} %get-tuple-element.717), channel_id=1, source_target_pairs={{1,0},{2,1},{3,2},{4,3},{5,4},{6,5},{7,6},{0,7},{9,8},{10,9},{11,1... | collective-permute-start | bytes 589832 | tf_op jit(solution)/shard_map/while/body/ppermute | solution.py:341
  14.9 8.5 %collective-permute-start.1 = (f32[384,128]{1,0:T(8,128)S(1)}, f32[384,128]{1,0:T(8,128)S(1)}, u32[]{:S(2)}, u32[]{:S(2)}) collective-permute-start(f32[384,128]{1,0:T(8,128)S(1)} %get-tuple-element.718), channel_id=1, source_target_pairs={{0,1},{1,2},{2,3},{3,4},{4,5},{5,6},{6,7},{7,0},{8,9},{9,10},{10,1... | collective-permute-start | bytes 589832 | tf_op jit(solution)/shard_map/while/body/ppermute | solution.py:341
  29.7 42.0 %collective-permute-start.23 = (f32[3,16,32,128]{3,2,1,0:T(8,128)}, f32[3,16,32,128]{3,2,1,0:T(8,128)}, u32[]{:S(2)}, u32[]{:S(2)}) collective-permute-start(f32[3,16,32,128]{3,2,1,0:T(8,128)} %get-tuple-element.864), channel_id=1, source_target_pairs={{0,16},{8,24},{16,0},{24,8},{1,17},{9,25},{17,1},{25,9},{2,18},{10... | collective-permute-start | bytes 2359304 | tf_op jit(solution)/shard_map/ppermute | solution.py:322
  31.2 40.6 %collective-permute-start.24 = (f32[3,16,32,128]{3,2,1,0:T(8,128)}, f32[3,16,32,128]{3,2,1,0:T(8,128)}, u32[]{:S(2)}, u32[]{:S(2)}) collective-permute-start(f32[3,16,32,128]{3,2,1,0:T(8,128)} %get-tuple-element.865), channel_id=1, source_target_pairs={{0,16},{8,24},{16,0},{24,8},{1,17},{9,25},{17,1},{25,9},{2,18},{10... | collective-permute-start | bytes 2359304 | tf_op jit(solution)/shard_map/ppermute | solution.py:322
  31.7 2.9 %copy-start.15 = (f32[2056,128]{1,0:T(8,128)}, f32[2056,128]{1,0:T(8,128)S(1)}, u32[]{:S(2)}) copy-start(f32[2056,128]{1,0:T(8,128)S(1)} %collective-permute-done.26) | copy-start | bytes 3158020
  34.6 10.6 %collective-permute-start.3 = (f32[1,3,128,128]{3,2,1,0:T(8,128)S(1)}, f32[1,3,128,128]{3,2,1,0:T(8,128)S(1)}, u32[]{:S(2)}, u32[]{:S(2)}) collective-permute-start(f32[1,3,128,128]{3,2,1,0:T(8,128)S(1)} %bitcast.23), channel_id=1, source_target_pairs={{0,1},{1,0},{2,3},{3,2},{4,5},{5,4},{6,7},{7,6},{8,9},{9,8},{10,11... | collective-permute-start | bytes 589832 | tf_op jit(solution)/shard_map/while/body/ppermute | solution.py:328
  36.7 14.8 %copy-start = (f32[128,3,16,256]{3,2,1,0:T(8,128)S(1)}, f32[128,3,16,256]{3,2,1,0:T(8,128)}, u32[]{:S(2)}) copy-start(f32[128,3,16,256]{3,2,1,0:T(8,128)} %get-tuple-element.856) | copy-start | bytes 18874372 | tf_op jit(solution)/shard_map/while
  39.5 6.8 %collective-permute-start.2 = (f32[384,128]{1,0:T(8,128)S(1)}, f32[384,128]{1,0:T(8,128)S(1)}, u32[]{:S(2)}, u32[]{:S(2)}) collective-permute-start(f32[384,128]{1,0:T(8,128)S(1)} %get-tuple-element.731), channel_id=1, source_target_pairs={{1,0},{2,1},{3,2},{4,3},{5,4},{6,5},{7,6},{0,7},{9,8},{10,9},{11,1... | collective-permute-start | bytes 589832 | tf_op jit(solution)/shard_map/while/body/ppermute | solution.py:341
  43.1 8.4 %collective-permute-start.4 = (f32[384,128]{1,0:T(8,128)S(1)}, f32[384,128]{1,0:T(8,128)S(1)}, u32[]{:S(2)}, u32[]{:S(2)}) collective-permute-start(f32[384,128]{1,0:T(8,128)S(1)} %get-tuple-element.734), channel_id=1, source_target_pairs={{0,1},{1,2},{2,3},{3,4},{4,5},{5,6},{6,7},{7,0},{8,9},{9,10},{10,1... | collective-permute-start | bytes 589832 | tf_op jit(solution)/shard_map/while/body/ppermute | solution.py:341
  45.3 8.9 %copy-start.12 = (f32[2048,128]{1,0:T(8,128)}, f32[2048,128]{1,0:T(8,128)S(1)}, u32[]{:S(2)}) copy-start(f32[2048,128]{1,0:T(8,128)S(1)} %turn_state.3.refs_2_) | copy-start | bytes 3145732 | tf_op jit(solution)/shard_map/while
  54.2 15.4 %copy-start.9 = (f32[3,16,128,128]{3,2,1,0:T(8,128)}, f32[3,16,128,128]{3,2,1,0:T(8,128)S(1)}, u32[]{:S(2)}) copy-start(f32[3,16,128,128]{3,2,1,0:T(8,128)S(1)} %first_stencil.3) | copy-start | bytes 9437188 | tf_op jit(solution)/shard_map/while
  54.2 15.4 %collective-permute-start.5 = (f32[3,16,128,128]{3,2,1,0:T(8,128)S(1)}, f32[3,16,128,128]{3,2,1,0:T(8,128)}, u32[]{:S(2)}, u32[]{:S(2)}) collective-permute-start(f32[3,16,128,128]{3,2,1,0:T(8,128)S(1)} %first_stencil.3), channel_id=1, source_target_pairs={{0,8},{8,0},{16,24},{24,16},{1,9},{9,1},{17,25},{25,17},{2,10},{10... | collective-permute-start | bytes 9437192 | tf_op jit(solution)/shard_map/while/body/ppermute | solution.py:325
  54.3 11.8 %collective-permute-start.6 = (f32[2,3,128,128]{3,2,1,0:T(8,128)}, f32[2,3,128,128]{3,2,1,0:T(8,128)}, u32[]{:S(2)}, u32[]{:S(2)}) collective-permute-start(f32[2,3,128,128]{3,2,1,0:T(8,128)} %pad_maximum_fusion.4), channel_id=1, source_target_pairs={{0,2},{1,3},{2,0},{3,1},{4,6},{5,7},{6,4},{7,5},{8,10},{9,11},{10,... | collective-permute-start | bytes 1179656 | tf_op jit(solution)/shard_map/while/body/ppermute | solution.py:328
  54.4 12.8 %copy-start.18 = (f32[3,512,128]{2,1,0:T(8,128)S(1)}, f32[3,512,128]{2,1,0:T(8,128)}, u32[]{:S(2)}) copy-start(f32[3,512,128]{2,1,0:T(8,128)} %get-tuple-element.858.own) | copy-start | bytes 2359300 | tf_op jit(solution)/shard_map/while
  69.6 42.9 %collective-permute-start.29 = (f32[3,16,32,128]{3,2,1,0:T(8,128)}, f32[3,16,32,128]{3,2,1,0:T(8,128)}, u32[]{:S(2)}, u32[]{:S(2)}) collective-permute-start(f32[3,16,32,128]{3,2,1,0:T(8,128)} %get-tuple-element.906), channel_id=1, source_target_pairs={{0,16},{8,24},{16,0},{24,8},{1,17},{9,25},{17,1},{25,9},{2,18},{10... | collective-permute-start | bytes 2359304 | tf_op jit(solution)/shard_map/ppermute | solution.py:322
  71.3 41.2 %collective-permute-start.30 = (f32[3,16,32,128]{3,2,1,0:T(8,128)}, f32[3,16,32,128]{3,2,1,0:T(8,128)}, u32[]{:S(2)}, u32[]{:S(2)}) collective-permute-start(f32[3,16,32,128]{3,2,1,0:T(8,128)} %get-tuple-element.907), channel_id=1, source_target_pairs={{0,16},{8,24},{16,0},{24,8},{1,17},{9,25},{17,1},{25,9},{2,18},{10... | collective-permute-start | bytes 2359304 | tf_op jit(solution)/shard_map/ppermute | solution.py:322
  71.7 2.5 %collective-permute-start.11 = (f32[3,16,32,128]{3,2,1,0:T(8,128)}, f32[3,16,32,128]{3,2,1,0:T(8,128)S(1)}, u32[]{:S(2)}, u32[]{:S(2)}) collective-permute-start(f32[3,16,32,128]{3,2,1,0:T(8,128)} %get-tuple-element.877.far), channel_id=1, source_target_pairs={{0,8},{8,0},{16,24},{24,16},{1,9},{9,1},{17,25},{25,17},{2,10},{10... | collective-permute-start | bytes 2359304 | tf_op jit(solution)/shard_map/while/body/ppermute | solution.py:325
  71.7 16.6 %collective-permute-start.7 = (f32[3,16,32,128]{3,2,1,0:T(8,128)}, f32[3,16,32,128]{3,2,1,0:T(8,128)S(1)}, u32[]{:S(2)}, u32[]{:S(2)}) collective-permute-start(f32[3,16,32,128]{3,2,1,0:T(8,128)} %get-tuple-element.876.far), channel_id=1, source_target_pairs={{0,8},{8,0},{16,24},{24,16},{1,9},{9,1},{17,25},{25,17},{2,10},{10... | collective-permute-start | bytes 2359304 | tf_op jit(solution)/shard_map/while/body/ppermute | solution.py:325
  74.2 13.6 %copy-start.13 = (f32[2048,128]{1,0:T(8,128)S(1)}, f32[2048,128]{1,0:T(8,128)}, u32[]{:S(2)}) copy-start(f32[2048,128]{1,0:T(8,128)} %get-tuple-element.899.refs_3_) | copy-start | bytes 3145732 | tf_op jit(solution)/shard_map/while
  74.2 13.6 %copy-start.16 = (f32[2056,128]{1,0:T(8,128)S(1)}, f32[2056,128]{1,0:T(8,128)}, u32[]{:S(2)}) copy-start(f32[2056,128]{1,0:T(8,128)} %get-tuple-element.900.refs_4_) | copy-start | bytes 3158020 | tf_op jit(solution)/shard_map/while
  78.1 4.9 %collective-permute-start.12 = (f32[3,32,256]{2,1,0:T(8,128)S(1)}, f32[3,32,256]{2,1,0:T(8,128)S(1)}, u32[]{:S(2)}, u32[]{:S(2)}) collective-permute-start(f32[3,32,256]{2,1,0:T(8,128)S(1)} %get-tuple-element.754), channel_id=1, source_target_pairs={{1,0},{2,1},{3,2},{4,3},{5,4},{6,5},{7,6},{0,7},{9,8},{10,9},{11,1... | collective-permute-start | bytes 294920 | tf_op jit(solution)/shard_map/while/body/ppermute | solution.py:341
  80.5 7.3 %collective-permute-start.13 = (f32[3,32,256]{2,1,0:T(8,128)S(1)}, f32[3,32,256]{2,1,0:T(8,128)S(1)}, u32[]{:S(2)}, u32[]{:S(2)}) collective-permute-start(f32[3,32,256]{2,1,0:T(8,128)S(1)} %get-tuple-element.755), channel_id=1, source_target_pairs={{0,1},{1,2},{2,3},{3,4},{4,5},{5,6},{6,7},{7,0},{8,9},{9,10},{10,1... | collective-permute-start | bytes 294920 | tf_op jit(solution)/shard_map/while/body/ppermute | solution.py:341
  87.9 2.4 %copy-start.10 = (f32[3,16,128,128]{3,2,1,0:T(8,128)S(1)}, f32[3,16,128,128]{3,2,1,0:T(8,128)}, u32[]{:S(2)}) copy-start(f32[3,16,128,128]{3,2,1,0:T(8,128)} %get-tuple-element.895.own) | copy-start | bytes 9437188 | tf_op jit(solution)/shard_map/while
  88.3 13.3 %collective-permute-start.14 = (f32[3,16,32,256]{3,2,1,0:T(8,128)S(1)}, f32[3,16,32,256]{3,2,1,0:T(8,128)}, u32[]{:S(2)}, u32[]{:S(2)}) collective-permute-start(f32[3,16,32,256]{3,2,1,0:T(8,128)S(1)} %second_stencil_1.1.own), channel_id=1, source_target_pairs={{0,8},{8,0},{16,24},{24,16},{1,9},{9,1},{17,25},{25,17},{2,10},{10... | collective-permute-start | bytes 4718600 | tf_op jit(solution)/shard_map/while/body/ppermute | solution.py:325
  93.5 4.7 %collective-permute-start.8 = (f32[3,32,256]{2,1,0:T(8,128)S(1)}, f32[3,32,256]{2,1,0:T(8,128)S(1)}, u32[]{:S(2)}, u32[]{:S(2)}) collective-permute-start(f32[3,32,256]{2,1,0:T(8,128)S(1)} %get-tuple-element.750), channel_id=1, source_target_pairs={{1,0},{2,1},{3,2},{4,3},{5,4},{6,5},{7,6},{0,7},{9,8},{10,9},{11,1... | collective-permute-start | bytes 294920 | tf_op jit(solution)/shard_map/while/body/ppermute | solution.py:341
  93.8 7.3 %collective-permute-start.9 = (f32[3,32,256]{2,1,0:T(8,128)S(1)}, f32[3,32,256]{2,1,0:T(8,128)S(1)}, u32[]{:S(2)}, u32[]{:S(2)}) collective-permute-start(f32[3,32,256]{2,1,0:T(8,128)S(1)} %get-tuple-element.751), channel_id=1, source_target_pairs={{0,1},{1,2},{2,3},{3,4},{4,5},{5,6},{6,7},{7,0},{8,9},{9,10},{10,1... | collective-permute-start | bytes 294920 | tf_op jit(solution)/shard_map/while/body/ppermute | solution.py:341
  101.5 4.8 %collective-permute-start.10 = (f32[3,16,32,256]{3,2,1,0:T(8,128)S(1)}, f32[3,16,32,256]{3,2,1,0:T(8,128)}, u32[]{:S(2)}, u32[]{:S(2)}) collective-permute-start(f32[3,16,32,256]{3,2,1,0:T(8,128)S(1)} %second_stencil_0.1.own), channel_id=1, source_target_pairs={{0,8},{8,0},{16,24},{24,16},{1,9},{9,1},{17,25},{25,17},{2,10},{10... | collective-permute-start | bytes 4718600 | tf_op jit(solution)/shard_map/while/body/ppermute | solution.py:325
  101.6 4.7 %copy-start.2 = (bf16[3,512,256]{2,1,0:T(8,128)(2,1)S(1)}, bf16[3,512,256]{2,1,0:T(8,128)(2,1)}, u32[]{:S(2)}) copy-start(bf16[3,512,256]{2,1,0:T(8,128)(2,1)} %get-tuple-element.897.high) | copy-start | bytes 2359300 | tf_op jit(solution)/shard_map/while
  101.6 4.7 %copy-start.6 = (bf16[3,512,256]{2,1,0:T(8,128)(2,1)S(1)}, bf16[3,512,256]{2,1,0:T(8,128)(2,1)}, u32[]{:S(2)}) copy-start(bf16[3,512,256]{2,1,0:T(8,128)(2,1)} %get-tuple-element.898.low) | copy-start | bytes 2359300 | tf_op jit(solution)/shard_map/while
  110.5 46.5 %collective-permute-start.27 = (f32[3,16,32,128]{3,2,1,0:T(8,128)}, f32[3,16,32,128]{3,2,1,0:T(8,128)}, u32[]{:S(2)}, u32[]{:S(2)}) collective-permute-start(f32[3,16,32,128]{3,2,1,0:T(8,128)} %get-tuple-element.326), channel_id=1, source_target_pairs={{0,16},{8,24},{16,0},{24,8},{1,17},{9,25},{17,1},{25,9},{2,18},{10... | collective-permute-start | bytes 2359304 | tf_op jit(solution)/shard_map/ppermute | solution.py:322
  112.2 44.9 %collective-permute-start.28 = (f32[3,16,32,128]{3,2,1,0:T(8,128)}, f32[3,16,32,128]{3,2,1,0:T(8,128)}, u32[]{:S(2)}, u32[]{:S(2)}) collective-permute-start(f32[3,16,32,128]{3,2,1,0:T(8,128)} %get-tuple-element.327), channel_id=1, source_target_pairs={{0,16},{8,24},{16,0},{24,8},{1,17},{9,25},{17,1},{25,9},{2,18},{10... | collective-permute-start | bytes 2359304 | tf_op jit(solution)/shard_map/ppermute | solution.py:322
  112.6 2.5 %collective-permute-start.19 = (f32[3,16,32,128]{3,2,1,0:T(8,128)}, f32[3,16,32,128]{3,2,1,0:T(8,128)S(1)}, u32[]{:S(2)}, u32[]{:S(2)}) collective-permute-start(f32[3,16,32,128]{3,2,1,0:T(8,128)} %get-tuple-element.919.far), channel_id=1, source_target_pairs={{0,8},{8,0},{16,24},{24,16},{1,9},{9,1},{17,25},{25,17},{2,10},{10... | collective-permute-start | bytes 2359304 | tf_op jit(solution)/shard_map/while/body/ppermute | solution.py:325
  112.7 14.5 %collective-permute-start.15 = (f32[3,16,32,128]{3,2,1,0:T(8,128)}, f32[3,16,32,128]{3,2,1,0:T(8,128)S(1)}, u32[]{:S(2)}, u32[]{:S(2)}) collective-permute-start(f32[3,16,32,128]{3,2,1,0:T(8,128)} %get-tuple-element.918.far), channel_id=1, source_target_pairs={{0,8},{8,0},{16,24},{24,16},{1,9},{9,1},{17,25},{25,17},{2,10},{10... | collective-permute-start | bytes 2359304 | tf_op jit(solution)/shard_map/while/body/ppermute | solution.py:325
  115.1 11.5 %copy-start.14 = (f32[2048,128]{1,0:T(8,128)S(1)}, f32[2048,128]{1,0:T(8,128)}, u32[]{:S(2)}) copy-start(f32[2048,128]{1,0:T(8,128)} %get-tuple-element.941.refs_3_) | copy-start | bytes 3145732 | tf_op jit(solution)/shard_map/while
  115.1 11.5 %copy-start.17 = (f32[2056,128]{1,0:T(8,128)S(1)}, f32[2056,128]{1,0:T(8,128)}, u32[]{:S(2)}) copy-start(f32[2056,128]{1,0:T(8,128)} %get-tuple-element.942.refs_4_) | copy-start | bytes 3158020 | tf_op jit(solution)/shard_map/while
  119.0 4.9 %collective-permute-start.20 = (f32[3,32,256]{2,1,0:T(8,128)S(1)}, f32[3,32,256]{2,1,0:T(8,128)S(1)}, u32[]{:S(2)}, u32[]{:S(2)}) collective-permute-start(f32[3,32,256]{2,1,0:T(8,128)S(1)} %get-tuple-element.775), channel_id=1, source_target_pairs={{1,0},{2,1},{3,2},{4,3},{5,4},{6,5},{7,6},{0,7},{9,8},{10,9},{11,1... | collective-permute-start | bytes 294920 | tf_op jit(solution)/shard_map/while/body/ppermute | solution.py:341
  119.1 7.6 %collective-permute-start.21 = (f32[3,32,256]{2,1,0:T(8,128)S(1)}, f32[3,32,256]{2,1,0:T(8,128)S(1)}, u32[]{:S(2)}, u32[]{:S(2)}) collective-permute-start(f32[3,32,256]{2,1,0:T(8,128)S(1)} %get-tuple-element.776), channel_id=1, source_target_pairs={{0,1},{1,2},{2,3},{3,4},{4,5},{5,6},{6,7},{7,0},{8,9},{9,10},{10,1... | collective-permute-start | bytes 294920 | tf_op jit(solution)/shard_map/while/body/ppermute | solution.py:341
  127.0 13.4 %collective-permute-start.22 = (f32[3,16,32,256]{3,2,1,0:T(8,128)S(1)}, f32[3,16,32,256]{3,2,1,0:T(8,128)}, u32[]{:S(2)}, u32[]{:S(2)}) collective-permute-start(f32[3,16,32,256]{3,2,1,0:T(8,128)S(1)} %second_stencil_3.1.own), channel_id=1, source_target_pairs={{0,8},{8,0},{16,24},{24,16},{1,9},{9,1},{17,25},{25,17},{2,10},{10... | collective-permute-start | bytes 4718600 | tf_op jit(solution)/shard_map/while/body/ppermute | solution.py:325
  132.3 4.7 %collective-permute-start.16 = (f32[3,32,256]{2,1,0:T(8,128)S(1)}, f32[3,32,256]{2,1,0:T(8,128)S(1)}, u32[]{:S(2)}, u32[]{:S(2)}) collective-permute-start(f32[3,32,256]{2,1,0:T(8,128)S(1)} %get-tuple-element.771), channel_id=1, source_target_pairs={{1,0},{2,1},{3,2},{4,3},{5,4},{6,5},{7,6},{0,7},{9,8},{10,9},{11,1... | collective-permute-start | bytes 294920 | tf_op jit(solution)/shard_map/while/body/ppermute | solution.py:341
  132.6 7.3 %collective-permute-start.17 = (f32[3,32,256]{2,1,0:T(8,128)S(1)}, f32[3,32,256]{2,1,0:T(8,128)S(1)}, u32[]{:S(2)}, u32[]{:S(2)}) collective-permute-start(f32[3,32,256]{2,1,0:T(8,128)S(1)} %get-tuple-element.772), channel_id=1, source_target_pairs={{0,1},{1,2},{2,3},{3,4},{4,5},{5,6},{6,7},{7,0},{8,9},{9,10},{10,1... | collective-permute-start | bytes 294920 | tf_op jit(solution)/shard_map/while/body/ppermute | solution.py:341
  140.3 4.8 %collective-permute-start.18 = (f32[3,16,32,256]{3,2,1,0:T(8,128)S(1)}, f32[3,16,32,256]{3,2,1,0:T(8,128)}, u32[]{:S(2)}, u32[]{:S(2)}) collective-permute-start(f32[3,16,32,256]{3,2,1,0:T(8,128)S(1)} %second_stencil_2.1.own), channel_id=1, source_target_pairs={{0,8},{8,0},{16,24},{24,16},{1,9},{9,1},{17,25},{25,17},{2,10},{10... | collective-permute-start | bytes 4718600 | tf_op jit(solution)/shard_map/while/body/ppermute | solution.py:325
  140.4 4.7 %copy-start.4 = (bf16[3,512,256]{2,1,0:T(8,128)(2,1)S(1)}, bf16[3,512,256]{2,1,0:T(8,128)(2,1)}, u32[]{:S(2)}) copy-start(bf16[3,512,256]{2,1,0:T(8,128)(2,1)} %get-tuple-element.939.high) | copy-start | bytes 2359300 | tf_op jit(solution)/shard_map/while
  140.4 4.7 %copy-start.8 = (bf16[3,512,256]{2,1,0:T(8,128)(2,1)S(1)}, bf16[3,512,256]{2,1,0:T(8,128)(2,1)}, u32[]{:S(2)}) copy-start(bf16[3,512,256]{2,1,0:T(8,128)(2,1)} %get-tuple-element.940.low) | copy-start | bytes 2359300 | tf_op jit(solution)/shard_map/while
  149.4 20.6 %collective-permute-start.31 = (f32[3,16,32,128]{3,2,1,0:T(8,128)}, f32[3,16,32,128]{3,2,1,0:T(8,128)S(1)}, u32[]{:S(2)}, u32[]{:S(2)}) collective-permute-start(f32[3,16,32,128]{3,2,1,0:T(8,128)} %get-tuple-element.335), channel_id=1, source_target_pairs={{0,16},{8,24},{16,0},{24,8},{1,17},{9,25},{17,1},{25,9},{2,18},{10... | collective-permute-start | bytes 2359304 | tf_op jit(solution)/shard_map/ppermute | solution.py:322
  151.0 35.4 %collective-permute-start.32 = (f32[3,16,32,128]{3,2,1,0:T(8,128)}, f32[3,16,32,128]{3,2,1,0:T(8,128)S(1)}, u32[]{:S(2)}, u32[]{:S(2)}) collective-permute-start(f32[3,16,32,128]{3,2,1,0:T(8,128)} %get-tuple-element.336), channel_id=1, source_target_pairs={{0,16},{8,24},{16,0},{24,8},{1,17},{9,25},{17,1},{25,9},{2,18},{10... | collective-permute-start | bytes 2359304 | tf_op jit(solution)/shard_map/ppermute | solution.py:322
  (5 other events, 7.4 us)

commit v5 on v3

--- a/solution.py
+++ b/solution.py
@@ -6,7 +6,9 @@
 from jax.sharding import PartitionSpec as P
 
 SECTIONS = 2
-CHUNKS = 4
+GROUPS = 2
+PARTS = 2
+RATE_ROWS = 8
 PIECES = 4
 
 diffusion_coeff = 0.2
@@ -53,32 +55,44 @@
     return dot(high, h_high) + (dot(high, h_low) + dot(low, h_high))
 
 
-def state_kernel(where, state, rate, out, *, modes, nz):
+def state_kernel(where, state, *refs, modes, nz):
+    out = refs[-1]
     width = state.shape[1]
+    rows = nz * width
     for z in range(nz):
         out[z * width : (z + 1) * width, :] = state[pl.ds(z, modes, stride=nz), :].T
-    if out.shape[0] > nz * width:
-        out[nz * width :, :] = jnp.broadcast_to(rate[...], (out.shape[0] - nz * width, modes))
-
-
-def turn_state(where, state, rate, foreign, extra):
+    if len(refs) > 1:
+        rate, helm = refs[:2]
+        out[rows : rows + RATE_ROWS, :] = jnp.broadcast_to(rate[...], (RATE_ROWS, modes))
+        out[rows + RATE_ROWS :, :] = helm[...].reshape(-1, modes)
+
+
+def turn_state(where, state, foreign, rate=None, helm=None):
     modes, nz, nphi = state.shape
     half = nphi // 2
     side = (lambda i, w: (0, 1 - (w[0] >> 1))) if foreign else (lambda i, w: (0, w[0] >> 1))
-    rows = nz * half + extra
+    rows, more, more_specs = nz * half, (), []
+    if helm is not None:
+        comps = helm.shape[0]
+        rows += RATE_ROWS + comps * modes
+        more = (rate, helm)
+        more_specs = [
+            pl.BlockSpec((1, modes), lambda i, w: (0, 0)),
+            pl.BlockSpec((comps, modes, modes), lambda i, w: (0, w[1], 0)),
+        ]
     return pl.pallas_call(
         lambda *refs: state_kernel(*refs, modes=modes, nz=nz),
         out_shape=shape((rows, modes)),
         grid_spec=pltpu.PrefetchScalarGridSpec(
             num_scalar_prefetch=1,
             grid=(1,),
-            in_specs=[pl.BlockSpec((modes * nz, half), side), pl.BlockSpec((1, modes), lambda i, w: (0, 0))],
+            in_specs=[pl.BlockSpec((modes * nz, half), side)] + more_specs,
             out_specs=pl.BlockSpec((rows, modes), lambda i, w: (0, 0)),
         ),
         compiler_params=params(16),
         cost_estimate=cost(rows * modes, 8 * rows * modes),
         name="turn_state",
-    )(where, state.reshape(modes * nz, nphi), rate)
+    )(where, state.reshape(modes * nz, nphi), *more)
 
 
 def edge_kernel(where, cot, leading, last, *, modes, nz):
@@ -164,17 +178,29 @@
     )(where, cot.reshape(modes * comps * nz, nphi), state_turned, after, before, rate)
 
 
-def helm_kernel(where, own, far, high, low):
-    for g, part in enumerate((own[...], far[0])):
-        h, l = split(part)
-        cols = slice(g * part.shape[2], (g + 1) * part.shape[2])
-        high[:, :, cols] = h
-        low[:, :, cols] = l
+def helm_kernel(where, own, *refs):
+    far, (high, low) = refs[:-2], refs[-2:]
+    rows, modes = own.shape[1:]
+    k = pl.program_id(0)
+    wanted = block_of(k, where) ^ where[1]
+    h, l = split(own[...])
+    high[:, :, :modes] = h
+    low[:, :, :modes] = l
+    for d, ref in enumerate(far):
+
+        @pl.when(wanted == d)
+        def _(ref=ref):
+            h, l = split(ref[...])
+            high[:, :, modes:] = h
+            low[:, :, modes:] = l
+
+
+def block_of(k, where):
+    return where[0] ^ (((k & 1) << 1) | (k >> 1))
 
 
 def split_helm(where, own, far):
     comps, rows, modes = own.shape
-    block = lambda k, w: w[0] ^ (((k & 1) << 1) | (k >> 1))
     out = (comps, rows, 2 * modes)
     return pl.pallas_call(
         helm_kernel,
@@ -182,16 +208,14 @@
         grid_spec=pltpu.PrefetchScalarGridSpec(
             num_scalar_prefetch=1,
             grid=(rows // modes,),
-            in_specs=[
-                pl.BlockSpec((comps, modes, modes), lambda k, w: (0, block(k, w), 0)),
-                pl.BlockSpec((1, comps, modes, modes), lambda k, w: (block(k, w) ^ w[1], 0, 0, 0)),
-            ],
+            in_specs=[pl.BlockSpec((comps, modes, modes), lambda k, w: (0, block_of(k, w), 0))]
+            + [pl.BlockSpec((comps, modes, modes), lambda k, w: (0, 0, 0))] * len(far),
             out_specs=[pl.BlockSpec((comps, modes, 2 * modes), lambda k, w: (0, k, 0))] * 2,
         ),
         compiler_params=params(16),
         cost_estimate=cost(4 * comps * rows * modes, 16 * comps * rows * modes),
         name="split_helm",
-    )(where, own, far)
+    )(where, own, *far)
 
 
 def map1_kernel(own, far, own_peer, far_peer, high, low, out, first, last):
@@ -206,9 +230,10 @@
 
 def map1(own, far, own_peer, far_peer, high, low, k):
     comps, nz, width, modes = far.shape
+    width //= PARTS
     rows, cols = high.shape[1:]
     here = pl.BlockSpec((1, nz, width, modes), lambda c: (c, 0, k, 0))
-    chunk = pl.BlockSpec((1, nz, width, modes), lambda c: (c, 0, 0, 0))
+    chunk = pl.BlockSpec((1, nz, width, modes), lambda c: (c, 0, k % PARTS, 0))
     helm = pl.BlockSpec((1, rows, cols), lambda c: (c, 0, 0))
     layer = pl.BlockSpec((1, width, cols), lambda c: (c, 0, 0))
     return pl.pallas_call(
@@ -251,7 +276,8 @@
     )(cur, after, before, state_own, state_far, rate)
 
 
-def map2_kernel(own, peer, high, low, out_own, out_far):
+def map2_kernel(own, peer, high, low, *refs):
+    out_own, out_far = refs[-2:]
     _, nz, width, cols = own.shape
     parts = [ref[0].reshape(nz * width, cols) for ref in (own, peer)]
     res = product(parts, high[0], low[0]).reshape(nz, width, cols)
@@ -259,22 +285,23 @@
     out_far[0] = res[:, :, cols // 2 :]
 
 
-def map2(own, peer, high, low, k):
+def map2(own, peer, high, low, k, base):
     comps, nz, width, cols = own.shape
     rows = high.shape[1]
     chunk = pl.BlockSpec((1, nz, width, cols), lambda c: (c, 0, 0, 0))
     helm = pl.BlockSpec((1, rows, cols), lambda c: (c, 0, 0))
-    out = (comps, nz, width, cols // 2)
+    out = (comps, nz, width * PARTS, cols // 2)
     return pl.pallas_call(
         map2_kernel,
         out_shape=[shape(out)] * 2,
         grid=(comps,),
-        in_specs=[chunk, chunk, helm, helm],
-        out_specs=[pl.BlockSpec((1, nz, width, cols // 2), lambda c: (c, 0, 0, 0))] * 2,
+        in_specs=[chunk, chunk, helm, helm] + [pl.BlockSpec(memory_space=pl.ANY)] * len(base),
+        out_specs=[pl.BlockSpec((1, nz, width, cols // 2), lambda c: (c, 0, k % PARTS, 0))] * 2,
+        input_output_aliases={4 + i: i for i in range(len(base))},
         compiler_params=params(24),
         cost_estimate=cost(6 * comps * nz * width * rows * cols, 4 * comps * (nz * width * (rows + cols) + rows * cols)),
         name=f"map2_{k}",
-    )(own, peer, high, low)
+    )(own, peer, high, low, *base)
 
 
 def last_kernel(where, *refs, nz, chunks):
@@ -332,8 +359,7 @@
 
     once = 1 + (where[0] >> 8)
 
-    piece = across(lax.dynamic_slice_in_dim(helm_inverse, lot * modes, modes, axis=1))
-    state_foreign = turn_state(where, state_axial, rate, True, 8)
+    state_foreign = turn_state(where, state_axial, True, rate, helm_inverse)
     state_far = across(state_foreign)
 
     def halos(leading, last):
@@ -342,25 +368,25 @@
     def foreign_half(step, sent):
         here = where + (step >> 8)
         edges = halos(*edge_layers(here, cotangent, True))
-        return tuple(first_stencil(here, cotangent, state_foreign, *edges, rate, True, CHUNKS))
-
-    chunk = (comps, nz, half // CHUNKS, modes)
-    sent = lax.fori_loop(0, once, foreign_half, tuple(blanks(*[(chunk, F32)] * CHUNKS)))
-    far = [across(s) for k, s in enumerate(sent)]
+        return tuple(first_stencil(here, cotangent, state_foreign, *edges, rate, True, GROUPS))
+
+    chunk = (comps, nz, half // GROUPS, modes)
+    sent = lax.fori_loop(0, once, foreign_half, tuple(blanks(*[(chunk, F32)] * GROUPS)))
+    far = [across(tied(s, state_far) if k else s) for k, s in enumerate(sent)]
 
     def own_half(step, carry):
         here = where + (step >> 8)
         edges = halos(*edge_layers(here, entry, False))
-        helm_far, mask = tied(piece, here)[None], 1
-        while mask < PIECES:
-            helm_far = jnp.concatenate([helm_far, hop(helm_far, mask)])
-            mask *= 2
-        state_own = turn_state(here, state_axial, rate, False, 0)
+        blocks = [tied(state_far, here)[nz * half + RATE_ROWS :].reshape(comps, modes, modes)]
+        blocks += [hop(blocks[0], 1), hop(blocks[0], 2)]
+        blocks += [hop(blocks[2], 1)]
+        edges = tuple(tied(e, *blocks[1:]) for e in edges)
+        state_own = turn_state(here, state_axial, False)
         (own,) = first_stencil(here, entry, state_own, *edges, rate, False, 1)
         own_peer = beside(own)
-        return (state_own, own, own_peer, *split_helm(here, helm_inverse, helm_far))
-
-    entry = tied(cotangent, sent[0])
+        return (state_own, own, own_peer, *split_helm(here, helm_inverse, blocks))
+
+    entry = tied(cotangent, sent[0], state_far)
     columns = (comps, nz, half, modes)
     helm = (comps, peers * modes, 2 * modes)
     state_own, own, own_peer, high, low = lax.fori_loop(
@@ -368,17 +394,26 @@
     )
 
     kept, back = [], []
-    for k in range(CHUNKS):
-
-        def chain(_, pair, k=k):
-            here = pair[0]
-            cur, leading, last = map1(own, here, own_peer, beside(here), high, low, k)
-            nxt = second_stencil(cur, *halos(leading, last), state_own, state_far, rate, k, half)
-            mine, theirs = map2(nxt, beside(nxt), high, low, k)
-            return theirs, mine
-
-        spare = tied(sent[k], kept[-1], back[0]) if k > 2 else tied(sent[k], kept[-1]) if k else sent[k]
-        theirs, mine = lax.fori_loop(0, once, chain, (far[k], spare))
+    for g in range(GROUPS):
+        group = range(g * PARTS, (g + 1) * PARTS)
+
+        def chains(_, carry, group=group):
+            here = carry[0]
+            there = beside(here)
+            moved = []
+            for k in group:
+                cur, leading, last = map1(own, here, own_peer, there, high, low, k)
+                moved.append((cur, *halos(leading, last)))
+            moved = lax.optimization_barrier(tuple(moved))
+            nxt = [second_stencil(*m, state_own, state_far, rate, k, half) for k, m in zip(group, moved)]
+            there = [beside(n) for n in nxt]
+            mine_theirs = ()
+            for k, n, t in zip(group, nxt, there):
+                mine_theirs = tuple(map2(n, t, high, low, k, mine_theirs))
+            return mine_theirs[::-1]
+
+        spare = tied(sent[g], kept[-1]) if kept else sent[g]
+        theirs, mine = lax.fori_loop(0, once, chains, (far[g], spare))
         kept.append(mine)
         back.append(across(theirs))
     out = write_half(where, kept, nphi, False)

time: 205 us -> 193 us (0.941)
  waiting for transfers between devices: 102 us -> 74.6 us
  starting transfers between devices: 27.4 us -> 40.2 us
  local copies, waits for them, and re-layouts: 0.99 us -> 3.35 us
  Pallas kernels: 71.8 us -> 74 us
    ppermute x2 -> x3, waiting for transfers between devices: 18.3 us -> 2.51 us  [hop(): return lax.ppermute(array, 'col', [(i, i ^ mask) for i in range(cols)])]
    ppermute x10 -> x5, waiting for transfers between devices: 22.1 us -> 35.8 us  [across(): return lax.ppermute(array, 'rad', [(i, i ^ 2) for i in range(peers)])]
    ppermute x12, waiting for transfers between devices: 38.1 us -> 24.6 us  [halos(): return (lax.ppermute(leading, 'col', down), lax.ppermute(last, 'col', up))]
    ppermute x12, starting transfers between devices: 15.5 us -> 28.1 us  [halos(): return (lax.ppermute(leading, 'col', down), lax.ppermute(last, 'col', up))]
    ppermute x9 -> x7, waiting for transfers between devices: 23.4 us -> 11.7 us  [beside(): return lax.ppermute(array, 'rad', [(i, i ^ 1) for i in range(peers)])]
    ppermute x10 -> x5, starting transfers between devices: 11.2 us -> 7.15 us  [across(): return lax.ppermute(array, 'rad', [(i, i ^ 2) for i in range(peers)])]
    ppermute x2 -> x3, starting transfers between devices: 0.07 us -> 3.73 us  [hop(): return lax.ppermute(array, 'col', [(i, i ^ mask) for i in range(cols)])]
    while x16 -> x28, local copies, waits for them, and re-layouts: 0.03 us -> 2.4 us
  transfers between devices with their start and end apart: 33 -> 27, of which waited for: 24 -> 15; matrix products, arithmetic and copies ran while one was open for 1% -> 0% of each run, Pallas kernels for 32% -> 34%
where the time goes in v5:
time: 193 us; the launch traced here: 192 us
  waiting for transfers between devices  74.6 us (39%)
  Pallas kernels  74 us (38%)
  starting transfers between devices  40.2 us (21%)
  local copies, waits for them, and re-layouts  3.35 us (2%)
    ppermute x5, waiting for transfers between devices, across(): return lax.ppermute(array, 'rad', [(i, i ^ 2) for i in range(peers)])  35.8 us
    ppermute x12, starting transfers between devices, halos(): return (lax.ppermute(leading, 'col', down), lax.ppermute(last, 'col', up))  28.1 us
    ppermute x12, waiting for transfers between devices, halos(): return (lax.ppermute(leading, 'col', down), lax.ppermute(last, 'col', up))  24.6 us
    pallas_call x4, Pallas kernels, map2(): pl.pallas_call(map2_kernel, out_shape=[shape(out)] * 2, grid=(comps,), in...  17 us
    pallas_call x4, Pallas kernels, map1(): pl.pallas_call(map1_kernel, out_shape=[shape((comps, nz, width, cols)), s...  14.7 us
    ppermute x7, waiting for transfers between devices, beside(): return lax.ppermute(array, 'rad', [(i, i ^ 1) for i in range(peers)])  11.7 us
    pallas_call x2, Pallas kernels, write_half(): pl.pallas_call(lambda *refs: last_kernel(*refs, nz=nz, chunks=chunks), ou...  10.9 us
    pallas_call x2, Pallas kernels, first_stencil(): pl.pallas_call(lambda *refs: first_kernel(*refs, modes=modes, nz=nz, chun...  10.7 us
  transfers between devices with their start and end apart: 27, of which 15 were waited for; matrix products, arithmetic and copies ran while one was open for 0% of the time, Pallas kernels for 34%

profile of v5, /device:TPU:0, one launch (start us, length us, event | category | flops | bytes accessed | tf_op | source)
XLA Modules:
  0.0 192.4 jit_solution(17508336334769571977)
XLA Ops:
  0.1 3.3 %turn_state.2 = f32[2440,128]{1,0:T(8,128)} custom-call(s32[2]{0:T(128)S(1)} %pad_add_fusion.refs_0_, f32[2048,256]{1,0:T(8,128)} %bitcast.24, f32[1,128]{1,0:T(1,128)} %bitcast.26, f32[3,512,128]{2,1,0:T(8,128)} %refs_3_.1), custom_call_target="tpu_custom_call" | custom-call | flops 312320 | bytes 2498560 | tf_op jit(solution)/shard_map/turn_state/pallas_call | solution.py:83
  3.3 2.9 %collective-permute-start.23 = (f32[2440,128]{1,0:T(8,128)}, f32[2440,128]{1,0:T(8,128)}, u32[]{:S(2)}, u32[]{:S(2)}) collective-permute-start(f32[2440,128]{1,0:T(8,128)} %turn_state.2), channel_id=1, source_target_pairs={{0,16},{8,24},{16,0},{24,8},{1,17},{9,25},{17,1},{25,9},{2,18},{10... | collective-permute-start | bytes 3747848 | tf_op jit(solution)/shard_map/ppermute | solution.py:348
  6.3 22.4 %while.54 = (s32[]{:T(128)}, f32[3,16,64,128]{3,2,1,0:T(8,128)}, f32[3,16,64,128]{3,2,1,0:T(8,128)}, s32[]{:T(128)}, s32[2]{0:T(128)S(1)}, /*index=5*/f32[128,3,...) while((s32[]{:T(128)}, f32[3,16,64,128]{3,2,1,0:T(8,128)}, ...), condition=%wide.region_1.0_spmd, body=%wide.region_0.0_spmd.sunk | while | flops 9535493 | bytes 11010261 | solution.py:374
  6.3 2.6 %edge_layers.2 = (f32[384,128]{1,0:T(8,128)S(1)}, f32[384,128]{1,0:T(8,128)S(1)}) custom-call(s32[2]{0:T(128)S(1)} %broadcast_add_fusion.4.refs_0_, f32[6144,256]{1,0:T(8,128)} %bitcast.20), custom_call_target="tpu_custom_call" | custom-call | flops 98304 | bytes 3145728 | tf_op jit(solution)/shard_map/while/body/edge_layers/pallas_call | solution.py:109
  8.9 4.6 %collective-permute-start = (f32[384,128]{1,0:T(8,128)S(1)}, f32[384,128]{1,0:T(8,128)S(1)}, u32[]{:S(2)}, u32[]{:S(2)}) collective-permute-start(f32[384,128]{1,0:T(8,128)S(1)} %get-tuple-element.653), channel_id=1, source_target_pairs={{1,0},{2,1},{3,2},{4,3},{5,4},{6,5},{7,6},{0,7},{9,8},{10,9},{11,1... | collective-permute-start | bytes 589832 | tf_op jit(solution)/shard_map/while/body/ppermute | solution.py:366
  13.6 3.9 %collective-permute-done.refs_3_ = f32[384,128]{1,0:T(8,128)S(1)} collective-permute-done((f32[384,128]{1,0:T(8,128)S(1)}, f32[384,128]{1,0:T(8,128)S(1)}, u32[]{:S(2)}, u32[]{:S(2)}) %collective-permute-start) | collective-permute-done | bytes 196640 | tf_op jit(solution)/shard_map/while/body/ppermute | solution.py:366
  17.4 4.9 %collective-permute-done.1.refs_4_ = f32[384,128]{1,0:T(8,128)S(1)} collective-permute-done((f32[384,128]{1,0:T(8,128)S(1)}, f32[384,128]{1,0:T(8,128)S(1)}, u32[]{:S(2)}, u32[]{:S(2)}) %collective-permute-start.1) | collective-permute-done | bytes 196640 | tf_op jit(solution)/shard_map/while/body/ppermute | solution.py:366
  22.3 6.3 %first_stencil.2 = (f32[3,16,64,128]{3,2,1,0:T(8,128)}, f32[3,16,64,128]{3,2,1,0:T(8,128)}) custom-call(s32[2]{0:T(128)S(1)} %broadcast_add_fusion.4.refs_0_, f32[6144,256]{1,0:T(8,128)} %bitcast.21, f32[2440,128]{1,0:T(8,128)} %get-tuple-element.750.refs_2_, f32[384,128]{1,0:T(8,128)S(1)} %collective-permute-done.refs_3_, ...), custom_call_target="tpu_custom_call" | custom-call | flops 9437184 | bytes 6291456 | tf_op jit(solution)/shard_map/while/body/first_stencil/pallas_call | solution.py:159
  29.2 5.7 %collective-permute-done.23 = f32[2440,128]{1,0:T(8,128)} collective-permute-done((f32[2440,128]{1,0:T(8,128)}, f32[2440,128]{1,0:T(8,128)}, u32[]{:S(2)}, u32[]{:S(2)}) %collective-permute-start.23) | collective-permute-done | bytes 1249312 | tf_op jit(solution)/shard_map/ppermute | solution.py:348
  34.9 31.9 %while.55 = (s32[]{:T(128)}, f32[2048,128]{1,0:T(8,128)}, f32[3,16,128,128]{3,2,1,0:T(8,128)}, f32[3,16,128,128]{3,2,1,0:T(8,128)}, bf16[3,512,256]{2,1,0:T(8,12...) while((s32[]{:T(128)}, f32[2048,128]{1,0:T(8,128)}, ...), condition=%wide.region_3.0_spmd, body=%wide.region_2.0_spmd.sunk | while | flops 10584069 | bytes 60948948 | solution.py:392
  35.8 2.2 %collective-permute-start.4 = (f32[3,128,128]{2,1,0:T(8,128)S(1)}, f32[3,128,128]{2,1,0:T(8,128)S(1)}, u32[]{:S(2)}, u32[]{:S(2)}) collective-permute-start(f32[3,128,128]{2,1,0:T(8,128)S(1)} %bitcast.17), channel_id=1, source_target_pairs={{0,2},{1,3},{2,0},{3,1},{4,6},{5,7},{6,4},{7,5},{8,10},{9,11},{10,... | collective-permute-start | bytes 589832 | tf_op jit(solution)/shard_map/while/body/ppermute | solution.py:354
  38.0 1.5 collective-permute-start.3
  39.6 2.8 %edge_layers.3 = (f32[384,128]{1,0:T(8,128)S(1)}, f32[384,128]{1,0:T(8,128)S(1)}) custom-call(s32[2]{0:T(128)S(1)} %broadcast_add_fusion.5.refs_0_.where, f32[6144,256]{1,0:T(8,128)} %bitcast.22), custom_call_target="tpu_custom_call" | custom-call | flops 98304 | bytes 3145728 | tf_op jit(solution)/shard_map/while/body/edge_layers/pallas_call | solution.py:109
  42.4 2.5 %collective-permute-start.2 = (f32[384,128]{1,0:T(8,128)S(1)}, f32[384,128]{1,0:T(8,128)S(1)}, u32[]{:S(2)}, u32[]{:S(2)}) collective-permute-start(f32[384,128]{1,0:T(8,128)S(1)} %get-tuple-element.665), channel_id=1, source_target_pairs={{1,0},{2,1},{3,2},{4,3},{5,4},{6,5},{7,6},{0,7},{9,8},{10,9},{11,1... | collective-permute-start | bytes 589832 | tf_op jit(solution)/shard_map/while/body/ppermute | solution.py:366
  44.8 2.0 %collective-permute-start.6 = (f32[384,128]{1,0:T(8,128)S(1)}, f32[384,128]{1,0:T(8,128)S(1)}, u32[]{:S(2)}, u32[]{:S(2)}) collective-permute-start(f32[384,128]{1,0:T(8,128)S(1)} %get-tuple-element.668), channel_id=1, source_target_pairs={{0,1},{1,2},{2,3},{3,4},{4,5},{5,6},{6,7},{7,0},{8,9},{9,10},{10,1... | collective-permute-start | bytes 589832 | tf_op jit(solution)/shard_map/while/body/ppermute | solution.py:366
  48.3 5.9 %collective-permute-done.2.refs_3_ = f32[384,128]{1,0:T(8,128)S(1)} collective-permute-done((f32[384,128]{1,0:T(8,128)S(1)}, f32[384,128]{1,0:T(8,128)S(1)}, u32[]{:S(2)}, u32[]{:S(2)}) %collective-permute-start.2) | collective-permute-done | bytes 196640 | tf_op jit(solution)/shard_map/while/body/ppermute | solution.py:366
  54.2 2.1 %collective-permute-done.5.refs_3_ = f32[3,128,128]{2,1,0:T(8,128)S(1)} collective-permute-done((f32[3,128,128]{2,1,0:T(8,128)S(1)}, f32[3,128,128]{2,1,0:T(8,128)S(1)}, u32[]{:S(2)}, u32[]{:S(2)}) %collective-permute-start.5) | collective-permute-done | bytes 196640 | tf_op jit(solution)/shard_map/while/body/ppermute | solution.py:354
  56.4 4.4 %first_stencil.3 = f32[3,16,128,128]{3,2,1,0:T(8,128)} custom-call(s32[2]{0:T(128)S(1)} %broadcast_add_fusion.5.refs_0_.where, f32[6144,256]{1,0:T(8,128)S(1)} %bitcast.23, f32[2048,128]{1,0:T(8,128)S(1)} %turn_state.3.refs_2_, f32[384,128]{1,0:T(8,128)S(1)} %collective-permute-done.2.refs_3_, f32[384,128]{1,0:T(8,128)S(1)} %collective-permute-done.6.refs_4_, ...), custom_call_target="tpu_custom_call" | custom-call | flops 9437184 | bytes 6291456 | tf_op jit(solution)/shard_map/while/body/first_stencil/pallas_call | solution.py:159
  60.7 4.1 %split_helm.1 = (bf16[3,512,256]{2,1,0:T(8,128)(2,1)}, bf16[3,512,256]{2,1,0:T(8,128)(2,1)}) custom-call(s32[2]{0:T(128)S(1)} %broadcast_add_fusion.5.refs_0_.where, f32[3,512,128]{2,1,0:T(8,128)} %get-tuple-element.796.own, f32[3,128,128]{2,1,0:T(8,128)S(1)} %bitcast.19, f32[3,128,128]{2,1,0:T(8,128)S(1)} %collective-permute-done.3.refs_1_, ...), custom_call_target="tpu_custom_call" | custom-call | flops 786432 | bytes 3145728 | tf_op jit(solution)/shard_map/while/body/split_helm/pallas_call | solution.py:205
  64.9 1.9 collective-permute-done.7
  66.7 1.6 collective-permute-start.25
  68.4 38.0 %while.56 = (s32[]{:T(128)}, f32[3,16,64,128]{3,2,1,0:T(8,128)}, f32[3,16,64,128]{3,2,1,0:T(8,128)}, s32[]{:T(128)}, f32[3,16,128,128]{3,2,1,0:T(8,128)}, /*inde...) while((s32[]{:T(128)}, f32[3,16,64,128]{3,2,1,0:T(8,128)}, ...), condition=%wide.region_5.0_spmd, body=%wide.region_4.0_spmd.sunk | while | flops 4841275392 | bytes 74973744 | solution.py:416
  68.4 3.6 %collective-permute-done.8.far_peer = f32[3,16,64,128]{3,2,1,0:T(8,128)S(1)} collective-permute-done((f32[3,16,64,128]{3,2,1,0:T(8,128)}, f32[3,16,64,128]{3,2,1,0:T(8,128)S(1)}, u32[]{:S(2)}, u32[]{:S(2)}) %collective-permute-start.8) | collective-permute-done | bytes 1572896 | tf_op jit(solution)/shard_map/while/body/ppermute | solution.py:351
  72.0 3.9 %map1_0.1 = (f32[3,16,32,256]{3,2,1,0:T(8,128)S(1)}, f32[3,32,256]{2,1,0:T(8,128)S(1)}, f32[3,32,256]{2,1,0:T(8,128)S(1)}) custom-call(f32[3,16,128,128]{3,2,1,0:T(8,128)} %get-tuple-element.827.own, f32[3,16,64,128]{3,2,1,0:T(8,128)} %get-tuple-element.812.far, f32[3,16,128,128]{3,2,1,0:T(8,128)} %get-tuple-element.828.own_peer, ...), custom_call_target="tpu_custom_call" | custom-call | flops 1207959552 | bytes 6291456 | tf_op jit(solution)/shard_map/while/body/map1_0/pallas_call | solution.py:239
  75.9 1.6 collective-permute-start.10
  77.5 3.4 %map1_1.1 = (f32[3,16,32,256]{3,2,1,0:T(8,128)S(1)}, f32[3,32,256]{2,1,0:T(8,128)S(1)}, f32[3,32,256]{2,1,0:T(8,128)S(1)}) custom-call(f32[3,16,128,128]{3,2,1,0:T(8,128)} %get-tuple-element.827.own, f32[3,16,64,128]{3,2,1,0:T(8,128)} %get-tuple-element.812.far, f32[3,16,128,128]{3,2,1,0:T(8,128)} %get-tuple-element.828.own_peer, ...), custom_call_target="tpu_custom_call" | custom-call | flops 1207959552 | bytes 6291456 | tf_op jit(solution)/shard_map/while/body/map1_1/pallas_call | solution.py:239
  80.9 3.3 %collective-permute-start.11 = (f32[3,32,256]{2,1,0:T(8,128)S(1)}, f32[3,32,256]{2,1,0:T(8,128)S(1)}, u32[]{:S(2)}, u32[]{:S(2)}) collective-permute-start(f32[3,32,256]{2,1,0:T(8,128)S(1)} %get-tuple-element.686), channel_id=1, source_target_pairs={{1,0},{2,1},{3,2},{4,3},{5,4},{6,5},{7,6},{0,7},{9,8},{10,9},{11,1... | collective-permute-start | bytes 294920 | tf_op jit(solution)/shard_map/while/body/ppermute | solution.py:366
  84.2 4.7 %collective-permute-start.9 = (f32[3,32,256]{2,1,0:T(8,128)S(1)}, f32[3,32,256]{2,1,0:T(8,128)S(1)}, u32[]{:S(2)}, u32[]{:S(2)}) collective-permute-start(f32[3,32,256]{2,1,0:T(8,128)S(1)} %get-tuple-element.683), channel_id=1, source_target_pairs={{1,0},{2,1},{3,2},{4,3},{5,4},{6,5},{7,6},{0,7},{9,8},{10,9},{11,1... | collective-permute-start | bytes 294920 | tf_op jit(solution)/shard_map/while/body/ppermute | solution.py:366
  88.9 2.6 %collective-permute-done.12.refs_2_ = f32[3,32,256]{2,1,0:T(8,128)S(1)} collective-permute-done((f32[3,32,256]{2,1,0:T(8,128)S(1)}, f32[3,32,256]{2,1,0:T(8,128)S(1)}, u32[]{:S(2)}, u32[]{:S(2)}) %collective-permute-start.12) | collective-permute-done | bytes 98336 | tf_op jit(solution)/shard_map/while/body/ppermute | solution.py:366
  91.5 1.7 second_stencil_0.1.own
  93.2 1.7 second_stencil_1.1.own
  96.8 4.4 %map2_0.1 = (f32[3,16,64,128]{3,2,1,0:T(8,128)S(1)}, f32[3,16,64,128]{3,2,1,0:T(8,128)}) custom-call(f32[3,16,32,256]{3,2,1,0:T(8,128)S(1)} %second_stencil_0.1.own, f32[3,16,32,256]{3,2,1,0:T(8,128)} %collective-permute-done.14.peer, bf16[3,512,256]{2,1,0:T(8,128)(2,1)} %get-tuple-element.829.high, bf16[3,512,256]{2,1,0:T(8,128)(2,1)} %get-tuple-element.830.low), custom_call_target="tpu_custom_call" | custom-call | flops 1207959552 | bytes 6291456 | tf_op jit(solution)/shard_map/while/body/map2_0/pallas_call | solution.py:294
  101.2 4.1 %map2_1.1 = (f32[3,16,64,128]{3,2,1,0:T(8,128)S(1)}, f32[3,16,64,128]{3,2,1,0:T(8,128)}) custom-call(f32[3,16,32,256]{3,2,1,0:T(8,128)S(1)} %second_stencil_1.1.own, f32[3,16,32,256]{3,2,1,0:T(8,128)} %collective-permute-done.13.peer, bf16[3,512,256]{2,1,0:T(8,128)(2,1)S(1)} %copy-done.2, ...), custom_call_target="tpu_custom_call", output_to_operand_aliasing={{0}: (4, {}), {1}: (5, {})} | custom-call | flops 1207959552 | bytes 6291456 | tf_op jit(solution)/shard_map/while/body/map2_1/pallas_call | solution.py:294
  107.6 42.8 %while.57 = (s32[]{:T(128)}, f32[3,16,64,128]{3,2,1,0:T(8,128)}, f32[3,16,64,128]{3,2,1,0:T(8,128)}, s32[]{:T(128)}, f32[3,16,128,128]{3,2,1,0:T(8,128)}, /*inde...) while((s32[]{:T(128)}, f32[3,16,64,128]{3,2,1,0:T(8,128)}, ...), condition=%wide.region_7.0_spmd, body=%wide.region_6.0_spmd.sunk | while | flops 4841275392 | bytes 74973744 | solution.py:416
  107.6 3.6 %collective-permute-done.15.far_peer = f32[3,16,64,128]{3,2,1,0:T(8,128)S(1)} collective-permute-done((f32[3,16,64,128]{3,2,1,0:T(8,128)}, f32[3,16,64,128]{3,2,1,0:T(8,128)S(1)}, u32[]{:S(2)}, u32[]{:S(2)}) %collective-permute-start.15) | collective-permute-done | bytes 1572896 | tf_op jit(solution)/shard_map/while/body/ppermute | solution.py:351
  111.2 3.9 %map1_2.1 = (f32[3,16,32,256]{3,2,1,0:T(8,128)S(1)}, f32[3,32,256]{2,1,0:T(8,128)S(1)}, f32[3,32,256]{2,1,0:T(8,128)S(1)}) custom-call(f32[3,16,128,128]{3,2,1,0:T(8,128)} %get-tuple-element.863.own, f32[3,16,64,128]{3,2,1,0:T(8,128)} %get-tuple-element.848.far, f32[3,16,128,128]{3,2,1,0:T(8,128)} %get-tuple-element.864.own_peer, ...), custom_call_target="tpu_custom_call" | custom-call | flops 1207959552 | bytes 6291456 | tf_op jit(solution)/shard_map/while/body/map1_2/pallas_call | solution.py:239
  115.1 4.8 %collective-permute-start.16 = (f32[3,32,256]{2,1,0:T(8,128)S(1)}, f32[3,32,256]{2,1,0:T(8,128)S(1)}, u32[]{:S(2)}, u32[]{:S(2)}) collective-permute-start(f32[3,32,256]{2,1,0:T(8,128)S(1)} %get-tuple-element.709), channel_id=1, source_target_pairs={{1,0},{2,1},{3,2},{4,3},{5,4},{6,5},{7,6},{0,7},{9,8},{10,9},{11,1... | collective-permute-start | bytes 294920 | tf_op jit(solution)/shard_map/while/body/ppermute | solution.py:366
  119.9 3.5 %map1_3.1 = (f32[3,16,32,256]{3,2,1,0:T(8,128)S(1)}, f32[3,32,256]{2,1,0:T(8,128)S(1)}, f32[3,32,256]{2,1,0:T(8,128)S(1)}) custom-call(f32[3,16,128,128]{3,2,1,0:T(8,128)} %get-tuple-element.863.own, f32[3,16,64,128]{3,2,1,0:T(8,128)} %get-tuple-element.848.far, f32[3,16,128,128]{3,2,1,0:T(8,128)} %get-tuple-element.864.own_peer, ...), custom_call_target="tpu_custom_call" | custom-call | flops 1207959552 | bytes 6291456 | tf_op jit(solution)/shard_map/while/body/map1_3/pallas_call | solution.py:239
  123.4 4.7 %collective-permute-start.18 = (f32[3,32,256]{2,1,0:T(8,128)S(1)}, f32[3,32,256]{2,1,0:T(8,128)S(1)}, u32[]{:S(2)}, u32[]{:S(2)}) collective-permute-start(f32[3,32,256]{2,1,0:T(8,128)S(1)} %get-tuple-element.712), channel_id=1, source_target_pairs={{1,0},{2,1},{3,2},{4,3},{5,4},{6,5},{7,6},{0,7},{9,8},{10,9},{11,1... | collective-permute-start | bytes 294920 | tf_op jit(solution)/shard_map/while/body/ppermute | solution.py:366
  128.1 2.2 %collective-permute-done.18.refs_1_ = f32[3,32,256]{2,1,0:T(8,128)S(1)} collective-permute-done((f32[3,32,256]{2,1,0:T(8,128)S(1)}, f32[3,32,256]{2,1,0:T(8,128)S(1)}, u32[]{:S(2)}, u32[]{:S(2)}) %collective-permute-start.18) | collective-permute-done | bytes 98336 | tf_op jit(solution)/shard_map/while/body/ppermute | solution.py:366
  130.3 5.1 %collective-permute-done.19.refs_2_ = f32[3,32,256]{2,1,0:T(8,128)S(1)} collective-permute-done((f32[3,32,256]{2,1,0:T(8,128)S(1)}, f32[3,32,256]{2,1,0:T(8,128)S(1)}, u32[]{:S(2)}, u32[]{:S(2)}) %collective-permute-start.19) | collective-permute-done | bytes 98336 | tf_op jit(solution)/shard_map/while/body/ppermute | solution.py:366
  135.4 1.7 second_stencil_2.1.own
  137.2 1.7 second_stencil_3.1.own
  140.7 4.4 %map2_2.1 = (f32[3,16,64,128]{3,2,1,0:T(8,128)S(1)}, f32[3,16,64,128]{3,2,1,0:T(8,128)}) custom-call(f32[3,16,32,256]{3,2,1,0:T(8,128)S(1)} %second_stencil_2.1.own, f32[3,16,32,256]{3,2,1,0:T(8,128)} %collective-permute-done.21.peer, bf16[3,512,256]{2,1,0:T(8,128)(2,1)} %get-tuple-element.865.high, bf16[3,512,256]{2,1,0:T(8,128)(2,1)} %get-tuple-element.866.low), custom_call_target="tpu_custom_call" | custom-call | flops 1207959552 | bytes 6291456 | tf_op jit(solution)/shard_map/while/body/map2_2/pallas_call | solution.py:294
  145.1 4.1 %map2_3.1 = (f32[3,16,64,128]{3,2,1,0:T(8,128)S(1)}, f32[3,16,64,128]{3,2,1,0:T(8,128)}) custom-call(f32[3,16,32,256]{3,2,1,0:T(8,128)S(1)} %second_stencil_3.1.own, f32[3,16,32,256]{3,2,1,0:T(8,128)} %collective-permute-done.20.peer, bf16[3,512,256]{2,1,0:T(8,128)(2,1)S(1)} %copy-done.4, ...), custom_call_target="tpu_custom_call", output_to_operand_aliasing={{0}: (4, {}), {1}: (5, {})} | custom-call | flops 1207959552 | bytes 6291456 | tf_op jit(solution)/shard_map/while/body/map2_3/pallas_call | solution.py:294
  151.3 5.7 %write_own.1.refs_3_ = f32[128,48,256]{2,1,0:T(8,128)} custom-call(s32[2]{0:T(128)S(1)} %get-tuple-element.918, f32[3,16,64,128]{3,2,1,0:T(8,128)} %get-tuple-element.300.refs_1_, f32[3,16,64,128]{3,2,1,0:T(8,128)} %get-tuple-element.303.refs_2_), custom_call_target="tpu_custom_call" | custom-call | flops 1572864 | bytes 6291456 | tf_op jit(solution)/shard_map/write_own/pallas_call | solution.py:319
  157.0 30.1 %collective-permute-done.26.refs_2_ = f32[3,16,64,128]{3,2,1,0:T(8,128)S(1)} collective-permute-done((f32[3,16,64,128]{3,2,1,0:T(8,128)}, f32[3,16,64,128]{3,2,1,0:T(8,128)S(1)}, u32[]{:S(2)}, u32[]{:S(2)}) %collective-permute-start.26) | collective-permute-done | bytes 1572896 | tf_op jit(solution)/shard_map/ppermute | solution.py:348
  187.1 5.3 %write_foreign.1 = f32[128,48,256]{2,1,0:T(8,128)} custom-call(s32[2]{0:T(128)S(1)} %get-tuple-element.918, f32[3,16,64,128]{3,2,1,0:T(8,128)} %collective-permute-done.24.refs_1_, f32[3,16,64,128]{3,2,1,0:T(8,128)S(1)} %collective-permute-done.26.refs_2_, f32[128,48,256]{2,1,0:T(8,128)} %write_own.1.refs_3_), custom_call_target="tpu_custom_call", output_to_operand_aliasing={{}: (3, {})} | custom-call | flops 1572864 | bytes 6291456 | tf_op jit(solution)/shard_map/write_foreign/pallas_call | solution.py:319
  (69 shorter events, 11.4 us)
Async XLA Ops:
  0.1 6.2 %copy-start.15 = (f32[128]{0:T(128)S(1)}, f32[128]{0:T(128)}, u32[]{:S(2)}) copy-start(f32[128]{0:T(128)} %param.15) | copy-start | bytes 1540
  3.3 31.5 %collective-permute-start.23 = (f32[2440,128]{1,0:T(8,128)}, f32[2440,128]{1,0:T(8,128)}, u32[]{:S(2)}, u32[]{:S(2)}) collective-permute-start(f32[2440,128]{1,0:T(8,128)} %turn_state.2), channel_id=1, source_target_pairs={{0,16},{8,24},{16,0},{24,8},{1,17},{9,25},{17,1},{25,9},{2,18},{10... | collective-permute-start | bytes 3747848 | tf_op jit(solution)/shard_map/ppermute | solution.py:348
  6.3 28.6 %copy-start.12 = (f32[128,16,256]{2,1,0:T(8,128)S(1)}, f32[128,16,256]{2,1,0:T(8,128)}, u32[]{:S(2)}) copy-start(f32[128,16,256]{2,1,0:T(8,128)} %param.13) | copy-start | bytes 6291460
  8.9 8.5 %collective-permute-start = (f32[384,128]{1,0:T(8,128)S(1)}, f32[384,128]{1,0:T(8,128)S(1)}, u32[]{:S(2)}, u32[]{:S(2)}) collective-permute-start(f32[384,128]{1,0:T(8,128)S(1)} %get-tuple-element.653), channel_id=1, source_target_pairs={{1,0},{2,1},{3,2},{4,3},{5,4},{6,5},{7,6},{0,7},{9,8},{10,9},{11,1... | collective-permute-start | bytes 589832 | tf_op jit(solution)/shard_map/while/body/ppermute | solution.py:366
  13.5 8.8 %collective-permute-start.1 = (f32[384,128]{1,0:T(8,128)S(1)}, f32[384,128]{1,0:T(8,128)S(1)}, u32[]{:S(2)}, u32[]{:S(2)}) collective-permute-start(f32[384,128]{1,0:T(8,128)S(1)} %get-tuple-element.654), channel_id=1, source_target_pairs={{0,1},{1,2},{2,3},{3,4},{4,5},{5,6},{6,7},{7,0},{8,9},{9,10},{10,1... | collective-permute-start | bytes 589832 | tf_op jit(solution)/shard_map/while/body/ppermute | solution.py:366
  28.7 39.7 %collective-permute-start.22 = (f32[3,16,64,128]{3,2,1,0:T(8,128)}, f32[3,16,64,128]{3,2,1,0:T(8,128)}, u32[]{:S(2)}, u32[]{:S(2)}) collective-permute-start(f32[3,16,64,128]{3,2,1,0:T(8,128)} %get-tuple-element.801), channel_id=1, source_target_pairs={{0,16},{8,24},{16,0},{24,8},{1,17},{9,25},{17,1},{25,9},{2,18},{10... | collective-permute-start | bytes 4718600 | tf_op jit(solution)/shard_map/ppermute | solution.py:348
  35.8 9.0 %collective-permute-start.4 = (f32[3,128,128]{2,1,0:T(8,128)S(1)}, f32[3,128,128]{2,1,0:T(8,128)S(1)}, u32[]{:S(2)}, u32[]{:S(2)}) collective-permute-start(f32[3,128,128]{2,1,0:T(8,128)S(1)} %bitcast.17), channel_id=1, source_target_pairs={{0,2},{1,3},{2,0},{3,1},{4,6},{5,7},{6,4},{7,5},{8,10},{9,11},{10,... | collective-permute-start | bytes 589832 | tf_op jit(solution)/shard_map/while/body/ppermute | solution.py:354
  38.0 10.3 %collective-permute-start.3 = (f32[3,128,128]{2,1,0:T(8,128)S(1)}, f32[3,128,128]{2,1,0:T(8,128)S(1)}, u32[]{:S(2)}, u32[]{:S(2)}) collective-permute-start(f32[3,128,128]{2,1,0:T(8,128)S(1)} %bitcast.18), channel_id=1, source_target_pairs={{0,1},{1,0},{2,3},{3,2},{4,5},{5,4},{6,7},{7,6},{8,9},{9,8},{10,11... | collective-permute-start | bytes 589832 | tf_op jit(solution)/shard_map/while/body/ppermute | solution.py:354
  39.6 16.8 %copy-start = (f32[128,3,16,256]{3,2,1,0:T(8,128)S(1)}, f32[128,3,16,256]{3,2,1,0:T(8,128)}, u32[]{:S(2)}) copy-start(f32[128,3,16,256]{3,2,1,0:T(8,128)} %get-tuple-element.793) | copy-start | bytes 18874372 | tf_op jit(solution)/shard_map/while
  42.4 11.9 %collective-permute-start.2 = (f32[384,128]{1,0:T(8,128)S(1)}, f32[384,128]{1,0:T(8,128)S(1)}, u32[]{:S(2)}, u32[]{:S(2)}) collective-permute-start(f32[384,128]{1,0:T(8,128)S(1)} %get-tuple-element.665), channel_id=1, source_target_pairs={{1,0},{2,1},{3,2},{4,3},{5,4},{6,5},{7,6},{0,7},{9,8},{10,9},{11,1... | collective-permute-start | bytes 589832 | tf_op jit(solution)/shard_map/while/body/ppermute | solution.py:366
  44.8 11.5 %collective-permute-start.5 = (f32[3,128,128]{2,1,0:T(8,128)S(1)}, f32[3,128,128]{2,1,0:T(8,128)S(1)}, u32[]{:S(2)}, u32[]{:S(2)}) collective-permute-start(f32[3,128,128]{2,1,0:T(8,128)S(1)} %collective-permute-done.4.refs_2_), channel_id=1, source_target_pairs={{0,1},{1,0},{2,3},{3,2},{4,5},{5,4},{6,7},{7,6},{8,9},{9,8},{10,11... | collective-permute-start | bytes 589832 | tf_op jit(solution)/shard_map/while/body/ppermute | solution.py:354
  44.8 11.5 %collective-permute-start.6 = (f32[384,128]{1,0:T(8,128)S(1)}, f32[384,128]{1,0:T(8,128)S(1)}, u32[]{:S(2)}, u32[]{:S(2)}) collective-permute-start(f32[384,128]{1,0:T(8,128)S(1)} %get-tuple-element.668), channel_id=1, source_target_pairs={{0,1},{1,2},{2,3},{3,4},{4,5},{5,6},{6,7},{7,0},{8,9},{9,10},{10,1... | collective-permute-start | bytes 589832 | tf_op jit(solution)/shard_map/while/body/ppermute | solution.py:366
  47.9 12.8 %copy-start.9 = (f32[2048,128]{1,0:T(8,128)}, f32[2048,128]{1,0:T(8,128)S(1)}, u32[]{:S(2)}) copy-start(f32[2048,128]{1,0:T(8,128)S(1)} %turn_state.3.refs_2_) | copy-start | bytes 3145732 | tf_op jit(solution)/shard_map/while
  60.7 6.0 %collective-permute-start.7 = (f32[3,16,128,128]{3,2,1,0:T(8,128)}, f32[3,16,128,128]{3,2,1,0:T(8,128)}, u32[]{:S(2)}, u32[]{:S(2)}) collective-permute-start(f32[3,16,128,128]{3,2,1,0:T(8,128)} %first_stencil.3), channel_id=1, source_target_pairs={{0,8},{8,0},{16,24},{24,16},{1,9},{9,1},{17,25},{25,17},{2,10},{10... | collective-permute-start | bytes 9437192 | tf_op jit(solution)/shard_map/while/body/ppermute | solution.py:351
  66.7 40.9 %collective-permute-start.25 = (f32[3,16,64,128]{3,2,1,0:T(8,128)}, f32[3,16,64,128]{3,2,1,0:T(8,128)}, u32[]{:S(2)}, u32[]{:S(2)}) collective-permute-start(f32[3,16,64,128]{3,2,1,0:T(8,128)} %get-tuple-element.837), channel_id=1, source_target_pairs={{0,16},{8,24},{16,0},{24,8},{1,17},{9,25},{17,1},{25,9},{2,18},{10... | collective-permute-start | bytes 4718600 | tf_op jit(solution)/shard_map/ppermute | solution.py:348
  68.4 3.6 %collective-permute-start.8 = (f32[3,16,64,128]{3,2,1,0:T(8,128)}, f32[3,16,64,128]{3,2,1,0:T(8,128)S(1)}, u32[]{:S(2)}, u32[]{:S(2)}) collective-permute-start(f32[3,16,64,128]{3,2,1,0:T(8,128)} %get-tuple-element.812.far), channel_id=1, source_target_pairs={{0,8},{8,0},{16,24},{24,16},{1,9},{9,1},{17,25},{25,17},{2,10},{10... | collective-permute-start | bytes 4718600 | tf_op jit(solution)/shard_map/while/body/ppermute | solution.py:351
  72.0 5.5 %copy-start.1 = (bf16[3,512,256]{2,1,0:T(8,128)(2,1)S(1)}, bf16[3,512,256]{2,1,0:T(8,128)(2,1)}, u32[]{:S(2)}) copy-start(bf16[3,512,256]{2,1,0:T(8,128)(2,1)} %get-tuple-element.829.high) | copy-start | bytes 2359300 | tf_op jit(solution)/shard_map/while
  72.0 5.5 %copy-start.5 = (bf16[3,512,256]{2,1,0:T(8,128)(2,1)S(1)}, bf16[3,512,256]{2,1,0:T(8,128)(2,1)}, u32[]{:S(2)}) copy-start(bf16[3,512,256]{2,1,0:T(8,128)(2,1)} %get-tuple-element.830.low) | copy-start | bytes 2359300 | tf_op jit(solution)/shard_map/while
  75.9 15.6 %copy-start.10 = (f32[2048,128]{1,0:T(8,128)S(1)}, f32[2048,128]{1,0:T(8,128)}, u32[]{:S(2)}) copy-start(f32[2048,128]{1,0:T(8,128)} %get-tuple-element.831.refs_3_) | copy-start | bytes 3145732 | tf_op jit(solution)/shard_map/while
  75.9 13.0 %collective-permute-start.10 = (f32[3,32,256]{2,1,0:T(8,128)S(1)}, f32[3,32,256]{2,1,0:T(8,128)S(1)}, u32[]{:S(2)}, u32[]{:S(2)}) collective-permute-start(f32[3,32,256]{2,1,0:T(8,128)S(1)} %get-tuple-element.684), channel_id=1, source_target_pairs={{0,1},{1,2},{2,3},{3,4},{4,5},{5,6},{6,7},{7,0},{8,9},{9,10},{10,1... | collective-permute-start | bytes 294920 | tf_op jit(solution)/shard_map/while/body/ppermute | solution.py:366
  80.9 8.0 %collective-permute-start.11 = (f32[3,32,256]{2,1,0:T(8,128)S(1)}, f32[3,32,256]{2,1,0:T(8,128)S(1)}, u32[]{:S(2)}, u32[]{:S(2)}) collective-permute-start(f32[3,32,256]{2,1,0:T(8,128)S(1)} %get-tuple-element.686), channel_id=1, source_target_pairs={{1,0},{2,1},{3,2},{4,3},{5,4},{6,5},{7,6},{0,7},{9,8},{10,9},{11,1... | collective-permute-start | bytes 294920 | tf_op jit(solution)/shard_map/while/body/ppermute | solution.py:366
  84.2 7.3 %collective-permute-start.12 = (f32[3,32,256]{2,1,0:T(8,128)S(1)}, f32[3,32,256]{2,1,0:T(8,128)S(1)}, u32[]{:S(2)}, u32[]{:S(2)}) collective-permute-start(f32[3,32,256]{2,1,0:T(8,128)S(1)} %get-tuple-element.687), channel_id=1, source_target_pairs={{0,1},{1,2},{2,3},{3,4},{4,5},{5,6},{6,7},{7,0},{8,9},{9,10},{10,1... | collective-permute-start | bytes 294920 | tf_op jit(solution)/shard_map/while/body/ppermute | solution.py:366
  84.2 7.3 %collective-permute-start.9 = (f32[3,32,256]{2,1,0:T(8,128)S(1)}, f32[3,32,256]{2,1,0:T(8,128)S(1)}, u32[]{:S(2)}, u32[]{:S(2)}) collective-permute-start(f32[3,32,256]{2,1,0:T(8,128)S(1)} %get-tuple-element.683), channel_id=1, source_target_pairs={{1,0},{2,1},{3,2},{4,3},{5,4},{6,5},{7,6},{0,7},{9,8},{10,9},{11,1... | collective-permute-start | bytes 294920 | tf_op jit(solution)/shard_map/while/body/ppermute | solution.py:366
  93.1 3.6 %collective-permute-start.14 = (f32[3,16,32,256]{3,2,1,0:T(8,128)S(1)}, f32[3,16,32,256]{3,2,1,0:T(8,128)}, u32[]{:S(2)}, u32[]{:S(2)}) collective-permute-start(f32[3,16,32,256]{3,2,1,0:T(8,128)S(1)} %second_stencil_0.1.own), channel_id=1, source_target_pairs={{0,8},{8,0},{16,24},{24,16},{1,9},{9,1},{17,25},{25,17},{2,10},{10... | collective-permute-start | bytes 4718600 | tf_op jit(solution)/shard_map/while/body/ppermute | solution.py:351
  94.9 6.2 %collective-permute-start.13 = (f32[3,16,32,256]{3,2,1,0:T(8,128)S(1)}, f32[3,16,32,256]{3,2,1,0:T(8,128)}, u32[]{:S(2)}, u32[]{:S(2)}) collective-permute-start(f32[3,16,32,256]{3,2,1,0:T(8,128)S(1)} %second_stencil_1.1.own), channel_id=1, source_target_pairs={{0,8},{8,0},{16,24},{24,16},{1,9},{9,1},{17,25},{25,17},{2,10},{10... | collective-permute-start | bytes 4718600 | tf_op jit(solution)/shard_map/while/body/ppermute | solution.py:351
  95.5 5.7 %copy-start.2 = (bf16[3,512,256]{2,1,0:T(8,128)(2,1)S(1)}, bf16[3,512,256]{2,1,0:T(8,128)(2,1)}, u32[]{:S(2)}) copy-start(bf16[3,512,256]{2,1,0:T(8,128)(2,1)} %get-tuple-element.829.high) | copy-start | bytes 2359300 | tf_op jit(solution)/shard_map/while
  95.5 5.7 %copy-start.6 = (bf16[3,512,256]{2,1,0:T(8,128)(2,1)S(1)}, bf16[3,512,256]{2,1,0:T(8,128)(2,1)}, u32[]{:S(2)}) copy-start(bf16[3,512,256]{2,1,0:T(8,128)(2,1)} %get-tuple-element.830.low) | copy-start | bytes 2359300 | tf_op jit(solution)/shard_map/while
  105.3 1.1 copy-start.13
  106.4 50.6 %collective-permute-start.24 = (f32[3,16,64,128]{3,2,1,0:T(8,128)}, f32[3,16,64,128]{3,2,1,0:T(8,128)}, u32[]{:S(2)}, u32[]{:S(2)}) collective-permute-start(f32[3,16,64,128]{3,2,1,0:T(8,128)} %get-tuple-element.297), channel_id=1, source_target_pairs={{0,16},{8,24},{16,0},{24,8},{1,17},{9,25},{17,1},{25,9},{2,18},{10... | collective-permute-start | bytes 4718600 | tf_op jit(solution)/shard_map/ppermute | solution.py:348
  107.6 3.6 %collective-permute-start.15 = (f32[3,16,64,128]{3,2,1,0:T(8,128)}, f32[3,16,64,128]{3,2,1,0:T(8,128)S(1)}, u32[]{:S(2)}, u32[]{:S(2)}) collective-permute-start(f32[3,16,64,128]{3,2,1,0:T(8,128)} %get-tuple-element.848.far), channel_id=1, source_target_pairs={{0,8},{8,0},{16,24},{24,16},{1,9},{9,1},{17,25},{25,17},{2,10},{10... | collective-permute-start | bytes 4718600 | tf_op jit(solution)/shard_map/while/body/ppermute | solution.py:351
  111.2 8.6 %copy-start.3 = (bf16[3,512,256]{2,1,0:T(8,128)(2,1)S(1)}, bf16[3,512,256]{2,1,0:T(8,128)(2,1)}, u32[]{:S(2)}) copy-start(bf16[3,512,256]{2,1,0:T(8,128)(2,1)} %get-tuple-element.865.high) | copy-start | bytes 2359300 | tf_op jit(solution)/shard_map/while
  111.2 8.6 %copy-start.7 = (bf16[3,512,256]{2,1,0:T(8,128)(2,1)S(1)}, bf16[3,512,256]{2,1,0:T(8,128)(2,1)}, u32[]{:S(2)}) copy-start(bf16[3,512,256]{2,1,0:T(8,128)(2,1)} %get-tuple-element.866.low) | copy-start | bytes 2359300 | tf_op jit(solution)/shard_map/while
  115.1 13.0 %collective-permute-start.16 = (f32[3,32,256]{2,1,0:T(8,128)S(1)}, f32[3,32,256]{2,1,0:T(8,128)S(1)}, u32[]{:S(2)}, u32[]{:S(2)}) collective-permute-start(f32[3,32,256]{2,1,0:T(8,128)S(1)} %get-tuple-element.709), channel_id=1, source_target_pairs={{1,0},{2,1},{3,2},{4,3},{5,4},{6,5},{7,6},{0,7},{9,8},{10,9},{11,1... | collective-permute-start | bytes 294920 | tf_op jit(solution)/shard_map/while/body/ppermute | solution.py:366
  119.9 15.5 %copy-start.11 = (f32[2048,128]{1,0:T(8,128)S(1)}, f32[2048,128]{1,0:T(8,128)}, u32[]{:S(2)}) copy-start(f32[2048,128]{1,0:T(8,128)} %get-tuple-element.867.refs_3_) | copy-start | bytes 3145732 | tf_op jit(solution)/shard_map/while
  119.9 8.2 %collective-permute-start.17 = (f32[3,32,256]{2,1,0:T(8,128)S(1)}, f32[3,32,256]{2,1,0:T(8,128)S(1)}, u32[]{:S(2)}, u32[]{:S(2)}) collective-permute-start(f32[3,32,256]{2,1,0:T(8,128)S(1)} %get-tuple-element.710), channel_id=1, source_target_pairs={{0,1},{1,2},{2,3},{3,4},{4,5},{5,6},{6,7},{7,0},{8,9},{9,10},{10,1... | collective-permute-start | bytes 294920 | tf_op jit(solution)/shard_map/while/body/ppermute | solution.py:366
  123.4 6.9 %collective-permute-start.18 = (f32[3,32,256]{2,1,0:T(8,128)S(1)}, f32[3,32,256]{2,1,0:T(8,128)S(1)}, u32[]{:S(2)}, u32[]{:S(2)}) collective-permute-start(f32[3,32,256]{2,1,0:T(8,128)S(1)} %get-tuple-element.712), channel_id=1, source_target_pairs={{1,0},{2,1},{3,2},{4,3},{5,4},{6,5},{7,6},{0,7},{9,8},{10,9},{11,1... | collective-permute-start | bytes 294920 | tf_op jit(solution)/shard_map/while/body/ppermute | solution.py:366
  128.1 7.3 %collective-permute-start.19 = (f32[3,32,256]{2,1,0:T(8,128)S(1)}, f32[3,32,256]{2,1,0:T(8,128)S(1)}, u32[]{:S(2)}, u32[]{:S(2)}) collective-permute-start(f32[3,32,256]{2,1,0:T(8,128)S(1)} %get-tuple-element.713), channel_id=1, source_target_pairs={{0,1},{1,2},{2,3},{3,4},{4,5},{5,6},{6,7},{7,0},{8,9},{9,10},{10,1... | collective-permute-start | bytes 294920 | tf_op jit(solution)/shard_map/while/body/ppermute | solution.py:366
  137.1 3.6 %collective-permute-start.21 = (f32[3,16,32,256]{3,2,1,0:T(8,128)S(1)}, f32[3,16,32,256]{3,2,1,0:T(8,128)}, u32[]{:S(2)}, u32[]{:S(2)}) collective-permute-start(f32[3,16,32,256]{3,2,1,0:T(8,128)S(1)} %second_stencil_2.1.own), channel_id=1, source_target_pairs={{0,8},{8,0},{16,24},{24,16},{1,9},{9,1},{17,25},{25,17},{2,10},{10... | collective-permute-start | bytes 4718600 | tf_op jit(solution)/shard_map/while/body/ppermute | solution.py:351
  138.8 6.3 %collective-permute-start.20 = (f32[3,16,32,256]{3,2,1,0:T(8,128)S(1)}, f32[3,16,32,256]{3,2,1,0:T(8,128)}, u32[]{:S(2)}, u32[]{:S(2)}) collective-permute-start(f32[3,16,32,256]{3,2,1,0:T(8,128)S(1)} %second_stencil_3.1.own), channel_id=1, source_target_pairs={{0,8},{8,0},{16,24},{24,16},{1,9},{9,1},{17,25},{25,17},{2,10},{10... | collective-permute-start | bytes 4718600 | tf_op jit(solution)/shard_map/while/body/ppermute | solution.py:351
  139.4 5.7 %copy-start.4 = (bf16[3,512,256]{2,1,0:T(8,128)(2,1)S(1)}, bf16[3,512,256]{2,1,0:T(8,128)(2,1)}, u32[]{:S(2)}) copy-start(bf16[3,512,256]{2,1,0:T(8,128)(2,1)} %get-tuple-element.865.high) | copy-start | bytes 2359300 | tf_op jit(solution)/shard_map/while
  139.4 5.7 %copy-start.8 = (bf16[3,512,256]{2,1,0:T(8,128)(2,1)S(1)}, bf16[3,512,256]{2,1,0:T(8,128)(2,1)}, u32[]{:S(2)}) copy-start(bf16[3,512,256]{2,1,0:T(8,128)(2,1)} %get-tuple-element.866.low) | copy-start | bytes 2359300 | tf_op jit(solution)/shard_map/while
  149.2 1.2 copy-start.14
  150.5 36.6 %collective-permute-start.26 = (f32[3,16,64,128]{3,2,1,0:T(8,128)}, f32[3,16,64,128]{3,2,1,0:T(8,128)S(1)}, u32[]{:S(2)}, u32[]{:S(2)}) collective-permute-start(f32[3,16,64,128]{3,2,1,0:T(8,128)} %get-tuple-element.302), channel_id=1, source_target_pairs={{0,16},{8,24},{16,0},{24,8},{1,17},{9,25},{17,1},{25,9},{2,18},{10... | collective-permute-start | bytes 4718600 | tf_op jit(solution)/shard_map/ppermute | solution.py:348

commit v6 on v5

--- a/solution.py
+++ b/solution.py
@@ -7,7 +7,7 @@
 
 SECTIONS = 2
 GROUPS = 2
-PARTS = 2
+PARTS = 1
 RATE_ROWS = 8
 PIECES = 4
 
@@ -306,9 +306,11 @@
 
 def last_kernel(where, *refs, nz, chunks):
     ins, out = refs[:chunks], refs[-1]
+    modes, _, width = out.shape
+    rows = out.reshape(modes * nz, width)
     for z in range(nz):
         whole = jnp.concatenate([ref[0, z] for ref in ins], axis=0)
-        out[:, z, :] = whole.T
+        rows[pl.ds(z, modes, stride=nz), :] = whole.T
 
 
 def write_half(where, pieces, nphi, foreign, base=None):

time: 193 us -> 182 us (0.943)
  waiting for transfers between devices: 74.6 us -> 91.1 us
  Pallas kernels: 74 us -> 61.3 us
  starting transfers between devices: 40.2 us -> 27.9 us
  local copies, waits for them, and re-layouts: 3.35 us -> 0.96 us
    ppermute x12 -> x8, starting transfers between devices: 28.1 us -> 17.3 us  [halos(): return (lax.ppermute(leading, 'col', down), lax.ppermute(last, 'col', up))]
    ppermute x7 -> x5, waiting for transfers between devices: 11.7 us -> 20.7 us  [beside(): return lax.ppermute(array, 'rad', [(i, i ^ 1) for i in range(peers)])]
    ppermute x12 -> x8, waiting for transfers between devices: 24.6 us -> 31.7 us  [halos(): return (lax.ppermute(leading, 'col', down), lax.ppermute(last, 'col', up))]
    pallas_call x4 -> x2, Pallas kernels: 17 us -> 12.1 us  [map2(): pl.pallas_call(map2_kernel, out_shape=[shape(out)] * 2, grid=(comps,), in...]
    pallas_call x4 -> x2, Pallas kernels: 14.7 us -> 10.2 us  [map1(): pl.pallas_call(map1_kernel, out_shape=[shape((comps, nz, width, cols)), s...]
    pallas_call x4 -> x2, Pallas kernels: 6.69 us -> 4.11 us  [second_stencil(): pl.pallas_call(lambda *refs: second_kernel(*refs, k=k, half=half), out_sh...]
    while x28 -> x8, local copies, waits for them, and re-layouts: 2.4 us -> 0.01 us
  transfers between devices with their start and end apart: 27 -> 21, of which waited for: 15 -> 16; matrix products, arithmetic and copies ran while one was open for 0% -> 1% of each run, Pallas kernels for 34% -> 29%
where the time goes in v6:
time: 182 us
  waiting for transfers between devices  91.1 us (50%)
  Pallas kernels  61.3 us (34%)
  starting transfers between devices  27.9 us (15%)
    ppermute x5, waiting for transfers between devices, across(): return lax.ppermute(array, 'rad', [(i, i ^ 2) for i in range(peers)])  36.2 us
    ppermute x8, waiting for transfers between devices, halos(): return (lax.ppermute(leading, 'col', down), lax.ppermute(last, 'col', up))  31.7 us
    ppermute x5, waiting for transfers between devices, beside(): return lax.ppermute(array, 'rad', [(i, i ^ 1) for i in range(peers)])  20.7 us
    ppermute x8, starting transfers between devices, halos(): return (lax.ppermute(leading, 'col', down), lax.ppermute(last, 'col', up))  17.3 us
    pallas_call x2, Pallas kernels, map2(): pl.pallas_call(map2_kernel, out_shape=[shape(out)] * 2, grid=(comps,), in...  12.1 us
    pallas_call x2, Pallas kernels, first_stencil(): pl.pallas_call(lambda *refs: first_kernel(*refs, modes=modes, nz=nz, chun...  10.7 us
    pallas_call x2, Pallas kernels, write_half(): pl.pallas_call(lambda *refs: last_kernel(*refs, nz=nz, chunks=chunks), ou...  10.4 us
    pallas_call x2, Pallas kernels, map1(): pl.pallas_call(map1_kernel, out_shape=[shape((comps, nz, width, cols)), s...  10.2 us
  transfers between devices with their start and end apart: 21, of which 16 were waited for; matrix products, arithmetic and copies ran while one was open for 1% of the time, Pallas kernels for 29%

profile of v6, /device:TPU:0, one launch (start us, length us, event | category | flops | bytes accessed | tf_op | source)
XLA Modules:
  0.0 181.5 jit_solution(12873106485599294051)
XLA Ops:
  0.1 3.2 %turn_state.2 = f32[2440,128]{1,0:T(8,128)} custom-call(s32[2]{0:T(128)S(1)} %pad_add_fusion.refs_0_, f32[2048,256]{1,0:T(8,128)} %bitcast.24, f32[1,128]{1,0:T(1,128)} %bitcast.26, f32[3,512,128]{2,1,0:T(8,128)} %refs_3_.1), custom_call_target="tpu_custom_call" | custom-call | flops 312320 | bytes 2498560 | tf_op jit(solution)/shard_map/turn_state/pallas_call | solution.py:83
  3.3 2.9 %collective-permute-start.17 = (f32[2440,128]{1,0:T(8,128)}, f32[2440,128]{1,0:T(8,128)}, u32[]{:S(2)}, u32[]{:S(2)}) collective-permute-start(f32[2440,128]{1,0:T(8,128)} %turn_state.2), channel_id=1, source_target_pairs={{0,16},{8,24},{16,0},{24,8},{1,17},{9,25},{17,1},{25,9},{2,18},{10... | collective-permute-start | bytes 3747848 | tf_op jit(solution)/shard_map/ppermute | solution.py:350
  6.2 22.4 %while.54 = (s32[]{:T(128)}, f32[3,16,64,128]{3,2,1,0:T(8,128)}, f32[3,16,64,128]{3,2,1,0:T(8,128)}, s32[]{:T(128)}, s32[2]{0:T(128)S(1)}, /*index=5*/f32[128,3,...) while((s32[]{:T(128)}, f32[3,16,64,128]{3,2,1,0:T(8,128)}, ...), condition=%wide.region_1.0_spmd, body=%wide.region_0.0_spmd.sunk | while | flops 9535493 | bytes 11010261 | solution.py:376
  6.2 2.6 %edge_layers.2 = (f32[384,128]{1,0:T(8,128)S(1)}, f32[384,128]{1,0:T(8,128)S(1)}) custom-call(s32[2]{0:T(128)S(1)} %broadcast_add_fusion.4.refs_0_, f32[6144,256]{1,0:T(8,128)} %bitcast.20), custom_call_target="tpu_custom_call" | custom-call | flops 98304 | bytes 3145728 | tf_op jit(solution)/shard_map/while/body/edge_layers/pallas_call | solution.py:109
  8.9 4.6 %collective-permute-start = (f32[384,128]{1,0:T(8,128)S(1)}, f32[384,128]{1,0:T(8,128)S(1)}, u32[]{:S(2)}, u32[]{:S(2)}) collective-permute-start(f32[384,128]{1,0:T(8,128)S(1)} %get-tuple-element.621), channel_id=1, source_target_pairs={{1,0},{2,1},{3,2},{4,3},{5,4},{6,5},{7,6},{0,7},{9,8},{10,9},{11,1... | collective-permute-start | bytes 589832 | tf_op jit(solution)/shard_map/while/body/ppermute | solution.py:368
  13.5 3.9 %collective-permute-done.refs_3_ = f32[384,128]{1,0:T(8,128)S(1)} collective-permute-done((f32[384,128]{1,0:T(8,128)S(1)}, f32[384,128]{1,0:T(8,128)S(1)}, u32[]{:S(2)}, u32[]{:S(2)}) %collective-permute-start) | collective-permute-done | bytes 196640 | tf_op jit(solution)/shard_map/while/body/ppermute | solution.py:368
  17.4 4.9 %collective-permute-done.1.refs_4_ = f32[384,128]{1,0:T(8,128)S(1)} collective-permute-done((f32[384,128]{1,0:T(8,128)S(1)}, f32[384,128]{1,0:T(8,128)S(1)}, u32[]{:S(2)}, u32[]{:S(2)}) %collective-permute-start.1) | collective-permute-done | bytes 196640 | tf_op jit(solution)/shard_map/while/body/ppermute | solution.py:368
  22.3 6.4 %first_stencil.2 = (f32[3,16,64,128]{3,2,1,0:T(8,128)}, f32[3,16,64,128]{3,2,1,0:T(8,128)}) custom-call(s32[2]{0:T(128)S(1)} %broadcast_add_fusion.4.refs_0_, f32[6144,256]{1,0:T(8,128)} %bitcast.21, f32[2440,128]{1,0:T(8,128)} %get-tuple-element.702.refs_2_, f32[384,128]{1,0:T(8,128)S(1)} %collective-permute-done.refs_3_, ...), custom_call_target="tpu_custom_call" | custom-call | flops 9437184 | bytes 6291456 | tf_op jit(solution)/shard_map/while/body/first_stencil/pallas_call | solution.py:159
  28.6 0.5 collective-permute-start.16
  29.2 5.6 %collective-permute-done.17 = f32[2440,128]{1,0:T(8,128)} collective-permute-done((f32[2440,128]{1,0:T(8,128)}, f32[2440,128]{1,0:T(8,128)}, u32[]{:S(2)}, u32[]{:S(2)}) %collective-permute-start.17) | collective-permute-done | bytes 1249312 | tf_op jit(solution)/shard_map/ppermute | solution.py:350
  34.8 31.9 %while.55 = (s32[]{:T(128)}, f32[2048,128]{1,0:T(8,128)}, f32[3,16,128,128]{3,2,1,0:T(8,128)}, f32[3,16,128,128]{3,2,1,0:T(8,128)}, bf16[3,512,256]{2,1,0:T(8,12...) while((s32[]{:T(128)}, f32[2048,128]{1,0:T(8,128)}, ...), condition=%wide.region_3.0_spmd, body=%wide.region_2.0_spmd.sunk | while | flops 10584069 | bytes 60948948 | solution.py:394
  34.8 0.9 slice.4
  35.8 2.2 %collective-permute-start.4 = (f32[3,128,128]{2,1,0:T(8,128)S(1)}, f32[3,128,128]{2,1,0:T(8,128)S(1)}, u32[]{:S(2)}, u32[]{:S(2)}) collective-permute-start(f32[3,128,128]{2,1,0:T(8,128)S(1)} %bitcast.17), channel_id=1, source_target_pairs={{0,2},{1,3},{2,0},{3,1},{4,6},{5,7},{6,4},{7,5},{8,10},{9,11},{10,... | collective-permute-start | bytes 589832 | tf_op jit(solution)/shard_map/while/body/ppermute | solution.py:356
  38.0 1.5 collective-permute-start.3
  39.5 2.8 %edge_layers.3 = (f32[384,128]{1,0:T(8,128)S(1)}, f32[384,128]{1,0:T(8,128)S(1)}) custom-call(s32[2]{0:T(128)S(1)} %broadcast_add_fusion.5.refs_0_.where, f32[6144,256]{1,0:T(8,128)} %bitcast.22), custom_call_target="tpu_custom_call" | custom-call | flops 98304 | bytes 3145728 | tf_op jit(solution)/shard_map/while/body/edge_layers/pallas_call | solution.py:109
  42.3 2.5 %collective-permute-start.2 = (f32[384,128]{1,0:T(8,128)S(1)}, f32[384,128]{1,0:T(8,128)S(1)}, u32[]{:S(2)}, u32[]{:S(2)}) collective-permute-start(f32[384,128]{1,0:T(8,128)S(1)} %get-tuple-element.633), channel_id=1, source_target_pairs={{1,0},{2,1},{3,2},{4,3},{5,4},{6,5},{7,6},{0,7},{9,8},{10,9},{11,1... | collective-permute-start | bytes 589832 | tf_op jit(solution)/shard_map/while/body/ppermute | solution.py:368
  44.8 2.0 %collective-permute-start.6 = (f32[384,128]{1,0:T(8,128)S(1)}, f32[384,128]{1,0:T(8,128)S(1)}, u32[]{:S(2)}, u32[]{:S(2)}) collective-permute-start(f32[384,128]{1,0:T(8,128)S(1)} %get-tuple-element.636), channel_id=1, source_target_pairs={{0,1},{1,2},{2,3},{3,4},{4,5},{5,6},{6,7},{7,0},{8,9},{9,10},{10,1... | collective-permute-start | bytes 589832 | tf_op jit(solution)/shard_map/while/body/ppermute | solution.py:368
  46.8 1.1 turn_state.3.refs_2_
  48.3 5.9 %collective-permute-done.2.refs_3_ = f32[384,128]{1,0:T(8,128)S(1)} collective-permute-done((f32[384,128]{1,0:T(8,128)S(1)}, f32[384,128]{1,0:T(8,128)S(1)}, u32[]{:S(2)}, u32[]{:S(2)}) %collective-permute-start.2) | collective-permute-done | bytes 196640 | tf_op jit(solution)/shard_map/while/body/ppermute | solution.py:368
  54.2 2.1 %collective-permute-done.5.refs_3_ = f32[3,128,128]{2,1,0:T(8,128)S(1)} collective-permute-done((f32[3,128,128]{2,1,0:T(8,128)S(1)}, f32[3,128,128]{2,1,0:T(8,128)S(1)}, u32[]{:S(2)}, u32[]{:S(2)}) %collective-permute-start.5) | collective-permute-done | bytes 196640 | tf_op jit(solution)/shard_map/while/body/ppermute | solution.py:356
  56.3 4.4 %first_stencil.3 = f32[3,16,128,128]{3,2,1,0:T(8,128)} custom-call(s32[2]{0:T(128)S(1)} %broadcast_add_fusion.5.refs_0_.where, f32[6144,256]{1,0:T(8,128)S(1)} %bitcast.23, f32[2048,128]{1,0:T(8,128)S(1)} %turn_state.3.refs_2_, f32[384,128]{1,0:T(8,128)S(1)} %collective-permute-done.2.refs_3_, f32[384,128]{1,0:T(8,128)S(1)} %collective-permute-done.6.refs_4_, ...), custom_call_target="tpu_custom_call" | custom-call | flops 9437184 | bytes 6291456 | tf_op jit(solution)/shard_map/while/body/first_stencil/pallas_call | solution.py:159
  60.7 4.1 %split_helm.1 = (bf16[3,512,256]{2,1,0:T(8,128)(2,1)}, bf16[3,512,256]{2,1,0:T(8,128)(2,1)}) custom-call(s32[2]{0:T(128)S(1)} %broadcast_add_fusion.5.refs_0_.where, f32[3,512,128]{2,1,0:T(8,128)} %get-tuple-element.748.own, f32[3,128,128]{2,1,0:T(8,128)S(1)} %bitcast.19, f32[3,128,128]{2,1,0:T(8,128)S(1)} %collective-permute-done.3.refs_1_, ...), custom_call_target="tpu_custom_call" | custom-call | flops 786432 | bytes 3145728 | tf_op jit(solution)/shard_map/while/body/split_helm/pallas_call | solution.py:205
  64.8 1.9 %collective-permute-done.7 = f32[3,16,128,128]{3,2,1,0:T(8,128)} collective-permute-done((f32[3,16,128,128]{3,2,1,0:T(8,128)}, f32[3,16,128,128]{3,2,1,0:T(8,128)}, u32[]{:S(2)}, u32[]{:S(2)}) %collective-permute-start.7) | collective-permute-done | bytes 3145760 | tf_op jit(solution)/shard_map/while/body/ppermute | solution.py:353
  66.7 1.6 collective-permute-start.19
  68.3 35.2 %while.56 = (s32[]{:T(128)}, f32[3,16,64,128]{3,2,1,0:T(8,128)}, f32[3,16,64,128]{3,2,1,0:T(8,128)}, s32[]{:T(128)}, f32[3,16,128,128]{3,2,1,0:T(8,128)}, /*inde...) while((s32[]{:T(128)}, f32[3,16,64,128]{3,2,1,0:T(8,128)}, ...), condition=%wide.region_5.0_spmd, body=%wide.region_4.0_spmd.sunk | while | flops 4841275392 | bytes 52953392 | solution.py:418
  68.3 3.6 %collective-permute-done.8.far_peer = f32[3,16,64,128]{3,2,1,0:T(8,128)S(1)} collective-permute-done((f32[3,16,64,128]{3,2,1,0:T(8,128)}, f32[3,16,64,128]{3,2,1,0:T(8,128)S(1)}, u32[]{:S(2)}, u32[]{:S(2)}) %collective-permute-start.8) | collective-permute-done | bytes 1572896 | tf_op jit(solution)/shard_map/while/body/ppermute | solution.py:353
  72.0 5.1 %map1_0.1 = (f32[3,16,64,256]{3,2,1,0:T(8,128)S(1)}, f32[3,64,256]{2,1,0:T(8,128)S(1)}, f32[3,64,256]{2,1,0:T(8,128)S(1)}) custom-call(f32[3,16,128,128]{3,2,1,0:T(8,128)} %get-tuple-element.779.own, f32[3,16,64,128]{3,2,1,0:T(8,128)} %get-tuple-element.764.far, f32[3,16,128,128]{3,2,1,0:T(8,128)} %get-tuple-element.780.own_peer, ...), custom_call_target="tpu_custom_call" | custom-call | flops 2415919104 | bytes 11010048 | tf_op jit(solution)/shard_map/while/body/map1_0/pallas_call | solution.py:239
  77.1 1.6 collective-permute-start.10
  78.6 3.2 %collective-permute-start.9 = (f32[3,64,256]{2,1,0:T(8,128)S(1)}, f32[3,64,256]{2,1,0:T(8,128)S(1)}, u32[]{:S(2)}, u32[]{:S(2)}) collective-permute-start(f32[3,64,256]{2,1,0:T(8,128)S(1)} %get-tuple-element.651), channel_id=1, source_target_pairs={{1,0},{2,1},{3,2},{4,3},{5,4},{6,5},{7,6},{0,7},{9,8},{10,9},{11,1... | collective-permute-start | bytes 589832 | tf_op jit(solution)/shard_map/while/body/ppermute | solution.py:368
  81.8 5.5 %collective-permute-done.10.refs_2_ = f32[3,64,256]{2,1,0:T(8,128)S(1)} collective-permute-done((f32[3,64,256]{2,1,0:T(8,128)S(1)}, f32[3,64,256]{2,1,0:T(8,128)S(1)}, u32[]{:S(2)}, u32[]{:S(2)}) %collective-permute-start.10) | collective-permute-done | bytes 196640 | tf_op jit(solution)/shard_map/while/body/ppermute | solution.py:368
  87.3 2.2 %collective-permute-done.9.refs_1_ = f32[3,64,256]{2,1,0:T(8,128)S(1)} collective-permute-done((f32[3,64,256]{2,1,0:T(8,128)S(1)}, f32[3,64,256]{2,1,0:T(8,128)S(1)}, u32[]{:S(2)}, u32[]{:S(2)}) %collective-permute-start.9) | collective-permute-done | bytes 196640 | tf_op jit(solution)/shard_map/while/body/ppermute | solution.py:368
  89.5 2.1 %second_stencil_0.1.own = f32[3,16,64,256]{3,2,1,0:T(8,128)S(1)} custom-call(f32[3,16,64,256]{3,2,1,0:T(8,128)S(1)} %get-tuple-element.653.refs_0_, f32[3,64,256]{2,1,0:T(8,128)S(1)} %collective-permute-done.9.refs_1_, f32[3,64,256]{2,1,0:T(8,128)S(1)} %collective-permute-done.10.refs_2_, f32[2048,128]{1,0:T(8,128)S(1)} %copy-done.2, ...), custom_call_target="tpu_custom_call" | custom-call | flops 9437184 | bytes 6291456 | tf_op jit(solution)/shard_map/while/body/second_stencil_0/pallas_call | solution.py:270
  91.6 5.8 %collective-permute-done.11.peer = f32[3,16,64,256]{3,2,1,0:T(8,128)} collective-permute-done((f32[3,16,64,256]{3,2,1,0:T(8,128)S(1)}, f32[3,16,64,256]{3,2,1,0:T(8,128)}, u32[]{:S(2)}, u32[]{:S(2)}) %collective-permute-start.11) | collective-permute-done | bytes 3145760 | tf_op jit(solution)/shard_map/while/body/ppermute | solution.py:353
  97.4 6.1 %map2_0.1 = (f32[3,16,64,128]{3,2,1,0:T(8,128)}, f32[3,16,64,128]{3,2,1,0:T(8,128)}) custom-call(f32[3,16,64,256]{3,2,1,0:T(8,128)S(1)} %second_stencil_0.1.own, f32[3,16,64,256]{3,2,1,0:T(8,128)} %collective-permute-done.11.peer, bf16[3,512,256]{2,1,0:T(8,128)(2,1)} %get-tuple-element.781.high, bf16[3,512,256]{2,1,0:T(8,128)(2,1)} %get-tuple-element.782.low), custom_call_target="tpu_custom_call" | custom-call | flops 2415919104 | bytes 11010048 | tf_op jit(solution)/shard_map/while/body/map2_0/pallas_call | solution.py:294
  103.5 1.1 collective-permute-start.18
  104.6 35.4 %while.57 = (s32[]{:T(128)}, f32[3,16,64,128]{3,2,1,0:T(8,128)}, f32[3,16,64,128]{3,2,1,0:T(8,128)}, s32[]{:T(128)}, f32[3,16,128,128]{3,2,1,0:T(8,128)}, /*inde...) while((s32[]{:T(128)}, f32[3,16,64,128]{3,2,1,0:T(8,128)}, ...), condition=%wide.region_7.0_spmd, body=%wide.region_6.0_spmd.sunk | while | flops 4841275392 | bytes 52953392 | solution.py:418
  104.6 3.6 %collective-permute-done.12.far_peer = f32[3,16,64,128]{3,2,1,0:T(8,128)S(1)} collective-permute-done((f32[3,16,64,128]{3,2,1,0:T(8,128)}, f32[3,16,64,128]{3,2,1,0:T(8,128)S(1)}, u32[]{:S(2)}, u32[]{:S(2)}) %collective-permute-start.12) | collective-permute-done | bytes 1572896 | tf_op jit(solution)/shard_map/while/body/ppermute | solution.py:353
  108.3 5.1 %map1_1.1 = (f32[3,16,64,256]{3,2,1,0:T(8,128)S(1)}, f32[3,64,256]{2,1,0:T(8,128)S(1)}, f32[3,64,256]{2,1,0:T(8,128)S(1)}) custom-call(f32[3,16,128,128]{3,2,1,0:T(8,128)} %get-tuple-element.815.own, f32[3,16,64,128]{3,2,1,0:T(8,128)} %get-tuple-element.800.far, f32[3,16,128,128]{3,2,1,0:T(8,128)} %get-tuple-element.816.own_peer, ...), custom_call_target="tpu_custom_call" | custom-call | flops 2415919104 | bytes 11010048 | tf_op jit(solution)/shard_map/while/body/map1_1/pallas_call | solution.py:239
  113.4 3.4 %collective-permute-start.13 = (f32[3,64,256]{2,1,0:T(8,128)S(1)}, f32[3,64,256]{2,1,0:T(8,128)S(1)}, u32[]{:S(2)}, u32[]{:S(2)}) collective-permute-start(f32[3,64,256]{2,1,0:T(8,128)S(1)} %get-tuple-element.669), channel_id=1, source_target_pairs={{1,0},{2,1},{3,2},{4,3},{5,4},{6,5},{7,6},{0,7},{9,8},{10,9},{11,1... | collective-permute-start | bytes 589832 | tf_op jit(solution)/shard_map/while/body/ppermute | solution.py:368
  116.7 4.5 %collective-permute-done.13.refs_1_ = f32[3,64,256]{2,1,0:T(8,128)S(1)} collective-permute-done((f32[3,64,256]{2,1,0:T(8,128)S(1)}, f32[3,64,256]{2,1,0:T(8,128)S(1)}, u32[]{:S(2)}, u32[]{:S(2)}) %collective-permute-start.13) | collective-permute-done | bytes 196640 | tf_op jit(solution)/shard_map/while/body/ppermute | solution.py:368
  121.2 4.9 %collective-permute-done.14.refs_2_ = f32[3,64,256]{2,1,0:T(8,128)S(1)} collective-permute-done((f32[3,64,256]{2,1,0:T(8,128)S(1)}, f32[3,64,256]{2,1,0:T(8,128)S(1)}, u32[]{:S(2)}, u32[]{:S(2)}) %collective-permute-start.14) | collective-permute-done | bytes 196640 | tf_op jit(solution)/shard_map/while/body/ppermute | solution.py:368
  126.1 2.1 %second_stencil_1.1.own = f32[3,16,64,256]{3,2,1,0:T(8,128)S(1)} custom-call(f32[3,16,64,256]{3,2,1,0:T(8,128)S(1)} %get-tuple-element.671.refs_0_, f32[3,64,256]{2,1,0:T(8,128)S(1)} %collective-permute-done.13.refs_1_, f32[3,64,256]{2,1,0:T(8,128)S(1)} %collective-permute-done.14.refs_2_, f32[2048,128]{1,0:T(8,128)S(1)} %copy-done.3, ...), custom_call_target="tpu_custom_call" | custom-call | flops 9437184 | bytes 6291456 | tf_op jit(solution)/shard_map/while/body/second_stencil_1/pallas_call | solution.py:270
  128.2 5.8 %collective-permute-done.15.peer = f32[3,16,64,256]{3,2,1,0:T(8,128)} collective-permute-done((f32[3,16,64,256]{3,2,1,0:T(8,128)S(1)}, f32[3,16,64,256]{3,2,1,0:T(8,128)}, u32[]{:S(2)}, u32[]{:S(2)}) %collective-permute-start.15) | collective-permute-done | bytes 3145760 | tf_op jit(solution)/shard_map/while/body/ppermute | solution.py:353
  134.0 6.0 %map2_1.1 = (f32[3,16,64,128]{3,2,1,0:T(8,128)}, f32[3,16,64,128]{3,2,1,0:T(8,128)}) custom-call(f32[3,16,64,256]{3,2,1,0:T(8,128)S(1)} %second_stencil_1.1.own, f32[3,16,64,256]{3,2,1,0:T(8,128)} %collective-permute-done.15.peer, bf16[3,512,256]{2,1,0:T(8,128)(2,1)} %get-tuple-element.817.high, bf16[3,512,256]{2,1,0:T(8,128)(2,1)} %get-tuple-element.818.low), custom_call_target="tpu_custom_call" | custom-call | flops 2415919104 | bytes 11010048 | tf_op jit(solution)/shard_map/while/body/map2_1/pallas_call | solution.py:294
  140.0 0.5 collective-permute-start.20
  140.6 5.5 %write_own.1.refs_3_ = f32[128,48,256]{2,1,0:T(8,128)} custom-call(s32[2]{0:T(128)S(1)} %get-tuple-element.860, f32[3,16,64,128]{3,2,1,0:T(8,128)} %get-tuple-element.284.refs_1_, f32[3,16,64,128]{3,2,1,0:T(8,128)} %get-tuple-element.287.refs_2_), custom_call_target="tpu_custom_call" | custom-call | flops 1572864 | bytes 6291456 | tf_op jit(solution)/shard_map/write_own/pallas_call | solution.py:321
  146.1 30.6 %collective-permute-done.20.refs_2_ = f32[3,16,64,128]{3,2,1,0:T(8,128)S(1)} collective-permute-done((f32[3,16,64,128]{3,2,1,0:T(8,128)}, f32[3,16,64,128]{3,2,1,0:T(8,128)S(1)}, u32[]{:S(2)}, u32[]{:S(2)}) %collective-permute-start.20) | collective-permute-done | bytes 1572896 | tf_op jit(solution)/shard_map/ppermute | solution.py:350
  176.7 4.8 %write_foreign.1 = f32[128,48,256]{2,1,0:T(8,128)} custom-call(s32[2]{0:T(128)S(1)} %get-tuple-element.860, f32[3,16,64,128]{3,2,1,0:T(8,128)} %collective-permute-done.18.refs_1_, f32[3,16,64,128]{3,2,1,0:T(8,128)S(1)} %collective-permute-done.20.refs_2_, f32[128,48,256]{2,1,0:T(8,128)} %write_own.1.refs_3_), custom_call_target="tpu_custom_call", output_to_operand_aliasing={{}: (3, {})} | custom-call | flops 1572864 | bytes 6291456 | tf_op jit(solution)/shard_map/write_foreign/pallas_call | solution.py:321
  (31 shorter events, 0.7 us)
Async XLA Ops:
  0.1 6.2 %copy-start.5 = (f32[128]{0:T(128)S(1)}, f32[128]{0:T(128)}, u32[]{:S(2)}) copy-start(f32[128]{0:T(128)} %param.15) | copy-start | bytes 1540
  3.3 31.5 %collective-permute-start.17 = (f32[2440,128]{1,0:T(8,128)}, f32[2440,128]{1,0:T(8,128)}, u32[]{:S(2)}, u32[]{:S(2)}) collective-permute-start(f32[2440,128]{1,0:T(8,128)} %turn_state.2), channel_id=1, source_target_pairs={{0,16},{8,24},{16,0},{24,8},{1,17},{9,25},{17,1},{25,9},{2,18},{10... | collective-permute-start | bytes 3747848 | tf_op jit(solution)/shard_map/ppermute | solution.py:350
  6.2 28.6 %copy-start.4 = (f32[128,16,256]{2,1,0:T(8,128)S(1)}, f32[128,16,256]{2,1,0:T(8,128)}, u32[]{:S(2)}) copy-start(f32[128,16,256]{2,1,0:T(8,128)} %param.13) | copy-start | bytes 6291460
  8.9 8.5 %collective-permute-start = (f32[384,128]{1,0:T(8,128)S(1)}, f32[384,128]{1,0:T(8,128)S(1)}, u32[]{:S(2)}, u32[]{:S(2)}) collective-permute-start(f32[384,128]{1,0:T(8,128)S(1)} %get-tuple-element.621), channel_id=1, source_target_pairs={{1,0},{2,1},{3,2},{4,3},{5,4},{6,5},{7,6},{0,7},{9,8},{10,9},{11,1... | collective-permute-start | bytes 589832 | tf_op jit(solution)/shard_map/while/body/ppermute | solution.py:368
  13.5 8.8 %collective-permute-start.1 = (f32[384,128]{1,0:T(8,128)S(1)}, f32[384,128]{1,0:T(8,128)S(1)}, u32[]{:S(2)}, u32[]{:S(2)}) collective-permute-start(f32[384,128]{1,0:T(8,128)S(1)} %get-tuple-element.622), channel_id=1, source_target_pairs={{0,1},{1,2},{2,3},{3,4},{4,5},{5,6},{6,7},{7,0},{8,9},{9,10},{10,1... | collective-permute-start | bytes 589832 | tf_op jit(solution)/shard_map/while/body/ppermute | solution.py:368
  28.6 39.7 %collective-permute-start.16 = (f32[3,16,64,128]{3,2,1,0:T(8,128)}, f32[3,16,64,128]{3,2,1,0:T(8,128)}, u32[]{:S(2)}, u32[]{:S(2)}) collective-permute-start(f32[3,16,64,128]{3,2,1,0:T(8,128)} %get-tuple-element.753), channel_id=1, source_target_pairs={{0,16},{8,24},{16,0},{24,8},{1,17},{9,25},{17,1},{25,9},{2,18},{10... | collective-permute-start | bytes 4718600 | tf_op jit(solution)/shard_map/ppermute | solution.py:350
  35.8 9.0 %collective-permute-start.4 = (f32[3,128,128]{2,1,0:T(8,128)S(1)}, f32[3,128,128]{2,1,0:T(8,128)S(1)}, u32[]{:S(2)}, u32[]{:S(2)}) collective-permute-start(f32[3,128,128]{2,1,0:T(8,128)S(1)} %bitcast.17), channel_id=1, source_target_pairs={{0,2},{1,3},{2,0},{3,1},{4,6},{5,7},{6,4},{7,5},{8,10},{9,11},{10,... | collective-permute-start | bytes 589832 | tf_op jit(solution)/shard_map/while/body/ppermute | solution.py:356
  38.0 10.3 %collective-permute-start.3 = (f32[3,128,128]{2,1,0:T(8,128)S(1)}, f32[3,128,128]{2,1,0:T(8,128)S(1)}, u32[]{:S(2)}, u32[]{:S(2)}) collective-permute-start(f32[3,128,128]{2,1,0:T(8,128)S(1)} %bitcast.18), channel_id=1, source_target_pairs={{0,1},{1,0},{2,3},{3,2},{4,5},{5,4},{6,7},{7,6},{8,9},{9,8},{10,11... | collective-permute-start | bytes 589832 | tf_op jit(solution)/shard_map/while/body/ppermute | solution.py:356
  39.5 16.8 %copy-start = (f32[128,3,16,256]{3,2,1,0:T(8,128)S(1)}, f32[128,3,16,256]{3,2,1,0:T(8,128)}, u32[]{:S(2)}) copy-start(f32[128,3,16,256]{3,2,1,0:T(8,128)} %get-tuple-element.745) | copy-start | bytes 18874372 | tf_op jit(solution)/shard_map/while
  42.3 11.9 %collective-permute-start.2 = (f32[384,128]{1,0:T(8,128)S(1)}, f32[384,128]{1,0:T(8,128)S(1)}, u32[]{:S(2)}, u32[]{:S(2)}) collective-permute-start(f32[384,128]{1,0:T(8,128)S(1)} %get-tuple-element.633), channel_id=1, source_target_pairs={{1,0},{2,1},{3,2},{4,3},{5,4},{6,5},{7,6},{0,7},{9,8},{10,9},{11,1... | collective-permute-start | bytes 589832 | tf_op jit(solution)/shard_map/while/body/ppermute | solution.py:368
  44.8 11.5 %collective-permute-start.5 = (f32[3,128,128]{2,1,0:T(8,128)S(1)}, f32[3,128,128]{2,1,0:T(8,128)S(1)}, u32[]{:S(2)}, u32[]{:S(2)}) collective-permute-start(f32[3,128,128]{2,1,0:T(8,128)S(1)} %collective-permute-done.4.refs_2_), channel_id=1, source_target_pairs={{0,1},{1,0},{2,3},{3,2},{4,5},{5,4},{6,7},{7,6},{8,9},{9,8},{10,11... | collective-permute-start | bytes 589832 | tf_op jit(solution)/shard_map/while/body/ppermute | solution.py:356
  44.8 11.5 %collective-permute-start.6 = (f32[384,128]{1,0:T(8,128)S(1)}, f32[384,128]{1,0:T(8,128)S(1)}, u32[]{:S(2)}, u32[]{:S(2)}) collective-permute-start(f32[384,128]{1,0:T(8,128)S(1)} %get-tuple-element.636), channel_id=1, source_target_pairs={{0,1},{1,2},{2,3},{3,4},{4,5},{5,6},{6,7},{7,0},{8,9},{9,10},{10,1... | collective-permute-start | bytes 589832 | tf_op jit(solution)/shard_map/while/body/ppermute | solution.py:368
  47.9 12.8 %copy-start.1 = (f32[2048,128]{1,0:T(8,128)}, f32[2048,128]{1,0:T(8,128)S(1)}, u32[]{:S(2)}) copy-start(f32[2048,128]{1,0:T(8,128)S(1)} %turn_state.3.refs_2_) | copy-start | bytes 3145732 | tf_op jit(solution)/shard_map/while
  60.7 6.0 %collective-permute-start.7 = (f32[3,16,128,128]{3,2,1,0:T(8,128)}, f32[3,16,128,128]{3,2,1,0:T(8,128)}, u32[]{:S(2)}, u32[]{:S(2)}) collective-permute-start(f32[3,16,128,128]{3,2,1,0:T(8,128)} %first_stencil.3), channel_id=1, source_target_pairs={{0,8},{8,0},{16,24},{24,16},{1,9},{9,1},{17,25},{25,17},{2,10},{10... | collective-permute-start | bytes 9437192 | tf_op jit(solution)/shard_map/while/body/ppermute | solution.py:353
  66.7 37.9 %collective-permute-start.19 = (f32[3,16,64,128]{3,2,1,0:T(8,128)}, f32[3,16,64,128]{3,2,1,0:T(8,128)}, u32[]{:S(2)}, u32[]{:S(2)}) collective-permute-start(f32[3,16,64,128]{3,2,1,0:T(8,128)} %get-tuple-element.789), channel_id=1, source_target_pairs={{0,16},{8,24},{16,0},{24,8},{1,17},{9,25},{17,1},{25,9},{2,18},{10... | collective-permute-start | bytes 4718600 | tf_op jit(solution)/shard_map/ppermute | solution.py:350
  68.3 3.6 %collective-permute-start.8 = (f32[3,16,64,128]{3,2,1,0:T(8,128)}, f32[3,16,64,128]{3,2,1,0:T(8,128)S(1)}, u32[]{:S(2)}, u32[]{:S(2)}) collective-permute-start(f32[3,16,64,128]{3,2,1,0:T(8,128)} %get-tuple-element.764.far), channel_id=1, source_target_pairs={{0,8},{8,0},{16,24},{24,16},{1,9},{9,1},{17,25},{25,17},{2,10},{10... | collective-permute-start | bytes 4718600 | tf_op jit(solution)/shard_map/while/body/ppermute | solution.py:353
  72.0 17.6 %copy-start.2 = (f32[2048,128]{1,0:T(8,128)S(1)}, f32[2048,128]{1,0:T(8,128)}, u32[]{:S(2)}) copy-start(f32[2048,128]{1,0:T(8,128)} %get-tuple-element.783.refs_3_) | copy-start | bytes 3145732 | tf_op jit(solution)/shard_map/while
  77.1 10.2 %collective-permute-start.10 = (f32[3,64,256]{2,1,0:T(8,128)S(1)}, f32[3,64,256]{2,1,0:T(8,128)S(1)}, u32[]{:S(2)}, u32[]{:S(2)}) collective-permute-start(f32[3,64,256]{2,1,0:T(8,128)S(1)} %get-tuple-element.652), channel_id=1, source_target_pairs={{0,1},{1,2},{2,3},{3,4},{4,5},{5,6},{6,7},{7,0},{8,9},{9,10},{10,1... | collective-permute-start | bytes 589832 | tf_op jit(solution)/shard_map/while/body/ppermute | solution.py:368
  78.6 10.9 %collective-permute-start.9 = (f32[3,64,256]{2,1,0:T(8,128)S(1)}, f32[3,64,256]{2,1,0:T(8,128)S(1)}, u32[]{:S(2)}, u32[]{:S(2)}) collective-permute-start(f32[3,64,256]{2,1,0:T(8,128)S(1)} %get-tuple-element.651), channel_id=1, source_target_pairs={{1,0},{2,1},{3,2},{4,3},{5,4},{6,5},{7,6},{0,7},{9,8},{10,9},{11,1... | collective-permute-start | bytes 589832 | tf_op jit(solution)/shard_map/while/body/ppermute | solution.py:368
  91.6 5.9 %collective-permute-start.11 = (f32[3,16,64,256]{3,2,1,0:T(8,128)S(1)}, f32[3,16,64,256]{3,2,1,0:T(8,128)}, u32[]{:S(2)}, u32[]{:S(2)}) collective-permute-start(f32[3,16,64,256]{3,2,1,0:T(8,128)S(1)} %second_stencil_0.1.own), channel_id=1, source_target_pairs={{0,8},{8,0},{16,24},{24,16},{1,9},{9,1},{17,25},{25,17},{2,10},{10... | collective-permute-start | bytes 9437192 | tf_op jit(solution)/shard_map/while/body/ppermute | solution.py:353
  103.5 42.6 %collective-permute-start.18 = (f32[3,16,64,128]{3,2,1,0:T(8,128)}, f32[3,16,64,128]{3,2,1,0:T(8,128)}, u32[]{:S(2)}, u32[]{:S(2)}) collective-permute-start(f32[3,16,64,128]{3,2,1,0:T(8,128)} %get-tuple-element.281), channel_id=1, source_target_pairs={{0,16},{8,24},{16,0},{24,8},{1,17},{9,25},{17,1},{25,9},{2,18},{10... | collective-permute-start | bytes 4718600 | tf_op jit(solution)/shard_map/ppermute | solution.py:350
  104.6 3.6 %collective-permute-start.12 = (f32[3,16,64,128]{3,2,1,0:T(8,128)}, f32[3,16,64,128]{3,2,1,0:T(8,128)S(1)}, u32[]{:S(2)}, u32[]{:S(2)}) collective-permute-start(f32[3,16,64,128]{3,2,1,0:T(8,128)} %get-tuple-element.800.far), channel_id=1, source_target_pairs={{0,8},{8,0},{16,24},{24,16},{1,9},{9,1},{17,25},{25,17},{2,10},{10... | collective-permute-start | bytes 4718600 | tf_op jit(solution)/shard_map/while/body/ppermute | solution.py:353
  108.3 17.8 %copy-start.3 = (f32[2048,128]{1,0:T(8,128)S(1)}, f32[2048,128]{1,0:T(8,128)}, u32[]{:S(2)}) copy-start(f32[2048,128]{1,0:T(8,128)} %get-tuple-element.819.refs_3_) | copy-start | bytes 3145732 | tf_op jit(solution)/shard_map/while
  113.4 7.8 %collective-permute-start.13 = (f32[3,64,256]{2,1,0:T(8,128)S(1)}, f32[3,64,256]{2,1,0:T(8,128)S(1)}, u32[]{:S(2)}, u32[]{:S(2)}) collective-permute-start(f32[3,64,256]{2,1,0:T(8,128)S(1)} %get-tuple-element.669), channel_id=1, source_target_pairs={{1,0},{2,1},{3,2},{4,3},{5,4},{6,5},{7,6},{0,7},{9,8},{10,9},{11,1... | collective-permute-start | bytes 589832 | tf_op jit(solution)/shard_map/while/body/ppermute | solution.py:368
  116.7 9.4 %collective-permute-start.14 = (f32[3,64,256]{2,1,0:T(8,128)S(1)}, f32[3,64,256]{2,1,0:T(8,128)S(1)}, u32[]{:S(2)}, u32[]{:S(2)}) collective-permute-start(f32[3,64,256]{2,1,0:T(8,128)S(1)} %get-tuple-element.670), channel_id=1, source_target_pairs={{0,1},{1,2},{2,3},{3,4},{4,5},{5,6},{6,7},{7,0},{8,9},{9,10},{10,1... | collective-permute-start | bytes 589832 | tf_op jit(solution)/shard_map/while/body/ppermute | solution.py:368
  128.2 5.9 %collective-permute-start.15 = (f32[3,16,64,256]{3,2,1,0:T(8,128)S(1)}, f32[3,16,64,256]{3,2,1,0:T(8,128)}, u32[]{:S(2)}, u32[]{:S(2)}) collective-permute-start(f32[3,16,64,256]{3,2,1,0:T(8,128)S(1)} %second_stencil_1.1.own), channel_id=1, source_target_pairs={{0,8},{8,0},{16,24},{24,16},{1,9},{9,1},{17,25},{25,17},{2,10},{10... | collective-permute-start | bytes 9437192 | tf_op jit(solution)/shard_map/while/body/ppermute | solution.py:353
  140.0 36.6 %collective-permute-start.20 = (f32[3,16,64,128]{3,2,1,0:T(8,128)}, f32[3,16,64,128]{3,2,1,0:T(8,128)S(1)}, u32[]{:S(2)}, u32[]{:S(2)}) collective-permute-start(f32[3,16,64,128]{3,2,1,0:T(8,128)} %get-tuple-element.286), channel_id=1, source_target_pairs={{0,16},{8,24},{16,0},{24,8},{1,17},{9,25},{17,1},{25,9},{2,18},{10... | collective-permute-start | bytes 4718600 | tf_op jit(solution)/shard_map/ppermute | solution.py:350

commit v7 on v6

--- a/solution.py
+++ b/solution.py
@@ -7,7 +7,7 @@
 
 SECTIONS = 2
 GROUPS = 2
-PARTS = 1
+PIECES_BACK = 3
 RATE_ROWS = 8
 PIECES = 4
 
@@ -62,24 +62,18 @@
     for z in range(nz):
         out[z * width : (z + 1) * width, :] = state[pl.ds(z, modes, stride=nz), :].T
     if len(refs) > 1:
-        rate, helm = refs[:2]
-        out[rows : rows + RATE_ROWS, :] = jnp.broadcast_to(rate[...], (RATE_ROWS, modes))
-        out[rows + RATE_ROWS :, :] = helm[...].reshape(-1, modes)
-
-
-def turn_state(where, state, foreign, rate=None, helm=None):
+        out[rows:, :] = jnp.broadcast_to(refs[0][...], (RATE_ROWS, modes))
+
+
+def turn_state(where, state, foreign, rate=None):
     modes, nz, nphi = state.shape
     half = nphi // 2
     side = (lambda i, w: (0, 1 - (w[0] >> 1))) if foreign else (lambda i, w: (0, w[0] >> 1))
     rows, more, more_specs = nz * half, (), []
-    if helm is not None:
-        comps = helm.shape[0]
-        rows += RATE_ROWS + comps * modes
-        more = (rate, helm)
-        more_specs = [
-            pl.BlockSpec((1, modes), lambda i, w: (0, 0)),
-            pl.BlockSpec((comps, modes, modes), lambda i, w: (0, w[1], 0)),
-        ]
+    if rate is not None:
+        rows += RATE_ROWS
+        more = (rate,)
+        more_specs = [pl.BlockSpec((1, modes), lambda i, w: (0, 0))]
     return pl.pallas_call(
         lambda *refs: state_kernel(*refs, modes=modes, nz=nz),
         out_shape=shape((rows, modes)),
@@ -230,10 +224,9 @@
 
 def map1(own, far, own_peer, far_peer, high, low, k):
     comps, nz, width, modes = far.shape
-    width //= PARTS
     rows, cols = high.shape[1:]
     here = pl.BlockSpec((1, nz, width, modes), lambda c: (c, 0, k, 0))
-    chunk = pl.BlockSpec((1, nz, width, modes), lambda c: (c, 0, k % PARTS, 0))
+    chunk = pl.BlockSpec((1, nz, width, modes), lambda c: (c, 0, 0, 0))
     helm = pl.BlockSpec((1, rows, cols), lambda c: (c, 0, 0))
     layer = pl.BlockSpec((1, width, cols), lambda c: (c, 0, 0))
     return pl.pallas_call(
@@ -276,32 +269,36 @@
     )(cur, after, before, state_own, state_far, rate)
 
 
-def map2_kernel(own, peer, high, low, *refs):
-    out_own, out_far = refs[-2:]
+def map2_kernel(own, peer, high, low, out_own, *outs_far):
     _, nz, width, cols = own.shape
     parts = [ref[0].reshape(nz * width, cols) for ref in (own, peer)]
     res = product(parts, high[0], low[0]).reshape(nz, width, cols)
     out_own[0] = res[:, :, : cols // 2]
-    out_far[0] = res[:, :, cols // 2 :]
-
-
-def map2(own, peer, high, low, k, base):
+    per = pl.num_programs(0) // len(outs_far)
+    for i, out in enumerate(outs_far):
+
+        @pl.when(pl.program_id(0) // per == i)
+        def _(out=out):
+            out[0] = res[:, :, cols // 2 :]
+
+
+def map2(own, peer, high, low, k, pieces):
     comps, nz, width, cols = own.shape
-    rows = high.shape[1]
+    rows, per = high.shape[1], comps // pieces
     chunk = pl.BlockSpec((1, nz, width, cols), lambda c: (c, 0, 0, 0))
     helm = pl.BlockSpec((1, rows, cols), lambda c: (c, 0, 0))
-    out = (comps, nz, width * PARTS, cols // 2)
+    block = (1, nz, width, cols // 2)
+    far = [pl.BlockSpec(block, lambda c, i=i: (jnp.clip(c - i * per, 0, per - 1), 0, 0, 0)) for i in range(pieces)]
     return pl.pallas_call(
         map2_kernel,
-        out_shape=[shape(out)] * 2,
+        out_shape=[shape((comps, *block[1:]))] + [shape((per, *block[1:]))] * pieces,
         grid=(comps,),
-        in_specs=[chunk, chunk, helm, helm] + [pl.BlockSpec(memory_space=pl.ANY)] * len(base),
-        out_specs=[pl.BlockSpec((1, nz, width, cols // 2), lambda c: (c, 0, k % PARTS, 0))] * 2,
-        input_output_aliases={4 + i: i for i in range(len(base))},
+        in_specs=[chunk, chunk, helm, helm],
+        out_specs=[pl.BlockSpec(block, lambda c: (c, 0, 0, 0)), *far],
         compiler_params=params(24),
         cost_estimate=cost(6 * comps * nz * width * rows * cols, 4 * comps * (nz * width * (rows + cols) + rows * cols)),
         name=f"map2_{k}",
-    )(own, peer, high, low, *base)
+    )(own, peer, high, low)
 
 
 def last_kernel(where, *refs, nz, chunks):
@@ -313,25 +310,31 @@
         rows[pl.ds(z, modes, stride=nz), :] = whole.T
 
 
-def write_half(where, pieces, nphi, foreign, base=None):
-    comps, nz, width, modes = pieces[0].shape
+def write_half(where, pieces, nphi, foreign, base=None, first=0):
+    count = min(p.shape[0] for p in pieces)
+    comps = max(p.shape[0] for p in pieces)
+    nz, _, modes = pieces[0].shape[1:]
     chunks = len(pieces)
-    side = (lambda c, w: (0, c, 1 - (w[0] >> 1))) if foreign else (lambda c, w: (0, c, w[0] >> 1))
+    side = (lambda w: 1 - (w[0] >> 1)) if foreign else (lambda w: w[0] >> 1)
     extra = () if base is None else (base,)
+
+    def spec(piece):
+        begin = first if piece.shape[0] > count else 0
+        return pl.BlockSpec((1, *piece.shape[1:]), lambda c, w: (begin + c, 0, 0, 0))
+
     return pl.pallas_call(
         lambda *refs: last_kernel(*refs, nz=nz, chunks=chunks),
         out_shape=shape((modes, comps * nz, nphi)),
         grid_spec=pltpu.PrefetchScalarGridSpec(
             num_scalar_prefetch=1,
-            grid=(comps,),
-            in_specs=[pl.BlockSpec((1,) + p.shape[1:], lambda c, w: (c, 0, 0, 0)) for p in pieces]
-            + [pl.BlockSpec(memory_space=pl.ANY)] * len(extra),
-            out_specs=pl.BlockSpec((modes, nz, nphi // 2), side),
+            grid=(count,),
+            in_specs=[spec(p) for p in pieces] + [pl.BlockSpec(memory_space=pl.ANY)] * len(extra),
+            out_specs=pl.BlockSpec((modes, nz, nphi // 2), lambda c, w: (0, first + c, side(w))),
         ),
         input_output_aliases={1 + chunks: 0} if extra else {},
         compiler_params=params(24),
-        cost_estimate=cost(comps * nz * modes * nphi, 4 * comps * nz * modes * nphi),
-        name="write_foreign" if foreign else "write_own",
+        cost_estimate=cost(count * nz * modes * nphi, 4 * count * nz * modes * nphi),
+        name=f"write_foreign_{first}" if foreign else "write_own",
     )(where, *pieces, *extra)
 
 
@@ -361,34 +364,36 @@
 
     once = 1 + (where[0] >> 8)
 
-    state_foreign = turn_state(where, state_axial, True, rate, helm_inverse)
+    piece = across(lax.dynamic_slice_in_dim(helm_inverse, lot * modes, modes, axis=1))
+    state_foreign = turn_state(where, state_axial, True, rate)
     state_far = across(state_foreign)
 
     def halos(leading, last):
         return lax.ppermute(leading, "col", down), lax.ppermute(last, "col", up)
 
-    def foreign_half(step, sent):
+    def foreign_half(step, _):
         here = where + (step >> 8)
         edges = halos(*edge_layers(here, cotangent, True))
-        return tuple(first_stencil(here, cotangent, state_foreign, *edges, rate, True, GROUPS))
+        blocks = [tied(piece, here)]
+        blocks += [hop(blocks[0], 1), hop(blocks[0], 2)]
+        blocks += [hop(blocks[2], 1)]
+        return (*first_stencil(here, cotangent, state_foreign, *edges, rate, True, GROUPS), *blocks[1:])
 
     chunk = (comps, nz, half // GROUPS, modes)
-    sent = lax.fori_loop(0, once, foreign_half, tuple(blanks(*[(chunk, F32)] * GROUPS)))
-    far = [across(tied(s, state_far) if k else s) for k, s in enumerate(sent)]
+    block = (comps, modes, modes)
+    sent = lax.fori_loop(0, once, foreign_half, tuple(blanks(*[(chunk, F32)] * GROUPS, *[(block, F32)] * (PIECES - 1))))
+    sent, blocks = sent[:GROUPS], [piece, *sent[GROUPS:]]
+    far = [across(tied(s, state_far) if k else tied(s, piece)) for k, s in enumerate(sent)]
 
     def own_half(step, carry):
         here = where + (step >> 8)
         edges = halos(*edge_layers(here, entry, False))
-        blocks = [tied(state_far, here)[nz * half + RATE_ROWS :].reshape(comps, modes, modes)]
-        blocks += [hop(blocks[0], 1), hop(blocks[0], 2)]
-        blocks += [hop(blocks[2], 1)]
-        edges = tuple(tied(e, *blocks[1:]) for e in edges)
         state_own = turn_state(here, state_axial, False)
         (own,) = first_stencil(here, entry, state_own, *edges, rate, False, 1)
         own_peer = beside(own)
         return (state_own, own, own_peer, *split_helm(here, helm_inverse, blocks))
 
-    entry = tied(cotangent, sent[0], state_far)
+    entry = tied(cotangent, sent[0])
     columns = (comps, nz, half, modes)
     helm = (comps, peers * modes, 2 * modes)
     state_own, own, own_peer, high, low = lax.fori_loop(
@@ -396,30 +401,25 @@
     )
 
     kept, back = [], []
-    for g in range(GROUPS):
-        group = range(g * PARTS, (g + 1) * PARTS)
-
-        def chains(_, carry, group=group):
-            here = carry[0]
-            there = beside(here)
-            moved = []
-            for k in group:
-                cur, leading, last = map1(own, here, own_peer, there, high, low, k)
-                moved.append((cur, *halos(leading, last)))
-            moved = lax.optimization_barrier(tuple(moved))
-            nxt = [second_stencil(*m, state_own, state_far, rate, k, half) for k, m in zip(group, moved)]
-            there = [beside(n) for n in nxt]
-            mine_theirs = ()
-            for k, n, t in zip(group, nxt, there):
-                mine_theirs = tuple(map2(n, t, high, low, k, mine_theirs))
-            return mine_theirs[::-1]
-
-        spare = tied(sent[g], kept[-1]) if kept else sent[g]
-        theirs, mine = lax.fori_loop(0, once, chains, (far[g], spare))
+    width = half // GROUPS
+    for k in range(GROUPS):
+        pieces = PIECES_BACK if k == GROUPS - 1 else 1
+
+        def chain(step, _, k=k, pieces=pieces):
+            here = tied(far[k], step)
+            cur, leading, last = map1(own, here, own_peer, beside(here), high, low, k)
+            nxt = second_stencil(cur, *halos(leading, last), state_own, state_far, rate, k, half)
+            return tuple(map2(nxt, beside(nxt), high, low, k, pieces))
+
+        spare = tied(sent[k], kept[-1]) if kept else sent[k]
+        parts = blanks(*[((comps // pieces, nz, width, modes), F32)] * pieces)
+        mine, *theirs = lax.fori_loop(0, once, chain, (spare, *parts))
         kept.append(mine)
-        back.append(across(theirs))
+        back.append([across(t) for t in theirs])
     out = write_half(where, kept, nphi, False)
-    out = write_half(where, back, nphi, True, out)
+    for i in range(PIECES_BACK):
+        group = [b[0] if len(b) == 1 else b[i] for b in back]
+        out = write_half(where, group, nphi, True, out, i * (comps // PIECES_BACK))
     return out.reshape(modes, comps, nz, nphi)
 
 

time: 182 us -> 180 us (0.989)
  waiting for transfers between devices: 91.1 us -> 85.5 us
    pallas_call x2 -> x4, Pallas kernels: 10.4 us -> 14.4 us  [write_half(): pl.pallas_call(lambda *refs: last_kernel(*refs, nz=nz, chunks=chunks), ou...]
    ppermute x8, starting transfers between devices: 17.3 us -> 14.4 us  [halos(): return (lax.ppermute(leading, 'col', down), lax.ppermute(last, 'col', up))]
    pallas_call x2, Pallas kernels: 4.11 us -> 1.52 us  [second_stencil(): pl.pallas_call(lambda *refs: second_kernel(*refs, k=k, half=half), out_sh...]
    ppermute x3, waiting for transfers between devices: 2.51 us -> 0.06 us  [hop(): return lax.ppermute(array, 'col', [(i, i ^ mask) for i in range(cols)])]
    ppermute x5 -> x8, starting transfers between devices: 6.79 us -> 9.24 us  [across(): return lax.ppermute(array, 'rad', [(i, i ^ 2) for i in range(peers)])]
    ppermute x5 -> x8, waiting for transfers between devices: 36.2 us -> 35.4 us  [across(): return lax.ppermute(array, 'rad', [(i, i ^ 2) for i in range(peers)])]
  transfers between devices with their start and end apart: 21 -> 24, of which waited for: 16 -> 19; matrix products, arithmetic and copies ran while one was open for 1% -> 0% of each run, Pallas kernels for 29% -> 34%
where the time goes in v7:
time: 180 us; the launch traced here: 179 us
  waiting for transfers between devices  85.5 us (48%)
  Pallas kernels  63.1 us (35%)
  starting transfers between devices  27.7 us (15%)
  local copies, waits for them, and re-layouts  2.63 us (1%)
    ppermute x8, waiting for transfers between devices, across(): return lax.ppermute(array, 'rad', [(i, i ^ 2) for i in range(peers)])  35.4 us
    ppermute x8, waiting for transfers between devices, halos(): return (lax.ppermute(leading, 'col', down), lax.ppermute(last, 'col', up))  30.3 us
    ppermute x5, waiting for transfers between devices, beside(): return lax.ppermute(array, 'rad', [(i, i ^ 1) for i in range(peers)])  19.8 us
    ppermute x8, starting transfers between devices, halos(): return (lax.ppermute(leading, 'col', down), lax.ppermute(last, 'col', up))  14.4 us
    pallas_call x4, Pallas kernels, write_half(): pl.pallas_call(lambda *refs: last_kernel(*refs, nz=nz, chunks=chunks), ou...  14.4 us
    pallas_call x2, Pallas kernels, map2(): pl.pallas_call(map2_kernel, out_shape=[shape((comps, *block[1:]))] + [sha...  12.4 us
    pallas_call x2, Pallas kernels, map1(): pl.pallas_call(map1_kernel, out_shape=[shape((comps, nz, width, cols)), s...  10.3 us
    ppermute x8, starting transfers between devices, across(): return lax.ppermute(array, 'rad', [(i, i ^ 2) for i in range(peers)])  9.24 us
  transfers between devices with their start and end apart: 24, of which 19 were waited for; matrix products, arithmetic and copies ran while one was open for 0% of the time, Pallas kernels for 34%

profile of v7, /device:TPU:0, one launch (start us, length us, event | category | flops | bytes accessed | tf_op | source)
XLA Modules:
  0.0 179.2 jit_solution(863493799309947502)
XLA Ops:
  0.9 3.0 %collective-permute-start.16 = (f32[3,128,128]{2,1,0:T(8,128)S(1)}, f32[3,128,128]{2,1,0:T(8,128)S(1)}, u32[]{:S(2)}, u32[]{:S(2)}) collective-permute-start(f32[3,128,128]{2,1,0:T(8,128)S(1)} %constant_dynamic-slice_fusion), channel_id=1, source_target_pairs={{0,16},{8,24},{16,0},{24,8},{1,17},{9,25},{17,1},{25,9},{2,18},{10... | collective-permute-start | bytes 589832 | tf_op jit(solution)/shard_map/ppermute | solution.py:353
  4.0 3.1 %turn_state.2 = f32[2056,128]{1,0:T(8,128)} custom-call(s32[2]{0:T(128)S(1)} %pad_add_fusion.refs_0_, f32[2048,256]{1,0:T(8,128)} %bitcast.18, f32[1,128]{1,0:T(1,128)} %bitcast.20), custom_call_target="tpu_custom_call" | custom-call | flops 263168 | bytes 2105344 | tf_op jit(solution)/shard_map/turn_state/pallas_call | solution.py:77
  7.2 1.7 collective-permute-done.16
  8.9 23.5 %while.64 = (s32[]{:T(128)}, f32[3,16,64,128]{3,2,1,0:T(8,128)}, f32[3,16,64,128]{3,2,1,0:T(8,128)}, f32[3,128,128]{2,1,0:T(8,128)}, f32[3,128,128]{2,1,0:T(8,12...) while((s32[]{:T(128)}, f32[3,16,64,128]{3,2,1,0:T(8,128)}, ...), condition=%wide.region_1.0_spmd, body=%wide.region_0.0_spmd.sunk | while | flops 9535493 | bytes 15729089 | solution.py:384
  8.9 1.8 %collective-permute-start.3 = (f32[3,128,128]{2,1,0:T(8,128)S(1)}, f32[3,128,128]{2,1,0:T(8,128)S(1)}, u32[]{:S(2)}, u32[]{:S(2)}) collective-permute-start(f32[3,128,128]{2,1,0:T(8,128)S(1)} %get-tuple-element.760), channel_id=1, source_target_pairs={{0,2},{1,3},{2,0},{3,1},{4,6},{5,7},{6,4},{7,5},{8,10},{9,11},{10,... | collective-permute-start | bytes 589832 | tf_op jit(solution)/shard_map/while/body/ppermute | solution.py:359
  10.7 2.6 %edge_layers.2 = (f32[384,128]{1,0:T(8,128)S(1)}, f32[384,128]{1,0:T(8,128)S(1)}) custom-call(s32[2]{0:T(128)S(1)} %broadcast_add_fusion.4.refs_0_, f32[6144,256]{1,0:T(8,128)} %bitcast.14), custom_call_target="tpu_custom_call" | custom-call | flops 98304 | bytes 3145728 | tf_op jit(solution)/shard_map/while/body/edge_layers/pallas_call | solution.py:103
  13.3 3.5 %collective-permute-start = (f32[384,128]{1,0:T(8,128)S(1)}, f32[384,128]{1,0:T(8,128)S(1)}, u32[]{:S(2)}, u32[]{:S(2)}) collective-permute-start(f32[384,128]{1,0:T(8,128)S(1)} %get-tuple-element.756), channel_id=1, source_target_pairs={{1,0},{2,1},{3,2},{4,3},{5,4},{6,5},{7,6},{0,7},{9,8},{10,9},{11,1... | collective-permute-start | bytes 589832 | tf_op jit(solution)/shard_map/while/body/ppermute | solution.py:372
  16.7 1.0 collective-permute-start.2
  17.8 1.0 collective-permute-start.4
  18.8 1.5 collective-permute-done.refs_3_
  20.2 4.9 %collective-permute-done.1.refs_4_ = f32[384,128]{1,0:T(8,128)S(1)} collective-permute-done((f32[384,128]{1,0:T(8,128)S(1)}, f32[384,128]{1,0:T(8,128)S(1)}, u32[]{:S(2)}, u32[]{:S(2)}) %collective-permute-start.1) | collective-permute-done | bytes 196640 | tf_op jit(solution)/shard_map/while/body/ppermute | solution.py:372
  25.2 6.4 %first_stencil.2 = (f32[3,16,64,128]{3,2,1,0:T(8,128)}, f32[3,16,64,128]{3,2,1,0:T(8,128)}) custom-call(s32[2]{0:T(128)S(1)} %broadcast_add_fusion.4.refs_0_, f32[6144,256]{1,0:T(8,128)} %bitcast.15, f32[2056,128]{1,0:T(8,128)} %get-tuple-element.847.refs_2_, f32[384,128]{1,0:T(8,128)S(1)} %collective-permute-done.refs_3_, ...), custom_call_target="tpu_custom_call" | custom-call | flops 9437184 | bytes 6291456 | tf_op jit(solution)/shard_map/while/body/first_stencil/pallas_call | solution.py:153
  32.4 2.0 %collective-permute-start.17 = (f32[3,16,64,128]{3,2,1,0:T(8,128)}, f32[3,16,64,128]{3,2,1,0:T(8,128)}, u32[]{:S(2)}, u32[]{:S(2)}) collective-permute-start(f32[3,16,64,128]{3,2,1,0:T(8,128)} %get-tuple-element.329), channel_id=1, source_target_pairs={{0,16},{8,24},{16,0},{24,8},{1,17},{9,25},{17,1},{25,9},{2,18},{10... | collective-permute-start | bytes 4718600 | tf_op jit(solution)/shard_map/ppermute | solution.py:353
  35.4 23.5 %while.65 = (s32[]{:T(128)}, f32[2048,128]{1,0:T(8,128)}, f32[3,16,128,128]{3,2,1,0:T(8,128)}, f32[3,16,128,128]{3,2,1,0:T(8,128)}, bf16[3,512,256]{2,1,0:T(8,12...) while((s32[]{:T(128)}, f32[2048,128]{1,0:T(8,128)}, ...), condition=%wide.region_3.0_spmd, body=%wide.region_2.0_spmd.sunk | while | flops 10584069 | bytes 70779280 | solution.py:399
  35.4 2.8 %edge_layers.3 = (f32[384,128]{1,0:T(8,128)S(1)}, f32[384,128]{1,0:T(8,128)S(1)}) custom-call(s32[2]{0:T(128)S(1)} %broadcast_add_fusion.5.refs_0_.where, f32[6144,256]{1,0:T(8,128)} %bitcast.16), custom_call_target="tpu_custom_call" | custom-call | flops 98304 | bytes 3145728 | tf_op jit(solution)/shard_map/while/body/edge_layers/pallas_call | solution.py:103
  38.2 3.8 %collective-permute-start.5 = (f32[384,128]{1,0:T(8,128)S(1)}, f32[384,128]{1,0:T(8,128)S(1)}, u32[]{:S(2)}, u32[]{:S(2)}) collective-permute-start(f32[384,128]{1,0:T(8,128)S(1)} %get-tuple-element.772), channel_id=1, source_target_pairs={{1,0},{2,1},{3,2},{4,3},{5,4},{6,5},{7,6},{0,7},{9,8},{10,9},{11,1... | collective-permute-start | bytes 589832 | tf_op jit(solution)/shard_map/while/body/ppermute | solution.py:372
  42.0 2.1 %turn_state.3.refs_2_ = f32[2048,128]{1,0:T(8,128)S(1)} custom-call(s32[2]{0:T(128)S(1)} %broadcast_add_fusion.5.refs_0_.where, f32[2048,256]{1,0:T(8,128)} %bitcast.19), custom_call_target="tpu_custom_call" | custom-call | flops 262144 | bytes 2097152 | tf_op jit(solution)/shard_map/while/body/turn_state/pallas_call | solution.py:77
  44.1 1.0 collective-permute-done.5.refs_3_
  45.1 5.2 %collective-permute-done.6.refs_4_ = f32[384,128]{1,0:T(8,128)S(1)} collective-permute-done((f32[384,128]{1,0:T(8,128)S(1)}, f32[384,128]{1,0:T(8,128)S(1)}, u32[]{:S(2)}, u32[]{:S(2)}) %collective-permute-start.6) | collective-permute-done | bytes 196640 | tf_op jit(solution)/shard_map/while/body/ppermute | solution.py:372
  50.3 2.7 %first_stencil.3 = f32[3,16,128,128]{3,2,1,0:T(8,128)S(1)} custom-call(s32[2]{0:T(128)S(1)} %broadcast_add_fusion.5.refs_0_.where, f32[6144,256]{1,0:T(8,128)S(1)} %bitcast.17, f32[2048,128]{1,0:T(8,128)S(1)} %turn_state.3.refs_2_, f32[384,128]{1,0:T(8,128)S(1)} %collective-permute-done.5.refs_3_, f32[384,128]{1,0:T(8,128)S(1)} %collective-permute-done.6.refs_4_, ...), custom_call_target="tpu_custom_call" | custom-call | flops 9437184 | bytes 6291456 | tf_op jit(solution)/shard_map/while/body/first_stencil/pallas_call | solution.py:153
  53.1 4.8 %split_helm.1 = (bf16[3,512,256]{2,1,0:T(8,128)(2,1)}, bf16[3,512,256]{2,1,0:T(8,128)(2,1)}) custom-call(s32[2]{0:T(128)S(1)} %broadcast_add_fusion.5.refs_0_.where, f32[3,512,128]{2,1,0:T(8,128)} %get-tuple-element.899.own, f32[3,128,128]{2,1,0:T(8,128)S(1)} %get-tuple-element.900.refs_0_, f32[3,128,128]{2,1,0:T(8,128)S(1)} %get-tuple-element.901.refs_1_, ...), custom_call_target="tpu_custom_call" | custom-call | flops 786432 | bytes 3145728 | tf_op jit(solution)/shard_map/while/body/split_helm/pallas_call | solution.py:199
  58.9 11.1 %collective-permute-done.17 = f32[3,16,64,128]{3,2,1,0:T(8,128)} collective-permute-done((f32[3,16,64,128]{3,2,1,0:T(8,128)}, f32[3,16,64,128]{3,2,1,0:T(8,128)}, u32[]{:S(2)}, u32[]{:S(2)}) %collective-permute-start.17) | collective-permute-done | bytes 1572896 | tf_op jit(solution)/shard_map/ppermute | solution.py:353
  70.0 34.7 %while.66 = (s32[]{:T(128)}, f32[3,16,64,128]{3,2,1,0:T(8,128)}, f32[3,16,64,128]{3,2,1,0:T(8,128)}, s32[]{:T(128)}, f32[3,16,64,128]{3,2,1,0:T(8,128)}, /*index...) while((s32[]{:T(128)}, f32[3,16,64,128]{3,2,1,0:T(8,128)}, ...), condition=%wide.region_5.0_spmd, body=%wide.region_4.0_spmd.sunk | while | flops 4841275392 | bytes 57164116 | solution.py:416
  70.0 3.6 %collective-permute-done.8.far_peer = f32[3,16,64,128]{3,2,1,0:T(8,128)S(1)} collective-permute-done((f32[3,16,64,128]{3,2,1,0:T(8,128)}, f32[3,16,64,128]{3,2,1,0:T(8,128)S(1)}, u32[]{:S(2)}, u32[]{:S(2)}) %collective-permute-start.8) | collective-permute-done | bytes 1572896 | tf_op jit(solution)/shard_map/while/body/ppermute | solution.py:356
  73.6 5.2 %map1_0.1 = (f32[3,16,64,256]{3,2,1,0:T(8,128)S(1)}, f32[3,64,256]{2,1,0:T(8,128)S(1)}, f32[3,64,256]{2,1,0:T(8,128)S(1)}) custom-call(f32[3,16,128,128]{3,2,1,0:T(8,128)} %get-tuple-element.937.own, f32[3,16,64,128]{3,2,1,0:T(8,128)} %get-tuple-element.786.far, f32[3,16,128,128]{3,2,1,0:T(8,128)} %get-tuple-element.938.own_peer, ...), custom_call_target="tpu_custom_call" | custom-call | flops 2415919104 | bytes 11010048 | tf_op jit(solution)/shard_map/while/body/map1_0/pallas_call | solution.py:232
  78.8 2.2 %collective-permute-start.10 = (f32[3,64,256]{2,1,0:T(8,128)S(1)}, f32[3,64,256]{2,1,0:T(8,128)S(1)}, u32[]{:S(2)}, u32[]{:S(2)}) collective-permute-start(f32[3,64,256]{2,1,0:T(8,128)S(1)} %get-tuple-element.789), channel_id=1, source_target_pairs={{0,1},{1,2},{2,3},{3,4},{4,5},{5,6},{6,7},{7,0},{8,9},{9,10},{10,1... | collective-permute-start | bytes 589832 | tf_op jit(solution)/shard_map/while/body/ppermute | solution.py:372
  81.0 2.6 %collective-permute-start.9 = (f32[3,64,256]{2,1,0:T(8,128)S(1)}, f32[3,64,256]{2,1,0:T(8,128)S(1)}, u32[]{:S(2)}, u32[]{:S(2)}) collective-permute-start(f32[3,64,256]{2,1,0:T(8,128)S(1)} %get-tuple-element.788), channel_id=1, source_target_pairs={{1,0},{2,1},{3,2},{4,3},{5,4},{6,5},{7,6},{0,7},{9,8},{10,9},{11,1... | collective-permute-start | bytes 589832 | tf_op jit(solution)/shard_map/while/body/ppermute | solution.py:372
  83.6 6.1 %collective-permute-done.10.refs_2_ = f32[3,64,256]{2,1,0:T(8,128)S(1)} collective-permute-done((f32[3,64,256]{2,1,0:T(8,128)S(1)}, f32[3,64,256]{2,1,0:T(8,128)S(1)}, u32[]{:S(2)}, u32[]{:S(2)}) %collective-permute-start.10) | collective-permute-done | bytes 196640 | tf_op jit(solution)/shard_map/while/body/ppermute | solution.py:372
  89.7 2.2 %collective-permute-done.9.refs_1_ = f32[3,64,256]{2,1,0:T(8,128)S(1)} collective-permute-done((f32[3,64,256]{2,1,0:T(8,128)S(1)}, f32[3,64,256]{2,1,0:T(8,128)S(1)}, u32[]{:S(2)}, u32[]{:S(2)}) %collective-permute-start.9) | collective-permute-done | bytes 196640 | tf_op jit(solution)/shard_map/while/body/ppermute | solution.py:372
  92.7 5.8 %collective-permute-done.11.peer = f32[3,16,64,256]{3,2,1,0:T(8,128)} collective-permute-done((f32[3,16,64,256]{3,2,1,0:T(8,128)S(1)}, f32[3,16,64,256]{3,2,1,0:T(8,128)}, u32[]{:S(2)}, u32[]{:S(2)}) %collective-permute-start.11) | collective-permute-done | bytes 3145760 | tf_op jit(solution)/shard_map/while/body/ppermute | solution.py:356
  98.5 6.1 %map2_0.1 = (f32[3,16,64,128]{3,2,1,0:T(8,128)}, f32[3,16,64,128]{3,2,1,0:T(8,128)}) custom-call(f32[3,16,64,256]{3,2,1,0:T(8,128)S(1)} %second_stencil_0.1.own, f32[3,16,64,256]{3,2,1,0:T(8,128)} %collective-permute-done.11.peer, bf16[3,512,256]{2,1,0:T(8,128)(2,1)} %get-tuple-element.939.high, bf16[3,512,256]{2,1,0:T(8,128)(2,1)} %get-tuple-element.940.low), custom_call_target="tpu_custom_call" | custom-call | flops 2415919104 | bytes 11010048 | tf_op jit(solution)/shard_map/while/body/map2_0/pallas_call | solution.py:292
  104.7 1.5 collective-permute-start.19
  106.2 33.4 %while.67 = (s32[]{:T(128)}, f32[3,16,64,128]{3,2,1,0:T(8,128)}, f32[1,16,64,128]{3,2,1,0:T(8,128)}, f32[1,16,64,128]{3,2,1,0:T(8,128)}, f32[1,16,64,128]{3,2,1,...) while((s32[]{:T(128)}, f32[3,16,64,128]{3,2,1,0:T(8,128)}, ...), condition=%wide.region_7.0_spmd, body=%wide.region_6.0_spmd.sunk | while | flops 4841275392 | bytes 57164132 | solution.py:416
  106.2 3.6 %collective-permute-done.12.far_peer = f32[3,16,64,128]{3,2,1,0:T(8,128)S(1)} collective-permute-done((f32[3,16,64,128]{3,2,1,0:T(8,128)}, f32[3,16,64,128]{3,2,1,0:T(8,128)S(1)}, u32[]{:S(2)}, u32[]{:S(2)}) %collective-permute-start.12) | collective-permute-done | bytes 1572896 | tf_op jit(solution)/shard_map/while/body/ppermute | solution.py:356
  109.8 5.2 %map1_1.1 = (f32[3,16,64,256]{3,2,1,0:T(8,128)S(1)}, f32[3,64,256]{2,1,0:T(8,128)S(1)}, f32[3,64,256]{2,1,0:T(8,128)S(1)}) custom-call(f32[3,16,128,128]{3,2,1,0:T(8,128)} %get-tuple-element.982.own, f32[3,16,64,128]{3,2,1,0:T(8,128)} %get-tuple-element.802.far, f32[3,16,128,128]{3,2,1,0:T(8,128)} %get-tuple-element.983.own_peer, ...), custom_call_target="tpu_custom_call" | custom-call | flops 2415919104 | bytes 11010048 | tf_op jit(solution)/shard_map/while/body/map1_1/pallas_call | solution.py:232
  115.0 2.4 %collective-permute-start.13 = (f32[3,64,256]{2,1,0:T(8,128)S(1)}, f32[3,64,256]{2,1,0:T(8,128)S(1)}, u32[]{:S(2)}, u32[]{:S(2)}) collective-permute-start(f32[3,64,256]{2,1,0:T(8,128)S(1)} %get-tuple-element.804), channel_id=1, source_target_pairs={{1,0},{2,1},{3,2},{4,3},{5,4},{6,5},{7,6},{0,7},{9,8},{10,9},{11,1... | collective-permute-start | bytes 589832 | tf_op jit(solution)/shard_map/while/body/ppermute | solution.py:372
  117.4 4.6 %collective-permute-done.13.refs_1_ = f32[3,64,256]{2,1,0:T(8,128)S(1)} collective-permute-done((f32[3,64,256]{2,1,0:T(8,128)S(1)}, f32[3,64,256]{2,1,0:T(8,128)S(1)}, u32[]{:S(2)}, u32[]{:S(2)}) %collective-permute-start.13) | collective-permute-done | bytes 196640 | tf_op jit(solution)/shard_map/while/body/ppermute | solution.py:372
  122.0 4.7 %collective-permute-done.14.refs_2_ = f32[3,64,256]{2,1,0:T(8,128)S(1)} collective-permute-done((f32[3,64,256]{2,1,0:T(8,128)S(1)}, f32[3,64,256]{2,1,0:T(8,128)S(1)}, u32[]{:S(2)}, u32[]{:S(2)}) %collective-permute-start.14) | collective-permute-done | bytes 196640 | tf_op jit(solution)/shard_map/while/body/ppermute | solution.py:372
  127.6 5.8 %collective-permute-done.15.peer = f32[3,16,64,256]{3,2,1,0:T(8,128)} collective-permute-done((f32[3,16,64,256]{3,2,1,0:T(8,128)S(1)}, f32[3,16,64,256]{3,2,1,0:T(8,128)}, u32[]{:S(2)}, u32[]{:S(2)}) %collective-permute-start.15) | collective-permute-done | bytes 3145760 | tf_op jit(solution)/shard_map/while/body/ppermute | solution.py:356
  133.4 6.2 %map2_1.1 = (f32[3,16,64,128]{3,2,1,0:T(8,128)}, f32[1,16,64,128]{3,2,1,0:T(8,128)}, f32[1,16,64,128]{3,2,1,0:T(8,128)}, f32[1,16,64,128]{3,2,1,0:T(8,128)}) custom-call(f32[3,16,64,256]{3,2,1,0:T(8,128)S(1)} %second_stencil_1.1.own, f32[3,16,64,256]{3,2,1,0:T(8,128)} %collective-permute-done.15.peer, bf16[3,512,256]{2,1,0:T(8,128)(2,1)} %get-tuple-element.984.high, ...), custom_call_target="tpu_custom_call" | custom-call | flops 2415919104 | bytes 11010048 | tf_op jit(solution)/shard_map/while/body/map2_1/pallas_call | solution.py:292
  140.1 1.5 collective-permute-start.22
  142.2 5.5 %write_own.1.refs_3_ = f32[128,48,256]{2,1,0:T(8,128)} custom-call(s32[2]{0:T(128)S(1)} %get-tuple-element.1037, f32[3,16,64,128]{3,2,1,0:T(8,128)} %get-tuple-element.346.refs_1_, f32[3,16,64,128]{3,2,1,0:T(8,128)} %get-tuple-element.355.refs_2_), custom_call_target="tpu_custom_call" | custom-call | flops 1572864 | bytes 6291456 | tf_op jit(solution)/shard_map/write_own/pallas_call | solution.py:325
  147.7 6.9 %collective-permute-done.23.refs_2_ = f32[1,16,64,128]{3,2,1,0:T(8,128)S(1)} collective-permute-done((f32[1,16,64,128]{3,2,1,0:T(8,128)}, f32[1,16,64,128]{3,2,1,0:T(8,128)S(1)}, u32[]{:S(2)}, u32[]{:S(2)}) %collective-permute-start.23) | collective-permute-done | bytes 524320 | tf_op jit(solution)/shard_map/ppermute | solution.py:353
  154.6 3.0 %write_foreign_0.1.refs_3_ = f32[128,48,256]{2,1,0:T(8,128)} custom-call(s32[2]{0:T(128)S(1)} %get-tuple-element.1037, f32[3,16,64,128]{3,2,1,0:T(8,128)} %collective-permute-done.19.refs_1_, f32[1,16,64,128]{3,2,1,0:T(8,128)S(1)} %collective-permute-done.23.refs_2_, f32[128,48,256]{2,1,0:T(8,128)} %write_own.1.refs_3_), custom_call_target="tpu_custom_call", output_to_operand_aliasing={{}: (3, {})} | custom-call | flops 524288 | bytes 2097152 | tf_op jit(solution)/shard_map/write_foreign_0/pallas_call | solution.py:325
  157.6 8.3 %collective-permute-done.22.refs_2_ = f32[1,16,64,128]{3,2,1,0:T(8,128)S(1)} collective-permute-done((f32[1,16,64,128]{3,2,1,0:T(8,128)}, f32[1,16,64,128]{3,2,1,0:T(8,128)S(1)}, u32[]{:S(2)}, u32[]{:S(2)}) %collective-permute-start.22) | collective-permute-done | bytes 524320 | tf_op jit(solution)/shard_map/ppermute | solution.py:353
  165.8 3.0 %write_foreign_1.1.refs_3_ = f32[128,48,256]{2,1,0:T(8,128)} custom-call(s32[2]{0:T(128)S(1)} %get-tuple-element.1037, f32[3,16,64,128]{3,2,1,0:T(8,128)} %collective-permute-done.19.refs_1_, f32[1,16,64,128]{3,2,1,0:T(8,128)S(1)} %collective-permute-done.22.refs_2_, f32[128,48,256]{2,1,0:T(8,128)} %write_foreign_0.1.refs_3_), custom_call_target="tpu_custom_call", output_to_operand_aliasing={{}: (3, {})} | custom-call | flops 524288 | bytes 2097152 | tf_op jit(solution)/shard_map/write_foreign_1/pallas_call | solution.py:325
  168.8 7.4 %collective-permute-done.21.refs_2_ = f32[1,16,64,128]{3,2,1,0:T(8,128)S(1)} collective-permute-done((f32[1,16,64,128]{3,2,1,0:T(8,128)}, f32[1,16,64,128]{3,2,1,0:T(8,128)S(1)}, u32[]{:S(2)}, u32[]{:S(2)}) %collective-permute-start.21) | collective-permute-done | bytes 524320 | tf_op jit(solution)/shard_map/ppermute | solution.py:353
  176.2 3.0 %write_foreign_2.1 = f32[128,48,256]{2,1,0:T(8,128)} custom-call(s32[2]{0:T(128)S(1)} %get-tuple-element.1037, f32[3,16,64,128]{3,2,1,0:T(8,128)} %collective-permute-done.19.refs_1_, f32[1,16,64,128]{3,2,1,0:T(8,128)S(1)} %collective-permute-done.21.refs_2_, f32[128,48,256]{2,1,0:T(8,128)} %write_foreign_1.1.refs_3_), custom_call_target="tpu_custom_call", output_to_operand_aliasing={{}: (3, {})} | custom-call | flops 524288 | bytes 2097152 | tf_op jit(solution)/shard_map/write_foreign_2/pallas_call | solution.py:325
  (55 shorter events, 6.7 us)
Async XLA Ops:
  0.9 7.9 %collective-permute-start.16 = (f32[3,128,128]{2,1,0:T(8,128)S(1)}, f32[3,128,128]{2,1,0:T(8,128)S(1)}, u32[]{:S(2)}, u32[]{:S(2)}) collective-permute-start(f32[3,128,128]{2,1,0:T(8,128)S(1)} %constant_dynamic-slice_fusion), channel_id=1, source_target_pairs={{0,16},{8,24},{16,0},{24,8},{1,17},{9,25},{17,1},{25,9},{2,18},{10... | collective-permute-start | bytes 589832 | tf_op jit(solution)/shard_map/ppermute | solution.py:353
  4.0 4.8 %copy-start.12 = (f32[128]{0:T(128)S(1)}, f32[128]{0:T(128)}, u32[]{:S(2)}) copy-start(f32[128]{0:T(128)} %param.15) | copy-start | bytes 1540
  7.2 27.2 %collective-permute-start.18 = (f32[2056,128]{1,0:T(8,128)}, f32[2056,128]{1,0:T(8,128)S(1)}, u32[]{:S(2)}, u32[]{:S(2)}) collective-permute-start(f32[2056,128]{1,0:T(8,128)} %turn_state.2), channel_id=1, source_target_pairs={{0,16},{8,24},{16,0},{24,8},{1,17},{9,25},{17,1},{25,9},{2,18},{10... | collective-permute-start | bytes 3158024 | tf_op jit(solution)/shard_map/ppermute | solution.py:353
  8.9 8.9 %collective-permute-start.3 = (f32[3,128,128]{2,1,0:T(8,128)S(1)}, f32[3,128,128]{2,1,0:T(8,128)S(1)}, u32[]{:S(2)}, u32[]{:S(2)}) collective-permute-start(f32[3,128,128]{2,1,0:T(8,128)S(1)} %get-tuple-element.760), channel_id=1, source_target_pairs={{0,2},{1,3},{2,0},{3,1},{4,6},{5,7},{6,4},{7,5},{8,10},{9,11},{10,... | collective-permute-start | bytes 589832 | tf_op jit(solution)/shard_map/while/body/ppermute | solution.py:359
  13.3 7.0 %collective-permute-start = (f32[384,128]{1,0:T(8,128)S(1)}, f32[384,128]{1,0:T(8,128)S(1)}, u32[]{:S(2)}, u32[]{:S(2)}) collective-permute-start(f32[384,128]{1,0:T(8,128)S(1)} %get-tuple-element.756), channel_id=1, source_target_pairs={{1,0},{2,1},{3,2},{4,3},{5,4},{6,5},{7,6},{0,7},{9,8},{10,9},{11,1... | collective-permute-start | bytes 589832 | tf_op jit(solution)/shard_map/while/body/ppermute | solution.py:372
  16.7 8.4 %collective-permute-start.1 = (f32[384,128]{1,0:T(8,128)S(1)}, f32[384,128]{1,0:T(8,128)S(1)}, u32[]{:S(2)}, u32[]{:S(2)}) collective-permute-start(f32[384,128]{1,0:T(8,128)S(1)} %get-tuple-element.757), channel_id=1, source_target_pairs={{0,1},{1,2},{2,3},{3,4},{4,5},{5,6},{6,7},{7,0},{8,9},{9,10},{10,1... | collective-permute-start | bytes 589832 | tf_op jit(solution)/shard_map/while/body/ppermute | solution.py:372
  16.7 14.8 %collective-permute-start.2 = (f32[3,128,128]{2,1,0:T(8,128)S(1)}, f32[3,128,128]{2,1,0:T(8,128)S(1)}, u32[]{:S(2)}, u32[]{:S(2)}) collective-permute-start(f32[3,128,128]{2,1,0:T(8,128)S(1)} %get-tuple-element.760), channel_id=1, source_target_pairs={{0,1},{1,0},{2,3},{3,2},{4,5},{5,4},{6,7},{7,6},{8,9},{9,8},{10,11... | collective-permute-start | bytes 589832 | tf_op jit(solution)/shard_map/while/body/ppermute | solution.py:359
  17.8 13.8 %copy-start.10 = (f32[3,128,128]{2,1,0:T(8,128)}, f32[3,128,128]{2,1,0:T(8,128)S(1)}, u32[]{:S(2)}) copy-start(f32[3,128,128]{2,1,0:T(8,128)S(1)} %collective-permute-done.3) | copy-start | bytes 589828 | tf_op jit(solution)/shard_map/while
  17.8 13.9 %collective-permute-start.4 = (f32[3,128,128]{2,1,0:T(8,128)S(1)}, f32[3,128,128]{2,1,0:T(8,128)S(1)}, u32[]{:S(2)}, u32[]{:S(2)}) collective-permute-start(f32[3,128,128]{2,1,0:T(8,128)S(1)} %collective-permute-done.3), channel_id=1, source_target_pairs={{0,1},{1,0},{2,3},{3,2},{4,5},{5,4},{6,7},{7,6},{8,9},{9,8},{10,11... | collective-permute-start | bytes 589832 | tf_op jit(solution)/shard_map/while/body/ppermute | solution.py:359
  31.6 0.7 copy-start.8
  31.6 0.7 copy-start.11
  32.4 2.1 %copy-start.9 = (f32[3,128,128]{2,1,0:T(8,128)S(1)}, f32[3,128,128]{2,1,0:T(8,128)}, u32[]{:S(2)}) copy-start(f32[3,128,128]{2,1,0:T(8,128)} %get-tuple-element.865) | copy-start | bytes 589828
  32.4 37.6 %collective-permute-start.17 = (f32[3,16,64,128]{3,2,1,0:T(8,128)}, f32[3,16,64,128]{3,2,1,0:T(8,128)}, u32[]{:S(2)}, u32[]{:S(2)}) collective-permute-start(f32[3,16,64,128]{3,2,1,0:T(8,128)} %get-tuple-element.329), channel_id=1, source_target_pairs={{0,16},{8,24},{16,0},{24,8},{1,17},{9,25},{17,1},{25,9},{2,18},{10... | collective-permute-start | bytes 4718600 | tf_op jit(solution)/shard_map/ppermute | solution.py:353
  34.4 1.0 copy-start.5
  34.4 71.8 %collective-permute-start.20 = (f32[3,16,64,128]{3,2,1,0:T(8,128)}, f32[3,16,64,128]{3,2,1,0:T(8,128)}, u32[]{:S(2)}, u32[]{:S(2)}) collective-permute-start(f32[3,16,64,128]{3,2,1,0:T(8,128)} %get-tuple-element.351), channel_id=1, source_target_pairs={{0,16},{8,24},{16,0},{24,8},{1,17},{9,25},{17,1},{25,9},{2,18},{10... | collective-permute-start | bytes 4718600 | tf_op jit(solution)/shard_map/ppermute | solution.py:353
  35.4 14.9 %copy-start = (f32[128,3,16,256]{3,2,1,0:T(8,128)S(1)}, f32[128,3,16,256]{3,2,1,0:T(8,128)}, u32[]{:S(2)}) copy-start(f32[128,3,16,256]{3,2,1,0:T(8,128)} %get-tuple-element.897) | copy-start | bytes 18874372 | tf_op jit(solution)/shard_map/while
  38.2 6.9 %collective-permute-start.5 = (f32[384,128]{1,0:T(8,128)S(1)}, f32[384,128]{1,0:T(8,128)S(1)}, u32[]{:S(2)}, u32[]{:S(2)}) collective-permute-start(f32[384,128]{1,0:T(8,128)S(1)} %get-tuple-element.772), channel_id=1, source_target_pairs={{1,0},{2,1},{3,2},{4,3},{5,4},{6,5},{7,6},{0,7},{9,8},{10,9},{11,1... | collective-permute-start | bytes 589832 | tf_op jit(solution)/shard_map/while/body/ppermute | solution.py:372
  42.0 8.4 %collective-permute-start.6 = (f32[384,128]{1,0:T(8,128)S(1)}, f32[384,128]{1,0:T(8,128)S(1)}, u32[]{:S(2)}, u32[]{:S(2)}) collective-permute-start(f32[384,128]{1,0:T(8,128)S(1)} %get-tuple-element.773), channel_id=1, source_target_pairs={{0,1},{1,2},{2,3},{3,4},{4,5},{5,6},{6,7},{7,0},{8,9},{9,10},{10,1... | collective-permute-start | bytes 589832 | tf_op jit(solution)/shard_map/while/body/ppermute | solution.py:372
  44.1 8.9 %copy-start.2 = (f32[2048,128]{1,0:T(8,128)}, f32[2048,128]{1,0:T(8,128)S(1)}, u32[]{:S(2)}) copy-start(f32[2048,128]{1,0:T(8,128)S(1)} %turn_state.3.refs_2_) | copy-start | bytes 3145732 | tf_op jit(solution)/shard_map/while
  53.0 5.9 %copy-start.1 = (f32[3,16,128,128]{3,2,1,0:T(8,128)}, f32[3,16,128,128]{3,2,1,0:T(8,128)S(1)}, u32[]{:S(2)}) copy-start(f32[3,16,128,128]{3,2,1,0:T(8,128)S(1)} %first_stencil.3) | copy-start | bytes 9437188 | tf_op jit(solution)/shard_map/while
  53.1 5.9 %collective-permute-start.7 = (f32[3,16,128,128]{3,2,1,0:T(8,128)S(1)}, f32[3,16,128,128]{3,2,1,0:T(8,128)}, u32[]{:S(2)}, u32[]{:S(2)}) collective-permute-start(f32[3,16,128,128]{3,2,1,0:T(8,128)S(1)} %first_stencil.3), channel_id=1, source_target_pairs={{0,8},{8,0},{16,24},{24,16},{1,9},{9,1},{17,25},{25,17},{2,10},{10... | collective-permute-start | bytes 9437192 | tf_op jit(solution)/shard_map/while/body/ppermute | solution.py:356
  70.0 3.6 %collective-permute-start.8 = (f32[3,16,64,128]{3,2,1,0:T(8,128)}, f32[3,16,64,128]{3,2,1,0:T(8,128)S(1)}, u32[]{:S(2)}, u32[]{:S(2)}) collective-permute-start(f32[3,16,64,128]{3,2,1,0:T(8,128)} %get-tuple-element.786.far), channel_id=1, source_target_pairs={{0,8},{8,0},{16,24},{24,16},{1,9},{9,1},{17,25},{25,17},{2,10},{10... | collective-permute-start | bytes 4718600 | tf_op jit(solution)/shard_map/while/body/ppermute | solution.py:356
  73.6 18.3 %copy-start.3 = (f32[2048,128]{1,0:T(8,128)S(1)}, f32[2048,128]{1,0:T(8,128)}, u32[]{:S(2)}) copy-start(f32[2048,128]{1,0:T(8,128)} %get-tuple-element.941.refs_3_) | copy-start | bytes 3145732 | tf_op jit(solution)/shard_map/while
  73.6 18.3 %copy-start.6 = (f32[2056,128]{1,0:T(8,128)S(1)}, f32[2056,128]{1,0:T(8,128)}, u32[]{:S(2)}) copy-start(f32[2056,128]{1,0:T(8,128)} %get-tuple-element.942.refs_4_) | copy-start | bytes 3158020 | tf_op jit(solution)/shard_map/while
  78.8 10.9 %collective-permute-start.10 = (f32[3,64,256]{2,1,0:T(8,128)S(1)}, f32[3,64,256]{2,1,0:T(8,128)S(1)}, u32[]{:S(2)}, u32[]{:S(2)}) collective-permute-start(f32[3,64,256]{2,1,0:T(8,128)S(1)} %get-tuple-element.789), channel_id=1, source_target_pairs={{0,1},{1,2},{2,3},{3,4},{4,5},{5,6},{6,7},{7,0},{8,9},{9,10},{10,1... | collective-permute-start | bytes 589832 | tf_op jit(solution)/shard_map/while/body/ppermute | solution.py:372
  81.0 10.9 %collective-permute-start.9 = (f32[3,64,256]{2,1,0:T(8,128)S(1)}, f32[3,64,256]{2,1,0:T(8,128)S(1)}, u32[]{:S(2)}, u32[]{:S(2)}) collective-permute-start(f32[3,64,256]{2,1,0:T(8,128)S(1)} %get-tuple-element.788), channel_id=1, source_target_pairs={{1,0},{2,1},{3,2},{4,3},{5,4},{6,5},{7,6},{0,7},{9,8},{10,9},{11,1... | collective-permute-start | bytes 589832 | tf_op jit(solution)/shard_map/while/body/ppermute | solution.py:372
  92.6 5.9 %collective-permute-start.11 = (f32[3,16,64,256]{3,2,1,0:T(8,128)S(1)}, f32[3,16,64,256]{3,2,1,0:T(8,128)}, u32[]{:S(2)}, u32[]{:S(2)}) collective-permute-start(f32[3,16,64,256]{3,2,1,0:T(8,128)S(1)} %second_stencil_0.1.own), channel_id=1, source_target_pairs={{0,8},{8,0},{16,24},{24,16},{1,9},{9,1},{17,25},{25,17},{2,10},{10... | collective-permute-start | bytes 9437192 | tf_op jit(solution)/shard_map/while/body/ppermute | solution.py:356
  104.7 50.0 %collective-permute-start.19 = (f32[3,16,64,128]{3,2,1,0:T(8,128)}, f32[3,16,64,128]{3,2,1,0:T(8,128)}, u32[]{:S(2)}, u32[]{:S(2)}) collective-permute-start(f32[3,16,64,128]{3,2,1,0:T(8,128)} %get-tuple-element.344), channel_id=1, source_target_pairs={{0,16},{8,24},{16,0},{24,8},{1,17},{9,25},{17,1},{25,9},{2,18},{10... | collective-permute-start | bytes 4718600 | tf_op jit(solution)/shard_map/ppermute | solution.py:353
  106.2 3.6 %collective-permute-start.12 = (f32[3,16,64,128]{3,2,1,0:T(8,128)}, f32[3,16,64,128]{3,2,1,0:T(8,128)S(1)}, u32[]{:S(2)}, u32[]{:S(2)}) collective-permute-start(f32[3,16,64,128]{3,2,1,0:T(8,128)} %get-tuple-element.802.far), channel_id=1, source_target_pairs={{0,8},{8,0},{16,24},{24,16},{1,9},{9,1},{17,25},{25,17},{2,10},{10... | collective-permute-start | bytes 4718600 | tf_op jit(solution)/shard_map/while/body/ppermute | solution.py:356
  109.8 16.9 %copy-start.4 = (f32[2048,128]{1,0:T(8,128)S(1)}, f32[2048,128]{1,0:T(8,128)}, u32[]{:S(2)}) copy-start(f32[2048,128]{1,0:T(8,128)} %get-tuple-element.986.refs_3_) | copy-start | bytes 3145732 | tf_op jit(solution)/shard_map/while
  109.8 16.9 %copy-start.7 = (f32[2056,128]{1,0:T(8,128)S(1)}, f32[2056,128]{1,0:T(8,128)}, u32[]{:S(2)}) copy-start(f32[2056,128]{1,0:T(8,128)} %get-tuple-element.987.refs_4_) | copy-start | bytes 3158020 | tf_op jit(solution)/shard_map/while
  115.0 7.0 %collective-permute-start.13 = (f32[3,64,256]{2,1,0:T(8,128)S(1)}, f32[3,64,256]{2,1,0:T(8,128)S(1)}, u32[]{:S(2)}, u32[]{:S(2)}) collective-permute-start(f32[3,64,256]{2,1,0:T(8,128)S(1)} %get-tuple-element.804), channel_id=1, source_target_pairs={{1,0},{2,1},{3,2},{4,3},{5,4},{6,5},{7,6},{0,7},{9,8},{10,9},{11,1... | collective-permute-start | bytes 589832 | tf_op jit(solution)/shard_map/while/body/ppermute | solution.py:372
  117.4 9.4 %collective-permute-start.14 = (f32[3,64,256]{2,1,0:T(8,128)S(1)}, f32[3,64,256]{2,1,0:T(8,128)S(1)}, u32[]{:S(2)}, u32[]{:S(2)}) collective-permute-start(f32[3,64,256]{2,1,0:T(8,128)S(1)} %get-tuple-element.805), channel_id=1, source_target_pairs={{0,1},{1,2},{2,3},{3,4},{4,5},{5,6},{6,7},{7,0},{8,9},{9,10},{10,1... | collective-permute-start | bytes 589832 | tf_op jit(solution)/shard_map/while/body/ppermute | solution.py:372
  127.5 5.9 %collective-permute-start.15 = (f32[3,16,64,256]{3,2,1,0:T(8,128)S(1)}, f32[3,16,64,256]{3,2,1,0:T(8,128)}, u32[]{:S(2)}, u32[]{:S(2)}) collective-permute-start(f32[3,16,64,256]{3,2,1,0:T(8,128)S(1)} %second_stencil_1.1.own), channel_id=1, source_target_pairs={{0,8},{8,0},{16,24},{24,16},{1,9},{9,1},{17,25},{25,17},{2,10},{10... | collective-permute-start | bytes 9437192 | tf_op jit(solution)/shard_map/while/body/ppermute | solution.py:356
  139.6 15.0 %collective-permute-start.23 = (f32[1,16,64,128]{3,2,1,0:T(8,128)}, f32[1,16,64,128]{3,2,1,0:T(8,128)S(1)}, u32[]{:S(2)}, u32[]{:S(2)}) collective-permute-start(f32[1,16,64,128]{3,2,1,0:T(8,128)} %get-tuple-element.354), channel_id=1, source_target_pairs={{0,16},{8,24},{16,0},{24,8},{1,17},{9,25},{17,1},{25,9},{2,18},{10... | collective-permute-start | bytes 1572872 | tf_op jit(solution)/shard_map/ppermute | solution.py:353
  140.1 25.7 %collective-permute-start.22 = (f32[1,16,64,128]{3,2,1,0:T(8,128)}, f32[1,16,64,128]{3,2,1,0:T(8,128)S(1)}, u32[]{:S(2)}, u32[]{:S(2)}) collective-permute-start(f32[1,16,64,128]{3,2,1,0:T(8,128)} %get-tuple-element.353), channel_id=1, source_target_pairs={{0,16},{8,24},{16,0},{24,8},{1,17},{9,25},{17,1},{25,9},{2,18},{10... | collective-permute-start | bytes 1572872 | tf_op jit(solution)/shard_map/ppermute | solution.py:353
  141.7 34.6 %collective-permute-start.21 = (f32[1,16,64,128]{3,2,1,0:T(8,128)}, f32[1,16,64,128]{3,2,1,0:T(8,128)S(1)}, u32[]{:S(2)}, u32[]{:S(2)}) collective-permute-start(f32[1,16,64,128]{3,2,1,0:T(8,128)} %get-tuple-element.352), channel_id=1, source_target_pairs={{0,16},{8,24},{16,0},{24,8},{1,17},{9,25},{17,1},{25,9},{2,18},{10... | collective-permute-start | bytes 1572872 | tf_op jit(solution)/shard_map/ppermute | solution.py:353

commit v8 on v7

--- a/solution.py
+++ b/solution.py
@@ -124,52 +124,74 @@
     )()
 
 
-def first_kernel(where, cot, state, after, before, rate, *rest, modes, nz, chunks):
-    outs, turned = rest[:-1], rest[-1]
-    half = cot.shape[1]
-    width = half // chunks
-    for c in range(3):
-        turned[c, 0] = before[c * modes : (c + 1) * modes, :].T
+def turn_kernel(where, cot, out, *, modes, nz, comps):
+    for c in range(comps):
         for z in range(nz):
-            turned[c, z + 1] = cot[pl.ds(c * nz + z, modes, stride=3 * nz), :].T
-        turned[c, nz + 1] = after[c * modes : (c + 1) * modes, :].T
-    turn = rotation_coeff * rate[...]
-    for z in range(nz):
-        for k in range(chunks):
-            at = slice(k * width, (k + 1) * width)
-            st = state[z * half + k * width : z * half + (k + 1) * width, :]
-            cur = [turned[c, z + 1, at, :] for c in range(3)]
-            others = (turn * cur[1], -turn * cur[0], None)
-            for c in range(3):
-                outs[k][c, z] = stencil(cur[c], turned[c, z + 2, at, :], turned[c, z, at, :], others[c], st)
-
-
-def first_stencil(where, cot, state_turned, after, before, rate, foreign, chunks):
+            out[c, z] = cot[pl.ds(c * nz + z, modes, stride=comps * nz), :].T
+
+
+def turn_half(where, cot, foreign):
     modes, comps, nz, nphi = cot.shape
     half = nphi // 2
     side = (lambda i, w: (0, 1 - (w[0] >> 1))) if foreign else (lambda i, w: (0, w[0] >> 1))
-    whole = lambda i, w: (0, 0)
-    out = (comps, nz, half // chunks, modes)
-    return pl.pallas_call(
-        lambda *refs: first_kernel(*refs, modes=modes, nz=nz, chunks=chunks),
-        out_shape=[shape(out)] * chunks,
+    out = (comps, nz, half, modes)
+    return pl.pallas_call(
+        lambda *refs: turn_kernel(*refs, modes=modes, nz=nz, comps=comps),
+        out_shape=shape(out),
         grid_spec=pltpu.PrefetchScalarGridSpec(
             num_scalar_prefetch=1,
             grid=(1,),
-            in_specs=[
-                pl.BlockSpec((modes * comps * nz, half), side),
-                pl.BlockSpec((nz * half, modes), whole),
-                pl.BlockSpec((comps * modes, half), whole),
-                pl.BlockSpec((comps * modes, half), whole),
-                pl.BlockSpec((1, modes), whole),
-            ],
-            out_specs=[pl.BlockSpec(out, lambda i, w: (0, 0, 0, 0))] * chunks,
-            scratch_shapes=[pltpu.VMEM((comps, nz + 2, half, modes), F32)],
+            in_specs=[pl.BlockSpec((modes * comps * nz, half), side)],
+            out_specs=pl.BlockSpec(out, lambda i, w: (0, 0, 0, 0)),
         ),
+        compiler_params=params(20),
+        cost_estimate=cost(modes * comps * nz * half, 8 * modes * comps * nz * half),
+        name="turn_half",
+    )(where, cot.reshape(modes * comps * nz, nphi))
+
+
+def first_kernel(turned, state, after, before, rate, *rest):
+    outs, edges = rest[:-1], rest[-1]
+    comps, nz, half, modes = turned.shape
+    width = half // len(outs)
+    for c in range(comps):
+        edges[c, 0] = before[c * modes : (c + 1) * modes, :].T
+        edges[c, 1] = after[c * modes : (c + 1) * modes, :].T
+    turn = rotation_coeff * rate[...]
+    step = 32
+    for z in range(nz):
+        for p in range(0, half, step):
+            at = slice(p, p + step)
+            st = state[z * half + p : z * half + p + step, :]
+            cur = [turned[c, z, at, :] for c in range(comps)]
+            others = (turn * cur[1], -turn * cur[0], None)
+            for c in range(comps):
+                upper = turned[c, z + 1, at, :] if z + 1 < nz else edges[c, 1, at, :]
+                lower = turned[c, z - 1, at, :] if z else edges[c, 0, at, :]
+                to = p % width
+                outs[p // width][c, z, to : to + step, :] = stencil(cur[c], upper, lower, others[c], st)
+
+
+def first_stencil(turned, state_turned, after, before, rate, chunks):
+    comps, nz, half, modes = turned.shape
+    out = (comps, nz, half // chunks, modes)
+    return pl.pallas_call(
+        first_kernel,
+        out_shape=[shape(out)] * chunks,
+        grid=(1,),
+        in_specs=[
+            pl.BlockSpec(turned.shape, lambda i: (0, 0, 0, 0)),
+            pl.BlockSpec((nz * half, modes), lambda i: (0, 0)),
+            pl.BlockSpec((comps * modes, half), lambda i: (0, 0)),
+            pl.BlockSpec((comps * modes, half), lambda i: (0, 0)),
+            pl.BlockSpec((1, modes), lambda i: (0, 0)),
+        ],
+        out_specs=[pl.BlockSpec(out, lambda i: (0, 0, 0, 0))] * chunks,
+        scratch_shapes=[pltpu.VMEM((comps, 2, half, modes), F32)],
         compiler_params=params(32),
         cost_estimate=cost(12 * modes * comps * nz * half, 8 * modes * comps * nz * half),
         name="first_stencil",
-    )(where, cot.reshape(modes * comps * nz, nphi), state_turned, after, before, rate)
+    )(turned, state_turned, after, before, rate)
 
 
 def helm_kernel(where, own, *refs):
@@ -376,22 +398,23 @@
         edges = halos(*edge_layers(here, cotangent, True))
         blocks = [tied(piece, here)]
         blocks += [hop(blocks[0], 1), hop(blocks[0], 2)]
-        blocks += [hop(blocks[2], 1)]
-        return (*first_stencil(here, cotangent, state_foreign, *edges, rate, True, GROUPS), *blocks[1:])
+        return (*first_stencil(turn_half(here, cotangent, True), state_foreign, *edges, rate, GROUPS), *blocks[1:])
 
     chunk = (comps, nz, half // GROUPS, modes)
     block = (comps, modes, modes)
-    sent = lax.fori_loop(0, once, foreign_half, tuple(blanks(*[(chunk, F32)] * GROUPS, *[(block, F32)] * (PIECES - 1))))
+    sent = lax.fori_loop(0, once, foreign_half, tuple(blanks(*[(chunk, F32)] * GROUPS, *[(block, F32)] * (PIECES - 2))))
     sent, blocks = sent[:GROUPS], [piece, *sent[GROUPS:]]
     far = [across(tied(s, state_far) if k else tied(s, piece)) for k, s in enumerate(sent)]
 
     def own_half(step, carry):
         here = where + (step >> 8)
         edges = halos(*edge_layers(here, entry, False))
+        last_block = hop(tied(blocks[2], here), 1)
+        edges = tuple(tied(e, last_block) for e in edges)
         state_own = turn_state(here, state_axial, False)
-        (own,) = first_stencil(here, entry, state_own, *edges, rate, False, 1)
+        (own,) = first_stencil(turn_half(here, entry, False), state_own, *edges, rate, 1)
         own_peer = beside(own)
-        return (state_own, own, own_peer, *split_helm(here, helm_inverse, blocks))
+        return (state_own, own, own_peer, *split_helm(here, helm_inverse, [*blocks, last_block]))
 
     entry = tied(cotangent, sent[0])
     columns = (comps, nz, half, modes)

time: 180 us -> 177 us (0.983)
  waiting for transfers between devices: 85.5 us -> 81.4 us
    ppermute x8, waiting for transfers between devices: 30.3 us -> 25.7 us  [halos(): return (lax.ppermute(leading, 'col', down), lax.ppermute(last, 'col', up))]
    pallas_call x2 -> x4, Pallas kernels: 9.08 us -> 9.6 us  [the longest x2 5.31 us: turn_half(): pl.pallas_call(lambda *refs: turn_kernel(*refs, modes=modes, nz=nz, comps...]
  transfers between devices with their start and end apart: 24 -> 24, of which waited for: 19 -> 18; matrix products, arithmetic and copies ran while one was open for 0% -> 0% of each run, Pallas kernels for 34% -> 34%
where the time goes in v8:
time: 177 us; the launch traced here: 176 us
  waiting for transfers between devices  81.4 us (46%)
  Pallas kernels  63.6 us (36%)
  starting transfers between devices  28.8 us (16%)
  local copies, waits for them, and re-layouts  2.31 us (1%)
    ppermute x8, waiting for transfers between devices, across(): return lax.ppermute(array, 'rad', [(i, i ^ 2) for i in range(peers)])  35.9 us
    ppermute x8, waiting for transfers between devices, halos(): return (lax.ppermute(leading, 'col', down), lax.ppermute(last, 'col', up))  25.7 us
    ppermute x5, waiting for transfers between devices, beside(): return lax.ppermute(array, 'rad', [(i, i ^ 1) for i in range(peers)])  19.8 us
    ppermute x8, starting transfers between devices, halos(): return (lax.ppermute(leading, 'col', down), lax.ppermute(last, 'col', up))  16.2 us
    pallas_call x4, Pallas kernels, write_half(): pl.pallas_call(lambda *refs: last_kernel(*refs, nz=nz, chunks=chunks), ou...  14.4 us
    pallas_call x2, Pallas kernels, map2(): pl.pallas_call(map2_kernel, out_shape=[shape((comps, *block[1:]))] + [sha...  12.4 us
    pallas_call x2, Pallas kernels, map1(): pl.pallas_call(map1_kernel, out_shape=[shape((comps, nz, width, cols)), s...  10.3 us
    ppermute x8, starting transfers between devices, across(): return lax.ppermute(array, 'rad', [(i, i ^ 2) for i in range(peers)])  9.45 us
  transfers between devices with their start and end apart: 24, of which 18 were waited for; matrix products, arithmetic and copies ran while one was open for 0% of the time, Pallas kernels for 34%

profile of v8, /device:TPU:0, one launch (start us, length us, event | category | flops | bytes accessed | tf_op | source)
XLA Modules:
  0.0 176.4 jit_solution(7832300702975784111)
XLA Ops:
  0.9 3.0 %collective-permute-start.16 = (f32[3,128,128]{2,1,0:T(8,128)S(1)}, f32[3,128,128]{2,1,0:T(8,128)S(1)}, u32[]{:S(2)}, u32[]{:S(2)}) collective-permute-start(f32[3,128,128]{2,1,0:T(8,128)S(1)} %constant_dynamic-slice_fusion), channel_id=1, source_target_pairs={{0,16},{8,24},{16,0},{24,8},{1,17},{9,25},{17,1},{25,9},{2,18},{10... | collective-permute-start | bytes 589832 | tf_op jit(solution)/shard_map/ppermute | solution.py:375
  4.0 3.1 %turn_state.2 = f32[2056,128]{1,0:T(8,128)} custom-call(s32[2]{0:T(128)S(1)} %pad_add_fusion.refs_0_, f32[2048,256]{1,0:T(8,128)} %bitcast.18, f32[1,128]{1,0:T(1,128)} %bitcast.20), custom_call_target="tpu_custom_call" | custom-call | flops 263168 | bytes 2105344 | tf_op jit(solution)/shard_map/turn_state/pallas_call | solution.py:77
  7.2 1.7 collective-permute-done.16
  8.9 21.9 %while.62 = (s32[]{:T(128)}, f32[3,16,64,128]{3,2,1,0:T(8,128)}, f32[3,16,64,128]{3,2,1,0:T(8,128)}, f32[3,128,128]{2,1,0:T(8,128)}, f32[3,128,128]{2,1,0:T(8,12...) while((s32[]{:T(128)}, f32[3,16,64,128]{3,2,1,0:T(8,128)}, ...), condition=%wide.region_1.0_spmd, body=%wide.region_0.0_spmd.sunk | while | flops 10321925 | bytes 19661144 | solution.py:405
  8.9 2.6 %edge_layers.2 = (f32[384,128]{1,0:T(8,128)S(1)}, f32[384,128]{1,0:T(8,128)S(1)}) custom-call(s32[2]{0:T(128)S(1)} %broadcast_add_fusion.4.refs_0_, f32[6144,256]{1,0:T(8,128)} %bitcast.14), custom_call_target="tpu_custom_call" | custom-call | flops 98304 | bytes 3145728 | tf_op jit(solution)/shard_map/while/body/edge_layers/pallas_call | solution.py:103
  11.4 4.9 %collective-permute-start = (f32[384,128]{1,0:T(8,128)S(1)}, f32[384,128]{1,0:T(8,128)S(1)}, u32[]{:S(2)}, u32[]{:S(2)}) collective-permute-start(f32[384,128]{1,0:T(8,128)S(1)} %get-tuple-element.736), channel_id=1, source_target_pairs={{1,0},{2,1},{3,2},{4,3},{5,4},{6,5},{7,6},{0,7},{9,8},{10,9},{11,1... | collective-permute-start | bytes 589832 | tf_op jit(solution)/shard_map/while/body/ppermute | solution.py:394
  16.3 1.5 collective-permute-start.3
  17.8 3.4 %turn_half.2.turned = f32[3,16,128,128]{3,2,1,0:T(8,128)S(1)} custom-call(s32[2]{0:T(128)S(1)} %broadcast_add_fusion.4.refs_0_, f32[6144,256]{1,0:T(8,128)} %bitcast.15), custom_call_target="tpu_custom_call" | custom-call | flops 786432 | bytes 6291456 | tf_op jit(solution)/shard_map/while/body/turn_half/pallas_call | solution.py:138
  21.6 5.0 %collective-permute-done.1.before = f32[384,128]{1,0:T(8,128)S(1)} collective-permute-done((f32[384,128]{1,0:T(8,128)S(1)}, f32[384,128]{1,0:T(8,128)S(1)}, u32[]{:S(2)}, u32[]{:S(2)}) %collective-permute-start.1) | collective-permute-done | bytes 196640 | tf_op jit(solution)/shard_map/while/body/ppermute | solution.py:394
  26.6 3.5 %first_stencil.2 = (f32[3,16,64,128]{3,2,1,0:T(8,128)}, f32[3,16,64,128]{3,2,1,0:T(8,128)}) custom-call(f32[3,16,128,128]{3,2,1,0:T(8,128)S(1)} %turn_half.2.turned, f32[2056,128]{1,0:T(8,128)} %get-tuple-element.826.state, f32[384,128]{1,0:T(8,128)S(1)} %collective-permute-done.after, f32[384,128]{1,0:T(8,128)S(1)} %collective-permute-done.1.before, ...), custom_call_target="tpu_custom_call" | custom-call | flops 9437184 | bytes 6291456 | tf_op jit(solution)/shard_map/while/body/first_stencil/pallas_call | solution.py:178
  30.8 1.6 collective-permute-start.17
  32.3 1.2 collective-permute-done.18
  34.5 23.0 %while.63 = (s32[]{:T(128)}, f32[2048,128]{1,0:T(8,128)}, f32[3,16,128,128]{3,2,1,0:T(8,128)}, f32[3,16,128,128]{3,2,1,0:T(8,128)}, bf16[3,512,256]{2,1,0:T(8,12...) while((s32[]{:T(128)}, f32[2048,128]{1,0:T(8,128)}, ...), condition=%wide.region_3.0_spmd, body=%wide.region_2.0_spmd.sunk | while | flops 11370501 | bytes 77857200 | solution.py:422
  34.5 1.5 collective-permute-start.5
  36.1 2.8 %edge_layers.3 = (f32[384,128]{1,0:T(8,128)S(1)}, f32[384,128]{1,0:T(8,128)S(1)}) custom-call(s32[2]{0:T(128)S(1)} %broadcast_add_fusion.5.refs_0_.where, f32[6144,256]{1,0:T(8,128)} %bitcast.16), custom_call_target="tpu_custom_call" | custom-call | flops 98304 | bytes 3145728 | tf_op jit(solution)/shard_map/while/body/edge_layers/pallas_call | solution.py:103
  38.9 3.6 %collective-permute-start.4 = (f32[384,128]{1,0:T(8,128)S(1)}, f32[384,128]{1,0:T(8,128)S(1)}, u32[]{:S(2)}, u32[]{:S(2)}) collective-permute-start(f32[384,128]{1,0:T(8,128)S(1)} %get-tuple-element.751), channel_id=1, source_target_pairs={{1,0},{2,1},{3,2},{4,3},{5,4},{6,5},{7,6},{0,7},{9,8},{10,9},{11,1... | collective-permute-start | bytes 589832 | tf_op jit(solution)/shard_map/while/body/ppermute | solution.py:394
  42.5 2.1 %turn_state.3.state = f32[2048,128]{1,0:T(8,128)S(1)} custom-call(s32[2]{0:T(128)S(1)} %broadcast_add_fusion.5.refs_0_.where, f32[2048,256]{1,0:T(8,128)} %bitcast.19), custom_call_target="tpu_custom_call" | custom-call | flops 262144 | bytes 2097152 | tf_op jit(solution)/shard_map/while/body/turn_state/pallas_call | solution.py:77
  44.6 1.9 %turn_half.3.turned = f32[3,16,128,128]{3,2,1,0:T(8,128)S(1)} custom-call(s32[2]{0:T(128)S(1)} %broadcast_add_fusion.5.refs_0_.where, f32[6144,256]{1,0:T(8,128)S(1)} %bitcast.17), custom_call_target="tpu_custom_call" | custom-call | flops 786432 | bytes 6291456 | tf_op jit(solution)/shard_map/while/body/turn_half/pallas_call | solution.py:138
  46.5 4.3 %collective-permute-done.6.before = f32[384,128]{1,0:T(8,128)S(1)} collective-permute-done((f32[384,128]{1,0:T(8,128)S(1)}, f32[384,128]{1,0:T(8,128)S(1)}, u32[]{:S(2)}, u32[]{:S(2)}) %collective-permute-start.6) | collective-permute-done | bytes 196640 | tf_op jit(solution)/shard_map/while/body/ppermute | solution.py:394
  51.7 4.7 %split_helm.1 = (bf16[3,512,256]{2,1,0:T(8,128)(2,1)}, bf16[3,512,256]{2,1,0:T(8,128)(2,1)}) custom-call(s32[2]{0:T(128)S(1)} %broadcast_add_fusion.5.refs_0_.where, f32[3,512,128]{2,1,0:T(8,128)} %get-tuple-element.877.own, f32[3,128,128]{2,1,0:T(8,128)S(1)} %get-tuple-element.878.refs_0_, f32[3,128,128]{2,1,0:T(8,128)} %get-tuple-element.879.refs_1_, ...), custom_call_target="tpu_custom_call" | custom-call | flops 786432 | bytes 3145728 | tf_op jit(solution)/shard_map/while/body/split_helm/pallas_call | solution.py:221
  56.5 1.0 collective-permute-done.7
  57.5 10.9 %collective-permute-done.17 = f32[3,16,64,128]{3,2,1,0:T(8,128)} collective-permute-done((f32[3,16,64,128]{3,2,1,0:T(8,128)}, f32[3,16,64,128]{3,2,1,0:T(8,128)}, u32[]{:S(2)}, u32[]{:S(2)}) %collective-permute-start.17) | collective-permute-done | bytes 1572896 | tf_op jit(solution)/shard_map/ppermute | solution.py:375
  68.4 33.0 %while.64 = (s32[]{:T(128)}, f32[3,16,64,128]{3,2,1,0:T(8,128)}, f32[3,16,64,128]{3,2,1,0:T(8,128)}, s32[]{:T(128)}, f32[3,16,64,128]{3,2,1,0:T(8,128)}, /*index...) while((s32[]{:T(128)}, f32[3,16,64,128]{3,2,1,0:T(8,128)}, ...), condition=%wide.region_5.0_spmd, body=%wide.region_4.0_spmd.sunk | while | flops 4841275392 | bytes 57164116 | solution.py:439
  68.4 3.6 %collective-permute-done.8.far_peer = f32[3,16,64,128]{3,2,1,0:T(8,128)S(1)} collective-permute-done((f32[3,16,64,128]{3,2,1,0:T(8,128)}, f32[3,16,64,128]{3,2,1,0:T(8,128)S(1)}, u32[]{:S(2)}, u32[]{:S(2)}) %collective-permute-start.8) | collective-permute-done | bytes 1572896 | tf_op jit(solution)/shard_map/while/body/ppermute | solution.py:378
  72.0 5.2 %map1_0.1 = (f32[3,16,64,256]{3,2,1,0:T(8,128)S(1)}, f32[3,64,256]{2,1,0:T(8,128)S(1)}, f32[3,64,256]{2,1,0:T(8,128)S(1)}) custom-call(f32[3,16,128,128]{3,2,1,0:T(8,128)} %get-tuple-element.913.own, f32[3,16,64,128]{3,2,1,0:T(8,128)} %get-tuple-element.768.far, f32[3,16,128,128]{3,2,1,0:T(8,128)} %get-tuple-element.914.own_peer, ...), custom_call_target="tpu_custom_call" | custom-call | flops 2415919104 | bytes 11010048 | tf_op jit(solution)/shard_map/while/body/map1_0/pallas_call | solution.py:254
  77.7 4.3 %collective-permute-start.9 = (f32[3,64,256]{2,1,0:T(8,128)S(1)}, f32[3,64,256]{2,1,0:T(8,128)S(1)}, u32[]{:S(2)}, u32[]{:S(2)}) collective-permute-start(f32[3,64,256]{2,1,0:T(8,128)S(1)} %get-tuple-element.770), channel_id=1, source_target_pairs={{1,0},{2,1},{3,2},{4,3},{5,4},{6,5},{7,6},{0,7},{9,8},{10,9},{11,1... | collective-permute-start | bytes 589832 | tf_op jit(solution)/shard_map/while/body/ppermute | solution.py:394
  82.0 5.0 %collective-permute-done.10.refs_2_ = f32[3,64,256]{2,1,0:T(8,128)S(1)} collective-permute-done((f32[3,64,256]{2,1,0:T(8,128)S(1)}, f32[3,64,256]{2,1,0:T(8,128)S(1)}, u32[]{:S(2)}, u32[]{:S(2)}) %collective-permute-start.10) | collective-permute-done | bytes 196640 | tf_op jit(solution)/shard_map/while/body/ppermute | solution.py:394
  87.0 1.6 collective-permute-done.9.refs_1_
  89.4 5.8 %collective-permute-done.11.peer = f32[3,16,64,256]{3,2,1,0:T(8,128)} collective-permute-done((f32[3,16,64,256]{3,2,1,0:T(8,128)S(1)}, f32[3,16,64,256]{3,2,1,0:T(8,128)}, u32[]{:S(2)}, u32[]{:S(2)}) %collective-permute-start.11) | collective-permute-done | bytes 3145760 | tf_op jit(solution)/shard_map/while/body/ppermute | solution.py:378
  95.2 6.2 %map2_0.1 = (f32[3,16,64,128]{3,2,1,0:T(8,128)}, f32[3,16,64,128]{3,2,1,0:T(8,128)}) custom-call(f32[3,16,64,256]{3,2,1,0:T(8,128)S(1)} %second_stencil_0.1.own, f32[3,16,64,256]{3,2,1,0:T(8,128)} %collective-permute-done.11.peer, bf16[3,512,256]{2,1,0:T(8,128)(2,1)} %get-tuple-element.915.high, bf16[3,512,256]{2,1,0:T(8,128)(2,1)} %get-tuple-element.916.low), custom_call_target="tpu_custom_call" | custom-call | flops 2415919104 | bytes 11010048 | tf_op jit(solution)/shard_map/while/body/map2_0/pallas_call | solution.py:314
  101.4 1.5 collective-permute-start.19
  102.8 33.9 %while.65 = (s32[]{:T(128)}, f32[3,16,64,128]{3,2,1,0:T(8,128)}, f32[1,16,64,128]{3,2,1,0:T(8,128)}, f32[1,16,64,128]{3,2,1,0:T(8,128)}, f32[1,16,64,128]{3,2,1,...) while((s32[]{:T(128)}, f32[3,16,64,128]{3,2,1,0:T(8,128)}, ...), condition=%wide.region_7.0_spmd, body=%wide.region_6.0_spmd.sunk | while | flops 4841275392 | bytes 57164132 | solution.py:439
  102.8 3.6 %collective-permute-done.12.far_peer = f32[3,16,64,128]{3,2,1,0:T(8,128)S(1)} collective-permute-done((f32[3,16,64,128]{3,2,1,0:T(8,128)}, f32[3,16,64,128]{3,2,1,0:T(8,128)S(1)}, u32[]{:S(2)}, u32[]{:S(2)}) %collective-permute-start.12) | collective-permute-done | bytes 1572896 | tf_op jit(solution)/shard_map/while/body/ppermute | solution.py:378
  106.5 5.2 %map1_1.1 = (f32[3,16,64,256]{3,2,1,0:T(8,128)S(1)}, f32[3,64,256]{2,1,0:T(8,128)S(1)}, f32[3,64,256]{2,1,0:T(8,128)S(1)}) custom-call(f32[3,16,128,128]{3,2,1,0:T(8,128)} %get-tuple-element.958.own, f32[3,16,64,128]{3,2,1,0:T(8,128)} %get-tuple-element.784.far, f32[3,16,128,128]{3,2,1,0:T(8,128)} %get-tuple-element.959.own_peer, ...), custom_call_target="tpu_custom_call" | custom-call | flops 2415919104 | bytes 11010048 | tf_op jit(solution)/shard_map/while/body/map1_1/pallas_call | solution.py:254
  111.6 2.9 %collective-permute-start.13 = (f32[3,64,256]{2,1,0:T(8,128)S(1)}, f32[3,64,256]{2,1,0:T(8,128)S(1)}, u32[]{:S(2)}, u32[]{:S(2)}) collective-permute-start(f32[3,64,256]{2,1,0:T(8,128)S(1)} %get-tuple-element.786), channel_id=1, source_target_pairs={{1,0},{2,1},{3,2},{4,3},{5,4},{6,5},{7,6},{0,7},{9,8},{10,9},{11,1... | collective-permute-start | bytes 589832 | tf_op jit(solution)/shard_map/while/body/ppermute | solution.py:394
  114.6 4.4 %collective-permute-done.13.refs_1_ = f32[3,64,256]{2,1,0:T(8,128)S(1)} collective-permute-done((f32[3,64,256]{2,1,0:T(8,128)S(1)}, f32[3,64,256]{2,1,0:T(8,128)S(1)}, u32[]{:S(2)}, u32[]{:S(2)}) %collective-permute-start.13) | collective-permute-done | bytes 196640 | tf_op jit(solution)/shard_map/while/body/ppermute | solution.py:394
  119.0 4.9 %collective-permute-done.14.refs_2_ = f32[3,64,256]{2,1,0:T(8,128)S(1)} collective-permute-done((f32[3,64,256]{2,1,0:T(8,128)S(1)}, f32[3,64,256]{2,1,0:T(8,128)S(1)}, u32[]{:S(2)}, u32[]{:S(2)}) %collective-permute-start.14) | collective-permute-done | bytes 196640 | tf_op jit(solution)/shard_map/while/body/ppermute | solution.py:394
  124.8 5.8 %collective-permute-done.15.peer = f32[3,16,64,256]{3,2,1,0:T(8,128)} collective-permute-done((f32[3,16,64,256]{3,2,1,0:T(8,128)S(1)}, f32[3,16,64,256]{3,2,1,0:T(8,128)}, u32[]{:S(2)}, u32[]{:S(2)}) %collective-permute-start.15) | collective-permute-done | bytes 3145760 | tf_op jit(solution)/shard_map/while/body/ppermute | solution.py:378
  130.5 6.2 %map2_1.1 = (f32[3,16,64,128]{3,2,1,0:T(8,128)}, f32[1,16,64,128]{3,2,1,0:T(8,128)}, f32[1,16,64,128]{3,2,1,0:T(8,128)}, f32[1,16,64,128]{3,2,1,0:T(8,128)}) custom-call(f32[3,16,64,256]{3,2,1,0:T(8,128)S(1)} %second_stencil_1.1.own, f32[3,16,64,256]{3,2,1,0:T(8,128)} %collective-permute-done.15.peer, bf16[3,512,256]{2,1,0:T(8,128)(2,1)} %get-tuple-element.960.high, ...), custom_call_target="tpu_custom_call" | custom-call | flops 2415919104 | bytes 11010048 | tf_op jit(solution)/shard_map/while/body/map2_1/pallas_call | solution.py:314
  136.8 1.0 collective-permute-start.23
  138.8 1.0 collective-permute-start.21
  139.8 5.5 %write_own.1.refs_3_ = f32[128,48,256]{2,1,0:T(8,128)} custom-call(s32[2]{0:T(128)S(1)} %get-tuple-element.1011, f32[3,16,64,128]{3,2,1,0:T(8,128)} %get-tuple-element.336.refs_1_, f32[3,16,64,128]{3,2,1,0:T(8,128)} %get-tuple-element.345.refs_2_), custom_call_target="tpu_custom_call" | custom-call | flops 1572864 | bytes 6291456 | tf_op jit(solution)/shard_map/write_own/pallas_call | solution.py:347
  145.3 6.4 %collective-permute-done.23.refs_2_ = f32[1,16,64,128]{3,2,1,0:T(8,128)S(1)} collective-permute-done((f32[1,16,64,128]{3,2,1,0:T(8,128)}, f32[1,16,64,128]{3,2,1,0:T(8,128)S(1)}, u32[]{:S(2)}, u32[]{:S(2)}) %collective-permute-start.23) | collective-permute-done | bytes 524320 | tf_op jit(solution)/shard_map/ppermute | solution.py:375
  151.7 3.0 %write_foreign_0.1.refs_3_ = f32[128,48,256]{2,1,0:T(8,128)} custom-call(s32[2]{0:T(128)S(1)} %get-tuple-element.1011, f32[3,16,64,128]{3,2,1,0:T(8,128)} %collective-permute-done.19.refs_1_, f32[1,16,64,128]{3,2,1,0:T(8,128)S(1)} %collective-permute-done.23.refs_2_, f32[128,48,256]{2,1,0:T(8,128)} %write_own.1.refs_3_), custom_call_target="tpu_custom_call", output_to_operand_aliasing={{}: (3, {})} | custom-call | flops 524288 | bytes 2097152 | tf_op jit(solution)/shard_map/write_foreign_0/pallas_call | solution.py:347
  154.7 8.3 %collective-permute-done.22.refs_2_ = f32[1,16,64,128]{3,2,1,0:T(8,128)S(1)} collective-permute-done((f32[1,16,64,128]{3,2,1,0:T(8,128)}, f32[1,16,64,128]{3,2,1,0:T(8,128)S(1)}, u32[]{:S(2)}, u32[]{:S(2)}) %collective-permute-start.22) | collective-permute-done | bytes 524320 | tf_op jit(solution)/shard_map/ppermute | solution.py:375
  163.0 3.0 %write_foreign_1.1.refs_3_ = f32[128,48,256]{2,1,0:T(8,128)} custom-call(s32[2]{0:T(128)S(1)} %get-tuple-element.1011, f32[3,16,64,128]{3,2,1,0:T(8,128)} %collective-permute-done.19.refs_1_, f32[1,16,64,128]{3,2,1,0:T(8,128)S(1)} %collective-permute-done.22.refs_2_, f32[128,48,256]{2,1,0:T(8,128)} %write_foreign_0.1.refs_3_), custom_call_target="tpu_custom_call", output_to_operand_aliasing={{}: (3, {})} | custom-call | flops 524288 | bytes 2097152 | tf_op jit(solution)/shard_map/write_foreign_1/pallas_call | solution.py:347
  165.9 7.5 %collective-permute-done.21.refs_2_ = f32[1,16,64,128]{3,2,1,0:T(8,128)S(1)} collective-permute-done((f32[1,16,64,128]{3,2,1,0:T(8,128)}, f32[1,16,64,128]{3,2,1,0:T(8,128)S(1)}, u32[]{:S(2)}, u32[]{:S(2)}) %collective-permute-start.21) | collective-permute-done | bytes 524320 | tf_op jit(solution)/shard_map/ppermute | solution.py:375
  173.4 3.0 %write_foreign_2.1 = f32[128,48,256]{2,1,0:T(8,128)} custom-call(s32[2]{0:T(128)S(1)} %get-tuple-element.1011, f32[3,16,64,128]{3,2,1,0:T(8,128)} %collective-permute-done.19.refs_1_, f32[1,16,64,128]{3,2,1,0:T(8,128)S(1)} %collective-permute-done.21.refs_2_, f32[128,48,256]{2,1,0:T(8,128)} %write_foreign_1.1.refs_3_), custom_call_target="tpu_custom_call", output_to_operand_aliasing={{}: (3, {})} | custom-call | flops 524288 | bytes 2097152 | tf_op jit(solution)/shard_map/write_foreign_2/pallas_call | solution.py:347
  (51 shorter events, 7.3 us)
Async XLA Ops:
  0.9 7.9 %collective-permute-start.16 = (f32[3,128,128]{2,1,0:T(8,128)S(1)}, f32[3,128,128]{2,1,0:T(8,128)S(1)}, u32[]{:S(2)}, u32[]{:S(2)}) collective-permute-start(f32[3,128,128]{2,1,0:T(8,128)S(1)} %constant_dynamic-slice_fusion), channel_id=1, source_target_pairs={{0,16},{8,24},{16,0},{24,8},{1,17},{9,25},{17,1},{25,9},{2,18},{10... | collective-permute-start | bytes 589832 | tf_op jit(solution)/shard_map/ppermute | solution.py:375
  4.0 4.8 %copy-start.9 = (f32[128]{0:T(128)S(1)}, f32[128]{0:T(128)}, u32[]{:S(2)}) copy-start(f32[128]{0:T(128)} %param.15) | copy-start | bytes 1540
  7.1 26.4 %collective-permute-start.18 = (f32[2056,128]{1,0:T(8,128)}, f32[2056,128]{1,0:T(8,128)S(1)}, u32[]{:S(2)}, u32[]{:S(2)}) collective-permute-start(f32[2056,128]{1,0:T(8,128)} %turn_state.2), channel_id=1, source_target_pairs={{0,16},{8,24},{16,0},{24,8},{1,17},{9,25},{17,1},{25,9},{2,18},{10... | collective-permute-start | bytes 3158024 | tf_op jit(solution)/shard_map/ppermute | solution.py:375
  11.4 10.2 %collective-permute-start = (f32[384,128]{1,0:T(8,128)S(1)}, f32[384,128]{1,0:T(8,128)S(1)}, u32[]{:S(2)}, u32[]{:S(2)}) collective-permute-start(f32[384,128]{1,0:T(8,128)S(1)} %get-tuple-element.736), channel_id=1, source_target_pairs={{1,0},{2,1},{3,2},{4,3},{5,4},{6,5},{7,6},{0,7},{9,8},{10,9},{11,1... | collective-permute-start | bytes 589832 | tf_op jit(solution)/shard_map/while/body/ppermute | solution.py:394
  16.3 10.3 %collective-permute-start.1 = (f32[384,128]{1,0:T(8,128)S(1)}, f32[384,128]{1,0:T(8,128)S(1)}, u32[]{:S(2)}, u32[]{:S(2)}) collective-permute-start(f32[384,128]{1,0:T(8,128)S(1)} %get-tuple-element.737), channel_id=1, source_target_pairs={{0,1},{1,2},{2,3},{3,4},{4,5},{5,6},{6,7},{7,0},{8,9},{9,10},{10,1... | collective-permute-start | bytes 589832 | tf_op jit(solution)/shard_map/while/body/ppermute | solution.py:394
  16.3 13.8 %collective-permute-start.2 = (f32[3,128,128]{2,1,0:T(8,128)S(1)}, f32[3,128,128]{2,1,0:T(8,128)S(1)}, u32[]{:S(2)}, u32[]{:S(2)}) collective-permute-start(f32[3,128,128]{2,1,0:T(8,128)S(1)} %get-tuple-element.740), channel_id=1, source_target_pairs={{0,1},{1,0},{2,3},{3,2},{4,5},{5,4},{6,7},{7,6},{8,9},{9,8},{10,11... | collective-permute-start | bytes 589832 | tf_op jit(solution)/shard_map/while/body/ppermute | solution.py:381
  16.3 13.8 %collective-permute-start.3 = (f32[3,128,128]{2,1,0:T(8,128)S(1)}, f32[3,128,128]{2,1,0:T(8,128)}, u32[]{:S(2)}, u32[]{:S(2)}) collective-permute-start(f32[3,128,128]{2,1,0:T(8,128)S(1)} %get-tuple-element.740), channel_id=1, source_target_pairs={{0,2},{1,3},{2,0},{3,1},{4,6},{5,7},{6,4},{7,5},{8,10},{9,11},{10,... | collective-permute-start | bytes 589832 | tf_op jit(solution)/shard_map/while/body/ppermute | solution.py:381
  30.1 0.7 copy-start.8
  30.8 37.6 %collective-permute-start.17 = (f32[3,16,64,128]{3,2,1,0:T(8,128)}, f32[3,16,64,128]{3,2,1,0:T(8,128)}, u32[]{:S(2)}, u32[]{:S(2)}) collective-permute-start(f32[3,16,64,128]{3,2,1,0:T(8,128)} %get-tuple-element.320), channel_id=1, source_target_pairs={{0,16},{8,24},{16,0},{24,8},{1,17},{9,25},{17,1},{25,9},{2,18},{10... | collective-permute-start | bytes 4718600 | tf_op jit(solution)/shard_map/ppermute | solution.py:375
  33.5 1.0 copy-start.5
  33.5 69.3 %collective-permute-start.20 = (f32[3,16,64,128]{3,2,1,0:T(8,128)}, f32[3,16,64,128]{3,2,1,0:T(8,128)}, u32[]{:S(2)}, u32[]{:S(2)}) collective-permute-start(f32[3,16,64,128]{3,2,1,0:T(8,128)} %get-tuple-element.341), channel_id=1, source_target_pairs={{0,16},{8,24},{16,0},{24,8},{1,17},{9,25},{17,1},{25,9},{2,18},{10... | collective-permute-start | bytes 4718600 | tf_op jit(solution)/shard_map/ppermute | solution.py:375
  34.5 12.0 %collective-permute-start.5 = (f32[3,128,128]{2,1,0:T(8,128)}, f32[3,128,128]{2,1,0:T(8,128)S(1)}, u32[]{:S(2)}, u32[]{:S(2)}) collective-permute-start(f32[3,128,128]{2,1,0:T(8,128)} %get-tuple-element.752.refs_2_), channel_id=1, source_target_pairs={{0,1},{1,0},{2,3},{3,2},{4,5},{5,4},{6,7},{7,6},{8,9},{9,8},{10,11... | collective-permute-start | bytes 589832 | tf_op jit(solution)/shard_map/while/body/ppermute | solution.py:381
  36.0 8.5 %copy-start = (f32[128,3,16,256]{3,2,1,0:T(8,128)S(1)}, f32[128,3,16,256]{3,2,1,0:T(8,128)}, u32[]{:S(2)}) copy-start(f32[128,3,16,256]{3,2,1,0:T(8,128)} %get-tuple-element.874) | copy-start | bytes 18874372 | tf_op jit(solution)/shard_map/while
  38.9 7.7 %collective-permute-start.4 = (f32[384,128]{1,0:T(8,128)S(1)}, f32[384,128]{1,0:T(8,128)S(1)}, u32[]{:S(2)}, u32[]{:S(2)}) collective-permute-start(f32[384,128]{1,0:T(8,128)S(1)} %get-tuple-element.751), channel_id=1, source_target_pairs={{1,0},{2,1},{3,2},{4,3},{5,4},{6,5},{7,6},{0,7},{9,8},{10,9},{11,1... | collective-permute-start | bytes 589832 | tf_op jit(solution)/shard_map/while/body/ppermute | solution.py:394
  42.5 8.4 %collective-permute-start.6 = (f32[384,128]{1,0:T(8,128)S(1)}, f32[384,128]{1,0:T(8,128)S(1)}, u32[]{:S(2)}, u32[]{:S(2)}) collective-permute-start(f32[384,128]{1,0:T(8,128)S(1)} %get-tuple-element.754), channel_id=1, source_target_pairs={{0,1},{1,2},{2,3},{3,4},{4,5},{5,6},{6,7},{7,0},{8,9},{9,10},{10,1... | collective-permute-start | bytes 589832 | tf_op jit(solution)/shard_map/while/body/ppermute | solution.py:394
  44.6 6.2 %copy-start.2 = (f32[2048,128]{1,0:T(8,128)}, f32[2048,128]{1,0:T(8,128)S(1)}, u32[]{:S(2)}) copy-start(f32[2048,128]{1,0:T(8,128)S(1)} %turn_state.3.state) | copy-start | bytes 3145732 | tf_op jit(solution)/shard_map/while
  51.7 5.9 %copy-start.1 = (f32[3,16,128,128]{3,2,1,0:T(8,128)}, f32[3,16,128,128]{3,2,1,0:T(8,128)S(1)}, u32[]{:S(2)}) copy-start(f32[3,16,128,128]{3,2,1,0:T(8,128)S(1)} %first_stencil.3) | copy-start | bytes 9437188 | tf_op jit(solution)/shard_map/while
  51.7 5.9 %collective-permute-start.7 = (f32[3,16,128,128]{3,2,1,0:T(8,128)S(1)}, f32[3,16,128,128]{3,2,1,0:T(8,128)}, u32[]{:S(2)}, u32[]{:S(2)}) collective-permute-start(f32[3,16,128,128]{3,2,1,0:T(8,128)S(1)} %first_stencil.3), channel_id=1, source_target_pairs={{0,8},{8,0},{16,24},{24,16},{1,9},{9,1},{17,25},{25,17},{2,10},{10... | collective-permute-start | bytes 9437192 | tf_op jit(solution)/shard_map/while/body/ppermute | solution.py:378
  68.4 3.6 %collective-permute-start.8 = (f32[3,16,64,128]{3,2,1,0:T(8,128)}, f32[3,16,64,128]{3,2,1,0:T(8,128)S(1)}, u32[]{:S(2)}, u32[]{:S(2)}) collective-permute-start(f32[3,16,64,128]{3,2,1,0:T(8,128)} %get-tuple-element.768.far), channel_id=1, source_target_pairs={{0,8},{8,0},{16,24},{24,16},{1,9},{9,1},{17,25},{25,17},{2,10},{10... | collective-permute-start | bytes 4718600 | tf_op jit(solution)/shard_map/while/body/ppermute | solution.py:378
  72.0 16.6 %copy-start.3 = (f32[2048,128]{1,0:T(8,128)S(1)}, f32[2048,128]{1,0:T(8,128)}, u32[]{:S(2)}) copy-start(f32[2048,128]{1,0:T(8,128)} %get-tuple-element.917.refs_3_) | copy-start | bytes 3145732 | tf_op jit(solution)/shard_map/while
  72.0 16.6 %copy-start.6 = (f32[2056,128]{1,0:T(8,128)S(1)}, f32[2056,128]{1,0:T(8,128)}, u32[]{:S(2)}) copy-start(f32[2056,128]{1,0:T(8,128)} %get-tuple-element.918.refs_4_) | copy-start | bytes 3158020 | tf_op jit(solution)/shard_map/while
  77.2 9.8 %collective-permute-start.10 = (f32[3,64,256]{2,1,0:T(8,128)S(1)}, f32[3,64,256]{2,1,0:T(8,128)S(1)}, u32[]{:S(2)}, u32[]{:S(2)}) collective-permute-start(f32[3,64,256]{2,1,0:T(8,128)S(1)} %get-tuple-element.771), channel_id=1, source_target_pairs={{0,1},{1,2},{2,3},{3,4},{4,5},{5,6},{6,7},{7,0},{8,9},{9,10},{10,1... | collective-permute-start | bytes 589832 | tf_op jit(solution)/shard_map/while/body/ppermute | solution.py:394
  77.7 10.9 %collective-permute-start.9 = (f32[3,64,256]{2,1,0:T(8,128)S(1)}, f32[3,64,256]{2,1,0:T(8,128)S(1)}, u32[]{:S(2)}, u32[]{:S(2)}) collective-permute-start(f32[3,64,256]{2,1,0:T(8,128)S(1)} %get-tuple-element.770), channel_id=1, source_target_pairs={{1,0},{2,1},{3,2},{4,3},{5,4},{6,5},{7,6},{0,7},{9,8},{10,9},{11,1... | collective-permute-start | bytes 589832 | tf_op jit(solution)/shard_map/while/body/ppermute | solution.py:394
  89.4 5.9 %collective-permute-start.11 = (f32[3,16,64,256]{3,2,1,0:T(8,128)S(1)}, f32[3,16,64,256]{3,2,1,0:T(8,128)}, u32[]{:S(2)}, u32[]{:S(2)}) collective-permute-start(f32[3,16,64,256]{3,2,1,0:T(8,128)S(1)} %second_stencil_0.1.own), channel_id=1, source_target_pairs={{0,8},{8,0},{16,24},{24,16},{1,9},{9,1},{17,25},{25,17},{2,10},{10... | collective-permute-start | bytes 9437192 | tf_op jit(solution)/shard_map/while/body/ppermute | solution.py:378
  101.4 50.4 %collective-permute-start.19 = (f32[3,16,64,128]{3,2,1,0:T(8,128)}, f32[3,16,64,128]{3,2,1,0:T(8,128)}, u32[]{:S(2)}, u32[]{:S(2)}) collective-permute-start(f32[3,16,64,128]{3,2,1,0:T(8,128)} %get-tuple-element.334), channel_id=1, source_target_pairs={{0,16},{8,24},{16,0},{24,8},{1,17},{9,25},{17,1},{25,9},{2,18},{10... | collective-permute-start | bytes 4718600 | tf_op jit(solution)/shard_map/ppermute | solution.py:375
  102.8 3.6 %collective-permute-start.12 = (f32[3,16,64,128]{3,2,1,0:T(8,128)}, f32[3,16,64,128]{3,2,1,0:T(8,128)S(1)}, u32[]{:S(2)}, u32[]{:S(2)}) collective-permute-start(f32[3,16,64,128]{3,2,1,0:T(8,128)} %get-tuple-element.784.far), channel_id=1, source_target_pairs={{0,8},{8,0},{16,24},{24,16},{1,9},{9,1},{17,25},{25,17},{2,10},{10... | collective-permute-start | bytes 4718600 | tf_op jit(solution)/shard_map/while/body/ppermute | solution.py:378
  106.5 17.4 %copy-start.4 = (f32[2048,128]{1,0:T(8,128)S(1)}, f32[2048,128]{1,0:T(8,128)}, u32[]{:S(2)}) copy-start(f32[2048,128]{1,0:T(8,128)} %get-tuple-element.962.refs_3_) | copy-start | bytes 3145732 | tf_op jit(solution)/shard_map/while
  106.5 17.4 %copy-start.7 = (f32[2056,128]{1,0:T(8,128)S(1)}, f32[2056,128]{1,0:T(8,128)}, u32[]{:S(2)}) copy-start(f32[2056,128]{1,0:T(8,128)} %get-tuple-element.963.refs_4_) | copy-start | bytes 3158020 | tf_op jit(solution)/shard_map/while
  111.6 7.4 %collective-permute-start.13 = (f32[3,64,256]{2,1,0:T(8,128)S(1)}, f32[3,64,256]{2,1,0:T(8,128)S(1)}, u32[]{:S(2)}, u32[]{:S(2)}) collective-permute-start(f32[3,64,256]{2,1,0:T(8,128)S(1)} %get-tuple-element.786), channel_id=1, source_target_pairs={{1,0},{2,1},{3,2},{4,3},{5,4},{6,5},{7,6},{0,7},{9,8},{10,9},{11,1... | collective-permute-start | bytes 589832 | tf_op jit(solution)/shard_map/while/body/ppermute | solution.py:394
  114.6 9.4 %collective-permute-start.14 = (f32[3,64,256]{2,1,0:T(8,128)S(1)}, f32[3,64,256]{2,1,0:T(8,128)S(1)}, u32[]{:S(2)}, u32[]{:S(2)}) collective-permute-start(f32[3,64,256]{2,1,0:T(8,128)S(1)} %get-tuple-element.787), channel_id=1, source_target_pairs={{0,1},{1,2},{2,3},{3,4},{4,5},{5,6},{6,7},{7,0},{8,9},{9,10},{10,1... | collective-permute-start | bytes 589832 | tf_op jit(solution)/shard_map/while/body/ppermute | solution.py:394
  124.7 5.9 %collective-permute-start.15 = (f32[3,16,64,256]{3,2,1,0:T(8,128)S(1)}, f32[3,16,64,256]{3,2,1,0:T(8,128)}, u32[]{:S(2)}, u32[]{:S(2)}) collective-permute-start(f32[3,16,64,256]{3,2,1,0:T(8,128)S(1)} %second_stencil_1.1.own), channel_id=1, source_target_pairs={{0,8},{8,0},{16,24},{24,16},{1,9},{9,1},{17,25},{25,17},{2,10},{10... | collective-permute-start | bytes 9437192 | tf_op jit(solution)/shard_map/while/body/ppermute | solution.py:378
  136.8 15.0 %collective-permute-start.23 = (f32[1,16,64,128]{3,2,1,0:T(8,128)}, f32[1,16,64,128]{3,2,1,0:T(8,128)S(1)}, u32[]{:S(2)}, u32[]{:S(2)}) collective-permute-start(f32[1,16,64,128]{3,2,1,0:T(8,128)} %get-tuple-element.344), channel_id=1, source_target_pairs={{0,16},{8,24},{16,0},{24,8},{1,17},{9,25},{17,1},{25,9},{2,18},{10... | collective-permute-start | bytes 1572872 | tf_op jit(solution)/shard_map/ppermute | solution.py:375
  137.8 25.2 %collective-permute-start.22 = (f32[1,16,64,128]{3,2,1,0:T(8,128)}, f32[1,16,64,128]{3,2,1,0:T(8,128)S(1)}, u32[]{:S(2)}, u32[]{:S(2)}) collective-permute-start(f32[1,16,64,128]{3,2,1,0:T(8,128)} %get-tuple-element.343), channel_id=1, source_target_pairs={{0,16},{8,24},{16,0},{24,8},{1,17},{9,25},{17,1},{25,9},{2,18},{10... | collective-permute-start | bytes 1572872 | tf_op jit(solution)/shard_map/ppermute | solution.py:375
  138.8 34.6 %collective-permute-start.21 = (f32[1,16,64,128]{3,2,1,0:T(8,128)}, f32[1,16,64,128]{3,2,1,0:T(8,128)S(1)}, u32[]{:S(2)}, u32[]{:S(2)}) collective-permute-start(f32[1,16,64,128]{3,2,1,0:T(8,128)} %get-tuple-element.342), channel_id=1, source_target_pairs={{0,16},{8,24},{16,0},{24,8},{1,17},{9,25},{17,1},{25,9},{2,18},{10... | collective-permute-start | bytes 1572872 | tf_op jit(solution)/shard_map/ppermute | solution.py:375

commit v9 on v8

--- a/solution.py
+++ b/solution.py
@@ -234,33 +234,59 @@
     )(where, own, *far)
 
 
-def map1_kernel(own, far, own_peer, far_peer, high, low, out, first, last):
+def map1_kernel(own, far, own_peer, far_peer, high, low, out):
     _, nz, width, modes = own.shape
-    rows = nz * width
-    parts = [ref[0].reshape(rows, modes) for ref in (own, far, own_peer, far_peer)]
-    res = product(parts, high[0], low[0]).reshape(nz, width, high.shape[2])
-    out[0] = res
-    first[0] = res[0]
-    last[0] = res[nz - 1]
+    parts = [ref[0].reshape(nz * width, modes) for ref in (own, far, own_peer, far_peer)]
+    out[0] = product(parts, high[0], low[0]).reshape(nz, width, high.shape[2])
 
 
 def map1(own, far, own_peer, far_peer, high, low, k):
     comps, nz, width, modes = far.shape
     rows, cols = high.shape[1:]
     here = pl.BlockSpec((1, nz, width, modes), lambda c: (c, 0, k, 0))
-    chunk = pl.BlockSpec((1, nz, width, modes), lambda c: (c, 0, 0, 0))
+    group = pl.BlockSpec((1, nz, width, modes), lambda c: (c, 0, 0, 0))
     helm = pl.BlockSpec((1, rows, cols), lambda c: (c, 0, 0))
-    layer = pl.BlockSpec((1, width, cols), lambda c: (c, 0, 0))
     return pl.pallas_call(
         map1_kernel,
-        out_shape=[shape((comps, nz, width, cols)), shape((comps, width, cols)), shape((comps, width, cols))],
+        out_shape=shape((comps, nz, width, cols)),
         grid=(comps,),
-        in_specs=[here, chunk, here, chunk, helm, helm],
-        out_specs=[pl.BlockSpec((1, nz, width, cols), lambda c: (c, 0, 0, 0)), layer, layer],
+        in_specs=[here, group, here, group, helm, helm],
+        out_specs=pl.BlockSpec((1, nz, width, cols), lambda c: (c, 0, 0, 0)),
         compiler_params=params(24),
         cost_estimate=cost(6 * comps * nz * width * rows * cols, 4 * comps * (nz * width * (rows + cols) + rows * cols)),
         name=f"map1_{k}",
     )(own, far, own_peer, far_peer, high, low)
+
+
+def layers1_kernel(*refs):
+    firsts, lasts, (high, low, first, last) = refs[:4], refs[4:8], refs[8:]
+    width = first.shape[1]
+    parts = [jnp.concatenate([a[0, 0], b[0, 0]], axis=0) for a, b in zip(firsts, lasts)]
+    res = product(parts, high[0], low[0])
+    first[0] = res[:width]
+    last[0] = res[width:]
+
+
+def layers1(own, far, own_peer, far_peer, high, low, k):
+    comps, nz, width, modes = far.shape
+    rows, cols = high.shape[1:]
+    block = (1, 1, width, modes)
+    specs = []
+    for z in (0, nz - 1):
+        here = pl.BlockSpec(block, lambda c, z=z: (c, z, k, 0))
+        group = pl.BlockSpec(block, lambda c, z=z: (c, z, 0, 0))
+        specs += [here, group, here, group]
+    helm = pl.BlockSpec((1, rows, cols), lambda c: (c, 0, 0))
+    return pl.pallas_call(
+        layers1_kernel,
+        out_shape=[shape((comps, width, cols))] * 2,
+        grid=(comps,),
+        in_specs=[*specs, helm, helm],
+        out_specs=[pl.BlockSpec((1, width, cols), lambda c: (c, 0, 0))] * 2,
+        compiler_params=params(16),
+        cost_estimate=cost(12 * comps * width * rows * cols, 4 * comps * (2 * width * (rows + cols) + rows * cols)),
+        name=f"layers1_{k}",
+    )(*[own, far, own_peer, far_peer] * 2, high, low)
 
 
 def second_kernel(cur, after, before, state_own, state_far, rate, out, *, k, half):
@@ -430,8 +456,8 @@
 
         def chain(step, _, k=k, pieces=pieces):
             here = tied(far[k], step)
-            cur, leading, last = map1(own, here, own_peer, beside(here), high, low, k)
-            nxt = second_stencil(cur, *halos(leading, last), state_own, state_far, rate, k, half)
+            parts = (own, here, own_peer, beside(here), high, low)
+            nxt = second_stencil(map1(*parts, k), *halos(*layers1(*parts, k)), state_own, state_far, rate, k, half)
             return tuple(map2(nxt, beside(nxt), high, low, k, pieces))
 
         spare = tied(sent[k], kept[-1]) if kept else sent[k]

time: 177 us -> 174 us (0.983)
  waiting for transfers between devices: 81.4 us -> 72.2 us
  Pallas kernels: 63.6 us -> 69 us
    ppermute x8, waiting for transfers between devices: 25.7 us -> 16.5 us  [halos(): return (lax.ppermute(leading, 'col', down), lax.ppermute(last, 'col', up))]
    pallas_call x2 -> x4, Pallas kernels: 10.3 us -> 15.7 us  [the longest x2 9.11 us: map1(): pl.pallas_call(map1_kernel, out_shape=shape((comps, nz, width, cols)), gr...]
  transfers between devices with their start and end apart: 24 -> 24, of which waited for: 18 -> 17; matrix products, arithmetic and copies ran while one was open for 0% -> 0% of each run, Pallas kernels for 34% -> 38%
where the time goes in v9:
time: 174 us; the launch traced here: 173 us
  waiting for transfers between devices  72.2 us (41%)
  Pallas kernels  69 us (40%)
  starting transfers between devices  29.1 us (17%)
  local copies, waits for them, and re-layouts  2.32 us (1%)
    ppermute x8, waiting for transfers between devices, across(): return lax.ppermute(array, 'rad', [(i, i ^ 2) for i in range(peers)])  35.9 us
    ppermute x5, waiting for transfers between devices, beside(): return lax.ppermute(array, 'rad', [(i, i ^ 1) for i in range(peers)])  19.8 us
    ppermute x8, waiting for transfers between devices, halos(): return (lax.ppermute(leading, 'col', down), lax.ppermute(last, 'col', up))  16.5 us
    ppermute x8, starting transfers between devices, halos(): return (lax.ppermute(leading, 'col', down), lax.ppermute(last, 'col', up))  16.4 us
    pallas_call x4, Pallas kernels, write_half(): pl.pallas_call(lambda *refs: last_kernel(*refs, nz=nz, chunks=chunks), ou...  14.4 us
    pallas_call x2, Pallas kernels, map2(): pl.pallas_call(map2_kernel, out_shape=[shape((comps, *block[1:]))] + [sha...  12.4 us
    ppermute x8, starting transfers between devices, across(): return lax.ppermute(array, 'rad', [(i, i ^ 2) for i in range(peers)])  9.53 us
    pallas_call x2, Pallas kernels, map1(): pl.pallas_call(map1_kernel, out_shape=shape((comps, nz, width, cols)), gr...  9.11 us
  transfers between devices with their start and end apart: 24, of which 17 were waited for; matrix products, arithmetic and copies ran while one was open for 0% of the time, Pallas kernels for 38%

profile of v9, /device:TPU:0, one launch (start us, length us, event | category | flops | bytes accessed | tf_op | source)
XLA Modules:
  0.0 173.0 jit_solution(5774291582746870272)
XLA Ops:
  0.9 3.0 %collective-permute-start.16 = (f32[3,128,128]{2,1,0:T(8,128)S(1)}, f32[3,128,128]{2,1,0:T(8,128)S(1)}, u32[]{:S(2)}, u32[]{:S(2)}) collective-permute-start(f32[3,128,128]{2,1,0:T(8,128)S(1)} %constant_dynamic-slice_fusion), channel_id=1, source_target_pairs={{0,16},{8,24},{16,0},{24,8},{1,17},{9,25},{17,1},{25,9},{2,18},{10... | collective-permute-start | bytes 589832 | tf_op jit(solution)/shard_map/ppermute | solution.py:401
  4.0 3.1 %turn_state.2 = f32[2056,128]{1,0:T(8,128)} custom-call(s32[2]{0:T(128)S(1)} %pad_add_fusion.refs_0_, f32[2048,256]{1,0:T(8,128)} %bitcast.18, f32[1,128]{1,0:T(1,128)} %bitcast.20), custom_call_target="tpu_custom_call" | custom-call | flops 263168 | bytes 2105344 | tf_op jit(solution)/shard_map/turn_state/pallas_call | solution.py:77
  7.2 1.7 collective-permute-done.16
  8.9 21.9 %while.62 = (s32[]{:T(128)}, f32[3,16,64,128]{3,2,1,0:T(8,128)}, f32[3,16,64,128]{3,2,1,0:T(8,128)}, f32[3,128,128]{2,1,0:T(8,128)}, f32[3,128,128]{2,1,0:T(8,12...) while((s32[]{:T(128)}, f32[3,16,64,128]{3,2,1,0:T(8,128)}, ...), condition=%wide.region_1.0_spmd, body=%wide.region_0.0_spmd.sunk | while | flops 10321925 | bytes 19661144 | solution.py:431
  8.9 2.6 %edge_layers.2 = (f32[384,128]{1,0:T(8,128)S(1)}, f32[384,128]{1,0:T(8,128)S(1)}) custom-call(s32[2]{0:T(128)S(1)} %broadcast_add_fusion.4.refs_0_, f32[6144,256]{1,0:T(8,128)} %bitcast.14), custom_call_target="tpu_custom_call" | custom-call | flops 98304 | bytes 3145728 | tf_op jit(solution)/shard_map/while/body/edge_layers/pallas_call | solution.py:103
  11.4 4.9 %collective-permute-start = (f32[384,128]{1,0:T(8,128)S(1)}, f32[384,128]{1,0:T(8,128)S(1)}, u32[]{:S(2)}, u32[]{:S(2)}) collective-permute-start(f32[384,128]{1,0:T(8,128)S(1)} %get-tuple-element.732), channel_id=1, source_target_pairs={{1,0},{2,1},{3,2},{4,3},{5,4},{6,5},{7,6},{0,7},{9,8},{10,9},{11,1... | collective-permute-start | bytes 589832 | tf_op jit(solution)/shard_map/while/body/ppermute | solution.py:420
  16.3 1.5 collective-permute-start.3
  17.8 3.4 %turn_half.2.turned = f32[3,16,128,128]{3,2,1,0:T(8,128)S(1)} custom-call(s32[2]{0:T(128)S(1)} %broadcast_add_fusion.4.refs_0_, f32[6144,256]{1,0:T(8,128)} %bitcast.15), custom_call_target="tpu_custom_call" | custom-call | flops 786432 | bytes 6291456 | tf_op jit(solution)/shard_map/while/body/turn_half/pallas_call | solution.py:138
  21.6 5.0 %collective-permute-done.1.before = f32[384,128]{1,0:T(8,128)S(1)} collective-permute-done((f32[384,128]{1,0:T(8,128)S(1)}, f32[384,128]{1,0:T(8,128)S(1)}, u32[]{:S(2)}, u32[]{:S(2)}) %collective-permute-start.1) | collective-permute-done | bytes 196640 | tf_op jit(solution)/shard_map/while/body/ppermute | solution.py:420
  26.6 3.5 %first_stencil.2 = (f32[3,16,64,128]{3,2,1,0:T(8,128)}, f32[3,16,64,128]{3,2,1,0:T(8,128)}) custom-call(f32[3,16,128,128]{3,2,1,0:T(8,128)S(1)} %turn_half.2.turned, f32[2056,128]{1,0:T(8,128)} %get-tuple-element.820.state, f32[384,128]{1,0:T(8,128)S(1)} %collective-permute-done.after, f32[384,128]{1,0:T(8,128)S(1)} %collective-permute-done.1.before, ...), custom_call_target="tpu_custom_call" | custom-call | flops 9437184 | bytes 6291456 | tf_op jit(solution)/shard_map/while/body/first_stencil/pallas_call | solution.py:178
  30.8 1.6 collective-permute-start.17
  32.3 1.2 collective-permute-done.18
  34.5 23.0 %while.63 = (s32[]{:T(128)}, f32[2048,128]{1,0:T(8,128)}, f32[3,16,128,128]{3,2,1,0:T(8,128)}, f32[3,16,128,128]{3,2,1,0:T(8,128)}, bf16[3,512,256]{2,1,0:T(8,12...) while((s32[]{:T(128)}, f32[2048,128]{1,0:T(8,128)}, ...), condition=%wide.region_3.0_spmd, body=%wide.region_2.0_spmd.sunk | while | flops 11370501 | bytes 77857200 | solution.py:448
  34.5 1.5 collective-permute-start.5
  36.0 2.8 %edge_layers.3 = (f32[384,128]{1,0:T(8,128)S(1)}, f32[384,128]{1,0:T(8,128)S(1)}) custom-call(s32[2]{0:T(128)S(1)} %broadcast_add_fusion.5.refs_0_.where, f32[6144,256]{1,0:T(8,128)} %bitcast.16), custom_call_target="tpu_custom_call" | custom-call | flops 98304 | bytes 3145728 | tf_op jit(solution)/shard_map/while/body/edge_layers/pallas_call | solution.py:103
  38.8 3.6 %collective-permute-start.4 = (f32[384,128]{1,0:T(8,128)S(1)}, f32[384,128]{1,0:T(8,128)S(1)}, u32[]{:S(2)}, u32[]{:S(2)}) collective-permute-start(f32[384,128]{1,0:T(8,128)S(1)} %get-tuple-element.747), channel_id=1, source_target_pairs={{1,0},{2,1},{3,2},{4,3},{5,4},{6,5},{7,6},{0,7},{9,8},{10,9},{11,1... | collective-permute-start | bytes 589832 | tf_op jit(solution)/shard_map/while/body/ppermute | solution.py:420
  42.4 2.1 %turn_state.3.state = f32[2048,128]{1,0:T(8,128)S(1)} custom-call(s32[2]{0:T(128)S(1)} %broadcast_add_fusion.5.refs_0_.where, f32[2048,256]{1,0:T(8,128)} %bitcast.19), custom_call_target="tpu_custom_call" | custom-call | flops 262144 | bytes 2097152 | tf_op jit(solution)/shard_map/while/body/turn_state/pallas_call | solution.py:77
  44.6 1.9 %turn_half.3.turned = f32[3,16,128,128]{3,2,1,0:T(8,128)S(1)} custom-call(s32[2]{0:T(128)S(1)} %broadcast_add_fusion.5.refs_0_.where, f32[6144,256]{1,0:T(8,128)S(1)} %bitcast.17), custom_call_target="tpu_custom_call" | custom-call | flops 786432 | bytes 6291456 | tf_op jit(solution)/shard_map/while/body/turn_half/pallas_call | solution.py:138
  46.5 4.3 %collective-permute-done.6.before = f32[384,128]{1,0:T(8,128)S(1)} collective-permute-done((f32[384,128]{1,0:T(8,128)S(1)}, f32[384,128]{1,0:T(8,128)S(1)}, u32[]{:S(2)}, u32[]{:S(2)}) %collective-permute-start.6) | collective-permute-done | bytes 196640 | tf_op jit(solution)/shard_map/while/body/ppermute | solution.py:420
  51.7 4.8 %split_helm.1 = (bf16[3,512,256]{2,1,0:T(8,128)(2,1)}, bf16[3,512,256]{2,1,0:T(8,128)(2,1)}) custom-call(s32[2]{0:T(128)S(1)} %broadcast_add_fusion.5.refs_0_.where, f32[3,512,128]{2,1,0:T(8,128)} %get-tuple-element.871.own, f32[3,128,128]{2,1,0:T(8,128)S(1)} %get-tuple-element.872.refs_0_, f32[3,128,128]{2,1,0:T(8,128)} %get-tuple-element.873.refs_1_, ...), custom_call_target="tpu_custom_call" | custom-call | flops 786432 | bytes 3145728 | tf_op jit(solution)/shard_map/while/body/split_helm/pallas_call | solution.py:221
  56.5 1.0 collective-permute-done.7
  57.5 10.9 %collective-permute-done.17 = f32[3,16,64,128]{3,2,1,0:T(8,128)} collective-permute-done((f32[3,16,64,128]{3,2,1,0:T(8,128)}, f32[3,16,64,128]{3,2,1,0:T(8,128)}, u32[]{:S(2)}, u32[]{:S(2)}) %collective-permute-start.17) | collective-permute-done | bytes 1572896 | tf_op jit(solution)/shard_map/ppermute | solution.py:401
  68.4 31.1 %while.64 = (s32[]{:T(128)}, f32[3,16,64,128]{3,2,1,0:T(8,128)}, f32[3,16,64,128]{3,2,1,0:T(8,128)}, s32[]{:T(128)}, f32[3,16,64,128]{3,2,1,0:T(8,128)}, /*index...) while((s32[]{:T(128)}, f32[3,16,64,128]{3,2,1,0:T(8,128)}, ...), condition=%wide.region_5.0_spmd, body=%wide.region_4.0_spmd.sunk | while | flops 5143265280 | bytes 78791080 | solution.py:465
  68.4 3.6 %collective-permute-done.8.far_peer.refs_3_.refs_7_ = f32[3,16,64,128]{3,2,1,0:T(8,128)S(1)} collective-permute-done((f32[3,16,64,128]{3,2,1,0:T(8,128)}, f32[3,16,64,128]{3,2,1,0:T(8,128)S(1)}, u32[]{:S(2)}, u32[]{:S(2)}) %collective-permute-start.8) | collective-permute-done | bytes 1572896 | tf_op jit(solution)/shard_map/while/body/ppermute | solution.py:404
  72.0 3.3 %layers1_0.1 = (f32[3,64,256]{2,1,0:T(8,128)S(1)}, f32[3,64,256]{2,1,0:T(8,128)S(1)}) custom-call(f32[3,16,128,128]{3,2,1,0:T(8,128)} %get-tuple-element.907.own.refs_0_.refs_4_, f32[3,16,64,128]{3,2,1,0:T(8,128)} %get-tuple-element.764.far.refs_1_.refs_5_, f32[3,16,128,128]{3,2,1,0:T(8,128)} %get-tuple-element.908.own_peer.refs_2_.refs_6_, ...), custom_call_target="tpu_custom_call" | custom-call | flops 301989888 | bytes 2752512 | tf_op jit(solution)/shard_map/while/body/layers1_0/pallas_call | solution.py:280
  75.9 4.3 %collective-permute-start.9 = (f32[3,64,256]{2,1,0:T(8,128)S(1)}, f32[3,64,256]{2,1,0:T(8,128)S(1)}, u32[]{:S(2)}, u32[]{:S(2)}) collective-permute-start(f32[3,64,256]{2,1,0:T(8,128)S(1)} %get-tuple-element.765), channel_id=1, source_target_pairs={{1,0},{2,1},{3,2},{4,3},{5,4},{6,5},{7,6},{0,7},{9,8},{10,9},{11,1... | collective-permute-start | bytes 589832 | tf_op jit(solution)/shard_map/while/body/ppermute | solution.py:420
  80.2 4.5 %map1_0.1.refs_0_ = f32[3,16,64,256]{3,2,1,0:T(8,128)S(1)} custom-call(f32[3,16,128,128]{3,2,1,0:T(8,128)S(1)} %copy-done.1, f32[3,16,64,128]{3,2,1,0:T(8,128)} %get-tuple-element.764.far.refs_1_.refs_5_, f32[3,16,128,128]{3,2,1,0:T(8,128)} %get-tuple-element.908.own_peer.refs_2_.refs_6_, ...), custom_call_target="tpu_custom_call" | custom-call | flops 2415919104 | bytes 11010048 | tf_op jit(solution)/shard_map/while/body/map1_0/pallas_call | solution.py:249
  85.2 1.6 collective-permute-done.9.refs_1_
  87.6 5.8 %collective-permute-done.11.peer = f32[3,16,64,256]{3,2,1,0:T(8,128)} collective-permute-done((f32[3,16,64,256]{3,2,1,0:T(8,128)S(1)}, f32[3,16,64,256]{3,2,1,0:T(8,128)}, u32[]{:S(2)}, u32[]{:S(2)}) %collective-permute-start.11) | collective-permute-done | bytes 3145760 | tf_op jit(solution)/shard_map/while/body/ppermute | solution.py:404
  93.4 6.2 %map2_0.1 = (f32[3,16,64,128]{3,2,1,0:T(8,128)}, f32[3,16,64,128]{3,2,1,0:T(8,128)}) custom-call(f32[3,16,64,256]{3,2,1,0:T(8,128)S(1)} %second_stencil_0.1.own, f32[3,16,64,256]{3,2,1,0:T(8,128)} %collective-permute-done.11.peer, bf16[3,512,256]{2,1,0:T(8,128)(2,1)} %get-tuple-element.909.high.refs_8_, bf16[3,512,256]{2,1,0:T(8,128)(2,1)} %get-tuple-element.910.low.refs_9_), custom_call_target="tpu_custom_call" | custom-call | flops 2415919104 | bytes 11010048 | tf_op jit(solution)/shard_map/while/body/map2_0/pallas_call | solution.py:340
  99.5 1.5 collective-permute-start.19
  101.0 32.4 %while.65 = (s32[]{:T(128)}, f32[3,16,64,128]{3,2,1,0:T(8,128)}, f32[1,16,64,128]{3,2,1,0:T(8,128)}, f32[1,16,64,128]{3,2,1,0:T(8,128)}, f32[1,16,64,128]{3,2,1,...) while((s32[]{:T(128)}, f32[3,16,64,128]{3,2,1,0:T(8,128)}, ...), condition=%wide.region_7.0_spmd, body=%wide.region_6.0_spmd.sunk | while | flops 5143265280 | bytes 78791096 | solution.py:465
  101.0 3.6 %collective-permute-done.12.far_peer.refs_3_.refs_7_ = f32[3,16,64,128]{3,2,1,0:T(8,128)S(1)} collective-permute-done((f32[3,16,64,128]{3,2,1,0:T(8,128)}, f32[3,16,64,128]{3,2,1,0:T(8,128)S(1)}, u32[]{:S(2)}, u32[]{:S(2)}) %collective-permute-start.12) | collective-permute-done | bytes 1572896 | tf_op jit(solution)/shard_map/while/body/ppermute | solution.py:404
  104.7 3.3 %layers1_1.1 = (f32[3,64,256]{2,1,0:T(8,128)S(1)}, f32[3,64,256]{2,1,0:T(8,128)S(1)}) custom-call(f32[3,16,128,128]{3,2,1,0:T(8,128)} %get-tuple-element.952.own.refs_0_.refs_4_, f32[3,16,64,128]{3,2,1,0:T(8,128)} %get-tuple-element.779.far.refs_1_.refs_5_, f32[3,16,128,128]{3,2,1,0:T(8,128)} %get-tuple-element.953.own_peer.refs_2_.refs_6_, ...), custom_call_target="tpu_custom_call" | custom-call | flops 301989888 | bytes 2752512 | tf_op jit(solution)/shard_map/while/body/layers1_1/pallas_call | solution.py:280
  108.0 3.2 %collective-permute-start.13 = (f32[3,64,256]{2,1,0:T(8,128)S(1)}, f32[3,64,256]{2,1,0:T(8,128)S(1)}, u32[]{:S(2)}, u32[]{:S(2)}) collective-permute-start(f32[3,64,256]{2,1,0:T(8,128)S(1)} %get-tuple-element.780), channel_id=1, source_target_pairs={{1,0},{2,1},{3,2},{4,3},{5,4},{6,5},{7,6},{0,7},{9,8},{10,9},{11,1... | collective-permute-start | bytes 589832 | tf_op jit(solution)/shard_map/while/body/ppermute | solution.py:420
  111.2 4.6 %map1_1.1.refs_0_ = f32[3,16,64,256]{3,2,1,0:T(8,128)S(1)} custom-call(f32[3,16,128,128]{3,2,1,0:T(8,128)S(1)} %copy-done.2, f32[3,16,64,128]{3,2,1,0:T(8,128)} %get-tuple-element.779.far.refs_1_.refs_5_, f32[3,16,128,128]{3,2,1,0:T(8,128)} %get-tuple-element.953.own_peer.refs_2_.refs_6_, ...), custom_call_target="tpu_custom_call" | custom-call | flops 2415919104 | bytes 11010048 | tf_op jit(solution)/shard_map/while/body/map1_1/pallas_call | solution.py:249
  115.8 4.7 %collective-permute-done.14.refs_2_ = f32[3,64,256]{2,1,0:T(8,128)S(1)} collective-permute-done((f32[3,64,256]{2,1,0:T(8,128)S(1)}, f32[3,64,256]{2,1,0:T(8,128)S(1)}, u32[]{:S(2)}, u32[]{:S(2)}) %collective-permute-start.14) | collective-permute-done | bytes 196640 | tf_op jit(solution)/shard_map/while/body/ppermute | solution.py:420
  121.4 5.8 %collective-permute-done.15.peer = f32[3,16,64,256]{3,2,1,0:T(8,128)} collective-permute-done((f32[3,16,64,256]{3,2,1,0:T(8,128)S(1)}, f32[3,16,64,256]{3,2,1,0:T(8,128)}, u32[]{:S(2)}, u32[]{:S(2)}) %collective-permute-start.15) | collective-permute-done | bytes 3145760 | tf_op jit(solution)/shard_map/while/body/ppermute | solution.py:404
  127.1 6.2 %map2_1.1 = (f32[3,16,64,128]{3,2,1,0:T(8,128)}, f32[1,16,64,128]{3,2,1,0:T(8,128)}, f32[1,16,64,128]{3,2,1,0:T(8,128)}, f32[1,16,64,128]{3,2,1,0:T(8,128)}) custom-call(f32[3,16,64,256]{3,2,1,0:T(8,128)S(1)} %second_stencil_1.1.own, f32[3,16,64,256]{3,2,1,0:T(8,128)} %collective-permute-done.15.peer, bf16[3,512,256]{2,1,0:T(8,128)(2,1)} %get-tuple-element.954.high.refs_8_, ...), custom_call_target="tpu_custom_call" | custom-call | flops 2415919104 | bytes 11010048 | tf_op jit(solution)/shard_map/while/body/map2_1/pallas_call | solution.py:340
  133.4 1.1 collective-permute-start.23
  135.4 1.1 collective-permute-start.21
  136.5 5.5 %write_own.1.refs_3_ = f32[128,48,256]{2,1,0:T(8,128)} custom-call(s32[2]{0:T(128)S(1)} %get-tuple-element.1005, f32[3,16,64,128]{3,2,1,0:T(8,128)} %get-tuple-element.334.refs_1_, f32[3,16,64,128]{3,2,1,0:T(8,128)} %get-tuple-element.343.refs_2_), custom_call_target="tpu_custom_call" | custom-call | flops 1572864 | bytes 6291456 | tf_op jit(solution)/shard_map/write_own/pallas_call | solution.py:373
  142.0 6.3 %collective-permute-done.23.refs_2_ = f32[1,16,64,128]{3,2,1,0:T(8,128)S(1)} collective-permute-done((f32[1,16,64,128]{3,2,1,0:T(8,128)}, f32[1,16,64,128]{3,2,1,0:T(8,128)S(1)}, u32[]{:S(2)}, u32[]{:S(2)}) %collective-permute-start.23) | collective-permute-done | bytes 524320 | tf_op jit(solution)/shard_map/ppermute | solution.py:401
  148.4 3.0 %write_foreign_0.1.refs_3_ = f32[128,48,256]{2,1,0:T(8,128)} custom-call(s32[2]{0:T(128)S(1)} %get-tuple-element.1005, f32[3,16,64,128]{3,2,1,0:T(8,128)} %collective-permute-done.19.refs_1_, f32[1,16,64,128]{3,2,1,0:T(8,128)S(1)} %collective-permute-done.23.refs_2_, f32[128,48,256]{2,1,0:T(8,128)} %write_own.1.refs_3_), custom_call_target="tpu_custom_call", output_to_operand_aliasing={{}: (3, {})} | custom-call | flops 524288 | bytes 2097152 | tf_op jit(solution)/shard_map/write_foreign_0/pallas_call | solution.py:373
  151.3 8.3 %collective-permute-done.22.refs_2_ = f32[1,16,64,128]{3,2,1,0:T(8,128)S(1)} collective-permute-done((f32[1,16,64,128]{3,2,1,0:T(8,128)}, f32[1,16,64,128]{3,2,1,0:T(8,128)S(1)}, u32[]{:S(2)}, u32[]{:S(2)}) %collective-permute-start.22) | collective-permute-done | bytes 524320 | tf_op jit(solution)/shard_map/ppermute | solution.py:401
  159.6 3.0 %write_foreign_1.1.refs_3_ = f32[128,48,256]{2,1,0:T(8,128)} custom-call(s32[2]{0:T(128)S(1)} %get-tuple-element.1005, f32[3,16,64,128]{3,2,1,0:T(8,128)} %collective-permute-done.19.refs_1_, f32[1,16,64,128]{3,2,1,0:T(8,128)S(1)} %collective-permute-done.22.refs_2_, f32[128,48,256]{2,1,0:T(8,128)} %write_foreign_0.1.refs_3_), custom_call_target="tpu_custom_call", output_to_operand_aliasing={{}: (3, {})} | custom-call | flops 524288 | bytes 2097152 | tf_op jit(solution)/shard_map/write_foreign_1/pallas_call | solution.py:373
  162.6 7.5 %collective-permute-done.21.refs_2_ = f32[1,16,64,128]{3,2,1,0:T(8,128)S(1)} collective-permute-done((f32[1,16,64,128]{3,2,1,0:T(8,128)}, f32[1,16,64,128]{3,2,1,0:T(8,128)S(1)}, u32[]{:S(2)}, u32[]{:S(2)}) %collective-permute-start.21) | collective-permute-done | bytes 524320 | tf_op jit(solution)/shard_map/ppermute | solution.py:401
  170.0 3.0 %write_foreign_2.1 = f32[128,48,256]{2,1,0:T(8,128)} custom-call(s32[2]{0:T(128)S(1)} %get-tuple-element.1005, f32[3,16,64,128]{3,2,1,0:T(8,128)} %collective-permute-done.19.refs_1_, f32[1,16,64,128]{3,2,1,0:T(8,128)S(1)} %collective-permute-done.21.refs_2_, f32[128,48,256]{2,1,0:T(8,128)} %write_foreign_1.1.refs_3_), custom_call_target="tpu_custom_call", output_to_operand_aliasing={{}: (3, {})} | custom-call | flops 524288 | bytes 2097152 | tf_op jit(solution)/shard_map/write_foreign_2/pallas_call | solution.py:373
  (65 shorter events, 7.8 us)
Async XLA Ops:
  0.9 7.9 %collective-permute-start.16 = (f32[3,128,128]{2,1,0:T(8,128)S(1)}, f32[3,128,128]{2,1,0:T(8,128)S(1)}, u32[]{:S(2)}, u32[]{:S(2)}) collective-permute-start(f32[3,128,128]{2,1,0:T(8,128)S(1)} %constant_dynamic-slice_fusion), channel_id=1, source_target_pairs={{0,16},{8,24},{16,0},{24,8},{1,17},{9,25},{17,1},{25,9},{2,18},{10... | collective-permute-start | bytes 589832 | tf_op jit(solution)/shard_map/ppermute | solution.py:401
  4.0 4.8 %copy-start.15 = (f32[128]{0:T(128)S(1)}, f32[128]{0:T(128)}, u32[]{:S(2)}) copy-start(f32[128]{0:T(128)} %param.15) | copy-start | bytes 1540
  7.1 26.4 %collective-permute-start.18 = (f32[2056,128]{1,0:T(8,128)}, f32[2056,128]{1,0:T(8,128)S(1)}, u32[]{:S(2)}, u32[]{:S(2)}) collective-permute-start(f32[2056,128]{1,0:T(8,128)} %turn_state.2), channel_id=1, source_target_pairs={{0,16},{8,24},{16,0},{24,8},{1,17},{9,25},{17,1},{25,9},{2,18},{10... | collective-permute-start | bytes 3158024 | tf_op jit(solution)/shard_map/ppermute | solution.py:401
  11.4 10.2 %collective-permute-start = (f32[384,128]{1,0:T(8,128)S(1)}, f32[384,128]{1,0:T(8,128)S(1)}, u32[]{:S(2)}, u32[]{:S(2)}) collective-permute-start(f32[384,128]{1,0:T(8,128)S(1)} %get-tuple-element.732), channel_id=1, source_target_pairs={{1,0},{2,1},{3,2},{4,3},{5,4},{6,5},{7,6},{0,7},{9,8},{10,9},{11,1... | collective-permute-start | bytes 589832 | tf_op jit(solution)/shard_map/while/body/ppermute | solution.py:420
  16.3 10.3 %collective-permute-start.1 = (f32[384,128]{1,0:T(8,128)S(1)}, f32[384,128]{1,0:T(8,128)S(1)}, u32[]{:S(2)}, u32[]{:S(2)}) collective-permute-start(f32[384,128]{1,0:T(8,128)S(1)} %get-tuple-element.733), channel_id=1, source_target_pairs={{0,1},{1,2},{2,3},{3,4},{4,5},{5,6},{6,7},{7,0},{8,9},{9,10},{10,1... | collective-permute-start | bytes 589832 | tf_op jit(solution)/shard_map/while/body/ppermute | solution.py:420
  16.3 13.8 %collective-permute-start.2 = (f32[3,128,128]{2,1,0:T(8,128)S(1)}, f32[3,128,128]{2,1,0:T(8,128)S(1)}, u32[]{:S(2)}, u32[]{:S(2)}) collective-permute-start(f32[3,128,128]{2,1,0:T(8,128)S(1)} %get-tuple-element.736), channel_id=1, source_target_pairs={{0,1},{1,0},{2,3},{3,2},{4,5},{5,4},{6,7},{7,6},{8,9},{9,8},{10,11... | collective-permute-start | bytes 589832 | tf_op jit(solution)/shard_map/while/body/ppermute | solution.py:407
  16.3 13.8 %collective-permute-start.3 = (f32[3,128,128]{2,1,0:T(8,128)S(1)}, f32[3,128,128]{2,1,0:T(8,128)}, u32[]{:S(2)}, u32[]{:S(2)}) collective-permute-start(f32[3,128,128]{2,1,0:T(8,128)S(1)} %get-tuple-element.736), channel_id=1, source_target_pairs={{0,2},{1,3},{2,0},{3,1},{4,6},{5,7},{6,4},{7,5},{8,10},{9,11},{10,... | collective-permute-start | bytes 589832 | tf_op jit(solution)/shard_map/while/body/ppermute | solution.py:407
  30.1 0.7 copy-start.14
  30.8 37.6 %collective-permute-start.17 = (f32[3,16,64,128]{3,2,1,0:T(8,128)}, f32[3,16,64,128]{3,2,1,0:T(8,128)}, u32[]{:S(2)}, u32[]{:S(2)}) collective-permute-start(f32[3,16,64,128]{3,2,1,0:T(8,128)} %get-tuple-element.318), channel_id=1, source_target_pairs={{0,16},{8,24},{16,0},{24,8},{1,17},{9,25},{17,1},{25,9},{2,18},{10... | collective-permute-start | bytes 4718600 | tf_op jit(solution)/shard_map/ppermute | solution.py:401
  33.5 1.0 copy-start.11
  33.5 67.5 %collective-permute-start.20 = (f32[3,16,64,128]{3,2,1,0:T(8,128)}, f32[3,16,64,128]{3,2,1,0:T(8,128)}, u32[]{:S(2)}, u32[]{:S(2)}) collective-permute-start(f32[3,16,64,128]{3,2,1,0:T(8,128)} %get-tuple-element.339), channel_id=1, source_target_pairs={{0,16},{8,24},{16,0},{24,8},{1,17},{9,25},{17,1},{25,9},{2,18},{10... | collective-permute-start | bytes 4718600 | tf_op jit(solution)/shard_map/ppermute | solution.py:401
  34.5 12.0 %collective-permute-start.5 = (f32[3,128,128]{2,1,0:T(8,128)}, f32[3,128,128]{2,1,0:T(8,128)S(1)}, u32[]{:S(2)}, u32[]{:S(2)}) collective-permute-start(f32[3,128,128]{2,1,0:T(8,128)} %get-tuple-element.748.refs_2_), channel_id=1, source_target_pairs={{0,1},{1,0},{2,3},{3,2},{4,5},{5,4},{6,7},{7,6},{8,9},{9,8},{10,11... | collective-permute-start | bytes 589832 | tf_op jit(solution)/shard_map/while/body/ppermute | solution.py:407
  36.0 8.5 %copy-start.3 = (f32[128,3,16,256]{3,2,1,0:T(8,128)S(1)}, f32[128,3,16,256]{3,2,1,0:T(8,128)}, u32[]{:S(2)}) copy-start(f32[128,3,16,256]{3,2,1,0:T(8,128)} %get-tuple-element.868) | copy-start | bytes 18874372 | tf_op jit(solution)/shard_map/while
  38.8 7.7 %collective-permute-start.4 = (f32[384,128]{1,0:T(8,128)S(1)}, f32[384,128]{1,0:T(8,128)S(1)}, u32[]{:S(2)}, u32[]{:S(2)}) collective-permute-start(f32[384,128]{1,0:T(8,128)S(1)} %get-tuple-element.747), channel_id=1, source_target_pairs={{1,0},{2,1},{3,2},{4,3},{5,4},{6,5},{7,6},{0,7},{9,8},{10,9},{11,1... | collective-permute-start | bytes 589832 | tf_op jit(solution)/shard_map/while/body/ppermute | solution.py:420
  42.4 8.4 %collective-permute-start.6 = (f32[384,128]{1,0:T(8,128)S(1)}, f32[384,128]{1,0:T(8,128)S(1)}, u32[]{:S(2)}, u32[]{:S(2)}) collective-permute-start(f32[384,128]{1,0:T(8,128)S(1)} %get-tuple-element.750), channel_id=1, source_target_pairs={{0,1},{1,2},{2,3},{3,4},{4,5},{5,6},{6,7},{7,0},{8,9},{9,10},{10,1... | collective-permute-start | bytes 589832 | tf_op jit(solution)/shard_map/while/body/ppermute | solution.py:420
  44.6 6.2 %copy-start.8 = (f32[2048,128]{1,0:T(8,128)}, f32[2048,128]{1,0:T(8,128)S(1)}, u32[]{:S(2)}) copy-start(f32[2048,128]{1,0:T(8,128)S(1)} %turn_state.3.state) | copy-start | bytes 3145732 | tf_op jit(solution)/shard_map/while
  51.6 5.9 %copy-start = (f32[3,16,128,128]{3,2,1,0:T(8,128)}, f32[3,16,128,128]{3,2,1,0:T(8,128)S(1)}, u32[]{:S(2)}) copy-start(f32[3,16,128,128]{3,2,1,0:T(8,128)S(1)} %first_stencil.3) | copy-start | bytes 9437188 | tf_op jit(solution)/shard_map/while
  51.7 5.9 %collective-permute-start.7 = (f32[3,16,128,128]{3,2,1,0:T(8,128)S(1)}, f32[3,16,128,128]{3,2,1,0:T(8,128)}, u32[]{:S(2)}, u32[]{:S(2)}) collective-permute-start(f32[3,16,128,128]{3,2,1,0:T(8,128)S(1)} %first_stencil.3), channel_id=1, source_target_pairs={{0,8},{8,0},{16,24},{24,16},{1,9},{9,1},{17,25},{25,17},{2,10},{10... | collective-permute-start | bytes 9437192 | tf_op jit(solution)/shard_map/while/body/ppermute | solution.py:404
  68.4 3.6 %collective-permute-start.8 = (f32[3,16,64,128]{3,2,1,0:T(8,128)}, f32[3,16,64,128]{3,2,1,0:T(8,128)S(1)}, u32[]{:S(2)}, u32[]{:S(2)}) collective-permute-start(f32[3,16,64,128]{3,2,1,0:T(8,128)} %get-tuple-element.764.far.refs_1_.refs_5_), channel_id=1, source_target_pairs={{0,8},{8,0},{16,24},{24,16},{1,9},{9,1},{17,25},{25,17},{2,10},{10... | collective-permute-start | bytes 4718600 | tf_op jit(solution)/shard_map/while/body/ppermute | solution.py:404
  72.0 8.1 %copy-start.1 = (f32[3,16,128,128]{3,2,1,0:T(8,128)S(1)}, f32[3,16,128,128]{3,2,1,0:T(8,128)}, u32[]{:S(2)}) copy-start(f32[3,16,128,128]{3,2,1,0:T(8,128)} %get-tuple-element.907.own.refs_0_.refs_4_) | copy-start | bytes 9437188 | tf_op jit(solution)/shard_map/while
  72.0 8.1 %copy-start.4 = (bf16[3,512,256]{2,1,0:T(8,128)(2,1)S(1)}, bf16[3,512,256]{2,1,0:T(8,128)(2,1)}, u32[]{:S(2)}) copy-start(bf16[3,512,256]{2,1,0:T(8,128)(2,1)} %get-tuple-element.909.high.refs_8_) | copy-start | bytes 2359300 | tf_op jit(solution)/shard_map/while
  72.0 8.1 %copy-start.6 = (bf16[3,512,256]{2,1,0:T(8,128)(2,1)S(1)}, bf16[3,512,256]{2,1,0:T(8,128)(2,1)}, u32[]{:S(2)}) copy-start(bf16[3,512,256]{2,1,0:T(8,128)(2,1)} %get-tuple-element.910.low.refs_9_) | copy-start | bytes 2359300 | tf_op jit(solution)/shard_map/while
  75.4 9.8 %collective-permute-start.10 = (f32[3,64,256]{2,1,0:T(8,128)S(1)}, f32[3,64,256]{2,1,0:T(8,128)S(1)}, u32[]{:S(2)}, u32[]{:S(2)}) collective-permute-start(f32[3,64,256]{2,1,0:T(8,128)S(1)} %get-tuple-element.766), channel_id=1, source_target_pairs={{0,1},{1,2},{2,3},{3,4},{4,5},{5,6},{6,7},{7,0},{8,9},{9,10},{10,1... | collective-permute-start | bytes 589832 | tf_op jit(solution)/shard_map/while/body/ppermute | solution.py:420
  75.9 10.9 %copy-start.9 = (f32[2048,128]{1,0:T(8,128)S(1)}, f32[2048,128]{1,0:T(8,128)}, u32[]{:S(2)}) copy-start(f32[2048,128]{1,0:T(8,128)} %get-tuple-element.911.refs_3_) | copy-start | bytes 3145732 | tf_op jit(solution)/shard_map/while
  75.9 10.9 %copy-start.12 = (f32[2056,128]{1,0:T(8,128)S(1)}, f32[2056,128]{1,0:T(8,128)}, u32[]{:S(2)}) copy-start(f32[2056,128]{1,0:T(8,128)} %get-tuple-element.912.refs_4_) | copy-start | bytes 3158020 | tf_op jit(solution)/shard_map/while
  75.9 10.9 %collective-permute-start.9 = (f32[3,64,256]{2,1,0:T(8,128)S(1)}, f32[3,64,256]{2,1,0:T(8,128)S(1)}, u32[]{:S(2)}, u32[]{:S(2)}) collective-permute-start(f32[3,64,256]{2,1,0:T(8,128)S(1)} %get-tuple-element.765), channel_id=1, source_target_pairs={{1,0},{2,1},{3,2},{4,3},{5,4},{6,5},{7,6},{0,7},{9,8},{10,9},{11,1... | collective-permute-start | bytes 589832 | tf_op jit(solution)/shard_map/while/body/ppermute | solution.py:420
  87.5 5.9 %collective-permute-start.11 = (f32[3,16,64,256]{3,2,1,0:T(8,128)S(1)}, f32[3,16,64,256]{3,2,1,0:T(8,128)}, u32[]{:S(2)}, u32[]{:S(2)}) collective-permute-start(f32[3,16,64,256]{3,2,1,0:T(8,128)S(1)} %second_stencil_0.1.own), channel_id=1, source_target_pairs={{0,8},{8,0},{16,24},{24,16},{1,9},{9,1},{17,25},{25,17},{2,10},{10... | collective-permute-start | bytes 9437192 | tf_op jit(solution)/shard_map/while/body/ppermute | solution.py:404
  99.5 48.8 %collective-permute-start.19 = (f32[3,16,64,128]{3,2,1,0:T(8,128)}, f32[3,16,64,128]{3,2,1,0:T(8,128)}, u32[]{:S(2)}, u32[]{:S(2)}) collective-permute-start(f32[3,16,64,128]{3,2,1,0:T(8,128)} %get-tuple-element.332), channel_id=1, source_target_pairs={{0,16},{8,24},{16,0},{24,8},{1,17},{9,25},{17,1},{25,9},{2,18},{10... | collective-permute-start | bytes 4718600 | tf_op jit(solution)/shard_map/ppermute | solution.py:401
  101.0 3.6 %collective-permute-start.12 = (f32[3,16,64,128]{3,2,1,0:T(8,128)}, f32[3,16,64,128]{3,2,1,0:T(8,128)S(1)}, u32[]{:S(2)}, u32[]{:S(2)}) collective-permute-start(f32[3,16,64,128]{3,2,1,0:T(8,128)} %get-tuple-element.779.far.refs_1_.refs_5_), channel_id=1, source_target_pairs={{0,8},{8,0},{16,24},{24,16},{1,9},{9,1},{17,25},{25,17},{2,10},{10... | collective-permute-start | bytes 4718600 | tf_op jit(solution)/shard_map/while/body/ppermute | solution.py:404
  104.6 6.5 %copy-start.2 = (f32[3,16,128,128]{3,2,1,0:T(8,128)S(1)}, f32[3,16,128,128]{3,2,1,0:T(8,128)}, u32[]{:S(2)}) copy-start(f32[3,16,128,128]{3,2,1,0:T(8,128)} %get-tuple-element.952.own.refs_0_.refs_4_) | copy-start | bytes 9437188 | tf_op jit(solution)/shard_map/while
  104.6 6.5 %copy-start.5 = (bf16[3,512,256]{2,1,0:T(8,128)(2,1)S(1)}, bf16[3,512,256]{2,1,0:T(8,128)(2,1)}, u32[]{:S(2)}) copy-start(bf16[3,512,256]{2,1,0:T(8,128)(2,1)} %get-tuple-element.954.high.refs_8_) | copy-start | bytes 2359300 | tf_op jit(solution)/shard_map/while
  104.6 6.5 %copy-start.7 = (bf16[3,512,256]{2,1,0:T(8,128)(2,1)S(1)}, bf16[3,512,256]{2,1,0:T(8,128)(2,1)}, u32[]{:S(2)}) copy-start(bf16[3,512,256]{2,1,0:T(8,128)(2,1)} %get-tuple-element.955.low.refs_9_) | copy-start | bytes 2359300 | tf_op jit(solution)/shard_map/while
  108.0 7.8 %collective-permute-start.13 = (f32[3,64,256]{2,1,0:T(8,128)S(1)}, f32[3,64,256]{2,1,0:T(8,128)S(1)}, u32[]{:S(2)}, u32[]{:S(2)}) collective-permute-start(f32[3,64,256]{2,1,0:T(8,128)S(1)} %get-tuple-element.780), channel_id=1, source_target_pairs={{1,0},{2,1},{3,2},{4,3},{5,4},{6,5},{7,6},{0,7},{9,8},{10,9},{11,1... | collective-permute-start | bytes 589832 | tf_op jit(solution)/shard_map/while/body/ppermute | solution.py:420
  111.1 9.4 %copy-start.10 = (f32[2048,128]{1,0:T(8,128)S(1)}, f32[2048,128]{1,0:T(8,128)}, u32[]{:S(2)}) copy-start(f32[2048,128]{1,0:T(8,128)} %get-tuple-element.956.refs_3_) | copy-start | bytes 3145732 | tf_op jit(solution)/shard_map/while
  111.1 9.4 %copy-start.13 = (f32[2056,128]{1,0:T(8,128)S(1)}, f32[2056,128]{1,0:T(8,128)}, u32[]{:S(2)}) copy-start(f32[2056,128]{1,0:T(8,128)} %get-tuple-element.957.refs_4_) | copy-start | bytes 3158020 | tf_op jit(solution)/shard_map/while
  111.1 9.4 %collective-permute-start.14 = (f32[3,64,256]{2,1,0:T(8,128)S(1)}, f32[3,64,256]{2,1,0:T(8,128)S(1)}, u32[]{:S(2)}, u32[]{:S(2)}) collective-permute-start(f32[3,64,256]{2,1,0:T(8,128)S(1)} %get-tuple-element.781), channel_id=1, source_target_pairs={{0,1},{1,2},{2,3},{3,4},{4,5},{5,6},{6,7},{7,0},{8,9},{9,10},{10,1... | collective-permute-start | bytes 589832 | tf_op jit(solution)/shard_map/while/body/ppermute | solution.py:420
  121.3 5.9 %collective-permute-start.15 = (f32[3,16,64,256]{3,2,1,0:T(8,128)S(1)}, f32[3,16,64,256]{3,2,1,0:T(8,128)}, u32[]{:S(2)}, u32[]{:S(2)}) collective-permute-start(f32[3,16,64,256]{3,2,1,0:T(8,128)S(1)} %second_stencil_1.1.own), channel_id=1, source_target_pairs={{0,8},{8,0},{16,24},{24,16},{1,9},{9,1},{17,25},{25,17},{2,10},{10... | collective-permute-start | bytes 9437192 | tf_op jit(solution)/shard_map/while/body/ppermute | solution.py:404
  133.4 15.0 %collective-permute-start.23 = (f32[1,16,64,128]{3,2,1,0:T(8,128)}, f32[1,16,64,128]{3,2,1,0:T(8,128)S(1)}, u32[]{:S(2)}, u32[]{:S(2)}) collective-permute-start(f32[1,16,64,128]{3,2,1,0:T(8,128)} %get-tuple-element.342), channel_id=1, source_target_pairs={{0,16},{8,24},{16,0},{24,8},{1,17},{9,25},{17,1},{25,9},{2,18},{10... | collective-permute-start | bytes 1572872 | tf_op jit(solution)/shard_map/ppermute | solution.py:401
  134.5 25.1 %collective-permute-start.22 = (f32[1,16,64,128]{3,2,1,0:T(8,128)}, f32[1,16,64,128]{3,2,1,0:T(8,128)S(1)}, u32[]{:S(2)}, u32[]{:S(2)}) collective-permute-start(f32[1,16,64,128]{3,2,1,0:T(8,128)} %get-tuple-element.341), channel_id=1, source_target_pairs={{0,16},{8,24},{16,0},{24,8},{1,17},{9,25},{17,1},{25,9},{2,18},{10... | collective-permute-start | bytes 1572872 | tf_op jit(solution)/shard_map/ppermute | solution.py:401
  135.4 34.6 %collective-permute-start.21 = (f32[1,16,64,128]{3,2,1,0:T(8,128)}, f32[1,16,64,128]{3,2,1,0:T(8,128)S(1)}, u32[]{:S(2)}, u32[]{:S(2)}) collective-permute-start(f32[1,16,64,128]{3,2,1,0:T(8,128)} %get-tuple-element.340), channel_id=1, source_target_pairs={{0,16},{8,24},{16,0},{24,8},{1,17},{9,25},{17,1},{25,9},{2,18},{10... | collective-permute-start | bytes 1572872 | tf_op jit(solution)/shard_map/ppermute | solution.py:401

commit v10 on v9

--- a/solution.py
+++ b/solution.py
@@ -7,7 +7,7 @@
 
 SECTIONS = 2
 GROUPS = 2
-PIECES_BACK = 3
+PIECES_BACK = 6
 RATE_ROWS = 8
 PIECES = 4
 
@@ -322,24 +322,32 @@
     parts = [ref[0].reshape(nz * width, cols) for ref in (own, peer)]
     res = product(parts, high[0], low[0]).reshape(nz, width, cols)
     out_own[0] = res[:, :, : cols // 2]
-    per = pl.num_programs(0) // len(outs_far)
+    if len(outs_far) == 1:
+        outs_far[0][0] = res[:, :, cols // 2 :]
+        return
+    deep = outs_far[0].shape[1]
+    cuts = nz // deep
     for i, out in enumerate(outs_far):
 
-        @pl.when(pl.program_id(0) // per == i)
-        def _(out=out):
-            out[0] = res[:, :, cols // 2 :]
+        @pl.when(pl.program_id(0) == i // cuts)
+        def _(out=out, z=i % cuts * deep):
+            out[0] = res[z : z + deep, :, cols // 2 :]
 
 
 def map2(own, peer, high, low, k, pieces):
     comps, nz, width, cols = own.shape
-    rows, per = high.shape[1], comps // pieces
+    rows = high.shape[1]
     chunk = pl.BlockSpec((1, nz, width, cols), lambda c: (c, 0, 0, 0))
     helm = pl.BlockSpec((1, rows, cols), lambda c: (c, 0, 0))
     block = (1, nz, width, cols // 2)
-    far = [pl.BlockSpec(block, lambda c, i=i: (jnp.clip(c - i * per, 0, per - 1), 0, 0, 0)) for i in range(pieces)]
+    far = [pl.BlockSpec(block, lambda c: (c, 0, 0, 0))]
+    far_shapes = [shape((comps, *block[1:]))]
+    if pieces > 1:
+        part = (1, nz * comps // pieces, width, cols // 2)
+        far, far_shapes = [pl.BlockSpec(part, lambda c: (0, 0, 0, 0))] * pieces, [shape(part)] * pieces
     return pl.pallas_call(
         map2_kernel,
-        out_shape=[shape((comps, *block[1:]))] + [shape((per, *block[1:]))] * pieces,
+        out_shape=[shape((comps, *block[1:])), *far_shapes],
         grid=(comps,),
         in_specs=[chunk, chunk, helm, helm],
         out_specs=[pl.BlockSpec(block, lambda c: (c, 0, 0, 0)), *far],
@@ -358,30 +366,31 @@
         rows[pl.ds(z, modes, stride=nz), :] = whole.T
 
 
-def write_half(where, pieces, nphi, foreign, base=None, first=0):
+def write_half(where, pieces, comps, nz, nphi, foreign, base=None, first=0):
+    deep = min(p.shape[1] for p in pieces)
+    cuts = nz // deep
     count = min(p.shape[0] for p in pieces)
-    comps = max(p.shape[0] for p in pieces)
-    nz, _, modes = pieces[0].shape[1:]
+    modes = pieces[0].shape[3]
     chunks = len(pieces)
     side = (lambda w: 1 - (w[0] >> 1)) if foreign else (lambda w: w[0] >> 1)
     extra = () if base is None else (base,)
 
     def spec(piece):
-        begin = first if piece.shape[0] > count else 0
-        return pl.BlockSpec((1, *piece.shape[1:]), lambda c, w: (begin + c, 0, 0, 0))
-
-    return pl.pallas_call(
-        lambda *refs: last_kernel(*refs, nz=nz, chunks=chunks),
+        at = first if piece.shape[1] > deep else 0
+        return pl.BlockSpec((1, deep, *piece.shape[2:]), lambda c, w: (c + at // cuts, at % cuts, 0, 0))
+
+    return pl.pallas_call(
+        lambda *refs: last_kernel(*refs, nz=deep, chunks=chunks),
         out_shape=shape((modes, comps * nz, nphi)),
         grid_spec=pltpu.PrefetchScalarGridSpec(
             num_scalar_prefetch=1,
             grid=(count,),
             in_specs=[spec(p) for p in pieces] + [pl.BlockSpec(memory_space=pl.ANY)] * len(extra),
-            out_specs=pl.BlockSpec((modes, nz, nphi // 2), lambda c, w: (0, first + c, side(w))),
+            out_specs=pl.BlockSpec((modes, deep, nphi // 2), lambda c, w: (0, first + c, side(w))),
         ),
         input_output_aliases={1 + chunks: 0} if extra else {},
         compiler_params=params(24),
-        cost_estimate=cost(count * nz * modes * nphi, 4 * count * nz * modes * nphi),
+        cost_estimate=cost(count * deep * modes * nphi, 4 * count * deep * modes * nphi),
         name=f"write_foreign_{first}" if foreign else "write_own",
     )(where, *pieces, *extra)
 
@@ -461,14 +470,15 @@
             return tuple(map2(nxt, beside(nxt), high, low, k, pieces))
 
         spare = tied(sent[k], kept[-1]) if kept else sent[k]
-        parts = blanks(*[((comps // pieces, nz, width, modes), F32)] * pieces)
+        part = (comps, nz, width, modes) if pieces == 1 else (1, nz * comps // pieces, width, modes)
+        parts = blanks(*[(part, F32)] * pieces)
         mine, *theirs = lax.fori_loop(0, once, chain, (spare, *parts))
         kept.append(mine)
         back.append([across(t) for t in theirs])
-    out = write_half(where, kept, nphi, False)
+    out = write_half(where, kept, comps, nz, nphi, False)
     for i in range(PIECES_BACK):
         group = [b[0] if len(b) == 1 else b[i] for b in back]
-        out = write_half(where, group, nphi, True, out, i * (comps // PIECES_BACK))
+        out = write_half(where, group, comps, nz, nphi, True, out, i)
     return out.reshape(modes, comps, nz, nphi)
 
 

time: 174 us -> 173 us (level)
  waiting for transfers between devices: 72.2 us -> 62.7 us
  Pallas kernels: 69 us -> 75 us
  starting transfers between devices: 29.1 us -> 32.3 us
    ppermute x8 -> x11, waiting for transfers between devices: 35.9 us -> 26.3 us  [across(): return lax.ppermute(array, 'rad', [(i, i ^ 2) for i in range(peers)])]
    pallas_call x6 -> x9, Pallas kernels: 26.8 us -> 32.8 us  [the longest x7 20.4 us: write_half(): pl.pallas_call(lambda *refs: last_kernel(*refs, nz=deep, chunks=chunks),...]
    ppermute x8 -> x11, starting transfers between devices: 9.53 us -> 12.6 us  [across(): return lax.ppermute(array, 'rad', [(i, i ^ 2) for i in range(peers)])]
  transfers between devices with their start and end apart: 24 -> 27, of which waited for: 17 -> 18; matrix products, arithmetic and copies ran while one was open for 0% -> 0% of each run, Pallas kernels for 38% -> 42%
where the time goes in v10:
time: 173 us
  Pallas kernels  75 us (43%)
  waiting for transfers between devices  62.7 us (36%)
  starting transfers between devices  32.3 us (19%)
  local copies, waits for them, and re-layouts  2.33 us (1%)
    ppermute x11, waiting for transfers between devices, across(): return lax.ppermute(array, 'rad', [(i, i ^ 2) for i in range(peers)])  26.3 us
    pallas_call x7, Pallas kernels, write_half(): pl.pallas_call(lambda *refs: last_kernel(*refs, nz=deep, chunks=chunks),...  20.4 us
    ppermute x5, waiting for transfers between devices, beside(): return lax.ppermute(array, 'rad', [(i, i ^ 1) for i in range(peers)])  19.8 us
    ppermute x8, waiting for transfers between devices, halos(): return (lax.ppermute(leading, 'col', down), lax.ppermute(last, 'col', up))  16.5 us
    ppermute x8, starting transfers between devices, halos(): return (lax.ppermute(leading, 'col', down), lax.ppermute(last, 'col', up))  16.5 us
    ppermute x11, starting transfers between devices, across(): return lax.ppermute(array, 'rad', [(i, i ^ 2) for i in range(peers)])  12.6 us
    pallas_call x2, Pallas kernels, map2(): pl.pallas_call(map2_kernel, out_shape=[shape((comps, *block[1:])), *far_s...  12.3 us
    pallas_call x2, Pallas kernels, map1(): pl.pallas_call(map1_kernel, out_shape=shape((comps, nz, width, cols)), gr...  9.11 us
  transfers between devices with their start and end apart: 27, of which 18 were waited for; matrix products, arithmetic and copies ran while one was open for 0% of the time, Pallas kernels for 42%

profile of v10, /device:TPU:0, one launch (start us, length us, event | category | flops | bytes accessed | tf_op | source)
XLA Modules:
  0.0 172.6 jit_solution(1746273729048478283)
XLA Ops:
  0.9 3.0 %collective-permute-start.16 = (f32[3,128,128]{2,1,0:T(8,128)S(1)}, f32[3,128,128]{2,1,0:T(8,128)S(1)}, u32[]{:S(2)}, u32[]{:S(2)}) collective-permute-start(f32[3,128,128]{2,1,0:T(8,128)S(1)} %constant_dynamic-slice_fusion), channel_id=1, source_target_pairs={{0,16},{8,24},{16,0},{24,8},{1,17},{9,25},{17,1},{25,9},{2,18},{10... | collective-permute-start | bytes 589832 | tf_op jit(solution)/shard_map/ppermute | solution.py:410
  4.0 3.1 %turn_state.2 = f32[2056,128]{1,0:T(8,128)} custom-call(s32[2]{0:T(128)S(1)} %pad_add_fusion.refs_0_, f32[2048,256]{1,0:T(8,128)} %bitcast.18, f32[1,128]{1,0:T(1,128)} %bitcast.20), custom_call_target="tpu_custom_call" | custom-call | flops 263168 | bytes 2105344 | tf_op jit(solution)/shard_map/turn_state/pallas_call | solution.py:77
  7.2 1.7 collective-permute-done.16
  8.9 21.9 %while.68 = (s32[]{:T(128)}, f32[3,16,64,128]{3,2,1,0:T(8,128)}, f32[3,16,64,128]{3,2,1,0:T(8,128)}, f32[3,128,128]{2,1,0:T(8,128)}, f32[3,128,128]{2,1,0:T(8,12...) while((s32[]{:T(128)}, f32[3,16,64,128]{3,2,1,0:T(8,128)}, ...), condition=%wide.region_1.0_spmd, body=%wide.region_0.0_spmd.sunk | while | flops 10321925 | bytes 19661144 | solution.py:440
  8.9 2.6 %edge_layers.2 = (f32[384,128]{1,0:T(8,128)S(1)}, f32[384,128]{1,0:T(8,128)S(1)}) custom-call(s32[2]{0:T(128)S(1)} %broadcast_add_fusion.4.refs_0_, f32[6144,256]{1,0:T(8,128)} %bitcast.14), custom_call_target="tpu_custom_call" | custom-call | flops 98304 | bytes 3145728 | tf_op jit(solution)/shard_map/while/body/edge_layers/pallas_call | solution.py:103
  11.4 4.9 %collective-permute-start = (f32[384,128]{1,0:T(8,128)S(1)}, f32[384,128]{1,0:T(8,128)S(1)}, u32[]{:S(2)}, u32[]{:S(2)}) collective-permute-start(f32[384,128]{1,0:T(8,128)S(1)} %get-tuple-element.780), channel_id=1, source_target_pairs={{1,0},{2,1},{3,2},{4,3},{5,4},{6,5},{7,6},{0,7},{9,8},{10,9},{11,1... | collective-permute-start | bytes 589832 | tf_op jit(solution)/shard_map/while/body/ppermute | solution.py:429
  16.3 1.5 collective-permute-start.3
  17.8 3.4 %turn_half.2.turned = f32[3,16,128,128]{3,2,1,0:T(8,128)S(1)} custom-call(s32[2]{0:T(128)S(1)} %broadcast_add_fusion.4.refs_0_, f32[6144,256]{1,0:T(8,128)} %bitcast.15), custom_call_target="tpu_custom_call" | custom-call | flops 786432 | bytes 6291456 | tf_op jit(solution)/shard_map/while/body/turn_half/pallas_call | solution.py:138
  21.6 5.0 %collective-permute-done.1.before = f32[384,128]{1,0:T(8,128)S(1)} collective-permute-done((f32[384,128]{1,0:T(8,128)S(1)}, f32[384,128]{1,0:T(8,128)S(1)}, u32[]{:S(2)}, u32[]{:S(2)}) %collective-permute-start.1) | collective-permute-done | bytes 196640 | tf_op jit(solution)/shard_map/while/body/ppermute | solution.py:429
  26.6 3.5 %first_stencil.2 = (f32[3,16,64,128]{3,2,1,0:T(8,128)}, f32[3,16,64,128]{3,2,1,0:T(8,128)}) custom-call(f32[3,16,128,128]{3,2,1,0:T(8,128)S(1)} %turn_half.2.turned, f32[2056,128]{1,0:T(8,128)} %get-tuple-element.871.state, f32[384,128]{1,0:T(8,128)S(1)} %collective-permute-done.after, f32[384,128]{1,0:T(8,128)S(1)} %collective-permute-done.1.before, ...), custom_call_target="tpu_custom_call" | custom-call | flops 9437184 | bytes 6291456 | tf_op jit(solution)/shard_map/while/body/first_stencil/pallas_call | solution.py:178
  30.8 1.6 collective-permute-start.17
  34.5 23.0 %while.69 = (s32[]{:T(128)}, f32[2048,128]{1,0:T(8,128)}, f32[3,16,128,128]{3,2,1,0:T(8,128)}, f32[3,16,128,128]{3,2,1,0:T(8,128)}, bf16[3,512,256]{2,1,0:T(8,12...) while((s32[]{:T(128)}, f32[2048,128]{1,0:T(8,128)}, ...), condition=%wide.region_3.0_spmd, body=%wide.region_2.0_spmd.sunk | while | flops 11370501 | bytes 77857200 | solution.py:457
  34.5 1.5 collective-permute-start.5
  36.1 2.8 %edge_layers.3 = (f32[384,128]{1,0:T(8,128)S(1)}, f32[384,128]{1,0:T(8,128)S(1)}) custom-call(s32[2]{0:T(128)S(1)} %broadcast_add_fusion.5.refs_0_.where, f32[6144,256]{1,0:T(8,128)} %bitcast.16), custom_call_target="tpu_custom_call" | custom-call | flops 98304 | bytes 3145728 | tf_op jit(solution)/shard_map/while/body/edge_layers/pallas_call | solution.py:103
  38.9 3.6 %collective-permute-start.4 = (f32[384,128]{1,0:T(8,128)S(1)}, f32[384,128]{1,0:T(8,128)S(1)}, u32[]{:S(2)}, u32[]{:S(2)}) collective-permute-start(f32[384,128]{1,0:T(8,128)S(1)} %get-tuple-element.795), channel_id=1, source_target_pairs={{1,0},{2,1},{3,2},{4,3},{5,4},{6,5},{7,6},{0,7},{9,8},{10,9},{11,1... | collective-permute-start | bytes 589832 | tf_op jit(solution)/shard_map/while/body/ppermute | solution.py:429
  42.5 2.1 %turn_state.3.state = f32[2048,128]{1,0:T(8,128)S(1)} custom-call(s32[2]{0:T(128)S(1)} %broadcast_add_fusion.5.refs_0_.where, f32[2048,256]{1,0:T(8,128)} %bitcast.19), custom_call_target="tpu_custom_call" | custom-call | flops 262144 | bytes 2097152 | tf_op jit(solution)/shard_map/while/body/turn_state/pallas_call | solution.py:77
  44.6 1.9 %turn_half.3.turned = f32[3,16,128,128]{3,2,1,0:T(8,128)S(1)} custom-call(s32[2]{0:T(128)S(1)} %broadcast_add_fusion.5.refs_0_.where, f32[6144,256]{1,0:T(8,128)S(1)} %bitcast.17), custom_call_target="tpu_custom_call" | custom-call | flops 786432 | bytes 6291456 | tf_op jit(solution)/shard_map/while/body/turn_half/pallas_call | solution.py:138
  46.5 4.3 %collective-permute-done.6.before = f32[384,128]{1,0:T(8,128)S(1)} collective-permute-done((f32[384,128]{1,0:T(8,128)S(1)}, f32[384,128]{1,0:T(8,128)S(1)}, u32[]{:S(2)}, u32[]{:S(2)}) %collective-permute-start.6) | collective-permute-done | bytes 196640 | tf_op jit(solution)/shard_map/while/body/ppermute | solution.py:429
  51.8 4.8 %split_helm.1 = (bf16[3,512,256]{2,1,0:T(8,128)(2,1)}, bf16[3,512,256]{2,1,0:T(8,128)(2,1)}) custom-call(s32[2]{0:T(128)S(1)} %broadcast_add_fusion.5.refs_0_.where, f32[3,512,128]{2,1,0:T(8,128)} %get-tuple-element.922.own, f32[3,128,128]{2,1,0:T(8,128)S(1)} %get-tuple-element.923.refs_0_, f32[3,128,128]{2,1,0:T(8,128)} %get-tuple-element.924.refs_1_, ...), custom_call_target="tpu_custom_call" | custom-call | flops 786432 | bytes 3145728 | tf_op jit(solution)/shard_map/while/body/split_helm/pallas_call | solution.py:221
  57.5 10.9 %collective-permute-done.17 = f32[3,16,64,128]{3,2,1,0:T(8,128)} collective-permute-done((f32[3,16,64,128]{3,2,1,0:T(8,128)}, f32[3,16,64,128]{3,2,1,0:T(8,128)}, u32[]{:S(2)}, u32[]{:S(2)}) %collective-permute-start.17) | collective-permute-done | bytes 1572896 | tf_op jit(solution)/shard_map/ppermute | solution.py:410
  68.4 31.0 %while.70 = (s32[]{:T(128)}, f32[3,16,64,128]{3,2,1,0:T(8,128)}, f32[3,16,64,128]{3,2,1,0:T(8,128)}, s32[]{:T(128)}, f32[3,16,64,128]{3,2,1,0:T(8,128)}, /*index...) while((s32[]{:T(128)}, f32[3,16,64,128]{3,2,1,0:T(8,128)}, ...), condition=%wide.region_5.0_spmd, body=%wide.region_4.0_spmd.sunk | while | flops 5143265280 | bytes 78791080 | solution.py:475
  68.4 3.6 %collective-permute-done.8.far_peer.refs_3_.refs_7_ = f32[3,16,64,128]{3,2,1,0:T(8,128)S(1)} collective-permute-done((f32[3,16,64,128]{3,2,1,0:T(8,128)}, f32[3,16,64,128]{3,2,1,0:T(8,128)S(1)}, u32[]{:S(2)}, u32[]{:S(2)}) %collective-permute-start.8) | collective-permute-done | bytes 1572896 | tf_op jit(solution)/shard_map/while/body/ppermute | solution.py:413
  72.0 3.3 %layers1_0.1 = (f32[3,64,256]{2,1,0:T(8,128)S(1)}, f32[3,64,256]{2,1,0:T(8,128)S(1)}) custom-call(f32[3,16,128,128]{3,2,1,0:T(8,128)} %get-tuple-element.958.own.refs_0_.refs_4_, f32[3,16,64,128]{3,2,1,0:T(8,128)} %get-tuple-element.812.far.refs_1_.refs_5_, f32[3,16,128,128]{3,2,1,0:T(8,128)} %get-tuple-element.959.own_peer.refs_2_.refs_6_, ...), custom_call_target="tpu_custom_call" | custom-call | flops 301989888 | bytes 2752512 | tf_op jit(solution)/shard_map/while/body/layers1_0/pallas_call | solution.py:280
  75.9 4.3 %collective-permute-start.9 = (f32[3,64,256]{2,1,0:T(8,128)S(1)}, f32[3,64,256]{2,1,0:T(8,128)S(1)}, u32[]{:S(2)}, u32[]{:S(2)}) collective-permute-start(f32[3,64,256]{2,1,0:T(8,128)S(1)} %get-tuple-element.813), channel_id=1, source_target_pairs={{1,0},{2,1},{3,2},{4,3},{5,4},{6,5},{7,6},{0,7},{9,8},{10,9},{11,1... | collective-permute-start | bytes 589832 | tf_op jit(solution)/shard_map/while/body/ppermute | solution.py:429
  80.1 4.5 %map1_0.1.refs_0_ = f32[3,16,64,256]{3,2,1,0:T(8,128)S(1)} custom-call(f32[3,16,128,128]{3,2,1,0:T(8,128)S(1)} %copy-done.1, f32[3,16,64,128]{3,2,1,0:T(8,128)} %get-tuple-element.812.far.refs_1_.refs_5_, f32[3,16,128,128]{3,2,1,0:T(8,128)} %get-tuple-element.959.own_peer.refs_2_.refs_6_, ...), custom_call_target="tpu_custom_call" | custom-call | flops 2415919104 | bytes 11010048 | tf_op jit(solution)/shard_map/while/body/map1_0/pallas_call | solution.py:249
  85.2 1.6 collective-permute-done.9.refs_1_
  87.6 5.8 %collective-permute-done.11.peer = f32[3,16,64,256]{3,2,1,0:T(8,128)} collective-permute-done((f32[3,16,64,256]{3,2,1,0:T(8,128)S(1)}, f32[3,16,64,256]{3,2,1,0:T(8,128)}, u32[]{:S(2)}, u32[]{:S(2)}) %collective-permute-start.11) | collective-permute-done | bytes 3145760 | tf_op jit(solution)/shard_map/while/body/ppermute | solution.py:413
  93.4 6.1 %map2_0.1 = (f32[3,16,64,128]{3,2,1,0:T(8,128)}, f32[3,16,64,128]{3,2,1,0:T(8,128)}) custom-call(f32[3,16,64,256]{3,2,1,0:T(8,128)S(1)} %second_stencil_0.1.own, f32[3,16,64,256]{3,2,1,0:T(8,128)} %collective-permute-done.11.peer, bf16[3,512,256]{2,1,0:T(8,128)(2,1)} %get-tuple-element.960.high.refs_8_, bf16[3,512,256]{2,1,0:T(8,128)(2,1)} %get-tuple-element.961.low.refs_9_), custom_call_target="tpu_custom_call" | custom-call | flops 2415919104 | bytes 11010048 | tf_op jit(solution)/shard_map/while/body/map2_0/pallas_call | solution.py:348
  99.4 1.5 collective-permute-start.19
  100.9 32.5 %while.71 = (s32[]{:T(128)}, f32[3,16,64,128]{3,2,1,0:T(8,128)}, f32[1,8,64,128]{3,2,1,0:T(8,128)}, f32[1,8,64,128]{3,2,1,0:T(8,128)}, f32[1,8,64,128]{3,2,1,0:T...) while((s32[]{:T(128)}, f32[3,16,64,128]{3,2,1,0:T(8,128)}, ...), condition=%wide.region_7.0_spmd, body=%wide.region_6.0_spmd.sunk | while | flops 5143265280 | bytes 78791120 | solution.py:475
  100.9 3.6 %collective-permute-done.12.far_peer.refs_3_.refs_7_ = f32[3,16,64,128]{3,2,1,0:T(8,128)S(1)} collective-permute-done((f32[3,16,64,128]{3,2,1,0:T(8,128)}, f32[3,16,64,128]{3,2,1,0:T(8,128)S(1)}, u32[]{:S(2)}, u32[]{:S(2)}) %collective-permute-start.12) | collective-permute-done | bytes 1572896 | tf_op jit(solution)/shard_map/while/body/ppermute | solution.py:413
  104.6 3.3 %layers1_1.1 = (f32[3,64,256]{2,1,0:T(8,128)S(1)}, f32[3,64,256]{2,1,0:T(8,128)S(1)}) custom-call(f32[3,16,128,128]{3,2,1,0:T(8,128)} %get-tuple-element.1012.own.refs_0_.refs_4_, f32[3,16,64,128]{3,2,1,0:T(8,128)} %get-tuple-element.827.far.refs_1_.refs_5_, f32[3,16,128,128]{3,2,1,0:T(8,128)} %get-tuple-element.1013.own_peer.refs_2_.refs_6_, ...), custom_call_target="tpu_custom_call" | custom-call | flops 301989888 | bytes 2752512 | tf_op jit(solution)/shard_map/while/body/layers1_1/pallas_call | solution.py:280
  107.9 3.3 %collective-permute-start.13 = (f32[3,64,256]{2,1,0:T(8,128)S(1)}, f32[3,64,256]{2,1,0:T(8,128)S(1)}, u32[]{:S(2)}, u32[]{:S(2)}) collective-permute-start(f32[3,64,256]{2,1,0:T(8,128)S(1)} %get-tuple-element.828), channel_id=1, source_target_pairs={{1,0},{2,1},{3,2},{4,3},{5,4},{6,5},{7,6},{0,7},{9,8},{10,9},{11,1... | collective-permute-start | bytes 589832 | tf_op jit(solution)/shard_map/while/body/ppermute | solution.py:429
  111.2 4.6 %map1_1.1.refs_0_ = f32[3,16,64,256]{3,2,1,0:T(8,128)S(1)} custom-call(f32[3,16,128,128]{3,2,1,0:T(8,128)S(1)} %copy-done.2, f32[3,16,64,128]{3,2,1,0:T(8,128)} %get-tuple-element.827.far.refs_1_.refs_5_, f32[3,16,128,128]{3,2,1,0:T(8,128)} %get-tuple-element.1013.own_peer.refs_2_.refs_6_, ...), custom_call_target="tpu_custom_call" | custom-call | flops 2415919104 | bytes 11010048 | tf_op jit(solution)/shard_map/while/body/map1_1/pallas_call | solution.py:249
  115.8 4.7 %collective-permute-done.14.refs_2_ = f32[3,64,256]{2,1,0:T(8,128)S(1)} collective-permute-done((f32[3,64,256]{2,1,0:T(8,128)S(1)}, f32[3,64,256]{2,1,0:T(8,128)S(1)}, u32[]{:S(2)}, u32[]{:S(2)}) %collective-permute-start.14) | collective-permute-done | bytes 196640 | tf_op jit(solution)/shard_map/while/body/ppermute | solution.py:429
  121.4 5.8 %collective-permute-done.15.peer = f32[3,16,64,256]{3,2,1,0:T(8,128)} collective-permute-done((f32[3,16,64,256]{3,2,1,0:T(8,128)S(1)}, f32[3,16,64,256]{3,2,1,0:T(8,128)}, u32[]{:S(2)}, u32[]{:S(2)}) %collective-permute-start.15) | collective-permute-done | bytes 3145760 | tf_op jit(solution)/shard_map/while/body/ppermute | solution.py:413
  127.1 6.3 %map2_1.1 = (f32[3,16,64,128]{3,2,1,0:T(8,128)}, f32[1,8,64,128]{3,2,1,0:T(8,128)}, f32[1,8,64,128]{3,2,1,0:T(8,128)}, f32[1,8,64,128]{3,2,1,0:T(8,128)}, f32[1,...) custom-call(f32[3,16,64,256]{3,2,1,0:T(8,128)S(1)} %second_stencil_1.1.own, ...), custom_call_target="tpu_custom_call" | custom-call | flops 2415919104 | bytes 11010048 | tf_op jit(solution)/shard_map/while/body/map2_1/pallas_call | solution.py:348
  137.5 5.3 %collective-permute-done.26.refs_2_ = f32[1,8,64,128]{3,2,1,0:T(8,128)S(1)} collective-permute-done((f32[1,8,64,128]{3,2,1,0:T(8,128)}, f32[1,8,64,128]{3,2,1,0:T(8,128)S(1)}, u32[]{:S(2)}, u32[]{:S(2)}) %collective-permute-start.26) | collective-permute-done | bytes 262176 | tf_op jit(solution)/shard_map/ppermute | solution.py:410
  144.8 5.5 %write_own.1.refs_3_ = f32[128,48,256]{2,1,0:T(8,128)} custom-call(s32[2]{0:T(128)S(1)} %get-tuple-element.1068, f32[3,16,64,128]{3,2,1,0:T(8,128)} %get-tuple-element.355.refs_1_, f32[3,16,64,128]{3,2,1,0:T(8,128)} %get-tuple-element.370.refs_2_), custom_call_target="tpu_custom_call" | custom-call | flops 1572864 | bytes 6291456 | tf_op jit(solution)/shard_map/write_own/pallas_call | solution.py:382
  150.4 2.5 %write_foreign_0.1.refs_3_ = f32[128,48,256]{2,1,0:T(8,128)} custom-call(s32[2]{0:T(128)S(1)} %get-tuple-element.1068, f32[3,16,64,128]{3,2,1,0:T(8,128)} %collective-permute-done.19.refs_1_, f32[1,8,64,128]{3,2,1,0:T(8,128)S(1)} %collective-permute-done.26.refs_2_, f32[128,48,256]{2,1,0:T(8,128)} %write_own.1.refs_3_), custom_call_target="tpu_custom_call", output_to_operand_aliasing={{}: (3, {})} | custom-call | flops 262144 | bytes 1048576 | tf_op jit(solution)/shard_map/write_foreign_0/pallas_call | solution.py:382
  152.8 2.5 %write_foreign_1.1.refs_3_ = f32[128,48,256]{2,1,0:T(8,128)} custom-call(s32[2]{0:T(128)S(1)} %get-tuple-element.1068, f32[3,16,64,128]{3,2,1,0:T(8,128)} %collective-permute-done.19.refs_1_, f32[1,8,64,128]{3,2,1,0:T(8,128)S(1)} %collective-permute-done.25.refs_2_, f32[128,48,256]{2,1,0:T(8,128)} %write_foreign_0.1.refs_3_), custom_call_target="tpu_custom_call", output_to_operand_aliasing={{}: (3, {})} | custom-call | flops 262144 | bytes 1048576 | tf_op jit(solution)/shard_map/write_foreign_1/pallas_call | solution.py:382
  155.3 2.5 %write_foreign_2.1.refs_3_ = f32[128,48,256]{2,1,0:T(8,128)} custom-call(s32[2]{0:T(128)S(1)} %get-tuple-element.1068, f32[3,16,64,128]{3,2,1,0:T(8,128)} %collective-permute-done.19.refs_1_, f32[1,8,64,128]{3,2,1,0:T(8,128)S(1)} %collective-permute-done.24.refs_2_, f32[128,48,256]{2,1,0:T(8,128)} %write_foreign_1.1.refs_3_), custom_call_target="tpu_custom_call", output_to_operand_aliasing={{}: (3, {})} | custom-call | flops 262144 | bytes 1048576 | tf_op jit(solution)/shard_map/write_foreign_2/pallas_call | solution.py:382
  157.8 1.8 %collective-permute-done.23.refs_2_ = f32[1,8,64,128]{3,2,1,0:T(8,128)S(1)} collective-permute-done((f32[1,8,64,128]{3,2,1,0:T(8,128)}, f32[1,8,64,128]{3,2,1,0:T(8,128)S(1)}, u32[]{:S(2)}, u32[]{:S(2)}) %collective-permute-start.23) | collective-permute-done | bytes 262176 | tf_op jit(solution)/shard_map/ppermute | solution.py:410
  159.7 2.5 %write_foreign_3.1.refs_3_ = f32[128,48,256]{2,1,0:T(8,128)} custom-call(s32[2]{0:T(128)S(1)} %get-tuple-element.1068, f32[3,16,64,128]{3,2,1,0:T(8,128)} %collective-permute-done.19.refs_1_, f32[1,8,64,128]{3,2,1,0:T(8,128)S(1)} %collective-permute-done.23.refs_2_, f32[128,48,256]{2,1,0:T(8,128)} %write_foreign_2.1.refs_3_), custom_call_target="tpu_custom_call", output_to_operand_aliasing={{}: (3, {})} | custom-call | flops 262144 | bytes 1048576 | tf_op jit(solution)/shard_map/write_foreign_3/pallas_call | solution.py:382
  162.1 3.1 %collective-permute-done.22.refs_2_ = f32[1,8,64,128]{3,2,1,0:T(8,128)S(1)} collective-permute-done((f32[1,8,64,128]{3,2,1,0:T(8,128)}, f32[1,8,64,128]{3,2,1,0:T(8,128)S(1)}, u32[]{:S(2)}, u32[]{:S(2)}) %collective-permute-start.22) | collective-permute-done | bytes 262176 | tf_op jit(solution)/shard_map/ppermute | solution.py:410
  165.3 2.5 %write_foreign_4.1.refs_3_ = f32[128,48,256]{2,1,0:T(8,128)} custom-call(s32[2]{0:T(128)S(1)} %get-tuple-element.1068, f32[3,16,64,128]{3,2,1,0:T(8,128)} %collective-permute-done.19.refs_1_, f32[1,8,64,128]{3,2,1,0:T(8,128)S(1)} %collective-permute-done.22.refs_2_, f32[128,48,256]{2,1,0:T(8,128)} %write_foreign_3.1.refs_3_), custom_call_target="tpu_custom_call", output_to_operand_aliasing={{}: (3, {})} | custom-call | flops 262144 | bytes 1048576 | tf_op jit(solution)/shard_map/write_foreign_4/pallas_call | solution.py:382
  167.8 2.3 %collective-permute-done.21.refs_2_ = f32[1,8,64,128]{3,2,1,0:T(8,128)S(1)} collective-permute-done((f32[1,8,64,128]{3,2,1,0:T(8,128)}, f32[1,8,64,128]{3,2,1,0:T(8,128)S(1)}, u32[]{:S(2)}, u32[]{:S(2)}) %collective-permute-start.21) | collective-permute-done | bytes 262176 | tf_op jit(solution)/shard_map/ppermute | solution.py:410
  170.1 2.5 %write_foreign_5.1 = f32[128,48,256]{2,1,0:T(8,128)} custom-call(s32[2]{0:T(128)S(1)} %get-tuple-element.1068, f32[3,16,64,128]{3,2,1,0:T(8,128)} %collective-permute-done.19.refs_1_, f32[1,8,64,128]{3,2,1,0:T(8,128)S(1)} %collective-permute-done.21.refs_2_, f32[128,48,256]{2,1,0:T(8,128)} %write_foreign_4.1.refs_3_), custom_call_target="tpu_custom_call", output_to_operand_aliasing={{}: (3, {})} | custom-call | flops 262144 | bytes 1048576 | tf_op jit(solution)/shard_map/write_foreign_5/pallas_call | solution.py:382
  (74 shorter events, 15.2 us)
Async XLA Ops:
  0.9 7.9 %collective-permute-start.16 = (f32[3,128,128]{2,1,0:T(8,128)S(1)}, f32[3,128,128]{2,1,0:T(8,128)S(1)}, u32[]{:S(2)}, u32[]{:S(2)}) collective-permute-start(f32[3,128,128]{2,1,0:T(8,128)S(1)} %constant_dynamic-slice_fusion), channel_id=1, source_target_pairs={{0,16},{8,24},{16,0},{24,8},{1,17},{9,25},{17,1},{25,9},{2,18},{10... | collective-permute-start | bytes 589832 | tf_op jit(solution)/shard_map/ppermute | solution.py:410
  4.0 4.8 %copy-start.15 = (f32[128]{0:T(128)S(1)}, f32[128]{0:T(128)}, u32[]{:S(2)}) copy-start(f32[128]{0:T(128)} %param.15) | copy-start | bytes 1540
  7.1 26.4 %collective-permute-start.18 = (f32[2056,128]{1,0:T(8,128)}, f32[2056,128]{1,0:T(8,128)S(1)}, u32[]{:S(2)}, u32[]{:S(2)}) collective-permute-start(f32[2056,128]{1,0:T(8,128)} %turn_state.2), channel_id=1, source_target_pairs={{0,16},{8,24},{16,0},{24,8},{1,17},{9,25},{17,1},{25,9},{2,18},{10... | collective-permute-start | bytes 3158024 | tf_op jit(solution)/shard_map/ppermute | solution.py:410
  11.4 10.2 %collective-permute-start = (f32[384,128]{1,0:T(8,128)S(1)}, f32[384,128]{1,0:T(8,128)S(1)}, u32[]{:S(2)}, u32[]{:S(2)}) collective-permute-start(f32[384,128]{1,0:T(8,128)S(1)} %get-tuple-element.780), channel_id=1, source_target_pairs={{1,0},{2,1},{3,2},{4,3},{5,4},{6,5},{7,6},{0,7},{9,8},{10,9},{11,1... | collective-permute-start | bytes 589832 | tf_op jit(solution)/shard_map/while/body/ppermute | solution.py:429
  16.3 10.3 %collective-permute-start.1 = (f32[384,128]{1,0:T(8,128)S(1)}, f32[384,128]{1,0:T(8,128)S(1)}, u32[]{:S(2)}, u32[]{:S(2)}) collective-permute-start(f32[384,128]{1,0:T(8,128)S(1)} %get-tuple-element.781), channel_id=1, source_target_pairs={{0,1},{1,2},{2,3},{3,4},{4,5},{5,6},{6,7},{7,0},{8,9},{9,10},{10,1... | collective-permute-start | bytes 589832 | tf_op jit(solution)/shard_map/while/body/ppermute | solution.py:429
  16.3 13.8 %collective-permute-start.2 = (f32[3,128,128]{2,1,0:T(8,128)S(1)}, f32[3,128,128]{2,1,0:T(8,128)S(1)}, u32[]{:S(2)}, u32[]{:S(2)}) collective-permute-start(f32[3,128,128]{2,1,0:T(8,128)S(1)} %get-tuple-element.784), channel_id=1, source_target_pairs={{0,1},{1,0},{2,3},{3,2},{4,5},{5,4},{6,7},{7,6},{8,9},{9,8},{10,11... | collective-permute-start | bytes 589832 | tf_op jit(solution)/shard_map/while/body/ppermute | solution.py:416
  16.3 13.8 %collective-permute-start.3 = (f32[3,128,128]{2,1,0:T(8,128)S(1)}, f32[3,128,128]{2,1,0:T(8,128)}, u32[]{:S(2)}, u32[]{:S(2)}) collective-permute-start(f32[3,128,128]{2,1,0:T(8,128)S(1)} %get-tuple-element.784), channel_id=1, source_target_pairs={{0,2},{1,3},{2,0},{3,1},{4,6},{5,7},{6,4},{7,5},{8,10},{9,11},{10,... | collective-permute-start | bytes 589832 | tf_op jit(solution)/shard_map/while/body/ppermute | solution.py:416
  30.1 0.7 copy-start.14
  30.8 37.6 %collective-permute-start.17 = (f32[3,16,64,128]{3,2,1,0:T(8,128)}, f32[3,16,64,128]{3,2,1,0:T(8,128)}, u32[]{:S(2)}, u32[]{:S(2)}) collective-permute-start(f32[3,16,64,128]{3,2,1,0:T(8,128)} %get-tuple-element.339), channel_id=1, source_target_pairs={{0,16},{8,24},{16,0},{24,8},{1,17},{9,25},{17,1},{25,9},{2,18},{10... | collective-permute-start | bytes 4718600 | tf_op jit(solution)/shard_map/ppermute | solution.py:410
  33.5 1.0 copy-start.11
  33.5 67.4 %collective-permute-start.20 = (f32[3,16,64,128]{3,2,1,0:T(8,128)}, f32[3,16,64,128]{3,2,1,0:T(8,128)}, u32[]{:S(2)}, u32[]{:S(2)}) collective-permute-start(f32[3,16,64,128]{3,2,1,0:T(8,128)} %get-tuple-element.363), channel_id=1, source_target_pairs={{0,16},{8,24},{16,0},{24,8},{1,17},{9,25},{17,1},{25,9},{2,18},{10... | collective-permute-start | bytes 4718600 | tf_op jit(solution)/shard_map/ppermute | solution.py:410
  34.5 12.0 %collective-permute-start.5 = (f32[3,128,128]{2,1,0:T(8,128)}, f32[3,128,128]{2,1,0:T(8,128)S(1)}, u32[]{:S(2)}, u32[]{:S(2)}) collective-permute-start(f32[3,128,128]{2,1,0:T(8,128)} %get-tuple-element.796.refs_2_), channel_id=1, source_target_pairs={{0,1},{1,0},{2,3},{3,2},{4,5},{5,4},{6,7},{7,6},{8,9},{9,8},{10,11... | collective-permute-start | bytes 589832 | tf_op jit(solution)/shard_map/while/body/ppermute | solution.py:416
  36.1 8.5 %copy-start.3 = (f32[128,3,16,256]{3,2,1,0:T(8,128)S(1)}, f32[128,3,16,256]{3,2,1,0:T(8,128)}, u32[]{:S(2)}) copy-start(f32[128,3,16,256]{3,2,1,0:T(8,128)} %get-tuple-element.919) | copy-start | bytes 18874372 | tf_op jit(solution)/shard_map/while
  38.9 7.7 %collective-permute-start.4 = (f32[384,128]{1,0:T(8,128)S(1)}, f32[384,128]{1,0:T(8,128)S(1)}, u32[]{:S(2)}, u32[]{:S(2)}) collective-permute-start(f32[384,128]{1,0:T(8,128)S(1)} %get-tuple-element.795), channel_id=1, source_target_pairs={{1,0},{2,1},{3,2},{4,3},{5,4},{6,5},{7,6},{0,7},{9,8},{10,9},{11,1... | collective-permute-start | bytes 589832 | tf_op jit(solution)/shard_map/while/body/ppermute | solution.py:429
  42.5 8.4 %collective-permute-start.6 = (f32[384,128]{1,0:T(8,128)S(1)}, f32[384,128]{1,0:T(8,128)S(1)}, u32[]{:S(2)}, u32[]{:S(2)}) collective-permute-start(f32[384,128]{1,0:T(8,128)S(1)} %get-tuple-element.798), channel_id=1, source_target_pairs={{0,1},{1,2},{2,3},{3,4},{4,5},{5,6},{6,7},{7,0},{8,9},{9,10},{10,1... | collective-permute-start | bytes 589832 | tf_op jit(solution)/shard_map/while/body/ppermute | solution.py:429
  44.6 6.2 %copy-start.8 = (f32[2048,128]{1,0:T(8,128)}, f32[2048,128]{1,0:T(8,128)S(1)}, u32[]{:S(2)}) copy-start(f32[2048,128]{1,0:T(8,128)S(1)} %turn_state.3.state) | copy-start | bytes 3145732 | tf_op jit(solution)/shard_map/while
  51.7 5.9 %copy-start = (f32[3,16,128,128]{3,2,1,0:T(8,128)}, f32[3,16,128,128]{3,2,1,0:T(8,128)S(1)}, u32[]{:S(2)}) copy-start(f32[3,16,128,128]{3,2,1,0:T(8,128)S(1)} %first_stencil.3) | copy-start | bytes 9437188 | tf_op jit(solution)/shard_map/while
  51.7 5.9 %collective-permute-start.7 = (f32[3,16,128,128]{3,2,1,0:T(8,128)S(1)}, f32[3,16,128,128]{3,2,1,0:T(8,128)}, u32[]{:S(2)}, u32[]{:S(2)}) collective-permute-start(f32[3,16,128,128]{3,2,1,0:T(8,128)S(1)} %first_stencil.3), channel_id=1, source_target_pairs={{0,8},{8,0},{16,24},{24,16},{1,9},{9,1},{17,25},{25,17},{2,10},{10... | collective-permute-start | bytes 9437192 | tf_op jit(solution)/shard_map/while/body/ppermute | solution.py:413
  68.4 3.6 %collective-permute-start.8 = (f32[3,16,64,128]{3,2,1,0:T(8,128)}, f32[3,16,64,128]{3,2,1,0:T(8,128)S(1)}, u32[]{:S(2)}, u32[]{:S(2)}) collective-permute-start(f32[3,16,64,128]{3,2,1,0:T(8,128)} %get-tuple-element.812.far.refs_1_.refs_5_), channel_id=1, source_target_pairs={{0,8},{8,0},{16,24},{24,16},{1,9},{9,1},{17,25},{25,17},{2,10},{10... | collective-permute-start | bytes 4718600 | tf_op jit(solution)/shard_map/while/body/ppermute | solution.py:413
  72.0 8.1 %copy-start.1 = (f32[3,16,128,128]{3,2,1,0:T(8,128)S(1)}, f32[3,16,128,128]{3,2,1,0:T(8,128)}, u32[]{:S(2)}) copy-start(f32[3,16,128,128]{3,2,1,0:T(8,128)} %get-tuple-element.958.own.refs_0_.refs_4_) | copy-start | bytes 9437188 | tf_op jit(solution)/shard_map/while
  72.0 8.1 %copy-start.4 = (bf16[3,512,256]{2,1,0:T(8,128)(2,1)S(1)}, bf16[3,512,256]{2,1,0:T(8,128)(2,1)}, u32[]{:S(2)}) copy-start(bf16[3,512,256]{2,1,0:T(8,128)(2,1)} %get-tuple-element.960.high.refs_8_) | copy-start | bytes 2359300 | tf_op jit(solution)/shard_map/while
  72.0 8.1 %copy-start.6 = (bf16[3,512,256]{2,1,0:T(8,128)(2,1)S(1)}, bf16[3,512,256]{2,1,0:T(8,128)(2,1)}, u32[]{:S(2)}) copy-start(bf16[3,512,256]{2,1,0:T(8,128)(2,1)} %get-tuple-element.961.low.refs_9_) | copy-start | bytes 2359300 | tf_op jit(solution)/shard_map/while
  75.4 9.8 %collective-permute-start.10 = (f32[3,64,256]{2,1,0:T(8,128)S(1)}, f32[3,64,256]{2,1,0:T(8,128)S(1)}, u32[]{:S(2)}, u32[]{:S(2)}) collective-permute-start(f32[3,64,256]{2,1,0:T(8,128)S(1)} %get-tuple-element.814), channel_id=1, source_target_pairs={{0,1},{1,2},{2,3},{3,4},{4,5},{5,6},{6,7},{7,0},{8,9},{9,10},{10,1... | collective-permute-start | bytes 589832 | tf_op jit(solution)/shard_map/while/body/ppermute | solution.py:429
  75.9 10.9 %copy-start.9 = (f32[2048,128]{1,0:T(8,128)S(1)}, f32[2048,128]{1,0:T(8,128)}, u32[]{:S(2)}) copy-start(f32[2048,128]{1,0:T(8,128)} %get-tuple-element.962.refs_3_) | copy-start | bytes 3145732 | tf_op jit(solution)/shard_map/while
  75.9 10.9 %copy-start.12 = (f32[2056,128]{1,0:T(8,128)S(1)}, f32[2056,128]{1,0:T(8,128)}, u32[]{:S(2)}) copy-start(f32[2056,128]{1,0:T(8,128)} %get-tuple-element.963.refs_4_) | copy-start | bytes 3158020 | tf_op jit(solution)/shard_map/while
  75.9 10.9 %collective-permute-start.9 = (f32[3,64,256]{2,1,0:T(8,128)S(1)}, f32[3,64,256]{2,1,0:T(8,128)S(1)}, u32[]{:S(2)}, u32[]{:S(2)}) collective-permute-start(f32[3,64,256]{2,1,0:T(8,128)S(1)} %get-tuple-element.813), channel_id=1, source_target_pairs={{1,0},{2,1},{3,2},{4,3},{5,4},{6,5},{7,6},{0,7},{9,8},{10,9},{11,1... | collective-permute-start | bytes 589832 | tf_op jit(solution)/shard_map/while/body/ppermute | solution.py:429
  87.5 5.9 %collective-permute-start.11 = (f32[3,16,64,256]{3,2,1,0:T(8,128)S(1)}, f32[3,16,64,256]{3,2,1,0:T(8,128)}, u32[]{:S(2)}, u32[]{:S(2)}) collective-permute-start(f32[3,16,64,256]{3,2,1,0:T(8,128)S(1)} %second_stencil_0.1.own), channel_id=1, source_target_pairs={{0,8},{8,0},{16,24},{24,16},{1,9},{9,1},{17,25},{25,17},{2,10},{10... | collective-permute-start | bytes 9437192 | tf_op jit(solution)/shard_map/while/body/ppermute | solution.py:413
  99.4 44.5 %collective-permute-start.19 = (f32[3,16,64,128]{3,2,1,0:T(8,128)}, f32[3,16,64,128]{3,2,1,0:T(8,128)}, u32[]{:S(2)}, u32[]{:S(2)}) collective-permute-start(f32[3,16,64,128]{3,2,1,0:T(8,128)} %get-tuple-element.353), channel_id=1, source_target_pairs={{0,16},{8,24},{16,0},{24,8},{1,17},{9,25},{17,1},{25,9},{2,18},{10... | collective-permute-start | bytes 4718600 | tf_op jit(solution)/shard_map/ppermute | solution.py:410
  100.9 3.6 %collective-permute-start.12 = (f32[3,16,64,128]{3,2,1,0:T(8,128)}, f32[3,16,64,128]{3,2,1,0:T(8,128)S(1)}, u32[]{:S(2)}, u32[]{:S(2)}) collective-permute-start(f32[3,16,64,128]{3,2,1,0:T(8,128)} %get-tuple-element.827.far.refs_1_.refs_5_), channel_id=1, source_target_pairs={{0,8},{8,0},{16,24},{24,16},{1,9},{9,1},{17,25},{25,17},{2,10},{10... | collective-permute-start | bytes 4718600 | tf_op jit(solution)/shard_map/while/body/ppermute | solution.py:413
  104.5 6.6 %copy-start.2 = (f32[3,16,128,128]{3,2,1,0:T(8,128)S(1)}, f32[3,16,128,128]{3,2,1,0:T(8,128)}, u32[]{:S(2)}) copy-start(f32[3,16,128,128]{3,2,1,0:T(8,128)} %get-tuple-element.1012.own.refs_0_.refs_4_) | copy-start | bytes 9437188 | tf_op jit(solution)/shard_map/while
  104.5 6.6 %copy-start.5 = (bf16[3,512,256]{2,1,0:T(8,128)(2,1)S(1)}, bf16[3,512,256]{2,1,0:T(8,128)(2,1)}, u32[]{:S(2)}) copy-start(bf16[3,512,256]{2,1,0:T(8,128)(2,1)} %get-tuple-element.1014.high.refs_8_) | copy-start | bytes 2359300 | tf_op jit(solution)/shard_map/while
  104.6 6.6 %copy-start.7 = (bf16[3,512,256]{2,1,0:T(8,128)(2,1)S(1)}, bf16[3,512,256]{2,1,0:T(8,128)(2,1)}, u32[]{:S(2)}) copy-start(bf16[3,512,256]{2,1,0:T(8,128)(2,1)} %get-tuple-element.1015.low.refs_9_) | copy-start | bytes 2359300 | tf_op jit(solution)/shard_map/while
  107.9 7.9 %collective-permute-start.13 = (f32[3,64,256]{2,1,0:T(8,128)S(1)}, f32[3,64,256]{2,1,0:T(8,128)S(1)}, u32[]{:S(2)}, u32[]{:S(2)}) collective-permute-start(f32[3,64,256]{2,1,0:T(8,128)S(1)} %get-tuple-element.828), channel_id=1, source_target_pairs={{1,0},{2,1},{3,2},{4,3},{5,4},{6,5},{7,6},{0,7},{9,8},{10,9},{11,1... | collective-permute-start | bytes 589832 | tf_op jit(solution)/shard_map/while/body/ppermute | solution.py:429
  111.1 9.4 %copy-start.10 = (f32[2048,128]{1,0:T(8,128)S(1)}, f32[2048,128]{1,0:T(8,128)}, u32[]{:S(2)}) copy-start(f32[2048,128]{1,0:T(8,128)} %get-tuple-element.1016.refs_3_) | copy-start | bytes 3145732 | tf_op jit(solution)/shard_map/while
  111.1 9.4 %copy-start.13 = (f32[2056,128]{1,0:T(8,128)S(1)}, f32[2056,128]{1,0:T(8,128)}, u32[]{:S(2)}) copy-start(f32[2056,128]{1,0:T(8,128)} %get-tuple-element.1017.refs_4_) | copy-start | bytes 3158020 | tf_op jit(solution)/shard_map/while
  111.1 9.4 %collective-permute-start.14 = (f32[3,64,256]{2,1,0:T(8,128)S(1)}, f32[3,64,256]{2,1,0:T(8,128)S(1)}, u32[]{:S(2)}, u32[]{:S(2)}) collective-permute-start(f32[3,64,256]{2,1,0:T(8,128)S(1)} %get-tuple-element.829), channel_id=1, source_target_pairs={{0,1},{1,2},{2,3},{3,4},{4,5},{5,6},{6,7},{7,0},{8,9},{9,10},{10,1... | collective-permute-start | bytes 589832 | tf_op jit(solution)/shard_map/while/body/ppermute | solution.py:429
  121.3 5.9 %collective-permute-start.15 = (f32[3,16,64,256]{3,2,1,0:T(8,128)S(1)}, f32[3,16,64,256]{3,2,1,0:T(8,128)}, u32[]{:S(2)}, u32[]{:S(2)}) collective-permute-start(f32[3,16,64,256]{3,2,1,0:T(8,128)S(1)} %second_stencil_1.1.own), channel_id=1, source_target_pairs={{0,8},{8,0},{16,24},{24,16},{1,9},{9,1},{17,25},{25,17},{2,10},{10... | collective-permute-start | bytes 9437192 | tf_op jit(solution)/shard_map/while/body/ppermute | solution.py:413
  133.4 9.4 %collective-permute-start.26 = (f32[1,8,64,128]{3,2,1,0:T(8,128)}, f32[1,8,64,128]{3,2,1,0:T(8,128)S(1)}, u32[]{:S(2)}, u32[]{:S(2)}) collective-permute-start(f32[1,8,64,128]{3,2,1,0:T(8,128)} %get-tuple-element.369), channel_id=1, source_target_pairs={{0,16},{8,24},{16,0},{24,8},{1,17},{9,25},{17,1},{25,9},{2,18},{10... | collective-permute-start | bytes 786440 | tf_op jit(solution)/shard_map/ppermute | solution.py:410
  134.5 18.3 %collective-permute-start.25 = (f32[1,8,64,128]{3,2,1,0:T(8,128)}, f32[1,8,64,128]{3,2,1,0:T(8,128)S(1)}, u32[]{:S(2)}, u32[]{:S(2)}) collective-permute-start(f32[1,8,64,128]{3,2,1,0:T(8,128)} %get-tuple-element.368), channel_id=1, source_target_pairs={{0,16},{8,24},{16,0},{24,8},{1,17},{9,25},{17,1},{25,9},{2,18},{10... | collective-permute-start | bytes 786440 | tf_op jit(solution)/shard_map/ppermute | solution.py:410
  135.5 19.9 %collective-permute-start.24 = (f32[1,8,64,128]{3,2,1,0:T(8,128)}, f32[1,8,64,128]{3,2,1,0:T(8,128)S(1)}, u32[]{:S(2)}, u32[]{:S(2)}) collective-permute-start(f32[1,8,64,128]{3,2,1,0:T(8,128)} %get-tuple-element.367), channel_id=1, source_target_pairs={{0,16},{8,24},{16,0},{24,8},{1,17},{9,25},{17,1},{25,9},{2,18},{10... | collective-permute-start | bytes 786440 | tf_op jit(solution)/shard_map/ppermute | solution.py:410
  136.6 23.1 %collective-permute-start.23 = (f32[1,8,64,128]{3,2,1,0:T(8,128)}, f32[1,8,64,128]{3,2,1,0:T(8,128)S(1)}, u32[]{:S(2)}, u32[]{:S(2)}) collective-permute-start(f32[1,8,64,128]{3,2,1,0:T(8,128)} %get-tuple-element.366), channel_id=1, source_target_pairs={{0,16},{8,24},{16,0},{24,8},{1,17},{9,25},{17,1},{25,9},{2,18},{10... | collective-permute-start | bytes 786440 | tf_op jit(solution)/shard_map/ppermute | solution.py:410
  142.8 22.5 %collective-permute-start.22 = (f32[1,8,64,128]{3,2,1,0:T(8,128)}, f32[1,8,64,128]{3,2,1,0:T(8,128)S(1)}, u32[]{:S(2)}, u32[]{:S(2)}) collective-permute-start(f32[1,8,64,128]{3,2,1,0:T(8,128)} %get-tuple-element.365), channel_id=1, source_target_pairs={{0,16},{8,24},{16,0},{24,8},{1,17},{9,25},{17,1},{25,9},{2,18},{10... | collective-permute-start | bytes 786440 | tf_op jit(solution)/shard_map/ppermute | solution.py:410
  143.9 26.2 %collective-permute-start.21 = (f32[1,8,64,128]{3,2,1,0:T(8,128)}, f32[1,8,64,128]{3,2,1,0:T(8,128)S(1)}, u32[]{:S(2)}, u32[]{:S(2)}) collective-permute-start(f32[1,8,64,128]{3,2,1,0:T(8,128)} %get-tuple-element.364), channel_id=1, source_target_pairs={{0,16},{8,24},{16,0},{24,8},{1,17},{9,25},{17,1},{25,9},{2,18},{10... | collective-permute-start | bytes 786440 | tf_op jit(solution)/shard_map/ppermute | solution.py:410
